TPU v7x, 32 devices: a whole 2x2x4 slice. The times are simulated.
32 devices in a mesh: seq: 4 (over x, core), fsdp: 8 (over z, y).
Axes of the slice: x: 2, y: 2, z: 4, core: 2. Of those that a mesh axis runs over, the one named last changes fastest.
Arguments:
- tokens: bfloat16 [8, 2048, 1024], P('fsdp', 'seq'), may hold values from -6 to 6
- lengths: int32 [8], P('fsdp'), may hold values from 512 to 2048, as said below
- state_init: bfloat16 [8, 512, 1024], P('fsdp', None, 'seq'), may hold values from -6 to 6
- w_qkv: bfloat16 [1024, 3072], P('fsdp'), may hold values from -0.1875 to 0.1875
- w_out: bfloat16 [1024, 1024], P('fsdp'), may hold values from -1 to 1
- w_up: bfloat16 [1024, 4096], P('fsdp'), may hold values from -0.1875 to 0.1875
- w_down: bfloat16 [4096, 1024], P('fsdp'), may hold values from -0.09375 to 0.09375
- norm_attn: bfloat16 [1024], P('fsdp'), may hold values from 0.099609375 to 1.8984375
- norm_mlp: bfloat16 [1024], P('fsdp'), may hold values from 0.099609375 to 1.8984375
- rel_bias: float32 [8, 32], P('seq'), may hold values from -4 to 4
- state_query: bfloat16 [8, 128, 128], P('seq'), may hold values from -0.5 to 0.5
- gate_bias: float32 [8, 128], P('seq'), may hold values from -1 to 4
- out_grad: bfloat16 [8, 2048, 1024], P('fsdp', 'seq'), may hold values from -6 to 6
- state_grad: bfloat16 [8, 512, 1024], P('fsdp', None, 'seq'), may hold values from -6 to 6
Outputs:
- output: bfloat16 [8, 2048, 1024], P('fsdp', 'seq')
- final_state: float32 [8, 512, 1024], P('fsdp', None, 'seq')
- tokens_grad: float32 [8, 2048, 1024], P('fsdp', 'seq')
- w_qkv_grad: float32 [1024, 3072], P(('seq', 'fsdp'))
- w_out_grad: float32 [1024, 1024], P(('seq', 'fsdp'))
- w_up_grad: float32 [1024, 4096], P(('seq', 'fsdp'))
- w_down_grad: float32 [4096, 1024], P(('seq', 'fsdp'))
- norm_attn_grad: float32 [1024], P(('seq', 'fsdp'))
- norm_mlp_grad: float32 [1024], P(('seq', 'fsdp'))
- rel_bias_grad: float32 [8, 32], P('seq')
- state_query_grad: float32 [8, 128, 128], P('seq')
- gate_bias_grad: float32 [8, 128], P('seq')
Inputs may be any that keep to these rules, and one draw needn't show every extreme that they name: `lengths`: used positions of each slot; some slot is full, with 2048.
All inputs are finite; a program needn't handle non-finite values.
Results may differ from a plain program's by a relative error of at most 0.018.
Values may be sent and summed in bfloat16 or wider, within the bound.
A program may use at most 256 MiB of HBM per device.

v0:
```python
import jax
import jax.numpy as jnp
from jax import lax
from jax.sharding import PartitionSpec as P

H = 8
DH = 128
WINDOW_LENGTH = 512
STATE_VECTORS = 512


EPSILON = 1e-06
BUCKET_EDGES = (19, 21, 24, 27, 31, 35, 40, 46, 52, 59, 67, 77, 87, 99, 113)


def rms_norm(values, gain):
    return values * lax.rsqrt(jnp.mean(values * values, axis=-1, keepdims=True) + EPSILON) * gain


def softmax_rows(scores):
    row_max = jnp.max(scores, axis=-1, keepdims=True)
    expanded = jnp.exp(scores - row_max)
    return expanded / jnp.sum(expanded, axis=-1, keepdims=True)


def smooth_gate(values):
    return jax.nn.gelu(values, approximate=False)


def bucket_table():
    row_index = jnp.arange(WINDOW_LENGTH, dtype=jnp.int32)[:, None]
    col_index = jnp.arange(2 * WINDOW_LENGTH, dtype=jnp.int32)[None, :]
    distance = row_index + WINDOW_LENGTH - col_index
    clipped = jnp.clip(distance, 0, WINDOW_LENGTH)
    bucket_edges = jnp.array(BUCKET_EDGES, dtype=jnp.int32)
    bucket = jnp.minimum(clipped, 16) + jnp.sum(
        (clipped[:, :, None] >= bucket_edges).astype(jnp.int32), axis=-1
    )
    window = (distance >= 0) & (distance < WINDOW_LENGTH)
    return (bucket, window)


def head_bias(table, bucket):
    total = jnp.zeros((table.shape[0],) + bucket.shape, jnp.float32)
    for bucket_id in range(32):
        total = jnp.where((bucket == bucket_id)[None], table[:, bucket_id][:, None, None], total)
    return total


def table_grad(accumulated, bucket):
    columns = [
        jnp.sum(jnp.where((bucket == bucket_id)[None], accumulated, 0.0), axis=(1, 2))
        for bucket_id in range(32)
    ]
    return jnp.stack(columns, axis=1)


def block_pass(
    query_rows,
    key_ctx,
    context_value,
    memory,
    window,
    key_live,
    bias_window,
    query_weight,
    forget,
    live_flag,
    score_scale,
):
    block_width = query_rows.shape[0]
    memory_slots = memory.shape[0]
    lowered_memory = memory.astype(jnp.bfloat16)
    allowed = window & key_live[None, :]
    score_ctx = (
        jnp.einsum("qhd,khd->hqk", query_rows, key_ctx, preferred_element_type=jnp.float32)
        * score_scale
        + bias_window
    )
    score_ctx = jnp.where(allowed[None], score_ctx, -jnp.inf)
    memory_scores = (
        jnp.einsum("rub,yub->ury", query_rows, lowered_memory, preferred_element_type=jnp.float32)
        * score_scale
    )
    probabilities = softmax_rows(jnp.concatenate([score_ctx, memory_scores], axis=-1))
    lowered_probabilities = probabilities.astype(jnp.bfloat16)
    attended_output = jnp.einsum(
        "zvx,xzs->vzs",
        lowered_probabilities[:, :, : 2 * block_width],
        context_value,
        preferred_element_type=jnp.float32,
    )
    attended_output = attended_output + jnp.einsum(
        "rnf,fro->nro",
        lowered_probabilities[:, :, 2 * block_width :],
        lowered_memory,
        preferred_element_type=jnp.float32,
    )
    state_query_rows = jnp.einsum(
        "czy,zyg->czg", lowered_memory, query_weight, preferred_element_type=jnp.float32
    ).astype(jnp.bfloat16)
    current_key = key_ctx[block_width:]
    current_value = context_value[block_width:]
    self_scores = (
        jnp.einsum(
            "rtf,jtf->trj", state_query_rows, lowered_memory, preferred_element_type=jnp.float32
        )
        * score_scale
    )
    cross_scores = (
        jnp.einsum(
            "ecw,ycw->cey", state_query_rows, current_key, preferred_element_type=jnp.float32
        )
        * score_scale
    )
    cross_scores = jnp.where(key_live[block_width:][None, None, :], cross_scores, -jnp.inf)
    state_probabilities = softmax_rows(jnp.concatenate([self_scores, cross_scores], axis=-1))
    lowered_state = state_probabilities.astype(jnp.bfloat16)
    state_update = jnp.einsum(
        "rle,erv->lrv",
        lowered_state[:, :, :memory_slots],
        lowered_memory,
        preferred_element_type=jnp.float32,
    )
    state_update = state_update + jnp.einsum(
        "owg,goa->woa",
        lowered_state[:, :, memory_slots:],
        current_value,
        preferred_element_type=jnp.float32,
    )
    new_memory = jnp.where(live_flag, forget * memory + (1.0 - forget) * state_update, memory)
    return (
        attended_output,
        new_memory,
        probabilities,
        lowered_probabilities,
        state_query_rows,
        state_probabilities,
        lowered_state,
        state_update,
        lowered_memory,
    )


def block_back(
    query_rows,
    key_ctx,
    context_value,
    memory,
    window,
    key_live,
    bias_window,
    query_weight,
    forget,
    live_flag,
    score_scale,
    output_gradient,
    grad_memory,
):
    block_width = query_rows.shape[0]
    block_extent = key_ctx.shape[0]
    memory_slots = memory.shape[0]
    pieces = block_pass(
        query_rows,
        key_ctx,
        context_value,
        memory,
        window,
        key_live,
        bias_window,
        query_weight,
        forget,
        live_flag,
        score_scale,
    )
    (
        probabilities,
        lowered_probabilities,
        state_query_rows,
        state_probabilities,
        lowered_state,
        state_update,
        lowered_memory,
    ) = pieces[2:]
    current_key = key_ctx[block_width:]
    current_value = context_value[block_width:]
    update_gradient = jnp.where(live_flag, (1.0 - forget) * grad_memory, 0.0).astype(jnp.bfloat16)
    grad_forget = jnp.where(live_flag, jnp.sum(grad_memory * (memory - state_update), axis=0), 0.0)
    carry_memory = jnp.where(live_flag, forget * grad_memory, grad_memory)
    grad_sprob = jnp.concatenate(
        [
            jnp.einsum(
                "rtf,jtf->trj", update_gradient, lowered_memory, preferred_element_type=jnp.float32
            ),
            jnp.einsum(
                "ecw,ycw->cey", update_gradient, current_value, preferred_element_type=jnp.float32
            ),
        ],
        axis=-1,
    )
    grad_memlow = jnp.einsum(
        "kut,uki->tki",
        lowered_state[:, :, :memory_slots],
        update_gradient,
        preferred_element_type=jnp.float32,
    )
    grad_value_mem = jnp.einsum(
        "vyt,yvi->tvi",
        lowered_state[:, :, memory_slots:],
        update_gradient,
        preferred_element_type=jnp.float32,
    )
    grad_sscore = (
        state_probabilities
        * (grad_sprob - jnp.sum(grad_sprob * state_probabilities, axis=-1, keepdims=True))
    ).astype(jnp.bfloat16)
    state_query_gradient = jnp.einsum(
        "rle,erv->lrv",
        grad_sscore[:, :, :memory_slots],
        lowered_memory,
        preferred_element_type=jnp.float32,
    )
    state_query_gradient = (
        (
            state_query_gradient
            + jnp.einsum(
                "owg,goa->woa",
                grad_sscore[:, :, memory_slots:],
                current_key,
                preferred_element_type=jnp.float32,
            )
        )
        * score_scale
    ).astype(jnp.bfloat16)
    grad_memlow = (
        grad_memlow
        + jnp.einsum(
            "kut,uki->tki",
            grad_sscore[:, :, :memory_slots],
            state_query_rows,
            preferred_element_type=jnp.float32,
        )
        * score_scale
    )
    grad_key_mem = (
        jnp.einsum(
            "vyt,yvi->tvi",
            grad_sscore[:, :, memory_slots:],
            state_query_rows,
            preferred_element_type=jnp.float32,
        )
        * score_scale
    )
    grad_map = jnp.einsum(
        "tvf,tvj->vfj", lowered_memory, state_query_gradient, preferred_element_type=jnp.float32
    )
    grad_memlow = grad_memlow + jnp.einsum(
        "ifg,ftg->ift", state_query_gradient, query_weight, preferred_element_type=jnp.float32
    )
    grad_prob = jnp.concatenate(
        [
            jnp.einsum(
                "qhd,khd->hqk", output_gradient, context_value, preferred_element_type=jnp.float32
            ),
            jnp.einsum(
                "rub,yub->ury", output_gradient, lowered_memory, preferred_element_type=jnp.float32
            ),
        ],
        axis=-1,
    )
    grad_value_ctx = jnp.einsum(
        "hqk,qhd->khd",
        lowered_probabilities[:, :, :block_extent],
        output_gradient,
        preferred_element_type=jnp.float32,
    )
    grad_memlow = grad_memlow + jnp.einsum(
        "ojg,joa->goa",
        lowered_probabilities[:, :, block_extent:],
        output_gradient,
        preferred_element_type=jnp.float32,
    )
    lowered_gradient = (
        probabilities * (grad_prob - jnp.sum(grad_prob * probabilities, axis=-1, keepdims=True))
    ).astype(jnp.bfloat16)
    grad_bias = lowered_gradient[:, :, :block_extent].astype(jnp.float32)
    grad_query = jnp.einsum(
        "zvx,xzs->vzs",
        lowered_gradient[:, :, :block_extent],
        key_ctx,
        preferred_element_type=jnp.float32,
    )
    grad_query = (
        grad_query
        + jnp.einsum(
            "rnf,fro->nro",
            lowered_gradient[:, :, block_extent:],
            lowered_memory,
            preferred_element_type=jnp.float32,
        )
    ) * score_scale
    grad_key_ctx = (
        jnp.einsum(
            "hqk,qhd->khd",
            lowered_gradient[:, :, :block_extent],
            query_rows,
            preferred_element_type=jnp.float32,
        )
        * score_scale
    )
    grad_memlow = (
        grad_memlow
        + jnp.einsum(
            "ojg,joa->goa",
            lowered_gradient[:, :, block_extent:],
            query_rows,
            preferred_element_type=jnp.float32,
        )
        * score_scale
    )
    return (
        grad_query,
        grad_key_ctx,
        grad_value_ctx,
        grad_key_mem,
        grad_value_mem,
        grad_map,
        grad_forget,
        grad_bias,
        carry_memory + grad_memlow,
    )


def split_blocks(head_rows, blocks):
    local_heads = head_rows.shape[2]
    query_rows = head_rows[:, 0].reshape(blocks, WINDOW_LENGTH, local_heads, DH)
    keys_all = head_rows[:, 1].reshape(blocks, WINDOW_LENGTH, local_heads, DH)
    values_all = head_rows[:, 2].reshape(blocks, WINDOW_LENGTH, local_heads, DH)
    zero_block = jnp.zeros((1, WINDOW_LENGTH, local_heads, DH), jnp.bfloat16)
    key_prev = jnp.concatenate([zero_block, keys_all[:-1]], axis=0)
    value_prev = jnp.concatenate([zero_block, values_all[:-1]], axis=0)
    return (query_rows, keys_all, values_all, key_prev, value_prev)


def body(
    tokens,
    lengths,
    state_init,
    w_qkv,
    w_out,
    w_up,
    w_down,
    norm_attn,
    norm_mlp,
    rel_bias,
    state_query,
    gate_bias,
    out_grad,
    state_grad,
):
    seq_count = lax.axis_size("seq")
    local_heads = H // seq_count
    tok_rows = tokens.shape[1]
    slot_rows = tok_rows * seq_count
    blocks = slot_rows // WINDOW_LENGTH
    score_scale = DH ** (-0.5)
    length_now = lengths[0]
    positions = lax.axis_index("seq") * tok_rows + jnp.arange(tok_rows, dtype=jnp.int32)
    row_live = (positions < length_now).astype(jnp.float32)[:, None]
    inputs = tokens[0].astype(jnp.float32)
    full_qkv, full_out, full_up, full_down, gain_attn_low, gain_mlp_low = (
        lax.all_gather(w_qkv, "fsdp", axis=0, tiled=True),
        lax.all_gather(w_out, "fsdp", axis=0, tiled=True),
        lax.all_gather(w_up, "fsdp", axis=0, tiled=True),
        lax.all_gather(w_down, "fsdp", axis=0, tiled=True),
        lax.all_gather(norm_attn, "fsdp", axis=0, tiled=True),
        lax.all_gather(norm_mlp, "fsdp", axis=0, tiled=True),
    )
    gain_attn = gain_attn_low.astype(jnp.float32)
    gain_mlp = gain_mlp_low.astype(jnp.float32)
    normed = rms_norm(inputs, gain_attn).astype(jnp.bfloat16)
    projected = (
        jnp.dot(normed, full_qkv, preferred_element_type=jnp.float32)
        .astype(jnp.bfloat16)
        .reshape(tok_rows, 3, H, DH)
    )
    head_rows = lax.all_to_all(projected, "seq", split_axis=2, concat_axis=0, tiled=True)
    bucket, window = bucket_table()
    bias_window = head_bias(rel_bias, bucket)
    forget = jax.nn.sigmoid(gate_bias)
    memory_start = state_init[0].astype(jnp.float32).reshape(STATE_VECTORS, local_heads, DH)
    starts = jnp.arange(blocks, dtype=jnp.int32) * WINDOW_LENGTH

    def context(start):
        key_pos = start - WINDOW_LENGTH + jnp.arange(2 * WINDOW_LENGTH, dtype=jnp.int32)
        return ((key_pos >= 0) & (key_pos < length_now), start < length_now)

    def forward_step(memory, block_inputs):
        query_rows, current_key, current_value, key_prev, value_prev, start = block_inputs
        key_live, live_flag = context(start)
        pieces = block_pass(
            query_rows,
            jnp.concatenate([key_prev, current_key], axis=0),
            jnp.concatenate([value_prev, current_value], axis=0),
            memory,
            window,
            key_live,
            bias_window,
            state_query,
            forget,
            live_flag,
            score_scale,
        )
        return (pieces[1], (pieces[0].astype(jnp.bfloat16), memory))

    queries_f, keys_f, values_f, key_prev_f, value_prev_f = split_blocks(head_rows, blocks)
    final_memory, (attended_output, kept_memory) = lax.scan(
        forward_step, memory_start, (queries_f, keys_f, values_f, key_prev_f, value_prev_f, starts)
    )
    attended_tokens = lax.all_to_all(
        attended_output.reshape(slot_rows, local_heads, DH),
        "seq",
        split_axis=0,
        concat_axis=1,
        tiled=True,
    ).reshape(tok_rows, H * DH)
    mid = inputs + jnp.dot(attended_tokens, full_out, preferred_element_type=jnp.float32)
    normed_mid = rms_norm(mid, gain_mlp).astype(jnp.bfloat16)
    hidden_pre = jnp.dot(normed_mid, full_up, preferred_element_type=jnp.float32)
    hidden = smooth_gate(hidden_pre).astype(jnp.bfloat16)
    mlp_out = jnp.dot(hidden, full_down, preferred_element_type=jnp.float32)
    output = (row_live * (mid + mlp_out)).astype(jnp.bfloat16)[None]
    grad_rows = out_grad[0].astype(jnp.float32) * row_live
    grad_mlp = grad_rows.astype(jnp.bfloat16)
    grad_down = jnp.einsum("tf,td->fd", hidden, grad_mlp, preferred_element_type=jnp.float32)
    grad_hidden = jnp.einsum("td,fd->tf", grad_mlp, full_down, preferred_element_type=jnp.float32)
    gelu_value, gelu_back = jax.vjp(smooth_gate, hidden_pre)
    grad_pre = gelu_back(grad_hidden)[0].astype(jnp.bfloat16)
    grad_up = jnp.einsum("td,tf->df", normed_mid, grad_pre, preferred_element_type=jnp.float32)
    grad_normed_mid = jnp.einsum("tf,df->td", grad_pre, full_up, preferred_element_type=jnp.float32)
    norm_value, mlp_norm_back = jax.vjp(rms_norm, mid, gain_mlp)
    grad_mid_norm, grad_gain_mlp = mlp_norm_back(grad_normed_mid)
    grad_mid = grad_rows + grad_mid_norm
    grad_branch = grad_mid.astype(jnp.bfloat16)
    grad_out_w = jnp.einsum(
        "tc,td->cd", attended_tokens, grad_branch, preferred_element_type=jnp.float32
    )
    grad_attended = (
        jnp.einsum("td,cd->tc", grad_branch, full_out, preferred_element_type=jnp.float32)
        .astype(jnp.bfloat16)
        .reshape(tok_rows, H, DH)
    )
    grad_heads = lax.all_to_all(grad_attended, "seq", split_axis=1, concat_axis=0, tiled=True)
    normed_again = rms_norm(inputs, gain_attn).astype(jnp.bfloat16)
    projected_again = (
        jnp.dot(normed_again, full_qkv, preferred_element_type=jnp.float32)
        .astype(jnp.bfloat16)
        .reshape(tok_rows, 3, H, DH)
    )
    head_again = lax.all_to_all(projected_again, "seq", split_axis=2, concat_axis=0, tiled=True)
    queries_b, keys_b, values_b, key_prev_b, value_prev_b = split_blocks(head_again, blocks)
    grad_blocks = grad_heads.reshape(blocks, WINDOW_LENGTH, local_heads, DH)

    def backward_step(carry, block_inputs):
        (
            grad_memory,
            grad_key_next,
            grad_value_next,
            grad_map_sum,
            grad_forget_sum,
            grad_bias_sum,
        ) = carry
        (
            query_rows,
            current_key,
            current_value,
            key_prev,
            value_prev,
            start,
            memory,
            output_gradient,
        ) = block_inputs
        key_live, live_flag = context(start)
        results = block_back(
            query_rows,
            jnp.concatenate([key_prev, current_key], axis=0),
            jnp.concatenate([value_prev, current_value], axis=0),
            memory,
            window,
            key_live,
            bias_window,
            state_query,
            forget,
            live_flag,
            score_scale,
            output_gradient,
            grad_memory,
        )
        (
            grad_query,
            grad_key_ctx,
            grad_value_ctx,
            grad_key_mem,
            grad_value_mem,
            grad_map,
            grad_forget,
            grad_bias,
            grad_memory_prev,
        ) = results
        key_total = grad_key_ctx[WINDOW_LENGTH:] + grad_key_mem + grad_key_next
        value_total = grad_value_ctx[WINDOW_LENGTH:] + grad_value_mem + grad_value_next
        new_carry = (
            grad_memory_prev,
            grad_key_ctx[:WINDOW_LENGTH],
            grad_value_ctx[:WINDOW_LENGTH],
            grad_map_sum + grad_map,
            grad_forget_sum + grad_forget,
            grad_bias_sum + grad_bias,
        )
        return (new_carry, (grad_query, key_total, value_total))

    zero_rows = jnp.zeros((WINDOW_LENGTH, local_heads, DH), jnp.float32)
    carry_start = (
        state_grad[0].astype(jnp.float32).reshape(STATE_VECTORS, local_heads, DH),
        zero_rows,
        zero_rows,
        jnp.zeros((local_heads, DH, DH), jnp.float32),
        jnp.zeros((local_heads, DH), jnp.float32),
        jnp.zeros((local_heads, WINDOW_LENGTH, 2 * WINDOW_LENGTH), jnp.float32),
    )
    carry_end, (grad_q, grad_k, grad_v) = lax.scan(
        backward_step,
        carry_start,
        (queries_b, keys_b, values_b, key_prev_b, value_prev_b, starts, kept_memory, grad_blocks),
        reverse=True,
    )
    grad_qkv_heads = jnp.stack(
        [
            grad_q.reshape(slot_rows, local_heads, DH),
            grad_k.reshape(slot_rows, local_heads, DH),
            grad_v.reshape(slot_rows, local_heads, DH),
        ],
        axis=1,
    ).astype(jnp.bfloat16)
    grad_qkv = lax.all_to_all(
        grad_qkv_heads, "seq", split_axis=0, concat_axis=2, tiled=True
    ).reshape(tok_rows, 3 * H * DH)
    grad_qkv_w = jnp.einsum("tc,tk->ck", normed_again, grad_qkv, preferred_element_type=jnp.float32)
    grad_normed = jnp.einsum("tk,ck->tc", grad_qkv, full_qkv, preferred_element_type=jnp.float32)
    attn_value, attn_norm_back = jax.vjp(rms_norm, inputs, gain_attn)
    grad_in_norm, grad_gain_attn = attn_norm_back(grad_normed)
    tokens_grad = (grad_mid + grad_in_norm)[None]
    grad_gate = carry_end[4] * forget * (1.0 - forget)
    grad_table = table_grad(carry_end[5], bucket)
    head_sums = (
        lax.psum(carry_end[3].astype(jnp.bfloat16), "fsdp").astype(jnp.float32),
        lax.psum(grad_gate.astype(jnp.bfloat16), "fsdp").astype(jnp.float32),
        lax.psum(grad_table.astype(jnp.bfloat16), "fsdp").astype(jnp.float32),
    )
    weight_terms = (grad_qkv_w, grad_out_w, grad_up, grad_down, grad_gain_attn, grad_gain_mlp)
    weight_parts = (
        lax.psum_scatter(weight_terms[0], ("seq", "fsdp"), scatter_dimension=0, tiled=True),
        lax.psum_scatter(weight_terms[1], ("seq", "fsdp"), scatter_dimension=0, tiled=True),
        lax.psum_scatter(weight_terms[2], ("seq", "fsdp"), scatter_dimension=0, tiled=True),
        lax.psum_scatter(weight_terms[3], ("seq", "fsdp"), scatter_dimension=0, tiled=True),
        lax.psum_scatter(weight_terms[4], ("seq", "fsdp"), scatter_dimension=0, tiled=True),
        lax.psum_scatter(weight_terms[5], ("seq", "fsdp"), scatter_dimension=0, tiled=True),
    )
    final_state = final_memory.reshape(1, STATE_VECTORS, local_heads * DH)
    return (
        output,
        final_state,
        tokens_grad,
        weight_parts[0],
        weight_parts[1],
        weight_parts[2],
        weight_parts[3],
        weight_parts[4],
        weight_parts[5],
        head_sums[2],
        head_sums[0],
        head_sums[1],
    )


def solution(mesh):
    placed = (
        P("fsdp", "seq", None),
        P("fsdp"),
        P("fsdp", None, "seq"),
        P("fsdp", None),
        P("fsdp", None),
        P("fsdp", None),
        P("fsdp", None),
        P("fsdp"),
        P("fsdp"),
        P("seq", None),
        P("seq", None, None),
        P("seq", None),
        P("fsdp", "seq", None),
        P("fsdp", None, "seq"),
    )
    return jax.shard_map(
        body,
        mesh=mesh,
        in_specs=placed,
        out_specs=(
            P("fsdp", "seq", None),
            P("fsdp", None, "seq"),
            P("fsdp", "seq", None),
            P(("seq", "fsdp"), None),
            P(("seq", "fsdp"), None),
            P(("seq", "fsdp"), None),
            P(("seq", "fsdp"), None),
            P(("seq", "fsdp")),
            P(("seq", "fsdp")),
            P("seq", None),
            P("seq", None, None),
            P("seq", None),
        ),
        check_vma=False,
    )
```

profile of v0, /device:TPU:0, one launch (start us, length us, event | category | flops | bytes accessed | tf_op | source)
XLA Modules:
  0.0 2037.3 jit_solution(16021532254036627881)
XLA Ops:
  16.1 22.4 %all-gather = bf16[8,1,128]{2,1,0:T(2,128)(2,1)S(1)} all-gather(bf16[1,1,128]{2,1,0:T(2,128)(2,1)S(1)} %bitcast.589), channel_id=1, replica_groups=mesh['seq'=4,'fsdp'=8] {'fsdp'}, dimensions={0}, use_global_device_ids=true | all-gather | bytes 2304 | tf_op jit(solution)/shard_map/all_gather | solution.py:376
  39.3 4.5 convert_reduce_fusion
  43.8 68.3 %all-gather.7.cloned.1.call-done = bf16[1024,3072]{1,0:T(8,128)(2,1)} async-done(((bf16[128,3072]{1,0:T(8,128)(2,1)}), bf16[1024,3072]{1,0:T(8,128)(2,1)}) %all-gather.7.cloned.1.call-update) | async-done | bytes 6291472 | tf_op jit(solution)/shard_map/all_gather | solution.py:372
  112.0 6.6 fusion.185
  122.0 4.8 all-to-all-start
  126.8 16.1 broadcast_compare_fusion.29
  142.9 20.9 %all-to-all-done = bf16[512,3,8,128]{3,0,1,2:T(8,128)(2,1)} async-done(((bf16[512,3,8,128]{3,0,1,2:T(8,128)(2,1)}), bf16[512,3,8,128]{3,0,1,2:T(8,128)(2,1)}, u32[]{:S(2)}, u32[]{:S(2)}) %all-to-all-start) | async-done | bytes 3145760 | tf_op jit(solution)/shard_map/all_to_all | solution.py:387
  171.7 210.7 %while.48 = (s32[]{:T(128)}, f32[512,2,128]{2,0,1:T(8,128)S(1)}, bf16[4,512,2,128]{3,1,0,2:T(8,128)(2,1)}, f32[4,512,2,128]{3,1,2,0:T(8,128)}, s32[4]{0:T(128)S(...) while((s32[]{:T(128)}, f32[512,2,128]{2,0,1:T(8,128)S(1)}, ...), condition=%wide.region_9.10_spmd.clone, body=%wide.region_2.9_spmd.clone.sunk | while | flops 1441399040 | bytes 95578704 | solution.py:417
  191.1 21.9 %fusion.399 = (f32[2,512]{1,0:T(2,128)S(1)}, f32[2,512,1024]{2,1,0:T(8,128)}) fusion(f32[2]{0:T(128)} %get-tuple-element.4425, pred[512,1024]{1,0:T(8,128)(4,1)} %get-tuple-element.4426, f32[2]{0:T(128)} %get-tuple-element.4427, pred[512,1024]{1,0:T(8,128)(4,1)} %get-tuple-element.4428, f32[2]{0:T(128)S(1)} %get-tuple-element.4429, ...), kind=kOutput, calls=%fused_computation.414.clone.1 | convolution fusion | flops 307231744 | bytes 22294660 | tf_op jit(solution)/shard_map/while/body/eval_jaxpr/qhd,khd->hqk/dot_general | solution.py:76
  213.0 3.7 fusion.400
  244.3 21.8 %fusion.399 = (f32[2,512]{1,0:T(2,128)S(1)}, f32[2,512,1024]{2,1,0:T(8,128)}) fusion(f32[2]{0:T(128)} %get-tuple-element.4425, pred[512,1024]{1,0:T(8,128)(4,1)} %get-tuple-element.4426, f32[2]{0:T(128)} %get-tuple-element.4427, pred[512,1024]{1,0:T(8,128)(4,1)} %get-tuple-element.4428, f32[2]{0:T(128)S(1)} %get-tuple-element.4429, ...), kind=kOutput, calls=%fused_computation.414.clone.1 | convolution fusion | flops 307231744 | bytes 22294660 | tf_op jit(solution)/shard_map/while/body/eval_jaxpr/qhd,khd->hqk/dot_general | solution.py:76
  266.1 2.9 fusion.400
  296.5 22.1 %fusion.399 = (f32[2,512]{1,0:T(2,128)S(1)}, f32[2,512,1024]{2,1,0:T(8,128)}) fusion(f32[2]{0:T(128)} %get-tuple-element.4425, pred[512,1024]{1,0:T(8,128)(4,1)} %get-tuple-element.4426, f32[2]{0:T(128)} %get-tuple-element.4427, pred[512,1024]{1,0:T(8,128)(4,1)} %get-tuple-element.4428, f32[2]{0:T(128)S(1)} %get-tuple-element.4429, ...), kind=kOutput, calls=%fused_computation.414.clone.1 | convolution fusion | flops 307231744 | bytes 22294660 | tf_op jit(solution)/shard_map/while/body/eval_jaxpr/qhd,khd->hqk/dot_general | solution.py:76
  318.7 3.0 fusion.400
  349.2 21.9 %fusion.399 = (f32[2,512]{1,0:T(2,128)S(1)}, f32[2,512,1024]{2,1,0:T(8,128)}) fusion(f32[2]{0:T(128)} %get-tuple-element.4425, pred[512,1024]{1,0:T(8,128)(4,1)} %get-tuple-element.4426, f32[2]{0:T(128)} %get-tuple-element.4427, pred[512,1024]{1,0:T(8,128)(4,1)} %get-tuple-element.4428, f32[2]{0:T(128)S(1)} %get-tuple-element.4429, ...), kind=kOutput, calls=%fused_computation.414.clone.1 | convolution fusion | flops 307231744 | bytes 22294660 | tf_op jit(solution)/shard_map/while/body/eval_jaxpr/qhd,khd->hqk/dot_general | solution.py:76
  371.1 2.9 fusion.400
  382.6 3.7 copy.497
  386.3 3.5 all-to-all-start.1
  390.5 17.0 all-gather.1
  410.4 4.7 multiply_reduce_fusion.4
  415.1 26.6 %multiply_convert_fusion.2 = (bf16[512,4096]{1,0:T(8,128)(2,1)}, f32[512,4096]{1,0:T(8,128)}, f32[512,4096]{1,0:T(8,128)}) fusion(bf16[1024,4096]{1,0:T(8,128)(2,1)} %all-gather.11.cloned.1.call-done, f32[512,1024]{1,0:T(8,128)} %get-tuple-element.3213, f32[1024]{0:T(1024)S(1)} %bitcast.549, f32[512]{0:T(512)S(1)} %fusion.207), kind=kOutput, calls=%fused_computation.209 | convolution fusion | flops 4432855040 | bytes 31463424 | tf_op jit(solution)/shard_map/dot_general | solution.py:429
  441.8 14.6 add_convert_fusion
  456.4 7.8 multiply_reduce_fusion.2
  468.2 3.6 all-to-all-start.2
  472.3 14.0 all-to-all-done.2
  492.8 443.3 %while.49 = (s32[]{:T(128)}, f32[512,2,128]{2,0,1:T(8,128)S(1)}, f32[512,2,128]{2,0,1:T(8,128)}, f32[512,2,128]{0,2,1:T(8,128)}, f32[2,128,128]{2,1,0:T(8,128)},...) while((s32[]{:T(128)}, f32[512,2,128]{2,0,1:T(8,128)S(1)}, ...), condition=%wide.region_22.23_spmd.clone, body=%wide.region_12.0_spmd.clone.sunk | while | flops 3828946176 | bytes 286523936 | solution.py:531
  517.8 2.9 copy.662
  522.1 21.6 %fusion.464 = (f32[2,512]{1,0:T(2,128)S(1)}, f32[2,512,1024]{2,1,0:T(8,128)}) fusion(f32[2]{0:T(128)} %get-tuple-element.4693, pred[512,1024]{1,0:T(8,128)(4,1)} %get-tuple-element.4694, f32[2]{0:T(128)} %get-tuple-element.4695, pred[512,1024]{1,0:T(8,128)(4,1)} %get-tuple-element.4696, f32[2]{0:T(128)} %copy-done.83, ...), kind=kOutput, calls=%fused_computation.418.clone.1 | convolution fusion | flops 307231744 | bytes 22295668 | tf_op jit(solution)/shard_map/while/body/eval_jaxpr/qhd,khd->hqk/dot_general | solution.py:76
  543.8 3.6 fusion.465
  553.4 2.7 fusion.469
  556.2 15.4 multiply_convert_fusion.11
  589.7 4.9 select_add_fusion.7
  626.9 2.9 copy.662
  631.2 21.6 %fusion.464 = (f32[2,512]{1,0:T(2,128)S(1)}, f32[2,512,1024]{2,1,0:T(8,128)}) fusion(f32[2]{0:T(128)} %get-tuple-element.4693, pred[512,1024]{1,0:T(8,128)(4,1)} %get-tuple-element.4694, f32[2]{0:T(128)} %get-tuple-element.4695, pred[512,1024]{1,0:T(8,128)(4,1)} %get-tuple-element.4696, f32[2]{0:T(128)} %copy-done.83, ...), kind=kOutput, calls=%fused_computation.418.clone.1 | convolution fusion | flops 307231744 | bytes 22295668 | tf_op jit(solution)/shard_map/while/body/eval_jaxpr/qhd,khd->hqk/dot_general | solution.py:76
  652.9 3.6 fusion.465
  665.2 15.4 multiply_convert_fusion.11
  699.7 6.2 select_add_fusion.7
  738.1 2.9 copy.662
  742.5 21.6 %fusion.464 = (f32[2,512]{1,0:T(2,128)S(1)}, f32[2,512,1024]{2,1,0:T(8,128)}) fusion(f32[2]{0:T(128)} %get-tuple-element.4693, pred[512,1024]{1,0:T(8,128)(4,1)} %get-tuple-element.4694, f32[2]{0:T(128)} %get-tuple-element.4695, pred[512,1024]{1,0:T(8,128)(4,1)} %get-tuple-element.4696, f32[2]{0:T(128)} %copy-done.83, ...), kind=kOutput, calls=%fused_computation.418.clone.1 | convolution fusion | flops 307231744 | bytes 22295668 | tf_op jit(solution)/shard_map/while/body/eval_jaxpr/qhd,khd->hqk/dot_general | solution.py:76
  764.1 3.6 fusion.465
  776.5 15.4 multiply_convert_fusion.11
  810.9 6.2 select_add_fusion.7
  849.4 2.9 copy.662
  853.7 21.6 %fusion.464 = (f32[2,512]{1,0:T(2,128)S(1)}, f32[2,512,1024]{2,1,0:T(8,128)}) fusion(f32[2]{0:T(128)} %get-tuple-element.4693, pred[512,1024]{1,0:T(8,128)(4,1)} %get-tuple-element.4694, f32[2]{0:T(128)} %get-tuple-element.4695, pred[512,1024]{1,0:T(8,128)(4,1)} %get-tuple-element.4696, f32[2]{0:T(128)} %copy-done.83, ...), kind=kOutput, calls=%fused_computation.418.clone.1 | convolution fusion | flops 307231744 | bytes 22295668 | tf_op jit(solution)/shard_map/while/body/eval_jaxpr/qhd,khd->hqk/dot_general | solution.py:76
  875.4 3.6 fusion.465
  887.7 15.4 multiply_convert_fusion.11
  922.2 6.2 select_add_fusion.7
  937.7 5.2 fusion.196
  945.1 28.6 %copy.515 = bf16[2048,3,2,128]{3,2,1,0:T(2,128)(2,1)S(1)} copy(bf16[2048,3,2,128]{3,0,2,1:T(8,128)(2,1)S(1)} %pad_maximum_fusion.7) | data formatting | bytes 6291456 | tf_op jit(solution)/shard_map/stack | solution.py:537
  973.7 39.4 %all_to_all.68 = bf16[2048,3,2,128]{3,2,1,0:T(2,128)(2,1)S(1)} all-to-all(bf16[2048,3,2,128]{3,2,1,0:T(2,128)(2,1)S(1)} %copy.515), channel_id=1, replica_groups=mesh['seq'=4,'fsdp'=8] {'seq'}, dimensions={0} | all-to-all | bytes 6291456 | tf_op jit(solution)/shard_map/all_to_all | solution.py:545
  1013.6 2.8 copy.517
  1016.4 10.4 fusion.189
  1028.4 10.4 fusion.208
  1039.5 12.9 fusion.199
  1055.2 10.3 fusion.187
  1065.7 10.2 select_reduce_fusion.1
  1077.3 14.1 select_reduce_fusion
  1093.6 18.4 all-reduce.5
  1114.6 9.0 fusion.176
  1123.6 37.6 %all-reduce.4 = (f32[1024]{0:T(1024)S(1)}, f32[1024]{0:T(1024)S(1)}) all-reduce(f32[1024]{0:T(1024)S(1)} %get-tuple-element.2783, f32[1024]{0:T(1024)S(1)} %copy-done.78), channel_id=6, replica_groups=mesh['seq'=4,'fsdp'=8] {'seq','fsdp'}, use_global_device_ids=true, to_apply=%region_29.30.clone | all-reduce | flops 2048 | bytes 16384
  1162.4 3.6 fusion.183
  1166.0 144.1 %reduce-scatter.5.cloned.1.call-done = f32[32,3072]{1,0:T(8,128)} async-done(((f32[1024,3072]{1,0:T(8,128)}), f32[32,3072]{1,0:T(8,128)}) %reduce-scatter.5.cloned.1.call-update) | async-done | bytes 393232 | tf_op jit(solution)/shard_map/reduce_scatter | solution.py:562
  1310.1 360.2 %reduce-scatter.9.cloned.1.call-done = f32[32,4096]{1,0:T(8,128)} async-done(((f32[1024,4096]{1,0:T(8,128)}), f32[32,4096]{1,0:T(8,128)}) %reduce-scatter.9.cloned.1.call-update) | async-done | bytes 524304 | tf_op jit(solution)/shard_map/reduce_scatter | solution.py:564
  1670.3 360.3 %reduce-scatter.11.cloned.1.call-done = f32[128,1024]{1,0:T(8,128)} async-done(((f32[4096,1024]{1,0:T(8,128)}), f32[128,1024]{1,0:T(8,128)}) %reduce-scatter.11.cloned.1.call-update) | async-done | bytes 524304 | tf_op jit(solution)/shard_map/reduce_scatter | solution.py:565
  (880 shorter events, 386.0 us)
Async XLA Ops:
  7.2 32.1 %copy-start.112 = (s32[15]{0:T(128)S(1)}, s32[15]{0:T(128)}, u32[]{:S(2)}) copy-start(s32[15]{0:T(128)} %constant.295.clone) | copy-start | bytes 184
  7.2 31.3 %copy-start.31 = (bf16[1,512,1024]{2,1,0:T(8,128)(2,1)S(1)}, bf16[1,512,1024]{2,1,0:T(8,128)(2,1)}, u32[]{:S(2)}) copy-start(bf16[1,512,1024]{2,1,0:T(8,128)(2,1)} %param.19) | copy-start | bytes 3145732
  7.2 104.8 %all-gather.7.cloned.1.call-start = ((), (), s32[]{:S(2)}) async-start(), calls=%async_computation.8 | async-start | bytes 7077888 | tf_op jit(solution)/shard_map/all_gather | solution.py:372
  8.0 402.4 %all-gather.9.cloned.1.call-start = ((), (), s32[]{:S(2)}) async-start(), calls=%async_computation.9 | async-start | bytes 2359296 | tf_op jit(solution)/shard_map/all_gather | solution.py:373
  8.7 406.4 %all-gather.11.cloned.1.call-start = ((), (), s32[]{:S(2)}) async-start(), calls=%async_computation.10 | async-start | bytes 9437184 | tf_op jit(solution)/shard_map/all_gather | solution.py:374
  9.5 432.3 %all-gather.13.cloned.1.call-start = ((), (), s32[]{:S(2)}) async-start(), calls=%async_computation.11 | async-start | bytes 9437184 | tf_op jit(solution)/shard_map/all_gather | solution.py:375
  38.5 80.1 %copy-start.70 = (f32[8,1,128]{2,1,0:T(1,128)}, f32[8,1,128]{2,1,0:T(1,128)S(1)}, u32[]{:S(2)}) copy-start(f32[8,1,128]{2,1,0:T(1,128)S(1)} %convert_element_type.249) | copy-start | bytes 12292
  38.8 79.8 %copy-start.66 = (f32[512]{0:T(512)}, f32[512]{0:T(512)S(1)}, u32[]{:S(2)}) copy-start(f32[512]{0:T(512)S(1)} %fusion.177) | copy-start | bytes 6148
  38.8 79.8 %copy-start.72 = (f32[512]{0:T(512)}, f32[512]{0:T(512)S(1)}, u32[]{:S(2)}) copy-start(f32[512]{0:T(512)S(1)} %fusion.206) | copy-start | bytes 6148
  122.0 41.8 %all-to-all-start = ((bf16[512,3,8,128]{3,0,1,2:T(8,128)(2,1)}), bf16[512,3,8,128]{3,0,1,2:T(8,128)(2,1)}, u32[]{:S(2)}, u32[]{:S(2)}) async-start(bf16[512,3,8,128]{3,0,1,2:T(8,128)(2,1)} %copy.486), calls=%async_computation | async-start | bytes 6291456 | tf_op jit(solution)/shard_map/all_to_all | solution.py:387
  382.4 27.8 %copy-start.12 = (f32[512,2,128]{2,0,1:T(8,128)}, f32[512,2,128]{2,0,1:T(8,128)S(1)}, u32[]{:S(2)}) copy-start(f32[512,2,128]{2,0,1:T(8,128)S(1)} %get-tuple-element.651) | copy-start | bytes 1572868
  382.4 27.8 %copy-start.85 = (f32[2]{0:T(128)}, f32[2]{0:T(128)S(1)}, u32[]{:S(2)}) copy-start(f32[2]{0:T(128)S(1)} %get-tuple-element.4867) | copy-start | bytes 28
  382.4 27.8 %copy-start.87 = (f32[2]{0:T(128)}, f32[2]{0:T(128)S(1)}, u32[]{:S(2)}) copy-start(f32[2]{0:T(128)S(1)} %get-tuple-element.4868) | copy-start | bytes 28
  382.4 27.8 %copy-start.89 = (f32[2]{0:T(128)}, f32[2]{0:T(128)S(1)}, u32[]{:S(2)}) copy-start(f32[2]{0:T(128)S(1)} %get-tuple-element.4869) | copy-start | bytes 28
  382.4 27.8 %copy-start.91 = (f32[2]{0:T(128)}, f32[2]{0:T(128)S(1)}, u32[]{:S(2)}) copy-start(f32[2]{0:T(128)S(1)} %get-tuple-element.4870) | copy-start | bytes 28
  382.4 27.8 %copy-start.93 = (f32[2]{0:T(128)}, f32[2]{0:T(128)S(1)}, u32[]{:S(2)}) copy-start(f32[2]{0:T(128)S(1)} %get-tuple-element.4871) | copy-start | bytes 28
  382.4 27.8 %copy-start.95 = (f32[2]{0:T(128)}, f32[2]{0:T(128)S(1)}, u32[]{:S(2)}) copy-start(f32[2]{0:T(128)S(1)} %get-tuple-element.4872) | copy-start | bytes 28
  382.5 27.8 %copy-start.97 = (f32[2]{0:T(128)}, f32[2]{0:T(128)S(1)}, u32[]{:S(2)}) copy-start(f32[2]{0:T(128)S(1)} %get-tuple-element.4873) | copy-start | bytes 28
  382.5 27.8 %copy-start.99 = (f32[2]{0:T(128)}, f32[2]{0:T(128)S(1)}, u32[]{:S(2)}) copy-start(f32[2]{0:T(128)S(1)} %get-tuple-element.4874) | copy-start | bytes 28
  382.5 27.8 %copy-start.101 = (f32[2]{0:T(128)}, f32[2]{0:T(128)S(1)}, u32[]{:S(2)}) copy-start(f32[2]{0:T(128)S(1)} %get-tuple-element.4875) | copy-start | bytes 28
  382.5 27.8 %copy-start.103 = (f32[2]{0:T(128)}, f32[2]{0:T(128)S(1)}, u32[]{:S(2)}) copy-start(f32[2]{0:T(128)S(1)} %get-tuple-element.4876) | copy-start | bytes 28
  382.5 27.8 %copy-start.105 = (f32[2]{0:T(128)}, f32[2]{0:T(128)S(1)}, u32[]{:S(2)}) copy-start(f32[2]{0:T(128)S(1)} %get-tuple-element.4877) | copy-start | bytes 28
  382.5 27.8 %copy-start.107 = (f32[2]{0:T(128)}, f32[2]{0:T(128)S(1)}, u32[]{:S(2)}) copy-start(f32[2]{0:T(128)S(1)} %get-tuple-element.4878) | copy-start | bytes 28
  382.5 27.8 %copy-start.109 = (f32[2]{0:T(128)}, f32[2]{0:T(128)S(1)}, u32[]{:S(2)}) copy-start(f32[2]{0:T(128)S(1)} %get-tuple-element.4879) | copy-start | bytes 28
  382.5 27.8 %copy-start.111 = (f32[2]{0:T(128)}, f32[2]{0:T(128)S(1)}, u32[]{:S(2)}) copy-start(f32[2]{0:T(128)S(1)} %get-tuple-element.4880) | copy-start | bytes 28
  382.5 27.8 %copy-start.118 = (s32[4]{0:T(128)}, s32[4]{0:T(128)S(1)}, u32[]{:S(2)}) copy-start(s32[4]{0:T(128)S(1)} %get-tuple-element.4904) | copy-start | bytes 52
  382.6 27.8 %copy-start.32 = (bf16[1,512,1024]{2,1,0:T(8,128)(2,1)S(1)}, bf16[1,512,1024]{2,1,0:T(8,128)(2,1)}, u32[]{:S(2)}) copy-start(bf16[1,512,1024]{2,1,0:T(8,128)(2,1)} %param.19) | copy-start | bytes 3145732
  386.3 21.3 %all-to-all-start.1 = ((bf16[2048,2,128]{2,1,0:T(2,128)(2,1)}), bf16[2048,2,128]{2,1,0:T(2,128)(2,1)S(1)}, u32[]{:S(2)}, u32[]{:S(2)}) async-start(bf16[2048,2,128]{2,1,0:T(2,128)(2,1)} %copy.497), calls=%async_computation.1 | async-start | bytes 2097152 | tf_op jit(solution)/shard_map/all_to_all | solution.py:420
  407.5 56.6 %copy-start.68 = (f32[8,1,128]{2,1,0:T(1,128)}, f32[8,1,128]{2,1,0:T(1,128)S(1)}, u32[]{:S(2)}) copy-start(f32[8,1,128]{2,1,0:T(1,128)S(1)} %convert_element_type.250) | copy-start | bytes 12292
  407.5 56.6 %copy-start.74 = (f32[512]{0:T(512)}, f32[512]{0:T(512)S(1)}, u32[]{:S(2)}) copy-start(f32[512]{0:T(512)S(1)} %fusion.205) | copy-start | bytes 6148
  410.3 31.4 %copy-start.30 = (bf16[512,4,2,128]{0,3,2,1:T(8,128)(2,1)}, bf16[512,4,2,128]{0,3,2,1:T(8,128)(2,1)S(1)}, u32[]{:S(2)}) copy-start(bf16[512,4,2,128]{0,3,2,1:T(8,128)(2,1)S(1)} %copy.499) | copy-start | bytes 3145732
  415.1 49.1 %copy-start.76 = (f32[512]{0:T(512)}, f32[512]{0:T(512)S(1)}, u32[]{:S(2)}) copy-start(f32[512]{0:T(512)S(1)} %fusion.207) | copy-start | bytes 6148
  415.1 26.6 %copy-start.62 = (bf16[1,512,1024]{2,1,0:T(8,128)(2,1)S(1)}, bf16[1,512,1024]{2,1,0:T(8,128)(2,1)}, u32[]{:S(2)}) copy-start(bf16[1,512,1024]{2,1,0:T(8,128)(2,1)} %param.31) | copy-start | bytes 3145732
  441.7 14.6 copy-start.34
  441.8 14.6 copy-start.115
  468.2 18.0 all-to-all-start.2
  471.8 20.9 %copy-start.38 = (bf16[2,128,128]{2,1,0:T(8,128)(2,1)S(1)}, bf16[2,128,128]{2,1,0:T(8,128)(2,1)}, u32[]{:S(2)}) copy-start(bf16[2,128,128]{2,1,0:T(8,128)(2,1)} %param.29) | copy-start | bytes 196612
  471.8 20.9 %copy-start.86 = (f32[2]{0:T(128)S(1)}, f32[2]{0:T(128)}, u32[]{:S(2)}) copy-start(f32[2]{0:T(128)} %copy-done.85) | copy-start | bytes 28
  471.8 20.9 %copy-start.88 = (f32[2]{0:T(128)S(1)}, f32[2]{0:T(128)}, u32[]{:S(2)}) copy-start(f32[2]{0:T(128)} %copy-done.87) | copy-start | bytes 28
  471.8 20.9 %copy-start.90 = (f32[2]{0:T(128)S(1)}, f32[2]{0:T(128)}, u32[]{:S(2)}) copy-start(f32[2]{0:T(128)} %copy-done.89) | copy-start | bytes 28
  471.8 20.9 %copy-start.92 = (f32[2]{0:T(128)S(1)}, f32[2]{0:T(128)}, u32[]{:S(2)}) copy-start(f32[2]{0:T(128)} %copy-done.91) | copy-start | bytes 28
  471.8 20.9 %copy-start.94 = (f32[2]{0:T(128)S(1)}, f32[2]{0:T(128)}, u32[]{:S(2)}) copy-start(f32[2]{0:T(128)} %copy-done.93) | copy-start | bytes 28
  471.8 20.9 %copy-start.96 = (f32[2]{0:T(128)S(1)}, f32[2]{0:T(128)}, u32[]{:S(2)}) copy-start(f32[2]{0:T(128)} %copy-done.95) | copy-start | bytes 28
  471.8 20.9 %copy-start.98 = (f32[2]{0:T(128)S(1)}, f32[2]{0:T(128)}, u32[]{:S(2)}) copy-start(f32[2]{0:T(128)} %copy-done.97) | copy-start | bytes 28
  471.8 20.9 %copy-start.100 = (f32[2]{0:T(128)S(1)}, f32[2]{0:T(128)}, u32[]{:S(2)}) copy-start(f32[2]{0:T(128)} %copy-done.99) | copy-start | bytes 28
  471.9 20.9 %copy-start.102 = (f32[2]{0:T(128)S(1)}, f32[2]{0:T(128)}, u32[]{:S(2)}) copy-start(f32[2]{0:T(128)} %copy-done.101) | copy-start | bytes 28
  471.9 20.9 %copy-start.104 = (f32[2]{0:T(128)S(1)}, f32[2]{0:T(128)}, u32[]{:S(2)}) copy-start(f32[2]{0:T(128)} %copy-done.103) | copy-start | bytes 28
  471.9 20.9 %copy-start.106 = (f32[2]{0:T(128)S(1)}, f32[2]{0:T(128)}, u32[]{:S(2)}) copy-start(f32[2]{0:T(128)} %copy-done.105) | copy-start | bytes 28
  471.9 20.9 %copy-start.108 = (f32[2]{0:T(128)S(1)}, f32[2]{0:T(128)}, u32[]{:S(2)}) copy-start(f32[2]{0:T(128)} %copy-done.107) | copy-start | bytes 28
  471.9 20.9 %copy-start.110 = (f32[2]{0:T(128)S(1)}, f32[2]{0:T(128)}, u32[]{:S(2)}) copy-start(f32[2]{0:T(128)} %copy-done.109) | copy-start | bytes 28
  471.9 20.9 %copy-start.119 = (s32[4]{0:T(128)S(1)}, s32[4]{0:T(128)}, u32[]{:S(2)}) copy-start(s32[4]{0:T(128)} %copy-done.118) | copy-start | bytes 52
  471.9 641.2 %all-reduce.8.cloned.1.call-start = ((), (), s32[]{:S(2)}) async-start(), calls=%async_computation.16 | async-start | bytes 131072 | tf_op jit(solution)/shard_map/psum | solution.py:556
  937.7 228.3 %reduce-scatter.7.cloned.1.call-start = ((), (), s32[]{:S(2)}) async-start(), calls=%async_computation.13 | async-start | bytes 4325376 | tf_op jit(solution)/shard_map/reduce_scatter | solution.py:563
  942.9 367.2 %reduce-scatter.5.cloned.1.call-start = ((), (), s32[]{:S(2)}) async-start(), calls=%async_computation.12 | async-start | bytes 12976128 | tf_op jit(solution)/shard_map/reduce_scatter | solution.py:562
  1026.9 643.4 %reduce-scatter.9.cloned.1.call-start = ((), (), s32[]{:S(2)}) async-start(), calls=%async_computation.14 | async-start | bytes 17301504 | tf_op jit(solution)/shard_map/reduce_scatter | solution.py:564
  1038.9 991.7 %reduce-scatter.11.cloned.1.call-start = ((), (), s32[]{:S(2)}) async-start(), calls=%async_computation.15 | async-start | bytes 17301504 | tf_op jit(solution)/shard_map/reduce_scatter | solution.py:565
  1065.7 11.6 copy-start.43
  1065.7 11.6 copy-start.44
  1065.7 11.6 copy-start.45
  1065.7 11.6 copy-start.46
  1077.3 16.3 copy-start.80
  1077.3 37.3 %copy-start.33 = (bf16[1,512,1024]{2,1,0:T(8,128)(2,1)S(1)}, bf16[1,512,1024]{2,1,0:T(8,128)(2,1)}, u32[]{:S(2)}) copy-start(bf16[1,512,1024]{2,1,0:T(8,128)(2,1)} %param.19) | copy-start | bytes 3145732
  1114.6 47.8 %copy-start.67 = (f32[512]{0:T(512)S(1)}, f32[512]{0:T(512)}, u32[]{:S(2)}) copy-start(f32[512]{0:T(512)} %copy-done.66) | copy-start | bytes 6148
  1114.6 47.8 %copy-start.29 = (f32[512,1024]{1,0:T(8,128)S(1)}, f32[512,1024]{1,0:T(8,128)}, u32[]{:S(2)}) copy-start(f32[512,1024]{1,0:T(8,128)} %copy-done.28) | copy-start | bytes 6291460
  (174 other events, 831.9 us)
Sparse Core Ops, SparseCore 0:
  10.3 101.7 all-gather.6
  114.2 47.4 all-gather.8
  163.8 123.4 all-gather.10
  289.3 123.0 all-gather.12
  937.8 65.4 all-reduce.7
  1006.0 143.9 reduce-scatter.6
  1156.6 153.4 reduce-scatter.4
  1313.1 357.1 reduce-scatter.8
  1673.2 357.3 reduce-scatter.10
where the time goes:
time: 2050 us; the launch traced here: 2040 us
  waiting for transfers between devices  970 us (47%)
  matrix products  454 us (22%)
  other arithmetic  217 us (11%)
  local copies, waits for them, and re-layouts  214 us (10%)
  blocking collectives  135 us (7%)
    reduce_scatter x1, waiting for transfers between devices, body(): lax.psum_scatter(weight_terms[3], ('seq', 'fsdp'), scatter_dimension=0, t...  360 us
    reduce_scatter x1, waiting for transfers between devices, body(): lax.psum_scatter(weight_terms[2], ('seq', 'fsdp'), scatter_dimension=0, t...  360 us
    dot_general x8, matrix products, block_pass(): jnp.einsum('qhd,khd->hqk', query_rows, key_ctx, preferred_element_type=jn...  174 us
    reduce_scatter x1, waiting for transfers between devices, body(): lax.psum_scatter(weight_terms[0], ('seq', 'fsdp'), scatter_dimension=0, t...  144 us
    all_gather x1, waiting for transfers between devices, body(): lax.all_gather(w_qkv, 'fsdp', axis=0, tiled=True)  68.3 us
    sub x4, other arithmetic, block_back(): grad_prob - jnp.sum(grad_prob * probabilities, axis=-1, keepdims=True)  61.5 us
    while x296, local copies, waits for them, and re-layouts  51.2 us
  transfers between devices with their start and end apart: 12, of which 6 were waited for; matrix products, arithmetic and copies ran while one was open for 20% of the time, Pallas kernels for 0%

commit v1 on v0

v1 whole, which is shorter than its diff:
```python
import functools
import math

import jax
import jax.numpy as jnp
import numpy as np
from jax import lax
from jax.experimental import pallas as pl
from jax.experimental.pallas import tpu as pltpu
from jax.sharding import PartitionSpec as P

H = 8
DH = 128
BLOCK = 512
STATE_VECTORS = 512
QTILE = 256
SPAN = BLOCK + QTILE

EPSILON = 1e-06
BUCKET_EDGES = (19, 21, 24, 27, 31, 35, 40, 46, 52, 59, 67, 77, 87, 99, 113)
BUCKETS = 32
LOG2E = math.log2(math.e)
SCALE = DH ** (-0.5)
NEAR = 384

f32 = jnp.float32
bf16 = jnp.bfloat16


def bucket_of(distance):
    return np.minimum(distance, 16) + (distance[..., None] >= np.array(BUCKET_EDGES)).sum(-1)


def tile_distance():
    rows = np.arange(QTILE)[:, None]
    cols = np.arange(SPAN)[None, :]
    return rows + BLOCK - cols


def tile_bias(table):
    distance = jnp.arange(QTILE, dtype=jnp.int32)[:, None] + BLOCK - jnp.arange(SPAN, dtype=jnp.int32)[None, :]
    clipped = jnp.clip(distance, 0, BLOCK)
    edges = jnp.array(BUCKET_EDGES, dtype=jnp.int32)
    bucket = jnp.minimum(clipped, 16) + jnp.sum((clipped[:, :, None] >= edges).astype(jnp.int32), axis=-1)
    total = jnp.zeros((table.shape[0],) + bucket.shape, f32)
    for bucket_id in range(BUCKETS):
        total = jnp.where((bucket == bucket_id)[None], table[:, bucket_id][:, None, None], total)
    window = (distance >= 0) & (distance < BLOCK)
    return jnp.where(window[None], total * LOG2E, -jnp.inf)


def dot(a, b):
    return jnp.dot(a, b, preferred_element_type=f32)


def dot_t(a, b):
    return lax.dot_general(a, b, (((1,), (1,)), ((), ())), preferred_element_type=f32)


def t_dot(a, b):
    return lax.dot_general(a, b, (((0,), (0,)), ((), ())), preferred_element_type=f32)


def to_row(column):
    wide = jnp.broadcast_to(column, (column.shape[0], 128))
    return wide.T[0:1, :]


def context_pieces(tile):
    start = tile * QTILE
    pieces = []
    if start < BLOCK:
        pieces.append((0, start, BLOCK, 0))
    pieces.append((1, 0, start + QTILE, BLOCK - start))
    return pieces


def softmax_parts(scores):
    top = functools.reduce(jnp.maximum, [jnp.max(s, axis=-1, keepdims=True) for s in scores])
    raised = [jnp.exp2(s - top) for s in scores]
    total = functools.reduce(jnp.add, [jnp.sum(e, axis=-1, keepdims=True) for e in raised])
    return raised, total, top + jnp.log2(total)


def attend_kernel(
    heads,
    length_ref,
    cur_ref,
    prev_ref,
    init_ref,
    query_ref,
    forget_ref,
    bias_ref,
    att_ref,
    final_ref,
    mem_ref,
    upd_ref,
    lse_ref,
    slse_ref,
    memory_ref,
):
    block = pl.program_id(0)
    length = length_ref[0]
    width = heads * DH
    scale2 = SCALE * LOG2E

    @pl.when(block == 0)
    def _():
        memory_ref[...] = init_ref[...].astype(f32)

    live_block = block * BLOCK < length
    for head in range(heads):
        own = slice(head * DH, (head + 1) * DH)
        memory = memory_ref[:, own]
        low = memory.astype(bf16)
        mem_ref[0, :, own] = memory
        refs = (prev_ref, cur_ref)
        key_cols = slice(width + head * DH, width + (head + 1) * DH)
        value_cols = slice(2 * width + head * DH, 2 * width + (head + 1) * DH)
        for tile in range(BLOCK // QTILE):
            rows = slice(tile * QTILE, (tile + 1) * QTILE)
            query = cur_ref[rows, own]
            scores, values = [], []
            for which, lo, hi, col in context_pieces(tile):
                s = dot_t(query, refs[which][lo:hi, key_cols])
                position = (block - 1 + which) * BLOCK + lo + lax.broadcasted_iota(jnp.int32, (1, hi - lo), 1)
                live = (position >= 0) & (position < length)
                s = s * scale2 + bias_ref[head, :, col : col + hi - lo]
                scores.append(jnp.where(live, s, -jnp.inf))
                values.append(refs[which][lo:hi, value_cols])
            scores.append(dot_t(query, low) * scale2)
            values.append(low)
            raised, total, lse = softmax_parts(scores)
            out = functools.reduce(jnp.add, [dot(e.astype(bf16), v) for e, v in zip(raised, values)])
            att_ref[rows, own] = (out / total).astype(bf16)
            lse_ref[head : head + 1, rows] = to_row(lse)
        own_key = cur_ref[:, key_cols]
        own_value = cur_ref[:, value_cols]
        squeries = dot(low, query_ref[head]).astype(bf16)
        position = block * BLOCK + lax.broadcasted_iota(jnp.int32, (1, BLOCK), 1)
        for tile in range(STATE_VECTORS // QTILE):
            rows = slice(tile * QTILE, (tile + 1) * QTILE)
            squery = squeries[rows]
            scores = [
                dot_t(squery, low) * scale2,
                jnp.where(position < length, dot_t(squery, own_key) * scale2, -jnp.inf),
            ]
            raised, total, lse = softmax_parts(scores)
            update = dot(raised[0].astype(bf16), low) + dot(raised[1].astype(bf16), own_value)
            update = update / total
            upd_ref[0, rows, own] = update
            slse_ref[head : head + 1, rows] = to_row(lse)
            forget = forget_ref[:, own]
            old = memory[rows]
            memory_ref[rows, own] = jnp.where(live_block, forget * old + (1.0 - forget) * update, old)
    final_ref[...] = memory_ref[...]


def attend(qkv, init, length, state_query, forget, bias, heads):
    rows, width3 = qkv.shape
    width = heads * DH
    blocks = rows // BLOCK
    return pl.pallas_call(
        functools.partial(attend_kernel, heads),
        grid=(blocks,),
        out_shape=(
            jax.ShapeDtypeStruct((rows, width), bf16),
            jax.ShapeDtypeStruct((STATE_VECTORS, width), f32),
            jax.ShapeDtypeStruct((blocks, STATE_VECTORS, width), f32),
            jax.ShapeDtypeStruct((blocks, STATE_VECTORS, width), f32),
            jax.ShapeDtypeStruct((heads, rows), f32),
            jax.ShapeDtypeStruct((heads, blocks * STATE_VECTORS), f32),
        ),
        in_specs=[
            pl.BlockSpec(memory_space=pltpu.SMEM),
            pl.BlockSpec((BLOCK, width3), lambda b: (b, 0)),
            pl.BlockSpec((BLOCK, width3), lambda b: (jnp.maximum(b - 1, 0), 0)),
            pl.BlockSpec((STATE_VECTORS, width), lambda b: (0, 0)),
            pl.BlockSpec((heads, DH, DH), lambda b: (0, 0, 0)),
            pl.BlockSpec((1, width), lambda b: (0, 0)),
            pl.BlockSpec((heads, QTILE, SPAN), lambda b: (0, 0, 0)),
        ],
        out_specs=(
            pl.BlockSpec((BLOCK, width), lambda b: (b, 0)),
            pl.BlockSpec((STATE_VECTORS, width), lambda b: (0, 0)),
            pl.BlockSpec((1, STATE_VECTORS, width), lambda b: (b, 0, 0)),
            pl.BlockSpec((1, STATE_VECTORS, width), lambda b: (b, 0, 0)),
            pl.BlockSpec((heads, BLOCK), lambda b: (0, b)),
            pl.BlockSpec((heads, STATE_VECTORS), lambda b: (0, b)),
        ),
        scratch_shapes=[pltpu.VMEM((STATE_VECTORS, width), f32)],
        compiler_params=pltpu.CompilerParams(vmem_limit_bytes=40 << 20),
        cost_estimate=pl.CostEstimate(
            flops=blocks * heads * 512 * 2400 * 128 * 4, bytes_accessed=16 << 20, transcendentals=10 << 20
        ),
        name="attend",
    )(length, qkv, qkv, init, state_query, forget, bias)


def attend_back_kernel(
    heads,
    blocks,
    length_ref,
    cur_ref,
    prev_ref,
    dout_ref,
    out_ref,
    mem_ref,
    upd_ref,
    lse_ref,
    slse_ref,
    sgrad_ref,
    query_ref,
    forget_ref,
    bias_ref,
    dqkv_ref,
    dquery_ref,
    dforget_ref,
    near_ref,
    far_ref,
    dmem_ref,
    dnext_ref,
    dctx_ref,
):
    step = pl.program_id(0)
    block = blocks - 1 - step
    length = length_ref[0]
    width = heads * DH
    scale2 = SCALE * LOG2E

    @pl.when(step == 0)
    def _():
        dmem_ref[...] = sgrad_ref[...].astype(f32)
        dnext_ref[...] = jnp.zeros_like(dnext_ref)
        dquery_ref[...] = jnp.zeros_like(dquery_ref)
        dforget_ref[...] = jnp.zeros_like(dforget_ref)
        near_ref[...] = jnp.zeros_like(near_ref)
        far_ref[...] = jnp.zeros_like(far_ref)

    live_block = block * BLOCK < length
    refs = (prev_ref, cur_ref)
    for head in range(heads):
        own = slice(head * DH, (head + 1) * DH)
        key_cols = slice(width + head * DH, width + (head + 1) * DH)
        value_cols = slice(2 * width + head * DH, 2 * width + (head + 1) * DH)
        memory = mem_ref[0, :, own]
        update = upd_ref[0, :, own]
        low = memory.astype(bf16)
        forget = forget_ref[:, own]
        dmem = dmem_ref[:, own]
        dupd = jnp.where(live_block, (1.0 - forget) * dmem, 0.0).astype(bf16)
        moved = jnp.where(live_block, dmem * (memory - update), 0.0)
        dforget_ref[:, own] += jnp.sum(moved, axis=0, keepdims=True)
        dmem_new = jnp.where(live_block, forget * dmem, dmem)
        own_key = cur_ref[:, key_cols]
        own_value = cur_ref[:, value_cols]
        squeries = dot(low, query_ref[head]).astype(bf16)
        sdelta = jnp.sum((dupd.astype(f32) * update).T, axis=0, keepdims=True)
        slse = slse_ref[head : head + 1, :]
        dsquery = jnp.zeros((STATE_VECTORS, DH), f32)
        dkey = []
        dvalue = []
        for part in range(2 * STATE_VECTORS // QTILE):
            own_part = part >= STATE_VECTORS // QTILE
            lo = (part % (STATE_VECTORS // QTILE)) * QTILE
            keys = (own_key if own_part else low)[lo : lo + QTILE]
            values = (own_value if own_part else low)[lo : lo + QTILE]
            s = dot_t(keys, squeries) * scale2 - slse
            if own_part:
                position = block * BLOCK + lo + lax.broadcasted_iota(jnp.int32, (QTILE, 1), 0)
                s = jnp.where(position < length, s, -jnp.inf)
            p = jnp.exp2(s)
            dp = dot_t(values, dupd)
            ds = (p * (dp - sdelta)).astype(bf16)
            dvalue.append(dot(p.astype(bf16), dupd))
            dkey.append(dot(ds, squeries))
            dsquery += t_dot(ds, keys)
        half = STATE_VECTORS // QTILE
        dlow = [dvalue[i] + dkey[i] * SCALE for i in range(half)]
        dctx_ref[0, 0:BLOCK] = jnp.zeros((BLOCK, DH), f32)
        dctx_ref[1, 0:BLOCK] = jnp.zeros((BLOCK, DH), f32)
        for i in range(half):
            rows = slice(BLOCK + i * QTILE, BLOCK + (i + 1) * QTILE)
            old = slice(i * QTILE, (i + 1) * QTILE)
            dctx_ref[0, rows] = dkey[half + i] * SCALE + dnext_ref[0, old, own]
            dctx_ref[1, rows] = dvalue[half + i] + dnext_ref[1, old, own]
        dsq = (dsquery * SCALE).astype(bf16)
        dquery_ref[head] += t_dot(low, dsq)
        dmem_ref[:, own] = dmem_new + dot_t(dsq, query_ref[head])
        for tile in range(BLOCK // QTILE):
            rows = slice(tile * QTILE, (tile + 1) * QTILE)
            query = cur_ref[rows, own]
            dout = dout_ref[rows, own]
            lse = lse_ref[head : head + 1, rows]
            delta = jnp.sum((dout.astype(f32) * out_ref[rows, own].astype(f32)).T, axis=0, keepdims=True)
            dq = jnp.zeros((QTILE, DH), f32)
            for which, lo, hi, col in context_pieces(tile):
                for at in range(lo, hi, QTILE):
                    keys = refs[which][at : at + QTILE, key_cols]
                    values = refs[which][at : at + QTILE, value_cols]
                    band = col + at - lo
                    position = (block - 1 + which) * BLOCK + at + lax.broadcasted_iota(jnp.int32, (QTILE, 1), 0)
                    live = (position >= 0) & (position < length)
                    s = dot_t(keys, query) * scale2 + bias_ref[head, band : band + QTILE, :] - lse
                    p = jnp.exp2(jnp.where(live, s, -jnp.inf))
                    dp = dot_t(values, dout)
                    ds = (p * (dp - delta)).astype(bf16)
                    wide = ds.astype(f32)
                    if band + QTILE <= SPAN - NEAR:
                        far_ref[head] += functools.reduce(jnp.add, [wide[i : i + 8] for i in range(0, QTILE, 8)])
                    else:
                        edge = max(SPAN - NEAR - band, 0)
                        if edge:
                            far_ref[head] += functools.reduce(jnp.add, [wide[i : i + 8] for i in range(0, edge, 8)])
                        at_near = band + edge - (SPAN - NEAR)
                        near_ref[head, at_near : at_near + QTILE - edge] += wide[edge:]
                    into = slice(which * BLOCK + at, which * BLOCK + at + QTILE)
                    dctx_ref[1, into] += dot(p.astype(bf16), dout)
                    dctx_ref[0, into] += dot(ds, query) * SCALE
                    dq += t_dot(ds, keys)
            for part in range(half):
                keys = low[part * QTILE : (part + 1) * QTILE]
                s = dot_t(keys, query) * scale2 - lse
                p = jnp.exp2(s)
                dp = dot_t(keys, dout)
                ds = (p * (dp - delta)).astype(bf16)
                dlow[part] += dot(p.astype(bf16), dout) + dot(ds, query) * SCALE
                dq += t_dot(ds, keys)
            dqkv_ref[rows, own] = (dq * SCALE).astype(bf16)
        for part in range(half):
            dmem_ref[part * QTILE : (part + 1) * QTILE, own] += dlow[part]
        dnext_ref[0, :, own] = dctx_ref[0, 0:BLOCK]
        dnext_ref[1, :, own] = dctx_ref[1, 0:BLOCK]
        dqkv_ref[:, key_cols] = dctx_ref[0, BLOCK:].astype(bf16)
        dqkv_ref[:, value_cols] = dctx_ref[1, BLOCK:].astype(bf16)


def attend_back(qkv, dout, out, mem, upd, lse, slse, sgrad, length, state_query, forget, bias_t, heads):
    rows, width3 = qkv.shape
    width = heads * DH
    blocks = rows // BLOCK
    last = blocks - 1
    return pl.pallas_call(
        functools.partial(attend_back_kernel, heads, blocks),
        grid=(blocks,),
        out_shape=(
            jax.ShapeDtypeStruct((rows, width3), bf16),
            jax.ShapeDtypeStruct((heads, DH, DH), f32),
            jax.ShapeDtypeStruct((1, width), f32),
            jax.ShapeDtypeStruct((heads, NEAR, QTILE), f32),
            jax.ShapeDtypeStruct((heads, 8, QTILE), f32),
        ),
        in_specs=[
            pl.BlockSpec(memory_space=pltpu.SMEM),
            pl.BlockSpec((BLOCK, width3), lambda b: (last - b, 0)),
            pl.BlockSpec((BLOCK, width3), lambda b: (jnp.maximum(last - b - 1, 0), 0)),
            pl.BlockSpec((BLOCK, width), lambda b: (last - b, 0)),
            pl.BlockSpec((BLOCK, width), lambda b: (last - b, 0)),
            pl.BlockSpec((1, STATE_VECTORS, width), lambda b: (last - b, 0, 0)),
            pl.BlockSpec((1, STATE_VECTORS, width), lambda b: (last - b, 0, 0)),
            pl.BlockSpec((heads, BLOCK), lambda b: (0, last - b)),
            pl.BlockSpec((heads, STATE_VECTORS), lambda b: (0, last - b)),
            pl.BlockSpec((STATE_VECTORS, width), lambda b: (0, 0)),
            pl.BlockSpec((heads, DH, DH), lambda b: (0, 0, 0)),
            pl.BlockSpec((1, width), lambda b: (0, 0)),
            pl.BlockSpec((heads, SPAN, QTILE), lambda b: (0, 0, 0)),
        ],
        out_specs=(
            pl.BlockSpec((BLOCK, width3), lambda b: (last - b, 0)),
            pl.BlockSpec((heads, DH, DH), lambda b: (0, 0, 0)),
            pl.BlockSpec((1, width), lambda b: (0, 0)),
            pl.BlockSpec((heads, NEAR, QTILE), lambda b: (0, 0, 0)),
            pl.BlockSpec((heads, 8, QTILE), lambda b: (0, 0, 0)),
        ),
        scratch_shapes=[
            pltpu.VMEM((STATE_VECTORS, width), f32),
            pltpu.VMEM((2, BLOCK, width), f32),
            pltpu.VMEM((2, 2 * BLOCK, DH), f32),
        ],
        compiler_params=pltpu.CompilerParams(vmem_limit_bytes=40 << 20),
        cost_estimate=pl.CostEstimate(
            flops=blocks * heads * 512 * 2400 * 128 * 10, bytes_accessed=20 << 20, transcendentals=10 << 20
        ),
        name="attend_back",
    )(length, qkv, qkv, dout, out, mem, upd, lse, slse, sgrad, state_query, forget, bias_t)


def bias_table_grad(near, far):
    distance = tile_distance().T[SPAN - NEAR :]
    bucket = np.where((distance >= 0) & (distance < BLOCK), bucket_of(np.clip(distance, 0, BLOCK)), BUCKETS)
    bucket = jnp.asarray(bucket.astype(np.int32))
    columns = [jnp.sum(jnp.where((bucket == i)[None], near, 0.0), axis=(1, 2)) for i in range(BUCKETS)]
    columns[-1] = columns[-1] + jnp.sum(far, axis=(1, 2))
    return jnp.stack(columns, axis=1)


def inverse_rms(values):
    return lax.rsqrt(jnp.mean(values * values, axis=-1, keepdims=True) + EPSILON)


def norm_back(values, gain, rho, grad):
    scaled = gain * grad
    mean = jnp.mean(values * scaled, axis=-1, keepdims=True)
    return rho * scaled - values * (rho * rho * rho * mean), jnp.sum(grad * values * rho, axis=0)


def body(
    tokens,
    lengths,
    state_init,
    w_qkv,
    w_out,
    w_up,
    w_down,
    norm_attn,
    norm_mlp,
    rel_bias,
    state_query,
    gate_bias,
    out_grad,
    state_grad,
):
    seq_count = lax.axis_size("seq")
    fsdp_count = lax.axis_size("fsdp")
    seq_at = lax.axis_index("seq")
    heads = H // seq_count
    width = heads * DH
    tok_rows, dim = tokens.shape[1:]
    rows = tok_rows * seq_count
    hidden_all = w_up.shape[1]
    share = hidden_all // (seq_count * fsdp_count)

    all_tokens = lax.all_gather(tokens[0], "seq", axis=0, tiled=True)
    own_qkv = lax.dynamic_slice_in_dim(
        w_qkv.reshape(w_qkv.shape[0], 3, seq_count, width), seq_at, 1, axis=2
    ).reshape(w_qkv.shape[0], 3 * width)
    qkv_w = lax.all_gather(own_qkv, "fsdp", axis=0, tiled=True)
    gains = lax.all_gather(jnp.stack([norm_attn, norm_mlp]), "fsdp", axis=1, tiled=True).astype(f32)
    gain_attn, gain_mlp = gains[0], gains[1]
    own_up = lax.dynamic_slice_in_dim(
        w_up.reshape(w_up.shape[0], fsdp_count, seq_count, share), seq_at, 1, axis=2
    ).reshape(w_up.shape[0], fsdp_count * share)
    own_down = lax.dynamic_slice_in_dim(w_down, seq_at * share, share, axis=0)
    up_w = lax.all_gather(own_up, "fsdp", axis=0, tiled=True)
    down_w = lax.all_gather(own_down, "fsdp", axis=0, tiled=True)
    out_w = lax.all_gather(w_out, "fsdp", axis=0, tiled=True)
    all_grad = lax.all_gather(out_grad[0], "seq", axis=0, tiled=True)

    bias = tile_bias(rel_bias)
    bias_t = jnp.swapaxes(bias, 1, 2)
    forget = jax.nn.sigmoid(gate_bias)
    forget_row = forget.reshape(1, width)

    inputs = all_tokens.astype(f32)
    normed = (inputs * inverse_rms(inputs) * gain_attn).astype(bf16)
    qkv = dot(normed, qkv_w).astype(bf16)
    attended, final_memory, mem, upd, lse, slse = attend(
        qkv, state_init[0], lengths, state_query, forget_row, bias, heads
    )

    all_attended = lax.all_gather(attended, "seq", axis=1, tiled=True)
    mid = inputs + dot(all_attended, out_w)
    rho_mid = inverse_rms(mid)
    normed_mid = (mid * rho_mid * gain_mlp).astype(bf16)
    live = (jnp.arange(rows, dtype=jnp.int32) < lengths[0]).astype(bf16)[:, None]
    grad_low = all_grad * live
    pre = dot(normed_mid, up_w)
    hidden, gelu_pull = jax.vjp(lambda v: jax.nn.gelu(v, approximate=False), pre)
    hidden = hidden.astype(bf16)
    dpre = gelu_pull(dot_t(grad_low, down_w))[0].astype(bf16)
    dnormed_mid = lax.psum_scatter(dot_t(dpre, up_w).astype(bf16), "seq", scatter_dimension=0, tiled=True)
    mlp_out = lax.psum_scatter(dot(hidden, down_w).astype(bf16), "seq", scatter_dimension=0, tiled=True)
    down_grad = t_dot(hidden, grad_low)
    up_grad = t_dot(normed_mid, dpre)

    here = seq_at * tok_rows
    mid_here = lax.dynamic_slice_in_dim(mid, here, tok_rows, axis=0)
    live_here = (here + jnp.arange(tok_rows, dtype=jnp.int32) < lengths[0]).astype(f32)[:, None]
    output = (live_here * (mid_here + mlp_out.astype(f32))).astype(bf16)[None]
    grad_here = out_grad[0].astype(f32) * live_here
    through, mlp_gain_grad = norm_back(mid_here, gain_mlp, inverse_rms(mid_here), dnormed_mid.astype(f32))
    dmid = grad_here + through
    dbranch = lax.all_gather(dmid.astype(bf16), "seq", axis=0, tiled=True)
    own_out = lax.dynamic_slice_in_dim(out_w, seq_at * width, width, axis=0)
    dattended = dot_t(dbranch, own_out).astype(bf16)
    out_w_grad = t_dot(attended, dbranch)

    dqkv, dquery, dforget, near, far = attend_back(
        qkv, dattended, attended, mem, upd, lse, slse, state_grad[0], lengths, state_query, forget_row, bias_t, heads
    )
    dnormed = lax.psum_scatter(dot_t(dqkv, qkv_w).astype(bf16), "seq", scatter_dimension=0, tiled=True)
    qkv_grad = t_dot(normed, dqkv)
    inputs_here = tokens[0].astype(f32)
    through, attn_gain_grad = norm_back(inputs_here, gain_attn, inverse_rms(inputs_here), dnormed.astype(f32))
    tokens_grad = (dmid + through)[None]

    grad_gate = dforget.reshape(heads, DH) * forget * (1.0 - forget)
    grad_table = bias_table_grad(near, far)
    small = jnp.concatenate(
        [dquery.reshape(-1), grad_gate.reshape(-1), grad_table.reshape(-1)]
    )
    small = lax.psum(small, "fsdp")
    cut = heads * DH * DH
    dquery = small[:cut].reshape(heads, DH, DH)
    grad_gate = small[cut : cut + heads * DH].reshape(heads, DH)
    grad_table = small[cut + heads * DH :].reshape(heads, BUCKETS)

    def spread(term):
        return lax.psum_scatter(term, "fsdp", scatter_dimension=0, tiled=True)

    def exchange(term):
        return lax.all_to_all(term, "seq", split_axis=0, concat_axis=0, tiled=True)

    qkv_part = exchange(qkv_grad.astype(bf16)).reshape(seq_count, dim // seq_count, 3, width)
    qkv_part = spread(jnp.transpose(qkv_part, (1, 2, 0, 3)).reshape(dim // seq_count, 3 * H * DH)).astype(f32)
    out_part = spread(out_w_grad.astype(bf16)).astype(f32)
    up_part = exchange(up_grad.astype(bf16)).reshape(seq_count, dim // seq_count, fsdp_count, share)
    up_part = spread(jnp.transpose(up_part, (1, 2, 0, 3)).reshape(dim // seq_count, hidden_all)).astype(f32)
    down_part = jnp.transpose(
        down_grad.astype(bf16).reshape(seq_count, fsdp_count // seq_count, share, dim), (0, 1, 2, 3)
    )
    down_part = lax.all_to_all(down_part, "seq", split_axis=0, concat_axis=0, tiled=True)
    down_part = jnp.swapaxes(down_part, 0, 1).reshape(seq_count * (fsdp_count // seq_count) * share, dim)
    down_part = spread(down_part).astype(f32)
    attn_gain_grad, mlp_gain_grad = jnp.split(
        lax.psum_scatter(
            jnp.stack([attn_gain_grad, mlp_gain_grad]), ("seq", "fsdp"), scatter_dimension=1, tiled=True
        ),
        2,
    )
    return (
        output,
        final_memory[None],
        tokens_grad,
        qkv_part,
        out_part,
        up_part,
        down_part,
        attn_gain_grad[0],
        mlp_gain_grad[0],
        grad_table,
        dquery,
        grad_gate,
    )


def solution(mesh):
    placed = (
        P("fsdp", "seq", None),
        P("fsdp"),
        P("fsdp", None, "seq"),
        P("fsdp", None),
        P("fsdp", None),
        P("fsdp", None),
        P("fsdp", None),
        P("fsdp"),
        P("fsdp"),
        P("seq", None),
        P("seq", None, None),
        P("seq", None),
        P("fsdp", "seq", None),
        P("fsdp", None, "seq"),
    )
    return jax.shard_map(
        body,
        mesh=mesh,
        in_specs=placed,
        out_specs=(
            P("fsdp", "seq", None),
            P("fsdp", None, "seq"),
            P("fsdp", "seq", None),
            P(("seq", "fsdp"), None),
            P(("seq", "fsdp"), None),
            P(("seq", "fsdp"), None),
            P(("seq", "fsdp"), None),
            P(("seq", "fsdp")),
            P(("seq", "fsdp")),
            P("seq", None),
            P("seq", None, None),
            P("seq", None),
        ),
        check_vma=False,
    )
```

time: 2050 us -> 1080 us (0.53)
  waiting for transfers between devices: 970 us -> 612 us
  matrix products: 454 us -> 111 us
  other arithmetic: 217 us -> 58.3 us
  local copies, waits for them, and re-layouts: 214 us -> 140 us
  blocking collectives: 135 us -> 68.7 us
  Pallas kernels: 0 us -> 61.3 us
    reduce_scatter x4 -> x6, waiting for transfers between devices: 865 us -> 186 us  [the longest x3 60.4 us: spread(): return lax.psum_scatter(term, 'fsdp', scatter_dimension=0, tiled=True)]
    dot_general x148 -> x12, matrix products: 454 us -> 111 us  [the longest x4 54.8 us: dot(): return jnp.dot(a, b, preferred_element_type=f32)]
    unnamed x9 -> x19, waiting for transfers between devices: 2.66 us -> 195 us
    all_gather x4 -> x8, waiting for transfers between devices: 68.3 us -> 190 us  [the longest x1 43.6 us: body(): qkv_w = lax.all_gather(own_qkv, 'fsdp', axis=0, tiled=True)]
    sub x16 -> x0, other arithmetic: 71 us -> none  [the longest x4 61.5 us: block_back(): grad_prob - jnp.sum(grad_prob * probabilities, axis=-1, keepdims=True)]
    pallas_call x0 -> x2, Pallas kernels: none -> 61.3 us  [the longest x1 40.8 us: attend_back(): pl.pallas_call(functools.partial(attend_back_kernel, heads, blocks), grid...]
    unnamed x183 -> x297, local copies, waits for them, and re-layouts: 11.8 us -> 66.8 us
    while x297 -> x0, local copies, waits for them, and re-layouts: 51.6 us -> none
  transfers between devices with their start and end apart: 12 -> 19, of which waited for: 6 -> 13; matrix products, arithmetic and copies ran while one was open for 20% -> 25% of each run, Pallas kernels for 0% -> 6%
where the time goes in v1:
time: 1080 us
  waiting for transfers between devices  612 us (57%)
  local copies, waits for them, and re-layouts  140 us (13%)
  matrix products  111 us (10%)
  blocking collectives  68.7 us (6%)
  Pallas kernels  61.3 us (6%)
  other arithmetic  58.3 us (5%)
  between operations  16.4 us (2%)
    unnamed x19, waiting for transfers between devices  195 us
    unnamed x297, local copies, waits for them, and re-layouts  66.8 us
    reduce_scatter x3, waiting for transfers between devices, spread(): return lax.psum_scatter(term, 'fsdp', scatter_dimension=0, tiled=True)  60.4 us
    dot_general x4, matrix products, dot(): return jnp.dot(a, b, preferred_element_type=f32)  54.8 us
    all_to_all x1, blocking collectives, exchange(): return lax.all_to_all(term, 'seq', split_axis=0, concat_axis=0, tiled=True)  46.3 us
    reduce_scatter x1, waiting for transfers between devices, body(): lax.psum_scatter(dot(hidden, down_w).astype(bf16), 'seq', scatter_dimensi...  43.8 us
    all_gather x1, waiting for transfers between devices, body(): qkv_w = lax.all_gather(own_qkv, 'fsdp', axis=0, tiled=True)  43.6 us
    eq x32, local copies, waits for them, and re-layouts, tile_bias(): bucket == bucket_id  42.1 us
  transfers between devices with their start and end apart: 19, of which 13 were waited for; matrix products, arithmetic and copies ran while one was open for 25% of the time, Pallas kernels for 6%

profile of v1, /device:TPU:0, one launch (start us, length us, event | category | flops | bytes accessed | tf_op | source)
XLA Modules:
  0.0 1077.3 jit_solution(17922150420275858138)
XLA Ops:
  7.3 2.4 copy.251
  13.7 5.3 broadcast_compare_fusion.61
  19.7 22.4 %all_gather.28 = bf16[2,1024]{1,0:T(2,128)(2,1)S(1)} all-gather(bf16[2,128]{1,0:T(2,128)(2,1)S(1)} %pad_maximum_fusion.2), channel_id=1, replica_groups=mesh['seq'=4,'fsdp'=8] {'fsdp'}, dimensions={1}, use_global_device_ids=true | all-gather | bytes 4608 | tf_op jit(solution)/shard_map/all_gather | solution.py:438
  43.4 5.3 multiply_select_fusion.1.bias_ref
  48.7 3.1 fusion.1
  51.8 43.6 %all-gather.11.cloned.1.call-done = bf16[1024,768]{0,1:T(8,128)(2,1)} async-done(((bf16[128,768]{0,1:T(8,128)(2,1)}), bf16[1024,768]{0,1:T(8,128)(2,1)}) %all-gather.11.cloned.1.call-update) | async-done | bytes 1572880 | tf_op jit(solution)/shard_map/all_gather | solution.py:437
  95.4 6.6 convolution_convert_fusion.3.cur_ref.prev_ref
  102.0 20.5 %attend.1 = (bf16[2048,256]{1,0:T(8,128)(2,1)S(1)}, f32[512,256]{1,0:T(8,128)}, f32[4,512,256]{2,1,0:T(8,128)S(1)}, f32[4,512,256]{2,1,0:T(8,128)S(1)}, f32[2,2048]{1,0:T(2,128)S(1)}, /*index=5*/f32[2,2048]{1,0:T(2,128)S(1)}) custom-call(s32[1]{0:T(128)} %copy.376.length_ref, bf16[2048,768]{1,0:T(8,128)(2,1)S(1)} %convolution_convert_fusion.3.cur_ref.prev_ref, ...), custom_call_target="tpu_custom_call" | custom-call | flops 5033164800 | bytes 16777216 | tf_op jit(solution)/shard_map/attend/pallas_call | solution.py:163
  131.4 13.6 %all-gather.15.cloned.1.call-done = bf16[1024,1024]{1,0:T(8,128)(2,1)} async-done(((bf16[128,1024]{1,0:T(8,128)(2,1)}), bf16[1024,1024]{1,0:T(8,128)(2,1)}) %all-gather.15.cloned.1.call-update) | async-done | bytes 2097168 | tf_op jit(solution)/shard_map/all_gather | solution.py:446
  145.0 34.9 %all-gather.13.cloned.1.call-done = bf16[2048,1024]{1,0:T(8,128)(2,1)} async-done(((bf16[2048,256]{1,0:T(8,128)(2,1)}), bf16[2048,1024]{1,0:T(8,128)(2,1)}) %all-gather.13.cloned.1.call-update) | async-done | bytes 4194320 | tf_op jit(solution)/shard_map/all_gather | solution.py:461
  179.9 12.3 %multiply_reduce_fusion = (f32[2048]{0:T(1024)S(1)}, f32[2048,1024]{0,1:T(8,128)}) fusion(bf16[2048,1024]{1,0:T(8,128)(2,1)} %all-gather.13.cloned.1.call-done, bf16[1024,1024]{1,0:T(8,128)(2,1)} %all-gather.15.cloned.1.call-done, bf16[1,2048,1024]{1,2,0:T(8,128)(2,1)} %all-gather.23.cloned.1.call-done), kind=kOutput, calls=%fused_computation.24 | convolution fusion | flops 4303353856 | bytes 18882560 | tf_op jit(solution)/shard_map/dot_general | solution.py:53
  192.2 41.3 %all-gather.17.cloned.1.call-done = bf16[1024,1024]{0,1:T(8,128)(2,1)} async-done(((bf16[128,1024]{0,1:T(8,128)(2,1)}), bf16[1024,1024]{0,1:T(8,128)(2,1)}) %all-gather.17.cloned.1.call-update) | async-done | bytes 2097168 | tf_op jit(solution)/shard_map/all_gather | solution.py:444
  233.5 27.7 %multiply_convert_fusion = (bf16[2048,1024]{1,0:T(8,128)(2,1)}, f32[2048,1024]{1,0:T(8,128)}, f32[2048,1024]{1,0:T(8,128)}) fusion(bf16[1024,1024]{0,1:T(8,128)(2,1)} %all-gather.17.cloned.1.call-done, f32[2048,1024]{0,1:T(8,128)} %get-tuple-element.237, f32[1024]{0:T(1024)S(1)} %bitcast.212, f32[2048]{0:T(1024)S(1)} %add_rsqrt_fusion), kind=kOutput, calls=%fused_computation.10 | convolution fusion | flops 4437573632 | bytes 31469568 | tf_op jit(solution)/shard_map/dot_general | solution.py:53
  261.3 22.3 %all-gather.19.cloned.1.call-done = bf16[1024,1024]{1,0:T(8,128)(2,1)} async-done(((bf16[128,1024]{1,0:T(8,128)(2,1)}), bf16[1024,1024]{1,0:T(8,128)(2,1)}) %all-gather.19.cloned.1.call-update) | async-done | bytes 2097168 | tf_op jit(solution)/shard_map/all_gather | solution.py:445
  283.6 34.6 %all-gather.25.cloned.1.call-done = bf16[1,2048,1024]{2,1,0:T(8,128)(2,1)} async-done(((bf16[1,512,1024]{2,1,0:T(8,128)(2,1)}), bf16[1,2048,1024]{2,1,0:T(8,128)(2,1)}) %all-gather.25.cloned.1.call-update) | async-done | bytes 4194320 | tf_op jit(solution)/shard_map/all_gather | solution.py:447
  318.1 12.8 %add_convert_fusion = bf16[2048,1024]{1,0:T(8,128)(2,1)S(1)} fusion(f32[2048,1024]{1,0:T(8,128)} %get-tuple-element.163, f32[2048,1024]{1,0:T(8,128)} %get-tuple-element.238, bf16[1024,1024]{1,0:T(8,128)(2,1)} %all-gather.19.cloned.1.call-done, bf16[1,2048,1024]{2,1,0:T(8,128)(2,1)} %all-gather.25.cloned.1.call-done, bf16[2048]{0:T(1024)(128)(2,1)S(1)} %fusion.40), kind=kOutput, calls=%fused_computation.9 | convolution fusion | flops 4326424576 | bytes 27267072 | tf_op jit(solution)/shard_map/dot_general | solution.py:57
  331.0 1.9 copy-done.125
  332.9 6.2 convolution_convert_fusion.1
  341.3 2.2 multiply_reduce_fusion.1
  343.5 40.3 %reduce-scatter.15.cloned.1.call-done = bf16[512,1024]{0,1:T(8,128)(2,1)} async-done(((bf16[2048,1024]{0,1:T(8,128)(2,1)}), bf16[512,1024]{0,1:T(8,128)(2,1)}) %reduce-scatter.15.cloned.1.call-update) | async-done | bytes 1048592 | tf_op jit(solution)/shard_map/reduce_scatter | solution.py:471
  383.9 3.3 fusion.21
  387.2 3.2 fusion.45
  390.5 9.1 convolution_convert_fusion.5
  399.7 46.3 %all_to_all.23 = bf16[4,256,1024]{2,1,0:T(8,128)(2,1)S(1)} all-to-all(bf16[4,256,1024]{2,1,0:T(8,128)(2,1)S(1)} %bitcast.204), channel_id=1, replica_groups=mesh['seq'=4,'fsdp'=8] {'seq'}, dimensions={0} | all-to-all | bytes 4194304 | tf_op jit(solution)/shard_map/all_to_all | solution.py:512
  446.6 2.7 copy.342
  449.3 2.8 reshape.935
  452.2 9.4 fusion.28
  461.6 4.6 all-to-all-start.2
  466.3 6.0 broadcast_compare_fusion.29
  479.6 1.9 copy.280
  481.5 1.9 copy.279
  485.2 1.9 copy.277
  487.1 1.9 copy.276
  490.9 1.9 copy.274
  492.7 1.9 copy.273
  494.6 1.9 copy.272
  498.4 1.9 copy.270
  502.1 1.9 copy.268
  504.0 1.9 copy.267
  505.9 1.9 copy.266
  551.6 8.3 multiply_select_fusion.bias_ref
  559.8 3.1 copy.295
  563.1 3.8 convolution_convert_fusion.4.dout_ref
  567.1 40.8 %attend_back.1 = (bf16[2048,768]{1,0:T(8,128)(2,1)S(1)}, f32[2,128,128]{2,1,0:T(8,128)S(1)}, f32[1,256]{1,0:T(1,128)S(1)}, f32[2,384,256]{2,1,0:T(8,128)S(1)}, f32[2,8,256]{2,1,0:T(8,128)S(1)}) custom-call(s32[1]{0:T(128)} %copy.376.length_ref, bf16[2048,768]{1,0:T(8,128)(2,1)} %copy-done.12, bf16[2048,768]{1,0:T(8,128)(2,1)} %copy-done.12, ...), custom_call_target="tpu_custom_call" | custom-call | flops 12582912000 | bytes 20971520 | tf_op jit(solution)/shard_map/attend_back/pallas_call | solution.py:343
  607.9 3.5 convolution_convert_fusion.6
  613.1 4.5 all-to-all-start
  617.9 3.2 select_reduce_fusion.18
  622.5 3.8 select_reduce_fusion
  636.1 4.3 convolution_convert_fusion.7
  640.5 2.7 copy.293
  643.2 2.8 copy.334
  646.0 6.5 convolution_convert_fusion
  654.1 8.3 convolution_convert_fusion.2
  667.5 39.8 %all-reduce.2.cloned.1.call-done = f32[33088]{0:T(1024)} async-done(((f32[33088]{0:T(1024)}), f32[33088]{0:T(1024)}) %all-reduce.2.cloned.1.call-update) | async-done | bytes 132368 | tf_op jit(solution)/shard_map/psum | solution.py:502
  711.4 60.4 %reduce-scatter.19.cloned.1.call-done = bf16[32,1024]{1,0:T(8,128)(2,1)} async-done(((bf16[256,1024]{1,0:T(8,128)(2,1)}), bf16[32,1024]{1,0:T(8,128)(2,1)}) %reduce-scatter.19.cloned.1.call-update) | async-done | bytes 65552 | tf_op jit(solution)/shard_map/reduce_scatter | solution.py:509
  773.3 66.0 %reduce-scatter.25.cloned.1.call-done = bf16[32,3072]{1,0:T(8,128)(2,1)} async-done(((bf16[256,3072]{1,0:T(8,128)(2,1)}), bf16[32,3072]{1,0:T(8,128)(2,1)}) %reduce-scatter.25.cloned.1.call-update) | async-done | bytes 196624
  839.3 2.1 copy.335
  841.4 2.3 copy.330
  843.7 41.5 %reduce-scatter.17.cloned.1.call-done = bf16[512,1024]{0,1:T(8,128)(2,1)} async-done(((bf16[2048,1024]{0,1:T(8,128)(2,1)}), bf16[512,1024]{0,1:T(8,128)(2,1)}) %reduce-scatter.17.cloned.1.call-update) | async-done | bytes 1048592 | tf_op jit(solution)/shard_map/reduce_scatter | solution.py:491
  885.2 2.2 fusion.25
  888.5 43.8 %reduce-scatter.13.cloned.1.call-done = bf16[512,1024]{0,1:T(8,128)(2,1)} async-done(((bf16[2048,1024]{0,1:T(8,128)(2,1)}), bf16[512,1024]{0,1:T(8,128)(2,1)}) %reduce-scatter.13.cloned.1.call-update) | async-done | bytes 1048592 | tf_op jit(solution)/shard_map/reduce_scatter | solution.py:472
  932.3 4.1 fusion.16
  936.4 2.4 copy.328
  940.6 127.8 %reduce-scatter.27.cloned.1.call-done = f32[32,2]{1,0:T(8,128)} async-done(((f32[1024,2]{1,0:T(8,128)}), f32[32,2]{1,0:T(8,128)}) %reduce-scatter.27.cloned.1.call-update) | async-done | bytes 272
  (421 shorter events, 105.6 us)
Async XLA Ops:
  7.2 122.7 %copy-start = (bf16[512,1024]{1,0:T(8,128)(2,1)S(1)}, bf16[512,1024]{1,0:T(8,128)(2,1)}, u32[]{:S(2)}) copy-start(bf16[512,1024]{1,0:T(8,128)(2,1)} %param.22) | copy-start | bytes 3145732
  7.2 41.5 %all-gather.23.cloned.1.call-start = ((), (), s32[]{:S(2)}) async-start(), calls=%async_computation.24 | async-start | bytes 5242880 | tf_op jit(solution)/shard_map/all_gather | solution.py:433
  9.7 85.7 %all-gather.11.cloned.1.call-start = ((), (), s32[]{:S(2)}) async-start(), calls=%async_computation.11 | async-start | bytes 1769472 | tf_op jit(solution)/shard_map/all_gather | solution.py:437
  10.9 134.1 %all-gather.15.cloned.1.call-start = ((), (), s32[]{:S(2)}) async-start(), calls=%async_computation.13 | async-start | bytes 2359296 | tf_op jit(solution)/shard_map/all_gather | solution.py:446
  11.6 168.3 %all-gather.13.cloned.1.call-start = ((), (), s32[]{:S(2)}) async-start(), calls=%async_computation.12 | async-start | bytes 5242880 | tf_op jit(solution)/shard_map/all_gather | solution.py:461
  12.1 30.8 %copy-start.105 = (f32[2]{0:T(128)}, f32[2]{0:T(128)S(1)}, u32[]{:S(2)}) copy-start(f32[2]{0:T(128)S(1)} %get-tuple-element.149) | copy-start | bytes 28
  12.1 30.8 %copy-start.106 = (f32[2]{0:T(128)}, f32[2]{0:T(128)S(1)}, u32[]{:S(2)}) copy-start(f32[2]{0:T(128)S(1)} %get-tuple-element.150) | copy-start | bytes 28
  12.1 30.8 %copy-start.107 = (f32[2]{0:T(128)}, f32[2]{0:T(128)S(1)}, u32[]{:S(2)}) copy-start(f32[2]{0:T(128)S(1)} %get-tuple-element.151) | copy-start | bytes 28
  12.1 30.8 %copy-start.108 = (f32[2]{0:T(128)}, f32[2]{0:T(128)S(1)}, u32[]{:S(2)}) copy-start(f32[2]{0:T(128)S(1)} %get-tuple-element.152) | copy-start | bytes 28
  12.1 30.8 %copy-start.109 = (f32[2]{0:T(128)}, f32[2]{0:T(128)S(1)}, u32[]{:S(2)}) copy-start(f32[2]{0:T(128)S(1)} %get-tuple-element.153) | copy-start | bytes 28
  12.1 30.8 %copy-start.110 = (f32[2]{0:T(128)}, f32[2]{0:T(128)S(1)}, u32[]{:S(2)}) copy-start(f32[2]{0:T(128)S(1)} %get-tuple-element.154) | copy-start | bytes 28
  12.1 30.8 %copy-start.111 = (f32[2]{0:T(128)}, f32[2]{0:T(128)S(1)}, u32[]{:S(2)}) copy-start(f32[2]{0:T(128)S(1)} %get-tuple-element.155) | copy-start | bytes 28
  12.1 30.8 %copy-start.112 = (f32[2]{0:T(128)}, f32[2]{0:T(128)S(1)}, u32[]{:S(2)}) copy-start(f32[2]{0:T(128)S(1)} %get-tuple-element.156) | copy-start | bytes 28
  12.1 30.8 %copy-start.113 = (f32[2]{0:T(128)}, f32[2]{0:T(128)S(1)}, u32[]{:S(2)}) copy-start(f32[2]{0:T(128)S(1)} %get-tuple-element.157) | copy-start | bytes 28
  12.2 30.8 %copy-start.114 = (f32[2]{0:T(128)}, f32[2]{0:T(128)S(1)}, u32[]{:S(2)}) copy-start(f32[2]{0:T(128)S(1)} %get-tuple-element.158) | copy-start | bytes 28
  12.2 30.8 %copy-start.115 = (f32[2]{0:T(128)}, f32[2]{0:T(128)S(1)}, u32[]{:S(2)}) copy-start(f32[2]{0:T(128)S(1)} %get-tuple-element.159) | copy-start | bytes 28
  12.2 30.8 %copy-start.116 = (f32[2]{0:T(128)}, f32[2]{0:T(128)S(1)}, u32[]{:S(2)}) copy-start(f32[2]{0:T(128)S(1)} %get-tuple-element.160) | copy-start | bytes 28
  12.2 30.8 %copy-start.117 = (f32[2]{0:T(128)}, f32[2]{0:T(128)S(1)}, u32[]{:S(2)}) copy-start(f32[2]{0:T(128)S(1)} %get-tuple-element.161) | copy-start | bytes 28
  13.7 28.9 %copy-start.118 = (f32[2,128]{1,0:T(2,128)S(1)}, f32[2,128]{1,0:T(2,128)}, u32[]{:S(2)}) copy-start(f32[2,128]{1,0:T(2,128)} %param.27) | copy-start | bytes 3076
  42.8 59.1 %copy-start.6 = (f32[2,128]{1,0:T(2,128)}, f32[2,128]{1,0:T(2,128)S(1)}, u32[]{:S(2)}) copy-start(f32[2,128]{1,0:T(2,128)S(1)} %add_divide_fusion) | copy-start | bytes 3076
  42.8 52.5 %copy-start.68 = (f32[1,1024]{1,0:T(1,128)}, f32[1,1024]{1,0:T(1,128)S(1)}, u32[]{:S(2)}) copy-start(f32[1,1024]{1,0:T(1,128)S(1)} %get-tuple-element.233) | copy-start | bytes 12292
  42.9 347.7 %copy-start.66 = (f32[1,1024]{1,0:T(1,128)}, f32[1,1024]{1,0:T(1,128)S(1)}, u32[]{:S(2)}) copy-start(f32[1,1024]{1,0:T(1,128)S(1)} %get-tuple-element.232) | copy-start | bytes 12292
  51.8 50.2 %copy-start.80 = (f32[2048]{0:T(1024)}, f32[2048]{0:T(1024)S(1)}, u32[]{:S(2)}) copy-start(f32[2048]{0:T(1024)S(1)} %add_rsqrt_fusion.1) | copy-start | bytes 24580
  127.4 106.2 %all-gather.17.cloned.1.call-start = ((), (), s32[]{:S(2)}) async-start(), calls=%async_computation.14 | async-start | bytes 2359296 | tf_op jit(solution)/shard_map/all_gather | solution.py:444
  129.8 153.8 %all-gather.19.cloned.1.call-start = ((), (), s32[]{:S(2)}) async-start(), calls=%async_computation.15 | async-start | bytes 2359296 | tf_op jit(solution)/shard_map/all_gather | solution.py:445
  130.6 187.5 %all-gather.25.cloned.1.call-start = ((), (), s32[]{:S(2)}) async-start(), calls=%async_computation.25 | async-start | bytes 5242880 | tf_op jit(solution)/shard_map/all_gather | solution.py:447
  131.3 252.5 %reduce-scatter.15.cloned.1.call-start = ((), (), s32[]{:S(2)}) async-start(), calls=%async_computation.17 | async-start | bytes 5242880 | tf_op jit(solution)/shard_map/reduce_scatter | solution.py:471
  339.2 223.8 %all-gather.21.cloned.1.call-start = ((), (), s32[]{:S(2)}) async-start(), calls=%async_computation.18 | async-start | bytes 5242880 | tf_op jit(solution)/shard_map/all_gather | solution.py:483
  341.3 45.9 %copy-start.24 = (bf16[1,512,1024]{1,2,0:T(8,128)(2,1)}, bf16[1,512,1024]{1,2,0:T(8,128)(2,1)S(1)}, u32[]{:S(2)}) copy-start(bf16[1,512,1024]{1,2,0:T(8,128)(2,1)S(1)} %copy.255) | copy-start | bytes 3145732
  341.3 45.9 %copy-start.75 = (f32[512]{0:T(512)}, f32[512]{0:T(512)S(1)}, u32[]{:S(2)}) copy-start(f32[512]{0:T(512)S(1)} %fusion.43) | copy-start | bytes 6148
  343.5 46.9 %copy-start.71 = (f32[512]{0:T(512)}, f32[512]{0:T(512)S(1)}, u32[]{:S(2)}) copy-start(f32[512]{0:T(512)S(1)} %add_rsqrt_fusion.3) | copy-start | bytes 6148
  390.5 273.4 %reduce-scatter.21.cloned.1.call-start = ((), (), s32[]{:S(2)}) async-start(), calls=%async_computation.21 | async-start | bytes 2359296 | tf_op jit(solution)/shard_map/reduce_scatter | solution.py:509
  461.6 98.2 %all-to-all-start.2 = ((bf16[4,2,128,1024]{3,2,1,0:T(8,128)(2,1)}), bf16[4,2,128,1024]{3,2,1,0:T(8,128)(2,1)}, u32[]{:S(2)}, u32[]{:S(2)}) async-start(bf16[4,2,128,1024]{3,2,1,0:T(8,128)(2,1)} %bitcast.28), calls=%async_computation.7 | async-start | bytes 4194304 | tf_op jit(solution)/shard_map/all_to_all | solution.py:522
  466.3 199.4 %reduce-scatter.23.cloned.1.call-start = ((), (), s32[]{:S(2)}) async-start(), calls=%async_computation.22 | async-start | bytes 2359296 | tf_op jit(solution)/shard_map/reduce_scatter | solution.py:509
  512.5 28.2 %copy-start.65 = (pred[384,256]{1,0:T(32,128)(4,1)S(1)}, pred[384,256]{1,0:T(32,128)(4,1)}, u32[]{:S(2)}) copy-start(pred[384,256]{1,0:T(32,128)(4,1)} %constant.239) | copy-start | bytes 294916
  513.5 27.9 %copy-start.64 = (pred[384,256]{1,0:T(32,128)(4,1)S(1)}, pred[384,256]{1,0:T(32,128)(4,1)}, u32[]{:S(2)}) copy-start(pred[384,256]{1,0:T(32,128)(4,1)} %constant.238) | copy-start | bytes 294916
  513.5 28.6 %copy-start.63 = (pred[384,256]{1,0:T(32,128)(4,1)S(1)}, pred[384,256]{1,0:T(32,128)(4,1)}, u32[]{:S(2)}) copy-start(pred[384,256]{1,0:T(32,128)(4,1)} %constant.237) | copy-start | bytes 294916
  514.5 28.3 %copy-start.62 = (pred[384,256]{1,0:T(32,128)(4,1)S(1)}, pred[384,256]{1,0:T(32,128)(4,1)}, u32[]{:S(2)}) copy-start(pred[384,256]{1,0:T(32,128)(4,1)} %constant.236) | copy-start | bytes 294916
  514.5 29.0 %copy-start.61 = (pred[384,256]{1,0:T(32,128)(4,1)S(1)}, pred[384,256]{1,0:T(32,128)(4,1)}, u32[]{:S(2)}) copy-start(pred[384,256]{1,0:T(32,128)(4,1)} %constant.235) | copy-start | bytes 294916
  515.4 28.7 %copy-start.60 = (pred[384,256]{1,0:T(32,128)(4,1)S(1)}, pred[384,256]{1,0:T(32,128)(4,1)}, u32[]{:S(2)}) copy-start(pred[384,256]{1,0:T(32,128)(4,1)} %constant.234) | copy-start | bytes 294916
  517.0 27.8 %copy-start.59 = (pred[384,256]{1,0:T(32,128)(4,1)S(1)}, pred[384,256]{1,0:T(32,128)(4,1)}, u32[]{:S(2)}) copy-start(pred[384,256]{1,0:T(32,128)(4,1)} %constant.74) | copy-start | bytes 294916
  518.6 26.8 %copy-start.58 = (pred[384,256]{1,0:T(32,128)(4,1)S(1)}, pred[384,256]{1,0:T(32,128)(4,1)}, u32[]{:S(2)}) copy-start(pred[384,256]{1,0:T(32,128)(4,1)} %constant.73) | copy-start | bytes 294916
  520.2 25.9 %copy-start.57 = (pred[384,256]{1,0:T(32,128)(4,1)S(1)}, pred[384,256]{1,0:T(32,128)(4,1)}, u32[]{:S(2)}) copy-start(pred[384,256]{1,0:T(32,128)(4,1)} %constant.72) | copy-start | bytes 294916
  521.8 25.0 %copy-start.56 = (pred[384,256]{1,0:T(32,128)(4,1)S(1)}, pred[384,256]{1,0:T(32,128)(4,1)}, u32[]{:S(2)}) copy-start(pred[384,256]{1,0:T(32,128)(4,1)} %constant.71) | copy-start | bytes 294916
  523.4 24.1 %copy-start.55 = (pred[384,256]{1,0:T(32,128)(4,1)S(1)}, pred[384,256]{1,0:T(32,128)(4,1)}, u32[]{:S(2)}) copy-start(pred[384,256]{1,0:T(32,128)(4,1)} %constant.70) | copy-start | bytes 294916
  567.1 40.8 %copy-start.31 = (bf16[1,2048,1024]{1,2,0:T(8,128)(2,1)S(1)}, bf16[1,2048,1024]{1,2,0:T(8,128)(2,1)}, u32[]{:S(2)}) copy-start(bf16[1,2048,1024]{1,2,0:T(8,128)(2,1)} %all-gather.23.cloned.1.call-done) | copy-start | bytes 12582916
  567.1 40.9 %copy-start.69 = (f32[1,1024]{1,0:T(1,128)S(1)}, f32[1,1024]{1,0:T(1,128)}, u32[]{:S(2)}) copy-start(f32[1,1024]{1,0:T(1,128)} %copy-done.68) | copy-start | bytes 12292
  567.1 40.9 %copy-start.81 = (f32[2048]{0:T(1024)S(1)}, f32[2048]{0:T(1024)}, u32[]{:S(2)}) copy-start(f32[2048]{0:T(1024)} %copy-done.80) | copy-start | bytes 24580
  613.1 27.4 %all-to-all-start = ((bf16[4,256,768]{1,2,0:T(8,128)(2,1)}), bf16[4,256,768]{1,2,0:T(8,128)(2,1)}, u32[]{:S(2)}, u32[]{:S(2)}) async-start(bf16[4,256,768]{1,2,0:T(8,128)(2,1)} %copy.292), calls=%async_computation.3 | async-start | bytes 3145728 | tf_op jit(solution)/shard_map/all_to_all | solution.py:512
  617.7 89.6 %all-reduce.2.cloned.1.call-start = ((), (), s32[]{:S(2)}) async-start(), calls=%async_computation.23 | async-start | bytes 270336 | tf_op jit(solution)/shard_map/psum | solution.py:502
  636.1 135.7 %reduce-scatter.19.cloned.1.call-start = ((), (), s32[]{:S(2)}) async-start(), calls=%async_computation.20 | async-start | bytes 589824 | tf_op jit(solution)/shard_map/reduce_scatter | solution.py:509
  640.5 198.9 %reduce-scatter.25.cloned.1.call-start = ((), (), s32[]{:S(2)}) async-start(), calls=%async_computation.26 | async-start | bytes 1769472
  645.9 239.2 %reduce-scatter.17.cloned.1.call-start = ((), (), s32[]{:S(2)}) async-start(), calls=%async_computation.19 | async-start | bytes 5242880 | tf_op jit(solution)/shard_map/reduce_scatter | solution.py:491
  652.5 279.7 %reduce-scatter.13.cloned.1.call-start = ((), (), s32[]{:S(2)}) async-start(), calls=%async_computation.16 | async-start | bytes 5242880 | tf_op jit(solution)/shard_map/reduce_scatter | solution.py:472
  662.4 406.1 %reduce-scatter.27.cloned.1.call-start = ((), (), s32[]{:S(2)}) async-start(), calls=%async_computation.27 | async-start | bytes 540672
  663.9 221.3 %copy-start.70 = (f32[1,1024]{1,0:T(1,128)S(1)}, f32[1,1024]{1,0:T(1,128)}, u32[]{:S(2)}) copy-start(f32[1,1024]{1,0:T(1,128)} %copy-done.68) | copy-start | bytes 12292
  773.3 114.1 %copy-start.77 = (f32[1024]{0:T(1024)S(1)}, f32[1024]{0:T(1024)}, u32[]{:S(2)}) copy-start(f32[1024]{0:T(1024)} %get-tuple-element.94) | copy-start | bytes 12292
  841.4 90.9 %copy-start.25 = (bf16[1,512,1024]{1,2,0:T(8,128)(2,1)S(1)}, bf16[1,512,1024]{1,2,0:T(8,128)(2,1)}, u32[]{:S(2)}) copy-start(bf16[1,512,1024]{1,2,0:T(8,128)(2,1)} %copy-done.24) | copy-start | bytes 3145732
  841.4 90.9 %copy-start.27 = (bf16[512,1024]{0,1:T(8,128)(2,1)S(1)}, bf16[512,1024]{0,1:T(8,128)(2,1)}, u32[]{:S(2)}) copy-start(bf16[512,1024]{0,1:T(8,128)(2,1)} %reduce-scatter.15.cloned.1.call-done) | copy-start | bytes 3145732
  841.4 90.9 %copy-start.67 = (f32[1,1024]{1,0:T(1,128)S(1)}, f32[1,1024]{1,0:T(1,128)}, u32[]{:S(2)}) copy-start(f32[1,1024]{1,0:T(1,128)} %copy-done.66) | copy-start | bytes 12292
  841.4 90.9 %copy-start.72 = (f32[512]{0:T(512)S(1)}, f32[512]{0:T(512)}, u32[]{:S(2)}) copy-start(f32[512]{0:T(512)} %copy-done.71) | copy-start | bytes 6148
  841.4 90.9 %copy-start.74 = (f32[512]{0:T(512)S(1)}, f32[512]{0:T(512)}, u32[]{:S(2)}) copy-start(f32[512]{0:T(512)} %copy-done.73) | copy-start | bytes 6148
  841.4 90.9 %copy-start.76 = (f32[512]{0:T(512)S(1)}, f32[512]{0:T(512)}, u32[]{:S(2)}) copy-start(f32[512]{0:T(512)} %copy-done.75) | copy-start | bytes 6148
  938.8 131.7 %copy-start.1 = (bf16[512,1024]{1,0:T(8,128)(2,1)S(1)}, bf16[512,1024]{1,0:T(8,128)(2,1)}, u32[]{:S(2)}) copy-start(bf16[512,1024]{1,0:T(8,128)(2,1)} %param.22) | copy-start | bytes 3145732
  (81 other events, 517.5 us)
Sparse Core Ops, SparseCore 0:
  10.2 37.1 all-gather.22
  50.0 45.2 all-gather.10
  97.5 47.4 all-gather.14
  146.4 33.4 all-gather.12
  182.4 51.0 all-gather.16
  236.1 47.4 all-gather.18
  285.1 32.9 all-gather.24
  339.3 44.4 reduce-scatter.14
  390.6 52.7 all-gather.20
  452.3 67.7 reduce-scatter.20
  563.1 69.0 reduce-scatter.22
  636.3 70.8 all-reduce.1
  710.6 61.1 reduce-scatter.18
  775.5 63.8 reduce-scatter.24
  841.7 43.4 reduce-scatter.16
  887.7 44.4 reduce-scatter.12
  934.3 134.0 reduce-scatter.26

commit v2 on v1

--- a/solution.py
+++ b/solution.py
@@ -25,6 +25,7 @@
 
 f32 = jnp.float32
 bf16 = jnp.bfloat16
+MESH = pl.DeviceIdType.MESH
 
 
 def bucket_of(distance):
@@ -85,6 +86,7 @@
 def attend_kernel(
     heads,
     length_ref,
+    order_ref,
     cur_ref,
     prev_ref,
     init_ref,
@@ -156,13 +158,12 @@
     final_ref[...] = memory_ref[...]
 
 
-def attend(qkv, init, length, state_query, forget, bias, heads):
+def attend(qkv, init, length, state_query, forget, bias, heads, order):
     rows, width3 = qkv.shape
     width = heads * DH
     blocks = rows // BLOCK
     return pl.pallas_call(
         functools.partial(attend_kernel, heads),
-        grid=(blocks,),
         out_shape=(
             jax.ShapeDtypeStruct((rows, width), bf16),
             jax.ShapeDtypeStruct((STATE_VECTORS, width), f32),
@@ -171,36 +172,40 @@
             jax.ShapeDtypeStruct((heads, rows), f32),
             jax.ShapeDtypeStruct((heads, blocks * STATE_VECTORS), f32),
         ),
-        in_specs=[
-            pl.BlockSpec(memory_space=pltpu.SMEM),
-            pl.BlockSpec((BLOCK, width3), lambda b: (b, 0)),
-            pl.BlockSpec((BLOCK, width3), lambda b: (jnp.maximum(b - 1, 0), 0)),
-            pl.BlockSpec((STATE_VECTORS, width), lambda b: (0, 0)),
-            pl.BlockSpec((heads, DH, DH), lambda b: (0, 0, 0)),
-            pl.BlockSpec((1, width), lambda b: (0, 0)),
-            pl.BlockSpec((heads, QTILE, SPAN), lambda b: (0, 0, 0)),
-        ],
-        out_specs=(
-            pl.BlockSpec((BLOCK, width), lambda b: (b, 0)),
-            pl.BlockSpec((STATE_VECTORS, width), lambda b: (0, 0)),
-            pl.BlockSpec((1, STATE_VECTORS, width), lambda b: (b, 0, 0)),
-            pl.BlockSpec((1, STATE_VECTORS, width), lambda b: (b, 0, 0)),
-            pl.BlockSpec((heads, BLOCK), lambda b: (0, b)),
-            pl.BlockSpec((heads, STATE_VECTORS), lambda b: (0, b)),
-        ),
-        scratch_shapes=[pltpu.VMEM((STATE_VECTORS, width), f32)],
+        grid_spec=pltpu.PrefetchScalarGridSpec(
+            num_scalar_prefetch=2,
+            grid=(blocks,),
+            in_specs=[
+                pl.BlockSpec((BLOCK, width3), lambda b, _, at: (at[b], 0)),
+                pl.BlockSpec((BLOCK, width3), lambda b, _, at: (at[jnp.maximum(b - 1, 0)], 0)),
+                pl.BlockSpec((STATE_VECTORS, width), lambda b, _, at: (0, 0)),
+                pl.BlockSpec((heads, DH, DH), lambda b, _, at: (0, 0, 0)),
+                pl.BlockSpec((1, width), lambda b, _, at: (0, 0)),
+                pl.BlockSpec((heads, QTILE, SPAN), lambda b, _, at: (0, 0, 0)),
+            ],
+            out_specs=(
+                pl.BlockSpec((BLOCK, width), lambda b, _, at: (at[b], 0)),
+                pl.BlockSpec((STATE_VECTORS, width), lambda b, _, at: (0, 0)),
+                pl.BlockSpec((1, STATE_VECTORS, width), lambda b, _, at: (b, 0, 0)),
+                pl.BlockSpec((1, STATE_VECTORS, width), lambda b, _, at: (b, 0, 0)),
+                pl.BlockSpec((heads, BLOCK), lambda b, _, at: (0, b)),
+                pl.BlockSpec((heads, STATE_VECTORS), lambda b, _, at: (0, b)),
+            ),
+            scratch_shapes=[pltpu.VMEM((STATE_VECTORS, width), f32)],
+        ),
         compiler_params=pltpu.CompilerParams(vmem_limit_bytes=40 << 20),
         cost_estimate=pl.CostEstimate(
             flops=blocks * heads * 512 * 2400 * 128 * 4, bytes_accessed=16 << 20, transcendentals=10 << 20
         ),
         name="attend",
-    )(length, qkv, qkv, init, state_query, forget, bias)
+    )(length, order, qkv, qkv, init, state_query, forget, bias)
 
 
 def attend_back_kernel(
     heads,
     blocks,
     length_ref,
+    order_ref,
     cur_ref,
     prev_ref,
     dout_ref,
@@ -335,14 +340,13 @@
         dqkv_ref[:, value_cols] = dctx_ref[1, BLOCK:].astype(bf16)
 
 
-def attend_back(qkv, dout, out, mem, upd, lse, slse, sgrad, length, state_query, forget, bias_t, heads):
+def attend_back(qkv, dout, out, mem, upd, lse, slse, sgrad, length, state_query, forget, bias_t, heads, order):
     rows, width3 = qkv.shape
     width = heads * DH
     blocks = rows // BLOCK
     last = blocks - 1
     return pl.pallas_call(
         functools.partial(attend_back_kernel, heads, blocks),
-        grid=(blocks,),
         out_shape=(
             jax.ShapeDtypeStruct((rows, width3), bf16),
             jax.ShapeDtypeStruct((heads, DH, DH), f32),
@@ -350,39 +354,214 @@
             jax.ShapeDtypeStruct((heads, NEAR, QTILE), f32),
             jax.ShapeDtypeStruct((heads, 8, QTILE), f32),
         ),
-        in_specs=[
-            pl.BlockSpec(memory_space=pltpu.SMEM),
-            pl.BlockSpec((BLOCK, width3), lambda b: (last - b, 0)),
-            pl.BlockSpec((BLOCK, width3), lambda b: (jnp.maximum(last - b - 1, 0), 0)),
-            pl.BlockSpec((BLOCK, width), lambda b: (last - b, 0)),
-            pl.BlockSpec((BLOCK, width), lambda b: (last - b, 0)),
-            pl.BlockSpec((1, STATE_VECTORS, width), lambda b: (last - b, 0, 0)),
-            pl.BlockSpec((1, STATE_VECTORS, width), lambda b: (last - b, 0, 0)),
-            pl.BlockSpec((heads, BLOCK), lambda b: (0, last - b)),
-            pl.BlockSpec((heads, STATE_VECTORS), lambda b: (0, last - b)),
-            pl.BlockSpec((STATE_VECTORS, width), lambda b: (0, 0)),
-            pl.BlockSpec((heads, DH, DH), lambda b: (0, 0, 0)),
-            pl.BlockSpec((1, width), lambda b: (0, 0)),
-            pl.BlockSpec((heads, SPAN, QTILE), lambda b: (0, 0, 0)),
-        ],
-        out_specs=(
-            pl.BlockSpec((BLOCK, width3), lambda b: (last - b, 0)),
-            pl.BlockSpec((heads, DH, DH), lambda b: (0, 0, 0)),
-            pl.BlockSpec((1, width), lambda b: (0, 0)),
-            pl.BlockSpec((heads, NEAR, QTILE), lambda b: (0, 0, 0)),
-            pl.BlockSpec((heads, 8, QTILE), lambda b: (0, 0, 0)),
-        ),
-        scratch_shapes=[
-            pltpu.VMEM((STATE_VECTORS, width), f32),
-            pltpu.VMEM((2, BLOCK, width), f32),
-            pltpu.VMEM((2, 2 * BLOCK, DH), f32),
-        ],
+        grid_spec=pltpu.PrefetchScalarGridSpec(
+            num_scalar_prefetch=2,
+            grid=(blocks,),
+            in_specs=[
+                pl.BlockSpec((BLOCK, width3), lambda b, _, at: (at[last - b], 0)),
+                pl.BlockSpec((BLOCK, width3), lambda b, _, at: (at[jnp.maximum(last - b - 1, 0)], 0)),
+                pl.BlockSpec((BLOCK, width), lambda b, _, at: (at[last - b], 0)),
+                pl.BlockSpec((BLOCK, width), lambda b, _, at: (at[last - b], 0)),
+                pl.BlockSpec((1, STATE_VECTORS, width), lambda b, _, at: (last - b, 0, 0)),
+                pl.BlockSpec((1, STATE_VECTORS, width), lambda b, _, at: (last - b, 0, 0)),
+                pl.BlockSpec((heads, BLOCK), lambda b, _, at: (0, last - b)),
+                pl.BlockSpec((heads, STATE_VECTORS), lambda b, _, at: (0, last - b)),
+                pl.BlockSpec((STATE_VECTORS, width), lambda b, _, at: (0, 0)),
+                pl.BlockSpec((heads, DH, DH), lambda b, _, at: (0, 0, 0)),
+                pl.BlockSpec((1, width), lambda b, _, at: (0, 0)),
+                pl.BlockSpec((heads, SPAN, QTILE), lambda b, _, at: (0, 0, 0)),
+            ],
+            out_specs=(
+                pl.BlockSpec((BLOCK, width3), lambda b, _, at: (at[last - b], 0)),
+                pl.BlockSpec((heads, DH, DH), lambda b, _, at: (0, 0, 0)),
+                pl.BlockSpec((1, width), lambda b, _, at: (0, 0)),
+                pl.BlockSpec((heads, NEAR, QTILE), lambda b, _, at: (0, 0, 0)),
+                pl.BlockSpec((heads, 8, QTILE), lambda b, _, at: (0, 0, 0)),
+            ),
+            scratch_shapes=[
+                pltpu.VMEM((STATE_VECTORS, width), f32),
+                pltpu.VMEM((2, BLOCK, width), f32),
+                pltpu.VMEM((2, 2 * BLOCK, DH), f32),
+            ],
+        ),
         compiler_params=pltpu.CompilerParams(vmem_limit_bytes=40 << 20),
         cost_estimate=pl.CostEstimate(
             flops=blocks * heads * 512 * 2400 * 128 * 10, bytes_accessed=20 << 20, transcendentals=10 << 20
         ),
         name="attend_back",
-    )(length, qkv, qkv, dout, out, mem, upd, lse, slse, sgrad, state_query, forget, bias_t)
+    )(length, order, qkv, qkv, dout, out, mem, upd, lse, slse, sgrad, state_query, forget, bias_t)
+
+
+def gather_kernel(seq, hi, lo, tok_ref, w_ref, gain_ref, toks_ref, ws_ref, gains_ref, here_sem, seq_send, seq_recv, far_send, far_recv, lo_send, lo_recv):
+    me = lax.axis_index("seq")
+    f = lax.axis_index("fsdp")
+    z, y = f // lo, f % lo
+    pairs = ((w_ref, ws_ref), (gain_ref, gains_ref))
+
+    barrier = pltpu.get_barrier_semaphore()
+    greeted = 0
+    bit = 1
+    while bit < seq:
+        pl.semaphore_signal(barrier, inc=1, device_id={"seq": me ^ bit}, device_id_type=MESH)
+        greeted += 1
+        bit *= 2
+    for target in (lax.rem(z + 1, hi) * lo + y, lax.rem(z + hi - 1, hi) * lo + y):
+        pl.semaphore_signal(barrier, inc=1, device_id={"fsdp": target}, device_id_type=MESH)
+        greeted += 1
+    pl.semaphore_signal(barrier, inc=1, device_id={"fsdp": z * lo + 1 - y}, device_id_type=MESH)
+    greeted += 1
+    pl.semaphore_wait(barrier, greeted)
+
+    own_copies = [pltpu.make_async_copy(tok_ref, toks_ref.at[0], here_sem.at[0])]
+    own_copies += [pltpu.make_async_copy(a, b.at[f], here_sem.at[1 + i]) for i, (a, b) in enumerate(pairs)]
+    for c in own_copies:
+        c.start()
+
+    def seq_copy(source, slot, bit):
+        src = tok_ref if source == 0 else toks_ref.at[source]
+        return pltpu.make_async_remote_copy(
+            src_ref=src, dst_ref=toks_ref.at[slot], send_sem=seq_send.at[slot], recv_sem=seq_recv.at[slot],
+            device_id={"seq": me ^ bit}, device_id_type=MESH,
+        )
+
+    def fsdp_copy(i, origin, own, target, send, recv):
+        src, out = pairs[i]
+        return pltpu.make_async_remote_copy(
+            src_ref=src if own else out.at[origin], dst_ref=out.at[origin], send_sem=send, recv_sem=recv,
+            device_id={"fsdp": target}, device_id_type=MESH,
+        )
+
+    def right(i, t):
+        return fsdp_copy(i, (z - t) * lo + y, t == 0, (z + 1) * lo + y, far_send.at[i, 0, t], far_recv.at[i, 0, t])
+
+    def left(i, t):
+        return fsdp_copy(i, (z + t) * lo + y, t == 0, (z - 1) * lo + y, far_send.at[i, 1, t], far_recv.at[i, 1, t])
+
+    def across(i, d):
+        return fsdp_copy(i, (z + d) * lo + y, d == 0, z * lo + 1 - y, lo_send.at[i, d + hi - 1], lo_recv.at[i, d + hi - 1])
+
+    both = range(len(pairs))
+    seq_sends = []
+    bits = []
+    bit = seq // 2
+    while bit > 1:
+        bits.append(bit)
+        bit //= 2
+    have = [0]
+    if bits:
+        seq_sends.append(seq_copy(0, bits[0], bits[0]))
+        seq_sends[-1].start()
+    if seq > 1:
+        seq_sends.append(seq_copy(0, 1, 1))
+        seq_sends[-1].start()
+    for i in both:
+        pl.when(z + 1 < hi)(right(i, 0).start)
+        pl.when(z >= 1)(left(i, 0).start)
+        across(i, 0).start()
+    for t in range(hi - 1):
+        for i in both:
+            @pl.when(z - 1 - t >= 0)
+            def _():
+                fsdp_copy(i, (z - 1 - t) * lo + y, False, f, far_send.at[i, 0, t], far_recv.at[i, 0, t]).wait_recv()
+                across(i, -1 - t).start()
+                if t + 1 < hi - 1:
+                    pl.when(z + 1 < hi)(right(i, t + 1).start)
+
+            @pl.when(z + 1 + t < hi)
+            def _():
+                fsdp_copy(i, (z + 1 + t) * lo + y, False, f, far_send.at[i, 1, t], far_recv.at[i, 1, t]).wait_recv()
+                across(i, 1 + t).start()
+                if t + 1 < hi - 1:
+                    pl.when(z >= 1)(left(i, t + 1).start)
+    for n, bit in enumerate(bits):
+        if n:
+            for j in have:
+                seq_sends.append(seq_copy(j, j ^ bit, bit))
+                seq_sends[-1].start()
+        for j in list(have):
+            seq_copy(0, j ^ bit, bit).wait_recv()
+            seq_sends.append(seq_copy(j ^ bit, j ^ bit ^ 1, 1))
+            seq_sends[-1].start()
+        have += [j ^ bit for j in have]
+    for j in have if seq > 1 else []:
+        seq_copy(0, j ^ 1, 1).wait_recv()
+    for i in both:
+        for d in range(1 - hi, hi):
+            @pl.when((z + d >= 0) & (z + d < hi))
+            def _():
+                fsdp_copy(i, (z + d) * lo + 1 - y, False, f, lo_send.at[i, d + hi - 1], lo_recv.at[i, d + hi - 1]).wait_recv()
+                across(i, d).wait_send()
+        for t in range(hi - 1):
+            @pl.when((z + 1 < hi) & (z - t >= 0))
+            def _():
+                right(i, t).wait_send()
+
+            @pl.when((z >= 1) & (z + t < hi))
+            def _():
+                left(i, t).wait_send()
+    for c in seq_sends:
+        c.wait_send()
+    for c in own_copies:
+        c.wait()
+
+
+def gather_start(tokens, weights, gains, seq, fsdp):
+    lo = 2
+    hi = fsdp // lo
+    anywhere = pl.BlockSpec(memory_space=pl.ANY)
+    return pl.pallas_call(
+        functools.partial(gather_kernel, seq, hi, lo),
+        out_shape=(
+            jax.ShapeDtypeStruct((seq,) + tokens.shape, tokens.dtype),
+            jax.ShapeDtypeStruct((fsdp,) + weights.shape, weights.dtype),
+            jax.ShapeDtypeStruct((fsdp,) + gains.shape, gains.dtype),
+        ),
+        in_specs=[anywhere] * 3,
+        out_specs=(anywhere,) * 3,
+        scratch_shapes=[
+            pltpu.SemaphoreType.DMA((3,)),
+            pltpu.SemaphoreType.DMA((seq,)),
+            pltpu.SemaphoreType.DMA((seq,)),
+            pltpu.SemaphoreType.DMA((2, 2, hi)),
+            pltpu.SemaphoreType.DMA((2, 2, hi)),
+            pltpu.SemaphoreType.DMA((2, 2 * hi)),
+            pltpu.SemaphoreType.DMA((2, 2 * hi)),
+        ],
+        compiler_params=pltpu.CompilerParams(collective_id=0, has_side_effects=True),
+        name="gather_start",
+    )(tokens, weights, gains)
+
+
+def swap(value, bit):
+    count = lax.axis_size("seq")
+    return lax.ppermute(value, "seq", [(i, i ^ bit) for i in range(count)])
+
+
+def seq_bits():
+    count = lax.axis_size("seq")
+    return [1 << i for i in reversed(range(1, count.bit_length() - 1))]
+
+
+def seq_gather(value):
+    chunks = {0: value}
+    for bit in seq_bits():
+        for j in list(chunks):
+            chunks[j ^ bit] = swap(chunks[j], bit)
+    for j in list(chunks):
+        chunks[j ^ 1] = swap(chunks[j], 1)
+    return [chunks[j] for j in range(len(chunks))]
+
+
+def seq_reduce(parts):
+    count = len(parts)
+    parts = dict(enumerate(parts))
+    for j in range(count - 2, -1, -2):
+        parts[j] = parts[j].astype(f32) + swap(parts.pop(j ^ 1).astype(bf16), 1).astype(f32)
+    for bit in reversed(seq_bits()):
+        keep = [j for j in parts if not j & bit]
+        for j in sorted(keep, reverse=True):
+            parts[j] = parts[j] + swap(parts.pop(j ^ bit).astype(bf16), bit).astype(f32)
+    return parts[0]
 
 
 def bias_table_grad(near, far):
@@ -430,68 +609,85 @@
     hidden_all = w_up.shape[1]
     share = hidden_all // (seq_count * fsdp_count)
 
-    all_tokens = lax.all_gather(tokens[0], "seq", axis=0, tiled=True)
     own_qkv = lax.dynamic_slice_in_dim(
         w_qkv.reshape(w_qkv.shape[0], 3, seq_count, width), seq_at, 1, axis=2
     ).reshape(w_qkv.shape[0], 3 * width)
-    qkv_w = lax.all_gather(own_qkv, "fsdp", axis=0, tiled=True)
-    gains = lax.all_gather(jnp.stack([norm_attn, norm_mlp]), "fsdp", axis=1, tiled=True).astype(f32)
-    gain_attn, gain_mlp = gains[0], gains[1]
     own_up = lax.dynamic_slice_in_dim(
         w_up.reshape(w_up.shape[0], fsdp_count, seq_count, share), seq_at, 1, axis=2
     ).reshape(w_up.shape[0], fsdp_count * share)
     own_down = lax.dynamic_slice_in_dim(w_down, seq_at * share, share, axis=0)
+    out_w = lax.all_gather(w_out, "fsdp", axis=0, tiled=True)
     up_w = lax.all_gather(own_up, "fsdp", axis=0, tiled=True)
     down_w = lax.all_gather(own_down, "fsdp", axis=0, tiled=True)
-    out_w = lax.all_gather(w_out, "fsdp", axis=0, tiled=True)
-    all_grad = lax.all_gather(out_grad[0], "seq", axis=0, tiled=True)
+    all_tokens, qkv_w, gains = gather_start(
+        tokens[0], own_qkv, jnp.stack([norm_attn, norm_mlp]), seq_count, fsdp_count
+    )
+    qkv_w = qkv_w.reshape(dim, 3 * width)
+    gains = jnp.swapaxes(gains, 0, 1).reshape(2, dim).astype(f32)
+    gain_attn, gain_mlp = gains[0], gains[1]
+    all_grad = jnp.concatenate(seq_gather(out_grad[0]), axis=0)
 
     bias = tile_bias(rel_bias)
     bias_t = jnp.swapaxes(bias, 1, 2)
     forget = jax.nn.sigmoid(gate_bias)
     forget_row = forget.reshape(1, width)
-
-    inputs = all_tokens.astype(f32)
+    chunk_ids = jnp.arange(seq_count, dtype=jnp.int32)
+    order = chunk_ids ^ seq_at
+
+    inputs = all_tokens.reshape(rows, dim).astype(f32)
     normed = (inputs * inverse_rms(inputs) * gain_attn).astype(bf16)
     qkv = dot(normed, qkv_w).astype(bf16)
     attended, final_memory, mem, upd, lse, slse = attend(
-        qkv, state_init[0], lengths, state_query, forget_row, bias, heads
-    )
-
-    all_attended = lax.all_gather(attended, "seq", axis=1, tiled=True)
+        qkv, state_init[0], lengths, state_query, forget_row, bias, heads, order
+    )
+
+    from_heads = seq_gather(attended)
+    columns = []
+    for k in range(seq_count):
+        blocks = from_heads[k].reshape(seq_count, tok_rows, width)
+        columns.append(jnp.concatenate([blocks[j ^ k] for j in range(seq_count)], axis=0))
+    all_attended = jnp.concatenate(columns, axis=1)
+    out_w = out_w.reshape(seq_count, width, dim)
+    own_out = lax.dynamic_slice_in_dim(out_w, seq_at, 1, axis=0)[0]
+    out_w = jnp.concatenate(
+        [lax.dynamic_slice_in_dim(out_w, seq_at ^ k, 1, axis=0)[0] for k in range(seq_count)], axis=0
+    )
     mid = inputs + dot(all_attended, out_w)
     rho_mid = inverse_rms(mid)
     normed_mid = (mid * rho_mid * gain_mlp).astype(bf16)
-    live = (jnp.arange(rows, dtype=jnp.int32) < lengths[0]).astype(bf16)[:, None]
+    positions = (order[:, None] * tok_rows + jnp.arange(tok_rows, dtype=jnp.int32)).reshape(rows)
+    live = (positions < lengths[0]).astype(bf16)[:, None]
     grad_low = all_grad * live
     pre = dot(normed_mid, up_w)
     hidden, gelu_pull = jax.vjp(lambda v: jax.nn.gelu(v, approximate=False), pre)
     hidden = hidden.astype(bf16)
     dpre = gelu_pull(dot_t(grad_low, down_w))[0].astype(bf16)
-    dnormed_mid = lax.psum_scatter(dot_t(dpre, up_w).astype(bf16), "seq", scatter_dimension=0, tiled=True)
-    mlp_out = lax.psum_scatter(dot(hidden, down_w).astype(bf16), "seq", scatter_dimension=0, tiled=True)
+
+    def chunk(value, j):
+        return value[j * tok_rows : (j + 1) * tok_rows]
+
+    dnormed_mid = seq_reduce([dot_t(chunk(dpre, j), up_w) for j in range(seq_count)])
     down_grad = t_dot(hidden, grad_low)
     up_grad = t_dot(normed_mid, dpre)
-
-    here = seq_at * tok_rows
-    mid_here = lax.dynamic_slice_in_dim(mid, here, tok_rows, axis=0)
-    live_here = (here + jnp.arange(tok_rows, dtype=jnp.int32) < lengths[0]).astype(f32)[:, None]
-    output = (live_here * (mid_here + mlp_out.astype(f32))).astype(bf16)[None]
+    mlp_out = seq_reduce([dot(chunk(hidden, j), down_w) for j in range(seq_count)])
+
+    mid_here = chunk(mid, 0)
+    live_here = chunk(live, 0).astype(f32)
+    output = (live_here * (mid_here + mlp_out)).astype(bf16)[None]
     grad_here = out_grad[0].astype(f32) * live_here
-    through, mlp_gain_grad = norm_back(mid_here, gain_mlp, inverse_rms(mid_here), dnormed_mid.astype(f32))
+    through, mlp_gain_grad = norm_back(mid_here, gain_mlp, inverse_rms(mid_here), dnormed_mid)
     dmid = grad_here + through
-    dbranch = lax.all_gather(dmid.astype(bf16), "seq", axis=0, tiled=True)
-    own_out = lax.dynamic_slice_in_dim(out_w, seq_at * width, width, axis=0)
+    dbranch = jnp.concatenate(seq_gather(dmid.astype(bf16)), axis=0)
     dattended = dot_t(dbranch, own_out).astype(bf16)
     out_w_grad = t_dot(attended, dbranch)
 
     dqkv, dquery, dforget, near, far = attend_back(
-        qkv, dattended, attended, mem, upd, lse, slse, state_grad[0], lengths, state_query, forget_row, bias_t, heads
-    )
-    dnormed = lax.psum_scatter(dot_t(dqkv, qkv_w).astype(bf16), "seq", scatter_dimension=0, tiled=True)
+        qkv, dattended, attended, mem, upd, lse, slse, state_grad[0], lengths, state_query, forget_row, bias_t, heads, order
+    )
+    dnormed = seq_reduce([dot_t(chunk(dqkv, j), qkv_w) for j in range(seq_count)])
     qkv_grad = t_dot(normed, dqkv)
     inputs_here = tokens[0].astype(f32)
-    through, attn_gain_grad = norm_back(inputs_here, gain_attn, inverse_rms(inputs_here), dnormed.astype(f32))
+    through, attn_gain_grad = norm_back(inputs_here, gain_attn, inverse_rms(inputs_here), dnormed)
     tokens_grad = (dmid + through)[None]
 
     grad_gate = dforget.reshape(heads, DH) * forget * (1.0 - forget)
@@ -506,22 +702,32 @@
     grad_table = small[cut + heads * DH :].reshape(heads, BUCKETS)
 
     def spread(term):
-        return lax.psum_scatter(term, "fsdp", scatter_dimension=0, tiled=True)
+        return lax.psum_scatter(term.astype(bf16), "fsdp", scatter_dimension=0, tiled=True)
 
     def exchange(term):
-        return lax.all_to_all(term, "seq", split_axis=0, concat_axis=0, tiled=True)
-
-    qkv_part = exchange(qkv_grad.astype(bf16)).reshape(seq_count, dim // seq_count, 3, width)
-    qkv_part = spread(jnp.transpose(qkv_part, (1, 2, 0, 3)).reshape(dim // seq_count, 3 * H * DH)).astype(f32)
-    out_part = spread(out_w_grad.astype(bf16)).astype(f32)
-    up_part = exchange(up_grad.astype(bf16)).reshape(seq_count, dim // seq_count, fsdp_count, share)
-    up_part = spread(jnp.transpose(up_part, (1, 2, 0, 3)).reshape(dim // seq_count, hidden_all)).astype(f32)
-    down_part = jnp.transpose(
-        down_grad.astype(bf16).reshape(seq_count, fsdp_count // seq_count, share, dim), (0, 1, 2, 3)
-    )
-    down_part = lax.all_to_all(down_part, "seq", split_axis=0, concat_axis=0, tiled=True)
-    down_part = jnp.swapaxes(down_part, 0, 1).reshape(seq_count * (fsdp_count // seq_count) * share, dim)
+        return lax.all_to_all(term, "seq", split_axis=0, concat_axis=0, tiled=True).astype(f32)
+
+    piece = dim // (seq_count * fsdp_count)
+
+    def by_rows(grad):
+        columns = grad.shape[1]
+        grad = jnp.swapaxes(grad.reshape(seq_count, fsdp_count, piece, columns), 0, 1)
+        return spread(grad.reshape(dim, columns)).reshape(seq_count, piece, columns)
+
+    up_part = exchange(by_rows(up_grad)).reshape(seq_count, piece, fsdp_count, share)
+    up_part = jnp.transpose(up_part, (1, 2, 0, 3)).reshape(piece, hidden_all)
+    out_part = spread(out_w_grad).astype(f32)
+    span = fsdp_count // seq_count
+    down_low = down_grad.astype(bf16).reshape(seq_count, span, share, dim)
+    moved = [lax.dynamic_slice_in_dim(down_low, seq_at, 1, axis=0)]
+    for k in range(1, seq_count):
+        moved.append(swap(lax.dynamic_slice_in_dim(down_low, seq_at ^ k, 1, axis=0), k))
+    moved = jnp.concatenate(moved, axis=0)
+    moved = [lax.dynamic_slice_in_dim(moved, seq_at ^ k, 1, axis=0) for k in range(seq_count)]
+    down_part = jnp.swapaxes(jnp.concatenate(moved, axis=0), 0, 1).reshape(fsdp_count * share, dim)
     down_part = spread(down_part).astype(f32)
+    qkv_part = exchange(by_rows(qkv_grad)).reshape(seq_count, piece, 3, width)
+    qkv_part = jnp.transpose(qkv_part, (1, 2, 0, 3)).reshape(piece, 3 * H * DH)
     attn_gain_grad, mlp_gain_grad = jnp.split(
         lax.psum_scatter(
             jnp.stack([attn_gain_grad, mlp_gain_grad]), ("seq", "fsdp"), scatter_dimension=1, tiled=True

time: 1080 us -> 865 us (0.80)
  waiting for transfers between devices: 612 us -> 418 us
  blocking collectives: 68.7 us -> 0 us
  Pallas kernels: 61.3 us -> 107 us
  local copies, waits for them, and re-layouts: 140 us -> 121 us
    all_gather x5 -> x0, waiting for transfers between devices: 113 us -> none  [the longest x1 43.6 us: body(): qkv_w = lax.all_gather(own_qkv, 'fsdp', axis=0, tiled=True)]
    ppermute x0 -> x21, waiting for transfers between devices: none -> 76.1 us  [swap(): return lax.ppermute(value, 'seq', [(i, i ^ bit) for i in range(count)])]
    unnamed x19 -> x10, waiting for transfers between devices: 195 us -> 133 us
    all_to_all x1 -> x0, blocking collectives: 46.3 us -> none  [exchange(): return lax.all_to_all(term, 'seq', split_axis=0, concat_axis=0, tiled=True)]
    pallas_call x2 -> x3, Pallas kernels: 61.3 us -> 107 us  [the longest x1 44.6 us: gather_start(): pl.pallas_call(functools.partial(gather_kernel, seq, hi, lo), out_shape=(...]
    all_gather x1, waiting for transfers between devices: 41.3 us -> 0.02 us  [body(): up_w = lax.all_gather(own_up, 'fsdp', axis=0, tiled=True)]
    unnamed x297 -> x338, local copies, waits for them, and re-layouts: 66.8 us -> 33.4 us
    all_gather x1 -> x0, blocking collectives: 22.4 us -> none  [body(): lax.all_gather(jnp.stack([norm_attn, norm_mlp]), 'fsdp', axis=1, tiled=True)]
  transfers between devices with their start and end apart: 19 -> 32, of which waited for: 13 -> 9; matrix products, arithmetic and copies ran while one was open for 25% -> 32% of each run, Pallas kernels for 6% -> 12%
where the time goes in v2:
time: 865 us; the launch traced here: 859 us
  waiting for transfers between devices  418 us (48%)
  local copies, waits for them, and re-layouts  121 us (14%)
  matrix products  118 us (14%)
  Pallas kernels  107 us (12%)
  other arithmetic  58.9 us (7%)
  starting transfers between devices  19 us (2%)
  between operations  17 us (2%)
    reduce_scatter x4, waiting for transfers between devices, spread(): lax.psum_scatter(term.astype(bf16), 'fsdp', scatter_dimension=0, tiled=True)  183 us
    unnamed x10, waiting for transfers between devices  133 us
    ppermute x21, waiting for transfers between devices, swap(): return lax.ppermute(value, 'seq', [(i, i ^ bit) for i in range(count)])  76.1 us
    dot_general x7, matrix products, dot(): return jnp.dot(a, b, preferred_element_type=f32)  51.5 us
    eq x32, local copies, waits for them, and re-layouts, tile_bias(): bucket == bucket_id  50 us
    dot_general x10, matrix products, dot_t(): lax.dot_general(a, b, (((1,), (1,)), ((), ())), preferred_element_type=f32)  44.9 us
    pallas_call x1, Pallas kernels, gather_start(): pl.pallas_call(functools.partial(gather_kernel, seq, hi, lo), out_shape=(...  44.6 us
    pallas_call x1, Pallas kernels, attend_back(): pl.pallas_call(functools.partial(attend_back_kernel, heads, blocks), out_...  41.3 us
  transfers between devices with their start and end apart: 32, of which 9 were waited for; matrix products, arithmetic and copies ran while one was open for 32% of the time, Pallas kernels for 12%

profile of v2, /device:TPU:0, one launch (start us, length us, event | category | flops | bytes accessed | tf_op | source)
XLA Modules:
  0.0 859.0 jit_solution(9920149826330914676)
XLA Ops:
  12.2 44.6 %gather_start.1 = (bf16[4,512,1024]{2,1,0:T(8,128)(2,1)}, bf16[8,128,768]{2,1,0:T(8,128)(2,1)}, bf16[8,2,128]{2,1,0:T(2,128)(2,1)}) custom-call(bf16[512,1024]{1,0:T(8,128)(2,1)} %bitcast.227, bf16[128,768]{1,0:T(8,128)(2,1)} %copy.230.w_ref, bf16[2,128]{1,0:T(2,128)(2,1)} %pad_maximum_fusion.6.gain_ref), custom_call_target="tpu_custom_call" | custom-call | tf_op jit(solution)/shard_map/gather_start/pallas_call | solution.py:512
  57.5 3.2 fusion.1
  63.3 5.8 broadcast_compare_fusion.61
  71.7 3.6 convolution_convert_fusion.cur_ref.prev_ref
  75.7 7.9 multiply_select_fusion.1.bias_ref
  83.7 21.3 %attend.1 = (bf16[2048,256]{1,0:T(8,128)(2,1)S(1)}, f32[512,256]{1,0:T(8,128)}, f32[4,512,256]{2,1,0:T(8,128)S(1)}, f32[4,512,256]{2,1,0:T(8,128)S(1)}, f32[2,2048]{1,0:T(2,128)S(1)}, /*index=5*/f32[2,2048]{1,0:T(2,128)S(1)}) custom-call(s32[1]{0:T(128)} %copy.346.length_ref, s32[4]{0:T(128)S(1)} %get-tuple-element.214.order_ref, ...), custom_call_target="tpu_custom_call" | custom-call | flops 5033164800 | bytes 16777216 | tf_op jit(solution)/shard_map/attend/pallas_call | solution.py:165
  110.8 23.1 %collective-permute-done.1 = bf16[2048,256]{1,0:T(8,128)(2,1)} collective-permute-done((bf16[2048,256]{1,0:T(8,128)(2,1)S(1)}, bf16[2048,256]{1,0:T(8,128)(2,1)}, u32[]{:S(2)}, u32[]{:S(2)}) %collective-permute-start.1) | collective-permute-done | bytes 1048608 | tf_op jit(solution)/shard_map/ppermute | solution.py:537
  133.9 6.1 broadcast_compare_fusion.29
  143.8 1.9 copy.263
  145.7 1.9 copy.262
  147.6 1.9 copy.261
  150.5 1.9 copy.259
  152.4 1.9 copy.258
  154.2 1.9 copy.257
  156.1 1.9 copy.256
  159.8 1.9 copy.254
  161.7 1.9 copy.253
  163.6 1.9 copy.252
  169.3 1.9 copy.247
  171.3 1.9 copy.246
  173.1 1.9 copy.245
  175.0 1.9 copy.244
  176.9 1.9 copy.243
  178.8 1.9 copy.242
  180.7 1.9 copy.241
  191.6 2.2 fusion.101
  196.0 2.6 dynamic-slice_bitcast_fusion.3
  198.9 10.0 %multiply_reduce_fusion = (f32[2048]{0:T(1024)S(1)}, f32[2048,1024]{1,0:T(8,128)}) fusion(bf16[256,1024]{1,0:T(8,128)(2,1)S(1)} %get-tuple-element.122, bf16[256,1024]{1,0:T(8,128)(2,1)S(1)} %get-tuple-element.123, bf16[256,1024]{1,0:T(8,128)(2,1)} %get-tuple-element.124, bf16[256,1024]{1,0:T(8,128)(2,1)S(1)} %get-tuple-element.121, ...), kind=kOutput, calls=%fused_computation.27 | convolution fusion | flops 4357879808 | bytes 18882560 | tf_op jit(solution)/shard_map/dot_general | solution.py:54
  208.9 26.8 %multiply_convert_fusion = (bf16[2048,1024]{1,0:T(8,128)(2,1)}, f32[2048,1024]{1,0:T(8,128)}, f32[2048,1024]{1,0:T(8,128)}) fusion(bf16[1024,1024]{0,1:T(8,128)(2,1)} %all-gather.6.cloned.1.call-done, f32[2048,1024]{1,0:T(8,128)} %get-tuple-element.210, f32[1024]{0:T(1024)S(1)} %bitcast.257, f32[2048]{0:T(1024)S(1)} %add_rsqrt_fusion), kind=kOutput, calls=%fused_computation.13 | convolution fusion | flops 4437573632 | bytes 31469568 | tf_op jit(solution)/shard_map/dot_general | solution.py:54
  235.8 13.4 %add_convert_fusion = bf16[2048,1024]{1,0:T(8,128)(2,1)S(1)} fusion(f32[2048,1024]{1,0:T(8,128)} %get-tuple-element.111, f32[2048,1024]{1,0:T(8,128)} %get-tuple-element.211, bf16[1024,1024]{1,0:T(8,128)(2,1)} %all-gather.8.cloned.1.call-done, bf16[512,1024]{1,0:T(8,128)(2,1)} %collective-permute-done.8, bf16[512,1024]{1,0:T(8,128)(2,1)} %collective-permute-done.7, ...), kind=kOutput, calls=%fused_computation.12 | convolution fusion | flops 4345298944 | bytes 27267072 | tf_op jit(solution)/shard_map/dot_general | solution.py:58
  249.3 2.0 copy-done.143
  251.3 2.2 convolution_convert_fusion.6
  253.5 3.6 convolution_convert_fusion.7
  257.6 3.7 convolution_convert_fusion.8
  261.3 5.1 convolution_convert_fusion.3
  266.4 3.5 convolution_convert_fusion.9
  272.0 3.6 add_convert_fusion.2
  278.5 2.6 add_convert_fusion.3
  282.0 19.7 %collective-permute-done.11 = bf16[512,1024]{1,0:T(8,128)(2,1)S(1)} collective-permute-done((bf16[512,1024]{1,0:T(8,128)(2,1)S(1)}, bf16[512,1024]{1,0:T(8,128)(2,1)S(1)}, u32[]{:S(2)}, u32[]{:S(2)}) %collective-permute-start.11) | collective-permute-done | bytes 1048608 | tf_op jit(solution)/shard_map/ppermute | solution.py:537
  301.7 3.0 multiply_reduce_fusion.1
  304.7 18.5 %collective-permute-done.5 = bf16[512,1024]{1,0:T(8,128)(2,1)S(1)} collective-permute-done((bf16[512,1024]{1,0:T(8,128)(2,1)S(1)}, bf16[512,1024]{1,0:T(8,128)(2,1)S(1)}, u32[]{:S(2)}, u32[]{:S(2)}) %collective-permute-start.5) | collective-permute-done | bytes 1048608 | tf_op jit(solution)/shard_map/ppermute | solution.py:537
  323.2 4.1 fusion.99
  329.1 7.3 convolution_convert_fusion.2
  338.8 14.7 %collective-permute-done.13 = bf16[512,1024]{1,0:T(8,128)(2,1)} collective-permute-done((bf16[512,1024]{1,0:T(8,128)(2,1)S(1)}, bf16[512,1024]{1,0:T(8,128)(2,1)}, u32[]{:S(2)}, u32[]{:S(2)}) %collective-permute-start.13) | collective-permute-done | bytes 1048608 | tf_op jit(solution)/shard_map/ppermute | solution.py:537
  354.0 6.2 multiply_select_fusion.bias_ref
  383.4 3.1 convolution_convert_fusion.1.dout_ref
  386.7 41.3 %attend_back.1 = (bf16[2048,768]{1,0:T(8,128)(2,1)S(1)}, f32[2,128,128]{2,1,0:T(8,128)S(1)}, f32[1,256]{1,0:T(1,128)S(1)}, f32[2,384,256]{2,1,0:T(8,128)S(1)}, f32[2,8,256]{2,1,0:T(8,128)S(1)}) custom-call(s32[1]{0:T(128)} %copy.346.length_ref, s32[4]{0:T(128)S(1)} %copy-done.9, bf16[2048,768]{1,0:T(8,128)(2,1)} %copy-done.12, bf16[2048,768]{1,0:T(8,128)(2,1)} %copy-done.12, ...), custom_call_target="tpu_custom_call" | custom-call | flops 12582912000 | bytes 20971520 | tf_op jit(solution)/shard_map/attend_back/pallas_call | solution.py:348
  432.9 4.0 select_reduce_fusion
  445.9 4.1 fusion.5
  450.1 6.6 copy.266
  456.7 4.0 convolution_convert_fusion.10
  460.7 3.8 convolution_convert_fusion.4
  465.0 5.6 fusion.54
  471.9 3.8 convolution_convert_fusion.5
  475.7 3.6 add_convert_fusion.1
  481.2 3.4 all-to-all-start.1
  484.9 25.5 %all-reduce.2.cloned.1.call-done = f32[33088]{0:T(1024)} async-done(((f32[33088]{0:T(1024)}), f32[33088]{0:T(1024)}) %all-reduce.2.cloned.1.call-update) | async-done | bytes 132368 | tf_op jit(solution)/shard_map/psum | solution.py:698
  516.0 65.3 %reduce-scatter.14.cloned.1.call-done = bf16[128,1024]{1,0:T(8,128)(2,1)} async-done(((bf16[1024,1024]{1,0:T(8,128)(2,1)}), bf16[128,1024]{1,0:T(8,128)(2,1)}) %reduce-scatter.14.cloned.1.call-update) | async-done | bytes 262160 | tf_op jit(solution)/shard_map/reduce_scatter | solution.py:705
  583.1 63.0 %reduce-scatter.10.cloned.1.call-done = bf16[32,1024]{1,0:T(8,128)(2,1)} async-done(((bf16[256,1024]{1,0:T(8,128)(2,1)}), bf16[32,1024]{1,0:T(8,128)(2,1)}) %reduce-scatter.10.cloned.1.call-update) | async-done | bytes 65552 | tf_op jit(solution)/shard_map/reduce_scatter | solution.py:705
  647.6 4.7 fusion.43
  653.4 4.8 fusion.41
  658.2 55.2 %reduce-scatter.8.cloned.1.call-done = bf16[128,768]{1,0:T(8,128)(2,1)} async-done(((bf16[1024,768]{1,0:T(8,128)(2,1)}), bf16[128,768]{1,0:T(8,128)(2,1)}) %reduce-scatter.8.cloned.1.call-update) | async-done | bytes 196624 | tf_op jit(solution)/shard_map/reduce_scatter | solution.py:705
  713.3 3.4 all-to-all-start
  716.7 132.0 %reduce-scatter.16.cloned.1.call-done = f32[32,2]{1,0:T(8,128)} async-done(((f32[1024,2]{1,0:T(8,128)}), f32[32,2]{1,0:T(8,128)}) %reduce-scatter.16.cloned.1.call-update) | async-done | bytes 272
  (505 shorter events, 102.3 us)
Async XLA Ops:
  7.2 102.8 %copy-start = (bf16[512,1024]{1,0:T(8,128)(2,1)S(1)}, bf16[512,1024]{1,0:T(8,128)(2,1)}, u32[]{:S(2)}) copy-start(bf16[512,1024]{1,0:T(8,128)(2,1)} %param.22) | copy-start | bytes 3145732
  7.2 188.8 %all-gather.4.cloned.1.call-start = ((), (), s32[]{:S(2)}) async-start(), calls=%async_computation.7 | async-start | bytes 2359296 | tf_op jit(solution)/shard_map/all_gather | solution.py:619
  7.9 201.0 %all-gather.6.cloned.1.call-start = ((), (), s32[]{:S(2)}) async-start(), calls=%async_computation.8 | async-start | bytes 2359296 | tf_op jit(solution)/shard_map/all_gather | solution.py:620
  10.4 225.4 %all-gather.8.cloned.1.call-start = ((), (), s32[]{:S(2)}) async-start(), calls=%async_computation.9 | async-start | bytes 2359296 | tf_op jit(solution)/shard_map/all_gather | solution.py:621
  61.3 22.3 %copy-start.2 = (f32[2,128]{1,0:T(2,128)}, f32[2,128]{1,0:T(2,128)S(1)}, u32[]{:S(2)}) copy-start(f32[2,128]{1,0:T(2,128)S(1)} %add_divide_fusion) | copy-start | bytes 3076
  107.7 26.2 %collective-permute-start.1 = (bf16[2048,256]{1,0:T(8,128)(2,1)S(1)}, bf16[2048,256]{1,0:T(8,128)(2,1)}, u32[]{:S(2)}, u32[]{:S(2)}) collective-permute-start(bf16[2048,256]{1,0:T(8,128)(2,1)S(1)} %get-tuple-element.29.out_ref), channel_id=1, source_target_pairs={{0,16},{8,24},{16,0},{24,8},{1,17},{9,25},{17,1},{25,9},{2,18},{10... | collective-permute-start | bytes 3145736 | tf_op jit(solution)/shard_map/ppermute | solution.py:537
  109.2 82.4 %collective-permute-start = (bf16[2048,256]{1,0:T(8,128)(2,1)S(1)}, bf16[2048,256]{1,0:T(8,128)(2,1)}, u32[]{:S(2)}, u32[]{:S(2)}) collective-permute-start(bf16[2048,256]{1,0:T(8,128)(2,1)S(1)} %get-tuple-element.29.out_ref), channel_id=1, source_target_pairs={{0,8},{8,0},{16,24},{24,16},{1,9},{9,1},{17,25},{25,17},{2,10},{10... | collective-permute-start | bytes 3145736 | tf_op jit(solution)/shard_map/ppermute | solution.py:537
  109.2 81.9 %collective-permute-start.7 = (bf16[512,1024]{1,0:T(8,128)(2,1)}, bf16[512,1024]{1,0:T(8,128)(2,1)}, u32[]{:S(2)}, u32[]{:S(2)}) collective-permute-start(bf16[512,1024]{1,0:T(8,128)(2,1)} %bitcast.24), channel_id=1, source_target_pairs={{0,16},{8,24},{16,0},{24,8},{1,17},{9,25},{17,1},{25,9},{2,18},{10... | collective-permute-start | bytes 3145736 | tf_op jit(solution)/shard_map/ppermute | solution.py:537
  109.7 126.0 %collective-permute-start.6 = (bf16[512,1024]{1,0:T(8,128)(2,1)}, bf16[512,1024]{1,0:T(8,128)(2,1)}, u32[]{:S(2)}, u32[]{:S(2)}) collective-permute-start(bf16[512,1024]{1,0:T(8,128)(2,1)} %bitcast.24), channel_id=1, source_target_pairs={{0,8},{8,0},{16,24},{24,16},{1,9},{9,1},{17,25},{25,17},{2,10},{10... | collective-permute-start | bytes 3145736 | tf_op jit(solution)/shard_map/ppermute | solution.py:537
  110.7 370.5 %reduce-scatter.12.cloned.1.call-start = ((), (), s32[]{:S(2)}) async-start(), calls=%async_computation.12 | async-start | bytes 2359296 | tf_op jit(solution)/shard_map/reduce_scatter | solution.py:705
  133.9 61.1 %collective-permute-start.2 = (bf16[2048,256]{1,0:T(8,128)(2,1)}, bf16[2048,256]{1,0:T(8,128)(2,1)S(1)}, u32[]{:S(2)}, u32[]{:S(2)}) collective-permute-start(bf16[2048,256]{1,0:T(8,128)(2,1)} %collective-permute-done.1), channel_id=1, source_target_pairs={{0,8},{8,0},{16,24},{24,16},{1,9},{9,1},{17,25},{25,17},{2,10},{10... | collective-permute-start | bytes 3145736 | tf_op jit(solution)/shard_map/ppermute | solution.py:537
  145.7 19.8 %copy-start.64 = (pred[768,256]{0,1:T(8,128)(4,1)S(1)}, pred[768,256]{0,1:T(8,128)(4,1)}, u32[]{:S(2)}) copy-start(pred[768,256]{0,1:T(8,128)(4,1)} %get-tuple-element.152) | copy-start | bytes 589828
  147.6 18.9 %copy-start.63 = (pred[768,256]{0,1:T(8,128)(4,1)S(1)}, pred[768,256]{0,1:T(8,128)(4,1)}, u32[]{:S(2)}) copy-start(pred[768,256]{0,1:T(8,128)(4,1)} %get-tuple-element.151) | copy-start | bytes 589828
  149.5 17.9 %copy-start.62 = (pred[768,256]{0,1:T(8,128)(4,1)S(1)}, pred[768,256]{0,1:T(8,128)(4,1)}, u32[]{:S(2)}) copy-start(pred[768,256]{0,1:T(8,128)(4,1)} %get-tuple-element.150) | copy-start | bytes 589828
  150.5 17.9 %copy-start.61 = (pred[768,256]{0,1:T(8,128)(4,1)S(1)}, pred[768,256]{0,1:T(8,128)(4,1)}, u32[]{:S(2)}) copy-start(pred[768,256]{0,1:T(8,128)(4,1)} %get-tuple-element.149) | copy-start | bytes 589828
  166.5 17.9 %copy-start.60 = (pred[768,256]{0,1:T(8,128)(4,1)S(1)}, pred[768,256]{0,1:T(8,128)(4,1)}, u32[]{:S(2)}) copy-start(pred[768,256]{0,1:T(8,128)(4,1)} %get-tuple-element.140) | copy-start | bytes 589828
  167.4 17.9 %copy-start.59 = (pred[768,256]{0,1:T(8,128)(4,1)S(1)}, pred[768,256]{0,1:T(8,128)(4,1)}, u32[]{:S(2)}) copy-start(pred[768,256]{0,1:T(8,128)(4,1)} %get-tuple-element.139) | copy-start | bytes 589828
  168.4 17.9 %copy-start.58 = (pred[768,256]{0,1:T(8,128)(4,1)S(1)}, pred[768,256]{0,1:T(8,128)(4,1)}, u32[]{:S(2)}) copy-start(pred[768,256]{0,1:T(8,128)(4,1)} %get-tuple-element.138) | copy-start | bytes 589828
  169.3 17.9 %copy-start.57 = (pred[768,256]{0,1:T(8,128)(4,1)S(1)}, pred[768,256]{0,1:T(8,128)(4,1)}, u32[]{:S(2)}) copy-start(pred[768,256]{0,1:T(8,128)(4,1)} %get-tuple-element.137) | copy-start | bytes 589828
  191.1 44.7 %collective-permute-start.8 = (bf16[512,1024]{1,0:T(8,128)(2,1)}, bf16[512,1024]{1,0:T(8,128)(2,1)}, u32[]{:S(2)}, u32[]{:S(2)}) collective-permute-start(bf16[512,1024]{1,0:T(8,128)(2,1)} %collective-permute-done.7), channel_id=1, source_target_pairs={{0,8},{8,0},{16,24},{24,16},{1,9},{9,1},{17,25},{25,17},{2,10},{10... | collective-permute-start | bytes 3145736 | tf_op jit(solution)/shard_map/ppermute | solution.py:537
  253.5 18.5 %collective-permute-start.10 = (bf16[512,1024]{1,0:T(8,128)(2,1)}, bf16[512,1024]{1,0:T(8,128)(2,1)}, u32[]{:S(2)}, u32[]{:S(2)}) collective-permute-start(bf16[512,1024]{1,0:T(8,128)(2,1)} %convolution_convert_fusion.6), channel_id=1, source_target_pairs={{0,8},{8,0},{16,24},{24,16},{1,9},{9,1},{17,25},{25,17},{2,10},{10... | collective-permute-start | bytes 3145736 | tf_op jit(solution)/shard_map/ppermute | solution.py:537
  257.1 24.8 %collective-permute-start.9 = (bf16[512,1024]{1,0:T(8,128)(2,1)}, bf16[512,1024]{1,0:T(8,128)(2,1)S(1)}, u32[]{:S(2)}, u32[]{:S(2)}) collective-permute-start(bf16[512,1024]{1,0:T(8,128)(2,1)} %convolution_convert_fusion.7), channel_id=1, source_target_pairs={{0,8},{8,0},{16,24},{24,16},{1,9},{9,1},{17,25},{25,17},{2,10},{10... | collective-permute-start | bytes 3145736 | tf_op jit(solution)/shard_map/ppermute | solution.py:537
  261.3 17.2 %collective-permute-start.4 = (bf16[512,1024]{1,0:T(8,128)(2,1)}, bf16[512,1024]{1,0:T(8,128)(2,1)}, u32[]{:S(2)}, u32[]{:S(2)}) collective-permute-start(bf16[512,1024]{1,0:T(8,128)(2,1)} %convolution_convert_fusion.8), channel_id=1, source_target_pairs={{0,8},{8,0},{16,24},{24,16},{1,9},{9,1},{17,25},{25,17},{2,10},{10... | collective-permute-start | bytes 3145736 | tf_op jit(solution)/shard_map/ppermute | solution.py:537
  269.9 34.8 %collective-permute-start.3 = (bf16[512,1024]{1,0:T(8,128)(2,1)}, bf16[512,1024]{1,0:T(8,128)(2,1)S(1)}, u32[]{:S(2)}, u32[]{:S(2)}) collective-permute-start(bf16[512,1024]{1,0:T(8,128)(2,1)} %convolution_convert_fusion.9), channel_id=1, source_target_pairs={{0,8},{8,0},{16,24},{24,16},{1,9},{9,1},{17,25},{25,17},{2,10},{10... | collective-permute-start | bytes 3145736 | tf_op jit(solution)/shard_map/ppermute | solution.py:537
  271.9 238.5 %all-reduce.2.cloned.1.call-start = ((), (), s32[]{:S(2)}) async-start(), calls=%async_computation.14 | async-start | bytes 270336 | tf_op jit(solution)/shard_map/psum | solution.py:698
  275.6 26.1 %collective-permute-start.11 = (bf16[512,1024]{1,0:T(8,128)(2,1)S(1)}, bf16[512,1024]{1,0:T(8,128)(2,1)S(1)}, u32[]{:S(2)}, u32[]{:S(2)}) collective-permute-start(bf16[512,1024]{1,0:T(8,128)(2,1)S(1)} %add_convert_fusion.2), channel_id=1, source_target_pairs={{0,16},{8,24},{16,0},{24,8},{1,17},{9,25},{17,1},{25,9},{2,18},{10... | collective-permute-start | bytes 3145736 | tf_op jit(solution)/shard_map/ppermute | solution.py:537
  281.1 20.6 %copy-start.135 = (bf16[1024,1024]{0,1:T(8,128)(2,1)S(1)}, bf16[1024,1024]{0,1:T(8,128)(2,1)}, u32[]{:S(2)}) copy-start(bf16[1024,1024]{0,1:T(8,128)(2,1)} %all-gather.6.cloned.1.call-done) | copy-start | bytes 6291460
  281.1 42.1 %collective-permute-start.5 = (bf16[512,1024]{1,0:T(8,128)(2,1)S(1)}, bf16[512,1024]{1,0:T(8,128)(2,1)S(1)}, u32[]{:S(2)}, u32[]{:S(2)}) collective-permute-start(bf16[512,1024]{1,0:T(8,128)(2,1)S(1)} %add_convert_fusion.3), channel_id=1, source_target_pairs={{0,16},{8,24},{16,0},{24,8},{1,17},{9,25},{17,1},{25,9},{2,18},{10... | collective-permute-start | bytes 3145736 | tf_op jit(solution)/shard_map/ppermute | solution.py:537
  327.3 56.1 %copy-start.21 = (bf16[512,1024]{1,0:T(8,128)(2,1)}, bf16[512,1024]{1,0:T(8,128)(2,1)S(1)}, u32[]{:S(2)}) copy-start(bf16[512,1024]{1,0:T(8,128)(2,1)S(1)} %get-tuple-element.108) | copy-start | bytes 3145732
  327.3 26.3 %collective-permute-start.13 = (bf16[512,1024]{1,0:T(8,128)(2,1)S(1)}, bf16[512,1024]{1,0:T(8,128)(2,1)}, u32[]{:S(2)}, u32[]{:S(2)}) collective-permute-start(bf16[512,1024]{1,0:T(8,128)(2,1)S(1)} %get-tuple-element.108), channel_id=1, source_target_pairs={{0,16},{8,24},{16,0},{24,8},{1,17},{9,25},{17,1},{25,9},{2,18},{10... | collective-permute-start | bytes 3145736 | tf_op jit(solution)/shard_map/ppermute | solution.py:537
  329.0 24.6 %copy-start.45 = (pred[768,256]{1,0:T(8,128)(4,1)S(1)}, pred[768,256]{1,0:T(8,128)(4,1)}, u32[]{:S(2)}) copy-start(pred[768,256]{1,0:T(8,128)(4,1)} %copy.244) | copy-start | bytes 589828
  329.0 24.6 %copy-start.46 = (pred[768,256]{1,0:T(8,128)(4,1)S(1)}, pred[768,256]{1,0:T(8,128)(4,1)}, u32[]{:S(2)}) copy-start(pred[768,256]{1,0:T(8,128)(4,1)} %copy.243) | copy-start | bytes 589828
  329.0 24.6 %copy-start.47 = (pred[768,256]{1,0:T(8,128)(4,1)S(1)}, pred[768,256]{1,0:T(8,128)(4,1)}, u32[]{:S(2)}) copy-start(pred[768,256]{1,0:T(8,128)(4,1)} %copy.242) | copy-start | bytes 589828
  329.0 24.6 %copy-start.48 = (pred[768,256]{1,0:T(8,128)(4,1)S(1)}, pred[768,256]{1,0:T(8,128)(4,1)}, u32[]{:S(2)}) copy-start(pred[768,256]{1,0:T(8,128)(4,1)} %copy.241) | copy-start | bytes 589828
  329.0 24.6 %copy-start.49 = (pred[768,256]{1,0:T(8,128)(4,1)S(1)}, pred[768,256]{1,0:T(8,128)(4,1)}, u32[]{:S(2)}) copy-start(pred[768,256]{1,0:T(8,128)(4,1)} %copy.240) | copy-start | bytes 589828
  329.0 24.6 %copy-start.50 = (pred[768,256]{1,0:T(8,128)(4,1)S(1)}, pred[768,256]{1,0:T(8,128)(4,1)}, u32[]{:S(2)}) copy-start(pred[768,256]{1,0:T(8,128)(4,1)} %copy.239) | copy-start | bytes 589828
  329.0 24.6 %copy-start.51 = (pred[768,256]{1,0:T(8,128)(4,1)S(1)}, pred[768,256]{1,0:T(8,128)(4,1)}, u32[]{:S(2)}) copy-start(pred[768,256]{1,0:T(8,128)(4,1)} %copy.238) | copy-start | bytes 589828
  329.0 24.6 %copy-start.52 = (pred[768,256]{1,0:T(8,128)(4,1)S(1)}, pred[768,256]{1,0:T(8,128)(4,1)}, u32[]{:S(2)}) copy-start(pred[768,256]{1,0:T(8,128)(4,1)} %copy.237) | copy-start | bytes 589828
  329.0 24.6 %copy-start.53 = (pred[768,256]{1,0:T(8,128)(4,1)S(1)}, pred[768,256]{1,0:T(8,128)(4,1)}, u32[]{:S(2)}) copy-start(pred[768,256]{1,0:T(8,128)(4,1)} %copy.236) | copy-start | bytes 589828
  329.0 24.6 %copy-start.54 = (pred[768,256]{1,0:T(8,128)(4,1)S(1)}, pred[768,256]{1,0:T(8,128)(4,1)}, u32[]{:S(2)}) copy-start(pred[768,256]{1,0:T(8,128)(4,1)} %copy.235) | copy-start | bytes 589828
  329.0 24.6 %copy-start.55 = (pred[768,256]{1,0:T(8,128)(4,1)S(1)}, pred[768,256]{1,0:T(8,128)(4,1)}, u32[]{:S(2)}) copy-start(pred[768,256]{1,0:T(8,128)(4,1)} %copy.234) | copy-start | bytes 589828
  329.0 24.6 %copy-start.56 = (pred[768,256]{1,0:T(8,128)(4,1)S(1)}, pred[768,256]{1,0:T(8,128)(4,1)}, u32[]{:S(2)}) copy-start(pred[768,256]{1,0:T(8,128)(4,1)} %copy.233) | copy-start | bytes 589828
  336.4 17.3 %copy-start.24 = (pred[768,256]{1,0:T(8,128)(4,1)S(1)}, pred[768,256]{1,0:T(8,128)(4,1)}, u32[]{:S(2)}) copy-start(pred[768,256]{1,0:T(8,128)(4,1)} %copy.265) | copy-start | bytes 589828
  336.4 17.3 %copy-start.25 = (pred[768,256]{1,0:T(8,128)(4,1)S(1)}, pred[768,256]{1,0:T(8,128)(4,1)}, u32[]{:S(2)}) copy-start(pred[768,256]{1,0:T(8,128)(4,1)} %copy.264) | copy-start | bytes 589828
  336.4 17.3 %copy-start.26 = (pred[768,256]{1,0:T(8,128)(4,1)S(1)}, pred[768,256]{1,0:T(8,128)(4,1)}, u32[]{:S(2)}) copy-start(pred[768,256]{1,0:T(8,128)(4,1)} %copy.263) | copy-start | bytes 589828
  336.4 17.3 %copy-start.27 = (pred[768,256]{1,0:T(8,128)(4,1)S(1)}, pred[768,256]{1,0:T(8,128)(4,1)}, u32[]{:S(2)}) copy-start(pred[768,256]{1,0:T(8,128)(4,1)} %copy.262) | copy-start | bytes 589828
  336.4 17.3 %copy-start.28 = (pred[768,256]{1,0:T(8,128)(4,1)S(1)}, pred[768,256]{1,0:T(8,128)(4,1)}, u32[]{:S(2)}) copy-start(pred[768,256]{1,0:T(8,128)(4,1)} %copy.261) | copy-start | bytes 589828
  336.5 17.3 %copy-start.29 = (pred[768,256]{1,0:T(8,128)(4,1)S(1)}, pred[768,256]{1,0:T(8,128)(4,1)}, u32[]{:S(2)}) copy-start(pred[768,256]{1,0:T(8,128)(4,1)} %copy.260) | copy-start | bytes 589828
  336.9 44.9 %collective-permute-start.20 = (bf16[1,2,128,1024]{3,2,1,0:T(8,128)(2,1)S(1)}, bf16[1,2,128,1024]{3,2,1,0:T(8,128)(2,1)S(1)}, u32[]{:S(2)}, u32[]{:S(2)}) collective-permute-start(bf16[1,2,128,1024]{3,2,1,0:T(8,128)(2,1)S(1)} %get-tuple-element.118), channel_id=1, source_target_pairs={{0,24},{8,16},{16,8},{24,0},{1,25},{9,17},{17,9},{25,1},{2,26},{10... | collective-permute-start | bytes 1572872 | tf_op jit(solution)/shard_map/ppermute | solution.py:537
  337.0 44.8 %collective-permute-start.19 = (bf16[1,2,128,1024]{3,2,1,0:T(8,128)(2,1)S(1)}, bf16[1,2,128,1024]{3,2,1,0:T(8,128)(2,1)S(1)}, u32[]{:S(2)}, u32[]{:S(2)}) collective-permute-start(bf16[1,2,128,1024]{3,2,1,0:T(8,128)(2,1)S(1)} %get-tuple-element.119), channel_id=1, source_target_pairs={{0,16},{8,24},{16,0},{24,8},{1,17},{9,25},{17,1},{25,9},{2,18},{10... | collective-permute-start | bytes 1572872 | tf_op jit(solution)/shard_map/ppermute | solution.py:537
  337.5 22.7 %copy-start.89 = (pred[384,256]{1,0:T(32,128)(4,1)S(1)}, pred[384,256]{1,0:T(32,128)(4,1)}, u32[]{:S(2)}) copy-start(pred[384,256]{1,0:T(32,128)(4,1)} %constant.57) | copy-start | bytes 294916
  337.5 44.3 %collective-permute-start.18 = (bf16[1,2,128,1024]{3,2,1,0:T(8,128)(2,1)S(1)}, bf16[1,2,128,1024]{3,2,1,0:T(8,128)(2,1)S(1)}, u32[]{:S(2)}, u32[]{:S(2)}) collective-permute-start(bf16[1,2,128,1024]{3,2,1,0:T(8,128)(2,1)S(1)} %get-tuple-element.120), channel_id=1, source_target_pairs={{0,8},{8,0},{16,24},{24,16},{1,9},{9,1},{17,25},{25,17},{2,10},{10... | collective-permute-start | bytes 1572872 | tf_op jit(solution)/shard_map/ppermute | solution.py:537
  338.8 44.5 %collective-permute-start.12 = (bf16[512,1024]{1,0:T(8,128)(2,1)S(1)}, bf16[512,1024]{1,0:T(8,128)(2,1)}, u32[]{:S(2)}, u32[]{:S(2)}) collective-permute-start(bf16[512,1024]{1,0:T(8,128)(2,1)S(1)} %get-tuple-element.108), channel_id=1, source_target_pairs={{0,8},{8,0},{16,24},{24,16},{1,9},{9,1},{17,25},{25,17},{2,10},{10... | collective-permute-start | bytes 3145736 | tf_op jit(solution)/shard_map/ppermute | solution.py:537
  353.6 29.8 %collective-permute-start.14 = (bf16[512,1024]{1,0:T(8,128)(2,1)}, bf16[512,1024]{1,0:T(8,128)(2,1)}, u32[]{:S(2)}, u32[]{:S(2)}) collective-permute-start(bf16[512,1024]{1,0:T(8,128)(2,1)} %collective-permute-done.13), channel_id=1, source_target_pairs={{0,8},{8,0},{16,24},{24,16},{1,9},{9,1},{17,25},{25,17},{2,10},{10... | collective-permute-start | bytes 3145736 | tf_op jit(solution)/shard_map/ppermute | solution.py:537
  442.2 139.1 %reduce-scatter.14.cloned.1.call-start = ((), (), s32[]{:S(2)}) async-start(), calls=%async_computation.13 | async-start | bytes 2359296 | tf_op jit(solution)/shard_map/reduce_scatter | solution.py:705
  445.3 200.8 %reduce-scatter.10.cloned.1.call-start = ((), (), s32[]{:S(2)}) async-start(), calls=%async_computation.11 | async-start | bytes 589824 | tf_op jit(solution)/shard_map/reduce_scatter | solution.py:705
  460.6 252.7 %reduce-scatter.8.cloned.1.call-start = ((), (), s32[]{:S(2)}) async-start(), calls=%async_computation.10 | async-start | bytes 1769472 | tf_op jit(solution)/shard_map/reduce_scatter | solution.py:705
  464.5 11.2 %collective-permute-start.16 = (bf16[512,1024]{1,0:T(8,128)(2,1)}, bf16[512,1024]{1,0:T(8,128)(2,1)}, u32[]{:S(2)}, u32[]{:S(2)}) collective-permute-start(bf16[512,1024]{1,0:T(8,128)(2,1)} %convolution_convert_fusion.4), channel_id=1, source_target_pairs={{0,8},{8,0},{16,24},{24,16},{1,9},{9,1},{17,25},{25,17},{2,10},{10... | collective-permute-start | bytes 3145736 | tf_op jit(solution)/shard_map/ppermute | solution.py:537
  475.7 171.9 %collective-permute-start.15 = (bf16[512,1024]{1,0:T(8,128)(2,1)}, bf16[512,1024]{1,0:T(8,128)(2,1)S(1)}, u32[]{:S(2)}, u32[]{:S(2)}) collective-permute-start(bf16[512,1024]{1,0:T(8,128)(2,1)} %convolution_convert_fusion.5), channel_id=1, source_target_pairs={{0,8},{8,0},{16,24},{24,16},{1,9},{9,1},{17,25},{25,17},{2,10},{10... | collective-permute-start | bytes 3145736 | tf_op jit(solution)/shard_map/ppermute | solution.py:537
  479.3 168.2 %collective-permute-start.17 = (bf16[512,1024]{1,0:T(8,128)(2,1)}, bf16[512,1024]{1,0:T(8,128)(2,1)}, u32[]{:S(2)}, u32[]{:S(2)}) collective-permute-start(bf16[512,1024]{1,0:T(8,128)(2,1)} %add_convert_fusion.1), channel_id=1, source_target_pairs={{0,16},{8,24},{16,0},{24,8},{1,17},{9,25},{17,1},{25,9},{2,18},{10... | collective-permute-start | bytes 3145736 | tf_op jit(solution)/shard_map/ppermute | solution.py:537
  481.2 33.4 %all-to-all-start.1 = ((bf16[4,32,1024]{2,1,0:T(8,128)(2,1)}), bf16[4,32,1024]{2,1,0:T(8,128)(2,1)S(1)}, u32[]{:S(2)}, u32[]{:S(2)}) async-start(bf16[4,32,1024]{2,1,0:T(8,128)(2,1)} %bitcast.248), calls=%async_computation.4 | async-start | bytes 524288 | tf_op jit(solution)/shard_map/all_to_all | solution.py:708
  484.6 364.1 %reduce-scatter.16.cloned.1.call-start = ((), (), s32[]{:S(2)}) async-start(), calls=%async_computation.15 | async-start | bytes 540672
  653.4 198.8 %copy-start.1 = (bf16[512,1024]{1,0:T(8,128)(2,1)S(1)}, bf16[512,1024]{1,0:T(8,128)(2,1)}, u32[]{:S(2)}) copy-start(bf16[512,1024]{1,0:T(8,128)(2,1)} %param.22) | copy-start | bytes 3145732
  713.3 137.5 %all-to-all-start = ((bf16[4,32,768]{2,1,0:T(8,128)(2,1)}), bf16[4,32,768]{2,1,0:T(8,128)(2,1)S(1)}, u32[]{:S(2)}, u32[]{:S(2)}) async-start(bf16[4,32,768]{2,1,0:T(8,128)(2,1)} %bitcast.249), calls=%async_computation.1 | async-start | bytes 393216 | tf_op jit(solution)/shard_map/all_to_all | solution.py:708
  (117 other events, 1089.3 us)
Sparse Core Ops, SparseCore 0:
  10.2 54.7 all-gather.3
  67.0 51.7 all-gather.5
  120.9 47.4 all-gather.7
  272.1 66.0 reduce-scatter.11
  442.3 68.0 all-reduce.1
  514.3 66.9 reduce-scatter.13
  585.0 61.0 reduce-scatter.9
  649.5 63.8 reduce-scatter.7
  715.7 133.0 reduce-scatter.15

commit v3 on v2

--- a/solution.py
+++ b/solution.py
@@ -392,11 +392,11 @@
     )(length, order, qkv, qkv, dout, out, mem, upd, lse, slse, sgrad, state_query, forget, bias_t)
 
 
-def gather_kernel(seq, hi, lo, tok_ref, w_ref, gain_ref, toks_ref, ws_ref, gains_ref, here_sem, seq_send, seq_recv, far_send, far_recv, lo_send, lo_recv):
+def gather_kernel(seq, hi, lo, tok_ref, w_ref, gain_ref, out_ref, toks_ref, ws_ref, gains_ref, outs_ref, here_sem, seq_send, seq_recv, far_send, far_recv, lo_send, lo_recv):
     me = lax.axis_index("seq")
     f = lax.axis_index("fsdp")
     z, y = f // lo, f % lo
-    pairs = ((w_ref, ws_ref), (gain_ref, gains_ref))
+    pairs = ((w_ref, ws_ref), (gain_ref, gains_ref), (out_ref, outs_ref))
 
     barrier = pltpu.get_barrier_semaphore()
     greeted = 0
@@ -505,31 +505,422 @@
         c.wait()
 
 
-def gather_start(tokens, weights, gains, seq, fsdp):
+def gather_start(tokens, weights, seq, fsdp):
     lo = 2
     hi = fsdp // lo
+    count = len(weights)
     anywhere = pl.BlockSpec(memory_space=pl.ANY)
+    dma = pltpu.SemaphoreType.DMA
     return pl.pallas_call(
         functools.partial(gather_kernel, seq, hi, lo),
-        out_shape=(
-            jax.ShapeDtypeStruct((seq,) + tokens.shape, tokens.dtype),
-            jax.ShapeDtypeStruct((fsdp,) + weights.shape, weights.dtype),
-            jax.ShapeDtypeStruct((fsdp,) + gains.shape, gains.dtype),
-        ),
-        in_specs=[anywhere] * 3,
-        out_specs=(anywhere,) * 3,
+        out_shape=(jax.ShapeDtypeStruct((seq,) + tokens.shape, tokens.dtype),)
+        + tuple(jax.ShapeDtypeStruct((fsdp,) + w.shape, w.dtype) for w in weights),
+        in_specs=[anywhere] * (1 + count),
+        out_specs=(anywhere,) * (1 + count),
         scratch_shapes=[
-            pltpu.SemaphoreType.DMA((3,)),
-            pltpu.SemaphoreType.DMA((seq,)),
-            pltpu.SemaphoreType.DMA((seq,)),
-            pltpu.SemaphoreType.DMA((2, 2, hi)),
-            pltpu.SemaphoreType.DMA((2, 2, hi)),
-            pltpu.SemaphoreType.DMA((2, 2 * hi)),
-            pltpu.SemaphoreType.DMA((2, 2 * hi)),
+            dma((1 + count,)),
+            dma((seq,)),
+            dma((seq,)),
+            dma((count, 2, hi)),
+            dma((count, 2, hi)),
+            dma((count, 2 * hi)),
+            dma((count, 2 * hi)),
         ],
         compiler_params=pltpu.CompilerParams(collective_id=0, has_side_effects=True),
         name="gather_start",
-    )(tokens, weights, gains)
+    )(tokens, *weights)
+
+
+def finish_kernel(
+    seq,
+    hi,
+    lo,
+    chunks,
+    dn_ref,
+    gq_ref,
+    gu_ref,
+    gd_ref,
+    go_ref,
+    small_ref,
+    mlp_gain_ref,
+    tok_ref,
+    dmid_ref,
+    gain_ref,
+    tg_ref,
+    rq_ref,
+    ru_ref,
+    rd_ref,
+    ro_ref,
+    ssum_ref,
+    gsum_ref,
+    dn_own,
+    dn_in,
+    dn_low,
+    dn_acc,
+    tq,
+    tu,
+    td,
+    to,
+    yq,
+    yu,
+    yd,
+    yo,
+    lq,
+    lu,
+    ld,
+    lq_r,
+    lu_r,
+    ld_r,
+    lo_l,
+    lo_r,
+    xq,
+    xu,
+    sy,
+    sz,
+    gains,
+    gy,
+    gz,
+    gs,
+    load_sem,
+    dn_send,
+    dn_recv,
+    y_send,
+    y_recv,
+    z_send,
+    z_recv,
+    x_send,
+    x_recv,
+    s_send,
+    s_recv,
+    g_send,
+    g_recv,
+):
+    me = lax.axis_index("seq")
+    f = lax.axis_index("fsdp")
+    z, y = f // lo, f % lo
+    peer = z * lo + 1 - y
+    grads = (gq_ref, gu_ref, gd_ref, go_ref)
+    totals = (tq, tu, td, to)
+    from_y = (yq, yu, yd, yo)
+    from_z = ((lq, lq_r), (lu, lu_r), (ld, ld_r), (lo_l, lo_r))
+    tensors = range(4)
+    rows = dn_ref.shape[1] // chunks
+
+    barrier = pltpu.get_barrier_semaphore()
+    for k in range(1, seq):
+        pl.semaphore_signal(barrier, inc=1, device_id={"seq": me ^ k}, device_id_type=MESH)
+    for k in range(1, hi):
+        pl.semaphore_signal(barrier, inc=1, device_id={"fsdp": lax.rem(z + k, hi) * lo + y}, device_id_type=MESH)
+    pl.semaphore_signal(barrier, inc=1, device_id={"fsdp": peer}, device_id_type=MESH)
+    pl.semaphore_wait(barrier, seq + hi - 1)
+
+    def block(i, target):
+        return grads[i].at[:, target] if i < 2 else grads[i].at[target]
+
+    def remote(src, dst, send, recv, axis, target):
+        return pltpu.make_async_remote_copy(
+            src_ref=src, dst_ref=dst, send_sem=send, recv_sem=recv, device_id={axis: target}, device_id_type=MESH
+        )
+
+    evens = list(range(0, seq, 2))
+    loads = [pltpu.make_async_copy(dn_ref.at[j], dn_own.at[j // 2], load_sem.at[0, j // 2]) for j in evens]
+    for c in loads:
+        c.start()
+
+    levels = []
+    active = list(range(seq))
+    bit = 1
+    slot = 0
+    while bit < seq:
+        keep = [j for j in active if not j & bit]
+        levels.append((bit, keep, {j: slot + n for n, j in enumerate(keep)}))
+        slot += len(keep)
+        active = keep
+        bit *= 2
+    order = sorted(evens, reverse=True)
+
+    def piece_rows(c):
+        return pl.ds(c * rows, rows)
+
+    def dn_copy(level, j, c):
+        bit, _, slots = levels[level]
+        src = dn_ref.at[j ^ bit, piece_rows(c)] if level == 0 else dn_low.at[(j ^ bit) // 2, piece_rows(c)]
+        return remote(
+            src, dn_in.at[slots[j], piece_rows(c)], dn_send.at[slots[j], c], dn_recv.at[slots[j], c], "seq", me ^ bit
+        )
+
+    for c in range(chunks):
+        for j in order[:1]:
+            dn_copy(0, j, c).start()
+    y_copies = {}
+    for i in tensors:
+        for d in range(hi):
+            y_copies[i, d] = remote(
+                block(i, d * lo + 1 - y), from_y[i].at[d], y_send.at[i, d], y_recv.at[i, d], "fsdp", peer
+            )
+    grad_loads = {}
+    for i in tensors:
+        for d in range(hi):
+            grad_loads[i, d] = pltpu.make_async_copy(block(i, d * lo + y), totals[i].at[d], load_sem.at[1 + i, d])
+    small_y = remote(small_ref, sy, s_send.at[0], s_recv.at[0], "fsdp", peer)
+    small_y.start()
+    for d in range(hi):
+        y_copies[0, d].start()
+        grad_loads[0, d].start()
+    for j in order[1:]:
+        for c in range(chunks):
+            dn_copy(0, j, c).start()
+    for i in tensors[1:]:
+        for d in range(hi):
+            y_copies[i, d].start()
+            grad_loads[i, d].start()
+    for c in loads:
+        c.wait()
+    for level, (bit, keep, slots) in enumerate(levels):
+        later = levels[level + 1 :]
+        for j in sorted(keep, reverse=True):
+            for c in range(chunks):
+                if level == len(levels) - 1:
+                    continue
+                dn_copy(level, j, c).wait_recv()
+                at = piece_rows(c)
+                own = dn_own[j // 2, at].astype(f32) if level == 0 else dn_low[j // 2, at].astype(f32)
+                if j == 0:
+                    own = own if level == 0 else dn_acc[at]
+                    dn_acc[at] = own + dn_in[slots[j], at].astype(f32)
+                else:
+                    dn_low[j // 2, at] = (own + dn_in[slots[j], at].astype(f32)).astype(bf16)
+                    nxt = later[0]
+                    if j & nxt[0]:
+                        dn_copy(level + 1, j ^ nxt[0], c).start()
+
+    small_y.wait_recv()
+    sz[z] = small_ref[...] + sy[...]
+    small_z = []
+    for k in range(1, hi):
+        target = lax.rem(z + k, hi)
+        small_z.append(remote(sz.at[z], sz.at[z], s_send.at[k], s_recv.at[k], "fsdp", target * lo + y))
+        small_z[-1].start()
+
+    def reduce_tensor(i):
+        total = totals[i]
+        for d in range(hi):
+            grad_loads[i, d].wait()
+            y_copies[i, d].wait_recv()
+            total[d] = (total[d].astype(f32) + from_y[i][d].astype(f32)).astype(bf16)
+        from_right, from_left = from_z[i]
+        for t in range(hi - 1):
+            d = t - (hi - 1 - z)
+            m = hi - 1 - (t - z)
+
+            @pl.when((d >= 0) & (d < z))
+            def _():
+                at = jnp.clip(d, 0, hi - 1)
+                remote(
+                    total.at[at], from_right.at[t], z_send.at[i, 0, t], z_recv.at[i, 0, t], "fsdp", (z - 1) * lo + y
+                ).start()
+
+            @pl.when((m > z) & (m < hi))
+            def _():
+                at = jnp.clip(m, 0, hi - 1)
+                remote(
+                    total.at[at], from_left.at[t], z_send.at[i, 1, t], z_recv.at[i, 1, t], "fsdp", (z + 1) * lo + y
+                ).start()
+
+            dr = t - (hi - 2 - z)
+
+            @pl.when((z + 1 < hi) & (dr >= 0))
+            def _():
+                at = jnp.clip(dr, 0, hi - 1)
+                remote(
+                    total.at[at], from_right.at[t], z_send.at[i, 0, t], z_recv.at[i, 0, t], "fsdp", f
+                ).wait_recv()
+                total[at] = (total[at].astype(f32) + from_right[t].astype(f32)).astype(bf16)
+
+            ml = hi - 1 - (t - (z - 1))
+
+            @pl.when((z > 0) & (ml < hi))
+            def _():
+                at = jnp.clip(ml, 0, hi - 1)
+                remote(
+                    total.at[at], from_left.at[t], z_send.at[i, 1, t], z_recv.at[i, 1, t], "fsdp", f
+                ).wait_recv()
+                total[at] = (total[at].astype(f32) + from_left[t].astype(f32)).astype(bf16)
+
+    exchanged = (xq, xu)
+    results = (rq_ref, ru_ref, rd_ref, ro_ref)
+
+    def exchange(i):
+        for k in range(1, seq):
+            remote(
+                totals[i].at[z, me ^ k], exchanged[i].at[me], x_send.at[i, k], x_recv.at[i, k], "seq", me ^ k
+            ).start()
+
+    reduce_tensor(0)
+    exchange(0)
+
+    if levels:
+        bit, keep, slots = levels[-1]
+    gain = gain_ref[...]
+    part = jnp.zeros((8, gain.shape[1]), f32)
+    for c in range(chunks):
+        at = piece_rows(c)
+        if levels:
+            dn_copy(len(levels) - 1, 0, c).wait_recv()
+        if len(levels) > 1:
+            dn = dn_acc[at]
+        else:
+            dn = dn_own[0, at].astype(f32)
+        if levels:
+            dn = dn + dn_in[slots[0], at].astype(f32)
+        x = tok_ref[at].astype(f32)
+        rho = lax.rsqrt(jnp.mean(x * x, axis=-1, keepdims=True) + EPSILON)
+        scaled = gain * dn
+        mean = jnp.mean(x * scaled, axis=-1, keepdims=True)
+        tg_ref[at] = dmid_ref[at] + rho * scaled - x * (rho * rho * rho * mean)
+        prod = dn * x * rho
+        part += functools.reduce(jnp.add, [prod[n : n + 8] for n in range(0, rows, 8)])
+    gains[0:8] = mlp_gain_ref[...]
+    gains[8:16] = part
+    gain_y = remote(gains, gy, g_send.at[0], g_recv.at[0], "fsdp", peer)
+    gain_y.start()
+    reduce_tensor(1)
+    exchange(1)
+    gain_y.wait_recv()
+    gz[z] = gains[...] + gy[...]
+    gain_z = []
+    for k in range(1, hi):
+        target = lax.rem(z + k, hi)
+        gain_z.append(remote(gz.at[z], gz.at[z], g_send.at[k], g_recv.at[k], "fsdp", target * lo + y))
+        gain_z[-1].start()
+    reduce_tensor(2)
+    for k in range(1, hi):
+        source = lax.rem(z + hi - k, hi)
+        remote(gz.at[source], gz.at[source], g_send.at[k], g_recv.at[k], "fsdp", f).wait_recv()
+        remote(sz.at[source], sz.at[source], s_send.at[k], s_recv.at[k], "fsdp", f).wait_recv()
+    gs[me] = functools.reduce(jnp.add, [gz[d] for d in range(hi)])
+    gain_x = []
+    for k in range(1, seq):
+        gain_x.append(remote(gs.at[me], gs.at[me], g_send.at[hi + k], g_recv.at[hi + k], "seq", me ^ k))
+        gain_x[-1].start()
+    ssum_ref[...] = functools.reduce(jnp.add, [sz[d] for d in range(hi)])
+    reduce_tensor(3)
+    rd_ref[...] = td[z].astype(f32)
+    ro_ref[...] = to[z].astype(f32)
+    for i in range(2):
+        for k in range(1, seq):
+            remote(
+                totals[i].at[z, me], exchanged[i].at[me ^ k], x_send.at[i, k], x_recv.at[i, k], "seq", me
+            ).wait_recv()
+        exchanged[i][me] = totals[i][z, me]
+        for k in range(seq):
+            results[i][k] = exchanged[i][k].astype(f32)
+    for k in range(1, seq):
+        remote(gs.at[me ^ k], gs.at[me ^ k], g_send.at[hi + k], g_recv.at[hi + k], "seq", me).wait_recv()
+    gsum_ref[...] = functools.reduce(jnp.add, [gs[k] for k in range(seq)])
+
+    for level, (bit, keep, slots) in enumerate(levels):
+        for j in keep:
+            for c in range(chunks):
+                dn_copy(level, j, c).wait_send()
+    for i in tensors:
+        for d in range(hi):
+            y_copies[i, d].wait_send()
+        for t in range(hi - 1):
+            d = t - (hi - 1 - z)
+            m = hi - 1 - (t - z)
+
+            @pl.when((d >= 0) & (d < z))
+            def _():
+                remote(
+                    totals[i].at[0], from_z[i][0].at[t], z_send.at[i, 0, t], z_recv.at[i, 0, t], "fsdp", f
+                ).wait_send()
+
+            @pl.when((m > z) & (m < hi))
+            def _():
+                remote(
+                    totals[i].at[0], from_z[i][1].at[t], z_send.at[i, 1, t], z_recv.at[i, 1, t], "fsdp", f
+                ).wait_send()
+    for i in range(2):
+        for k in range(1, seq):
+            remote(
+                totals[i].at[z, me], exchanged[i].at[me], x_send.at[i, k], x_recv.at[i, k], "seq", me
+            ).wait_send()
+    for c in [small_y, gain_y] + small_z + gain_z + gain_x:
+        c.wait_send()
+
+
+def finish(dn, gq, gu, gd, go, small, mlp_gain, tok, dmid, gain, seq, fsdp):
+    lo = 2
+    hi = fsdp // lo
+    chunks = 4
+    anywhere = pl.BlockSpec(memory_space=pl.ANY)
+    vmem = pl.BlockSpec(memory_space=pltpu.VMEM)
+    block_q = (seq,) + gq.shape[2:]
+    block_u = (seq,) + gu.shape[2:]
+    block_d = gd.shape[1:]
+    block_o = go.shape[1:]
+    blocks = (block_q, block_u, block_d, block_o)
+    tok_rows, dim = tok.shape
+    sides = max(hi - 1, 1)
+
+    def buf(lead, shape, kind=bf16):
+        return pltpu.VMEM((lead,) + tuple(shape), kind)
+
+    scratch = [
+        buf(max(seq // 2, 1), (tok_rows, dim)),
+        buf(max(seq - 1, 1), (tok_rows, dim)),
+        buf(max(seq // 2, 1), (tok_rows, dim)),
+        pltpu.VMEM((tok_rows, dim), f32),
+    ]
+    scratch += [buf(hi, b) for b in blocks]
+    scratch += [buf(hi, b) for b in blocks]
+    scratch += [buf(sides, b) for b in (block_q, block_u, block_d)] * 2
+    scratch += [buf(sides, block_o), buf(sides, block_o)]
+    scratch += [pltpu.VMEM(block_q, bf16), pltpu.VMEM(block_u, bf16)]
+    scratch += [
+        pltpu.VMEM(small.shape, f32),
+        buf(hi, small.shape, f32),
+        pltpu.VMEM((16, dim), f32),
+        pltpu.VMEM((16, dim), f32),
+        buf(hi, (16, dim), f32),
+        buf(seq, (16, dim), f32),
+    ]
+    dma = pltpu.SemaphoreType.DMA
+    scratch += [
+        dma((5, max(hi, seq))),
+        dma((seq, chunks)),
+        dma((seq, chunks)),
+        dma((4, hi)),
+        dma((4, hi)),
+        dma((4, 2, hi)),
+        dma((4, 2, hi)),
+        dma((2, seq)),
+        dma((2, seq)),
+        dma((hi,)),
+        dma((hi,)),
+        dma((hi + seq,)),
+        dma((hi + seq,)),
+    ]
+    return pl.pallas_call(
+        functools.partial(finish_kernel, seq, hi, lo, chunks),
+        out_shape=(
+            jax.ShapeDtypeStruct((tok_rows, dim), f32),
+            jax.ShapeDtypeStruct(block_q, f32),
+            jax.ShapeDtypeStruct(block_u, f32),
+            jax.ShapeDtypeStruct(block_d, f32),
+            jax.ShapeDtypeStruct(block_o, f32),
+            jax.ShapeDtypeStruct(small.shape, f32),
+            jax.ShapeDtypeStruct((16, dim), f32),
+        ),
+        in_specs=[anywhere] * 5 + [vmem] * 5,
+        out_specs=(vmem,) * 7,
+        scratch_shapes=scratch,
+        compiler_params=pltpu.CompilerParams(
+            collective_id=1, has_side_effects=True, vmem_limit_bytes=56 << 20
+        ),
+        name="finish",
+    )(dn, gq, gu, gd, go, small, mlp_gain, tok, dmid, gain)
 
 
 def swap(value, bit):
@@ -580,7 +971,8 @@
 def norm_back(values, gain, rho, grad):
     scaled = gain * grad
     mean = jnp.mean(values * scaled, axis=-1, keepdims=True)
-    return rho * scaled - values * (rho * rho * rho * mean), jnp.sum(grad * values * rho, axis=0)
+    gain_grad = (grad * values * rho).reshape(-1, 8, values.shape[1])
+    return rho * scaled - values * (rho * rho * rho * mean), jnp.sum(gain_grad, axis=0)
 
 
 def body(
@@ -612,19 +1004,24 @@
     own_qkv = lax.dynamic_slice_in_dim(
         w_qkv.reshape(w_qkv.shape[0], 3, seq_count, width), seq_at, 1, axis=2
     ).reshape(w_qkv.shape[0], 3 * width)
-    own_up = lax.dynamic_slice_in_dim(
-        w_up.reshape(w_up.shape[0], fsdp_count, seq_count, share), seq_at, 1, axis=2
-    ).reshape(w_up.shape[0], fsdp_count * share)
+    own_up = lax.dynamic_slice_in_dim(w_up, seq_at * (hidden_all // seq_count), hidden_all // seq_count, axis=1)
     own_down = lax.dynamic_slice_in_dim(w_down, seq_at * share, share, axis=0)
-    out_w = lax.all_gather(w_out, "fsdp", axis=0, tiled=True)
+    down_w = lax.all_gather(own_down, "fsdp", axis=0, tiled=True)
     up_w = lax.all_gather(own_up, "fsdp", axis=0, tiled=True)
-    down_w = lax.all_gather(own_down, "fsdp", axis=0, tiled=True)
-    all_tokens, qkv_w, gains = gather_start(
-        tokens[0], own_qkv, jnp.stack([norm_attn, norm_mlp]), seq_count, fsdp_count
+    all_tokens, qkv_w, gains, out_w = gather_start(
+        tokens[0], (own_qkv, jnp.stack([norm_attn, norm_mlp]), w_out), seq_count, fsdp_count
     )
     qkv_w = qkv_w.reshape(dim, 3 * width)
     gains = jnp.swapaxes(gains, 0, 1).reshape(2, dim).astype(f32)
     gain_attn, gain_mlp = gains[0], gains[1]
+    span = fsdp_count // seq_count
+    down_w = down_w.reshape(seq_count, span, share, dim)
+    moved = [lax.dynamic_slice_in_dim(down_w, seq_at, 1, axis=0)]
+    for k in range(1, seq_count):
+        moved.append(swap(lax.dynamic_slice_in_dim(down_w, seq_at ^ k, 1, axis=0), k))
+    moved = jnp.concatenate(moved, axis=0)
+    moved = [lax.dynamic_slice_in_dim(moved, seq_at ^ k, 1, axis=0) for k in range(seq_count)]
+    down_w = jnp.swapaxes(jnp.concatenate(moved, axis=0), 0, 1).reshape(fsdp_count * share, dim)
     all_grad = jnp.concatenate(seq_gather(out_grad[0]), axis=0)
 
     bias = tile_bias(rel_bias)
@@ -684,56 +1081,42 @@
     dqkv, dquery, dforget, near, far = attend_back(
         qkv, dattended, attended, mem, upd, lse, slse, state_grad[0], lengths, state_query, forget_row, bias_t, heads, order
     )
-    dnormed = seq_reduce([dot_t(chunk(dqkv, j), qkv_w) for j in range(seq_count)])
-    qkv_grad = t_dot(normed, dqkv)
-    inputs_here = tokens[0].astype(f32)
-    through, attn_gain_grad = norm_back(inputs_here, gain_attn, inverse_rms(inputs_here), dnormed)
-    tokens_grad = (dmid + through)[None]
-
+    dnormed = dot_t(dqkv, qkv_w).astype(bf16).reshape(seq_count, tok_rows, dim)
+    piece = dim // (seq_count * fsdp_count)
+    qkv_grad = t_dot(normed, dqkv).astype(bf16).reshape(seq_count, fsdp_count, piece, 3 * width)
+    up_grad = up_grad.astype(bf16).reshape(seq_count, fsdp_count, piece, hidden_all // seq_count)
+    down_grad = down_grad.astype(bf16).reshape(fsdp_count, share, dim)
+    out_w_grad = out_w_grad.astype(bf16).reshape(fsdp_count, piece, dim)
     grad_gate = dforget.reshape(heads, DH) * forget * (1.0 - forget)
-    grad_table = bias_table_grad(near, far)
-    small = jnp.concatenate(
-        [dquery.reshape(-1), grad_gate.reshape(-1), grad_table.reshape(-1)]
+    grad_table = jnp.pad(bias_table_grad(near, far), ((0, 0), (0, DH - BUCKETS)))
+    cut = heads * DH
+    small = jnp.concatenate([dquery.reshape(cut, DH), grad_gate, grad_table], axis=0)
+    small = jnp.pad(small, ((0, -small.shape[0] % 8), (0, 0)))
+    tokens_grad, qkv_part, up_part, down_part, out_part, small, gain_sums = finish(
+        dnormed,
+        qkv_grad,
+        up_grad,
+        down_grad,
+        out_w_grad,
+        small,
+        mlp_gain_grad,
+        tokens[0],
+        dmid,
+        gain_attn.reshape(1, dim),
+        seq_count,
+        fsdp_count,
     )
-    small = lax.psum(small, "fsdp")
-    cut = heads * DH * DH
+    tokens_grad = tokens_grad[None]
     dquery = small[:cut].reshape(heads, DH, DH)
-    grad_gate = small[cut : cut + heads * DH].reshape(heads, DH)
-    grad_table = small[cut + heads * DH :].reshape(heads, BUCKETS)
-
-    def spread(term):
-        return lax.psum_scatter(term.astype(bf16), "fsdp", scatter_dimension=0, tiled=True)
-
-    def exchange(term):
-        return lax.all_to_all(term, "seq", split_axis=0, concat_axis=0, tiled=True).astype(f32)
-
-    piece = dim // (seq_count * fsdp_count)
-
-    def by_rows(grad):
-        columns = grad.shape[1]
-        grad = jnp.swapaxes(grad.reshape(seq_count, fsdp_count, piece, columns), 0, 1)
-        return spread(grad.reshape(dim, columns)).reshape(seq_count, piece, columns)
-
-    up_part = exchange(by_rows(up_grad)).reshape(seq_count, piece, fsdp_count, share)
-    up_part = jnp.transpose(up_part, (1, 2, 0, 3)).reshape(piece, hidden_all)
-    out_part = spread(out_w_grad).astype(f32)
-    span = fsdp_count // seq_count
-    down_low = down_grad.astype(bf16).reshape(seq_count, span, share, dim)
-    moved = [lax.dynamic_slice_in_dim(down_low, seq_at, 1, axis=0)]
-    for k in range(1, seq_count):
-        moved.append(swap(lax.dynamic_slice_in_dim(down_low, seq_at ^ k, 1, axis=0), k))
-    moved = jnp.concatenate(moved, axis=0)
-    moved = [lax.dynamic_slice_in_dim(moved, seq_at ^ k, 1, axis=0) for k in range(seq_count)]
-    down_part = jnp.swapaxes(jnp.concatenate(moved, axis=0), 0, 1).reshape(fsdp_count * share, dim)
-    down_part = spread(down_part).astype(f32)
-    qkv_part = exchange(by_rows(qkv_grad)).reshape(seq_count, piece, 3, width)
+    grad_gate = small[cut : cut + heads]
+    grad_table = small[cut + heads : cut + 2 * heads, :BUCKETS]
+    up_part = jnp.swapaxes(up_part, 0, 1).reshape(piece, hidden_all)
+    qkv_part = qkv_part.reshape(seq_count, piece, 3, width)
     qkv_part = jnp.transpose(qkv_part, (1, 2, 0, 3)).reshape(piece, 3 * H * DH)
-    attn_gain_grad, mlp_gain_grad = jnp.split(
-        lax.psum_scatter(
-            jnp.stack([attn_gain_grad, mlp_gain_grad]), ("seq", "fsdp"), scatter_dimension=1, tiled=True
-        ),
-        2,
-    )
+    gain_sums = jnp.sum(gain_sums.reshape(2, 8, seq_count * fsdp_count, piece), axis=1)
+    mine = seq_at * fsdp_count + lax.axis_index("fsdp")
+    gain_sums = lax.dynamic_slice_in_dim(gain_sums, mine, 1, axis=1)[:, 0]
+    mlp_gain_grad, attn_gain_grad = gain_sums[0], gain_sums[1]
     return (
         output,
         final_memory[None],
@@ -742,8 +1125,8 @@
         out_part,
         up_part,
         down_part,
-        attn_gain_grad[0],
-        mlp_gain_grad[0],
+        attn_gain_grad,
+        mlp_gain_grad,
         grad_table,
         dquery,
         grad_gate,

time: 865 us -> 594 us (0.69)
  waiting for transfers between devices: 418 us -> 55.1 us
  Pallas kernels: 107 us -> 241 us
  matrix products: 118 us -> 106 us
  local copies, waits for them, and re-layouts: 121 us -> 111 us
  starting transfers between devices: 19 us -> 9.52 us
    reduce_scatter x4 -> x0, waiting for transfers between devices: 183 us -> none  [spread(): lax.psum_scatter(term.astype(bf16), 'fsdp', scatter_dimension=0, tiled=True)]
    unnamed x10 -> x2, waiting for transfers between devices: 133 us -> 0.03 us
    pallas_call x0 -> x1, Pallas kernels: none -> 115 us  [finish(): pl.pallas_call(functools.partial(finish_kernel, seq, hi, lo, chunks), out...]
    psum x1 -> x0, waiting for transfers between devices: 25.5 us -> none  [body(): small = lax.psum(small, 'fsdp')]
    ppermute x21 -> x18, waiting for transfers between devices: 76.1 us -> 55.1 us  [swap(): return lax.ppermute(value, 'seq', [(i, i ^ bit) for i in range(count)])]
    pallas_call x1, Pallas kernels: 44.6 us -> 62.9 us  [gather_start(): pl.pallas_call(functools.partial(gather_kernel, seq, hi, lo), out_shape=(...]
    dot_general x10 -> x7, matrix products: 44.9 us -> 36.3 us  [dot_t(): lax.dot_general(a, b, (((1,), (1,)), ((), ())), preferred_element_type=f32)]
    unnamed x338 -> x240, local copies, waits for them, and re-layouts: 33.4 us -> 28.4 us
  transfers between devices with their start and end apart: 32 -> 20, of which waited for: 9 -> 3; matrix products, arithmetic and copies ran while one was open for 32% -> 33% of each run, Pallas kernels for 12% -> 14%
where the time goes in v3:
time: 594 us; the launch traced here: 589 us
  Pallas kernels  241 us (41%)
  local copies, waits for them, and re-layouts  111 us (19%)
  matrix products  106 us (18%)
  waiting for transfers between devices  55.1 us (9%)
  other arithmetic  50.3 us (8%)
  between operations  16.7 us (3%)
  starting transfers between devices  9.52 us (2%)
    pallas_call x1, Pallas kernels, finish(): pl.pallas_call(functools.partial(finish_kernel, seq, hi, lo, chunks), out...  115 us
    pallas_call x1, Pallas kernels, gather_start(): pl.pallas_call(functools.partial(gather_kernel, seq, hi, lo), out_shape=(...  62.9 us
    ppermute x18, waiting for transfers between devices, swap(): return lax.ppermute(value, 'seq', [(i, i ^ bit) for i in range(count)])  55.1 us
    eq x32, local copies, waits for them, and re-layouts, tile_bias(): bucket == bucket_id  50.2 us
    dot_general x7, matrix products, dot(): return jnp.dot(a, b, preferred_element_type=f32)  47.9 us
    pallas_call x1, Pallas kernels, attend_back(): pl.pallas_call(functools.partial(attend_back_kernel, heads, blocks), out_...  41.3 us
    dot_general x7, matrix products, dot_t(): lax.dot_general(a, b, (((1,), (1,)), ((), ())), preferred_element_type=f32)  36.3 us
    unnamed x240, local copies, waits for them, and re-layouts  28.4 us
  transfers between devices with their start and end apart: 20, of which 3 were waited for; matrix products, arithmetic and copies ran while one was open for 33% of the time, Pallas kernels for 14%

profile of v3, /device:TPU:0, one launch (start us, length us, event | category | flops | bytes accessed | tf_op | source)
XLA Modules:
  0.0 589.2 jit_solution(16655521239173036454)
XLA Ops:
  9.2 1.9 slice_reduce_fusion.31
  11.1 1.6 slice_reduce_fusion.30
  13.5 1.5 copy.235
  17.1 62.9 %gather_start.1 = (bf16[4,512,1024]{2,1,0:T(8,128)(2,1)}, bf16[8,128,768]{2,1,0:T(8,128)(2,1)}, bf16[8,2,128]{2,1,0:T(2,128)(2,1)}, bf16[8,128,1024]{2,1,0:T(8,128)(2,1)}) custom-call(bf16[512,1024]{1,0:T(8,128)(2,1)} %bitcast.196, bf16[128,768]{1,0:T(8,128)(2,1)} %copy.236.w_ref, bf16[2,128]{1,0:T(2,128)(2,1)} %pad_maximum_fusion.4.gain_ref, ...), custom_call_target="tpu_custom_call" | custom-call | tf_op jit(solution)/shard_map/gather_start/pallas_call | solution.py:514
  80.0 3.2 fusion.1
  87.2 3.6 convolution_convert_fusion.1.cur_ref.prev_ref
  90.9 5.1 broadcast_compare_fusion.61
  96.1 5.7 multiply_select_fusion.1.bias_ref
  101.9 21.2 %attend.1 = (bf16[2048,256]{1,0:T(8,128)(2,1)S(1)}, f32[512,256]{1,0:T(8,128)}, f32[4,512,256]{2,1,0:T(8,128)S(1)}, f32[4,512,256]{2,1,0:T(8,128)S(1)}, f32[2,2048]{1,0:T(2,128)S(1)}, /*index=5*/f32[2,2048]{1,0:T(2,128)S(1)}) custom-call(s32[1]{0:T(128)} %copy.343.length_ref, s32[4]{0:T(128)S(1)} %get-tuple-element.230.order_ref, ...), custom_call_target="tpu_custom_call" | custom-call | flops 5033164800 | bytes 16777216 | tf_op jit(solution)/shard_map/attend/pallas_call | solution.py:165
  128.1 1.7 constant_dynamic-slice_fusion.11
  129.8 6.0 %broadcast_compare_fusion.29 = (pred[768,256]{0,1:T(8,128)(4,1)S(1)}, pred[768,256]{0,1:T(8,128)(4,1)S(1)}, pred[768,256]{0,1:T(8,128)(4,1)}, pred[768,256]{0,1:...) fusion(s32[256,768]{1,0:T(8,128)S(1)} %convert_reduce_fusion, ...), kind=kLoop, calls=%fused_computation.172 | loop fusion | flops 7667712 | bytes 7275520 | tf_op jit(solution)/shard_map/eq | solution.py:48
  138.1 1.9 copy.242
  140.0 1.9 copy.243
  141.9 1.9 copy.244
  143.8 1.9 copy.245
  145.7 1.9 copy.246
  147.7 1.9 copy.247
  149.5 1.9 copy.248
  151.4 1.9 copy.249
  153.3 1.9 copy.250
  155.2 2.0 copy.251
  157.1 1.9 copy.252
  159.0 1.9 copy.253
  160.9 1.9 copy.254
  162.7 1.9 copy.255
  164.6 1.9 copy.256
  166.5 1.9 copy.257
  168.4 1.9 copy.258
  170.2 1.9 copy.259
  172.1 1.9 copy.260
  174.0 1.9 copy.261
  175.8 1.9 copy.262
  177.7 1.9 copy.263
  186.6 8.3 %multiply_select_fusion.bias_ref = f32[2,768,256]{2,1,0:T(8,128)S(1)} fusion(f32[2]{0:T(128)} %copy-done.79, f32[2]{0:T(128)} %copy-done.80, f32[2]{0:T(128)S(1)} %get-tuple-element.91, f32[2]{0:T(128)S(1)} %get-tuple-element.92, f32[2]{0:T(128)S(1)} %get-tuple-element.93, f32[2]{0:T(128)S(1)} %get-tuple-element.94, f32[2]{0:T(128)S(1)} %get-tuple-element.95, ...), kind=kLoop, calls=%fused_computation.76 | loop fusion | flops 13369344 | bytes 8061184 | tf_op jit(solution)/shard_map/jit(_where)/select_n | solution.py:50
  195.7 2.9 dynamic-slice_bitcast_fusion.3
  198.9 2.2 fusion.79
  202.4 2.2 fusion.81
  204.6 10.3 %multiply_reduce_fusion = (f32[2048]{0:T(1024)S(1)}, f32[2048,1024]{1,0:T(8,128)}) fusion(bf16[256,1024]{1,0:T(8,128)(2,1)} %get-tuple-element.128, bf16[256,1024]{1,0:T(8,128)(2,1)} %get-tuple-element.129, bf16[256,1024]{1,0:T(8,128)(2,1)} %get-tuple-element.130, bf16[256,1024]{1,0:T(8,128)(2,1)} %get-tuple-element.127, ...), kind=kOutput, calls=%fused_computation.27 | convolution fusion | flops 4357879808 | bytes 18882560 | tf_op jit(solution)/shard_map/dot_general | solution.py:54
  214.9 2.7 constant_dynamic-slice_fusion.9
  219.4 26.9 %multiply_convert_fusion = (bf16[2048,1024]{1,0:T(8,128)(2,1)}, f32[2048,1024]{1,0:T(8,128)}, f32[2048,1024]{1,0:T(8,128)}) fusion(bf16[1024,1024]{1,0:T(8,128)(2,1)} %all-gather.3.cloned.1.call-done, f32[2048,1024]{1,0:T(8,128)} %get-tuple-element.227, f32[1024]{0:T(1024)S(1)} %bitcast.222, f32[2048]{0:T(1024)S(1)} %add_rsqrt_fusion), kind=kOutput, calls=%fused_computation.13 | convolution fusion | flops 4437573632 | bytes 31469568 | tf_op jit(solution)/shard_map/dot_general | solution.py:54
  248.6 14.8 %add_convert_fusion = bf16[2048,1024]{1,0:T(8,128)(2,1)} fusion(f32[2048,1024]{1,0:T(8,128)} %get-tuple-element.125, f32[2048,1024]{1,0:T(8,128)} %get-tuple-element.228, bf16[1024,1024]{1,0:T(8,128)(2,1)S(1)} %bitcast.200, bf16[512,1024]{1,0:T(8,128)(2,1)} %collective-permute-done.11, bf16[512,1024]{1,0:T(8,128)(2,1)} %collective-permute-done.10, ...), kind=kOutput, calls=%fused_computation.12 | convolution fusion | flops 4345298944 | bytes 27267072 | tf_op jit(solution)/shard_map/dot_general | solution.py:58
  263.4 3.7 convolution_convert_fusion.6
  267.9 2.9 fusion.5
  287.0 3.3 convolution_convert_fusion.8
  292.3 2.7 add_convert_fusion.1
  301.2 19.8 %collective-permute-done.14 = bf16[512,1024]{1,0:T(8,128)(2,1)S(1)} collective-permute-done((bf16[512,1024]{1,0:T(8,128)(2,1)S(1)}, bf16[512,1024]{1,0:T(8,128)(2,1)S(1)}, u32[]{:S(2)}, u32[]{:S(2)}) %collective-permute-start.14) | collective-permute-done | bytes 1048608 | tf_op jit(solution)/shard_map/ppermute | solution.py:928
  321.0 1.7 multiply_reduce_fusion.2
  322.7 20.3 %collective-permute-done.8 = bf16[512,1024]{1,0:T(8,128)(2,1)S(1)} collective-permute-done((bf16[512,1024]{1,0:T(8,128)(2,1)S(1)}, bf16[512,1024]{1,0:T(8,128)(2,1)S(1)}, u32[]{:S(2)}, u32[]{:S(2)}) %collective-permute-start.8) | collective-permute-done | bytes 1048608 | tf_op jit(solution)/shard_map/ppermute | solution.py:928
  343.0 3.9 fusion.77
  348.4 8.3 %convolution_convert_fusion.3 = bf16[1024,1024]{1,0:T(8,128)(2,1)} fusion(bf16[2048,1024]{1,0:T(8,128)(2,1)S(1)} %copy-done.98, bf16[512,1024]{1,0:T(8,128)(2,1)} %collective-permute-done.11, bf16[512,1024]{1,0:T(8,128)(2,1)} %collective-permute-done.10, bf16[512,1024]{1,0:T(8,128)(2,1)} %collective-permute-done.9, bf16[512,1024]{1,0:T(8,128)(2,1)} %bitcast.25, ...), kind=kOutput, calls=%fused_computation.73 | convolution fusion | flops 4316987392 | bytes 10489856 | tf_op jit(solution)/shard_map/dot_general | solution.py:62
  356.7 15.0 %collective-permute-done.16 = bf16[512,1024]{1,0:T(8,128)(2,1)S(1)} collective-permute-done((bf16[512,1024]{1,0:T(8,128)(2,1)S(1)}, bf16[512,1024]{1,0:T(8,128)(2,1)S(1)}, u32[]{:S(2)}, u32[]{:S(2)}) %collective-permute-start.16) | collective-permute-done | bytes 1048608 | tf_op jit(solution)/shard_map/ppermute | solution.py:928
  371.8 6.1 %convolution_convert_fusion.4 = bf16[1024,1024]{1,0:T(8,128)(2,1)} fusion(bf16[2048,1024]{1,0:T(8,128)(2,1)S(1)} %copy-done.97, f32[2048,1024]{1,0:T(8,128)S(1)} %bitcast.211, f32[1024]{0:T(1024)S(1)} %bitcast.225, f32[2048]{0:T(1024)S(1)} %add_rsqrt_fusion), kind=kOutput, calls=%fused_computation.74 | convolution fusion | flops 4302307328 | bytes 14692352 | tf_op jit(solution)/shard_map/dot_general | solution.py:62
  379.1 5.0 convolution_convert_fusion.2.dout_ref
  384.2 41.3 %attend_back.1 = (bf16[2048,768]{1,0:T(8,128)(2,1)S(1)}, f32[2,128,128]{2,1,0:T(8,128)S(1)}, f32[1,256]{1,0:T(1,128)S(1)}, f32[2,384,256]{2,1,0:T(8,128)S(1)}, f32[2,8,256]{2,1,0:T(8,128)S(1)}) custom-call(s32[1]{0:T(128)} %copy.343.length_ref, s32[4]{0:T(128)S(1)} %copy-done.12, bf16[2048,768]{1,0:T(8,128)(2,1)} %copy-done.15, ...), custom_call_target="tpu_custom_call" | custom-call | flops 12582912000 | bytes 20971520 | tf_op jit(solution)/shard_map/attend_back/pallas_call | solution.py:348
  425.5 1.7 copy-done.13
  427.3 3.9 select_reduce_fusion
  432.9 2.9 select_reduce_fusion.18
  438.0 7.2 %convolution_convert_fusion = bf16[2048,1024]{1,0:T(8,128)(2,1)} fusion(bf16[2048,768]{1,0:T(8,128)(2,1)} %copy-done.13, bf16[1024,768]{1,0:T(8,128)(2,1)S(1)} %bitcast.261), kind=kOutput, calls=%fused_computation.53 | convolution fusion | flops 3223322624 | bytes 8912896 | tf_op jit(solution)/shard_map/dot_general | solution.py:58
  445.2 4.7 convolution_convert_fusion.5
  449.9 2.2 convolution_convert_fusion.10
  452.2 115.2 %finish.1 = (f32[512,1024]{1,0:T(8,128)}, f32[4,32,768]{2,1,0:T(8,128)}, f32[4,32,1024]{2,1,0:T(8,128)}, f32[128,1024]{1,0:T(8,128)}, f32[32,1024]{1,0:T(8,128)}...) custom-call(bf16[4,512,1024]{2,1,0:T(8,128)(2,1)} %bitcast.195, bf16[4,8,32,768]{3,2,1,0:T(8,128)(2,1)} %bitcast.212, ...), custom_call_target="tpu_custom_call" | custom-call | tf_op jit(solution)/shard_map/finish/pallas_call | solution.py:905
  567.4 1.6 slice.268
  573.9 1.9 copy.305
  577.3 3.2 copy.344
  (361 shorter events, 68.0 us)
Async XLA Ops:
  7.2 207.7 %all-gather.5.cloned.1.call-start = ((), (), s32[]{:S(2)}) async-start(), calls=%async_computation.1 | async-start | bytes 2359296 | tf_op jit(solution)/shard_map/all_gather | solution.py:1009
  9.2 210.2 %all-gather.3.cloned.1.call-start = ((), (), s32[]{:S(2)}) async-start(), calls=%async_computation | async-start | bytes 2359296 | tf_op jit(solution)/shard_map/all_gather | solution.py:1010
  12.7 83.3 %copy-start.67 = (f32[2]{0:T(128)}, f32[2]{0:T(128)S(1)}, u32[]{:S(2)}) copy-start(f32[2]{0:T(128)S(1)} %get-tuple-element.111) | copy-start | bytes 28
  12.7 83.3 %copy-start.69 = (f32[2]{0:T(128)}, f32[2]{0:T(128)S(1)}, u32[]{:S(2)}) copy-start(f32[2]{0:T(128)S(1)} %get-tuple-element.112) | copy-start | bytes 28
  12.7 83.3 %copy-start.71 = (f32[2]{0:T(128)}, f32[2]{0:T(128)S(1)}, u32[]{:S(2)}) copy-start(f32[2]{0:T(128)S(1)} %get-tuple-element.113) | copy-start | bytes 28
  12.7 83.3 %copy-start.73 = (f32[2]{0:T(128)}, f32[2]{0:T(128)S(1)}, u32[]{:S(2)}) copy-start(f32[2]{0:T(128)S(1)} %get-tuple-element.114) | copy-start | bytes 28
  12.7 83.3 %copy-start.74 = (f32[2]{0:T(128)}, f32[2]{0:T(128)S(1)}, u32[]{:S(2)}) copy-start(f32[2]{0:T(128)S(1)} %get-tuple-element.115) | copy-start | bytes 28
  12.7 83.3 %copy-start.75 = (f32[2]{0:T(128)}, f32[2]{0:T(128)S(1)}, u32[]{:S(2)}) copy-start(f32[2]{0:T(128)S(1)} %get-tuple-element.116) | copy-start | bytes 28
  12.7 83.3 %copy-start.76 = (f32[2]{0:T(128)}, f32[2]{0:T(128)S(1)}, u32[]{:S(2)}) copy-start(f32[2]{0:T(128)S(1)} %get-tuple-element.117) | copy-start | bytes 28
  12.7 83.3 %copy-start.77 = (f32[2]{0:T(128)}, f32[2]{0:T(128)S(1)}, u32[]{:S(2)}) copy-start(f32[2]{0:T(128)S(1)} %get-tuple-element.118) | copy-start | bytes 28
  12.7 83.3 %copy-start.78 = (f32[2]{0:T(128)}, f32[2]{0:T(128)S(1)}, u32[]{:S(2)}) copy-start(f32[2]{0:T(128)S(1)} %get-tuple-element.119) | copy-start | bytes 28
  12.8 83.3 %copy-start.79 = (f32[2]{0:T(128)}, f32[2]{0:T(128)S(1)}, u32[]{:S(2)}) copy-start(f32[2]{0:T(128)S(1)} %get-tuple-element.120) | copy-start | bytes 28
  12.8 83.3 %copy-start.80 = (f32[2]{0:T(128)}, f32[2]{0:T(128)S(1)}, u32[]{:S(2)}) copy-start(f32[2]{0:T(128)S(1)} %get-tuple-element.121) | copy-start | bytes 28
  13.3 88.5 %copy-start.11 = (s32[4]{0:T(128)}, s32[4]{0:T(128)S(1)}, u32[]{:S(2)}) copy-start(s32[4]{0:T(128)S(1)} %get-tuple-element.230.order_ref) | copy-start | bytes 52
  13.5 71.0 %copy-start.82 = (f32[2,128]{1,0:T(2,128)S(1)}, f32[2,128]{1,0:T(2,128)}, u32[]{:S(2)}) copy-start(f32[2,128]{1,0:T(2,128)} %param.27) | copy-start | bytes 3076
  13.5 71.0 %copy-start.86 = (s32[15]{0:T(128)S(1)}, s32[15]{0:T(128)}, u32[]{:S(2)}) copy-start(s32[15]{0:T(128)} %constant.37.clone) | copy-start | bytes 184
  84.6 17.3 %copy-start.2 = (f32[2,128]{1,0:T(2,128)}, f32[2,128]{1,0:T(2,128)S(1)}, u32[]{:S(2)}) copy-start(f32[2,128]{1,0:T(2,128)S(1)} %add_divide_fusion) | copy-start | bytes 3076
  125.8 78.7 %copy-start.4 = (bf16[2048,256]{1,0:T(8,128)(2,1)}, bf16[2048,256]{1,0:T(8,128)(2,1)S(1)}, u32[]{:S(2)}) copy-start(bf16[2048,256]{1,0:T(8,128)(2,1)S(1)} %get-tuple-element.37.out_ref) | copy-start | bytes 3145732
  125.8 60.5 %collective-permute-start.1 = (bf16[2048,256]{1,0:T(8,128)(2,1)S(1)}, bf16[2048,256]{1,0:T(8,128)(2,1)}, u32[]{:S(2)}, u32[]{:S(2)}) collective-permute-start(bf16[2048,256]{1,0:T(8,128)(2,1)S(1)} %get-tuple-element.37.out_ref), channel_id=1, source_target_pairs={{0,16},{8,24},{16,0},{24,8},{1,17},{9,25},{17,1},{25,9},{2,18},{10... | collective-permute-start | bytes 3145736 | tf_op jit(solution)/shard_map/ppermute | solution.py:928
  127.3 71.6 %collective-permute-start = (bf16[2048,256]{1,0:T(8,128)(2,1)S(1)}, bf16[2048,256]{1,0:T(8,128)(2,1)}, u32[]{:S(2)}, u32[]{:S(2)}) collective-permute-start(bf16[2048,256]{1,0:T(8,128)(2,1)S(1)} %get-tuple-element.37.out_ref), channel_id=1, source_target_pairs={{0,8},{8,0},{16,24},{24,16},{1,9},{9,1},{17,25},{25,17},{2,10},{10... | collective-permute-start | bytes 3145736 | tf_op jit(solution)/shard_map/ppermute | solution.py:928
  127.3 71.3 %collective-permute-start.10 = (bf16[512,1024]{1,0:T(8,128)(2,1)}, bf16[512,1024]{1,0:T(8,128)(2,1)}, u32[]{:S(2)}, u32[]{:S(2)}) collective-permute-start(bf16[512,1024]{1,0:T(8,128)(2,1)} %bitcast.25), channel_id=1, source_target_pairs={{0,16},{8,24},{16,0},{24,8},{1,17},{9,25},{17,1},{25,9},{2,18},{10... | collective-permute-start | bytes 3145736 | tf_op jit(solution)/shard_map/ppermute | solution.py:928
  127.8 120.7 %collective-permute-start.9 = (bf16[512,1024]{1,0:T(8,128)(2,1)}, bf16[512,1024]{1,0:T(8,128)(2,1)}, u32[]{:S(2)}, u32[]{:S(2)}) collective-permute-start(bf16[512,1024]{1,0:T(8,128)(2,1)} %bitcast.25), channel_id=1, source_target_pairs={{0,8},{8,0},{16,24},{24,16},{1,9},{9,1},{17,25},{25,17},{2,10},{10... | collective-permute-start | bytes 3145736 | tf_op jit(solution)/shard_map/ppermute | solution.py:928
  140.0 39.6 %copy-start.31 = (pred[768,256]{0,1:T(8,128)(4,1)S(1)}, pred[768,256]{0,1:T(8,128)(4,1)}, u32[]{:S(2)}) copy-start(pred[768,256]{0,1:T(8,128)(4,1)} %get-tuple-element.174) | copy-start | bytes 589828
  141.9 38.7 %copy-start.30 = (pred[768,256]{0,1:T(8,128)(4,1)S(1)}, pred[768,256]{0,1:T(8,128)(4,1)}, u32[]{:S(2)}) copy-start(pred[768,256]{0,1:T(8,128)(4,1)} %get-tuple-element.175) | copy-start | bytes 589828
  143.8 37.7 %copy-start.29 = (pred[768,256]{0,1:T(8,128)(4,1)S(1)}, pred[768,256]{0,1:T(8,128)(4,1)}, u32[]{:S(2)}) copy-start(pred[768,256]{0,1:T(8,128)(4,1)} %get-tuple-element.176) | copy-start | bytes 589828
  145.7 36.7 %copy-start.28 = (pred[768,256]{0,1:T(8,128)(4,1)S(1)}, pred[768,256]{0,1:T(8,128)(4,1)}, u32[]{:S(2)}) copy-start(pred[768,256]{0,1:T(8,128)(4,1)} %get-tuple-element.177) | copy-start | bytes 589828
  153.3 33.3 %copy-start.68 = (f32[2]{0:T(128)S(1)}, f32[2]{0:T(128)}, u32[]{:S(2)}) copy-start(f32[2]{0:T(128)} %copy-done.67) | copy-start | bytes 28
  153.3 33.3 %copy-start.70 = (f32[2]{0:T(128)S(1)}, f32[2]{0:T(128)}, u32[]{:S(2)}) copy-start(f32[2]{0:T(128)} %copy-done.69) | copy-start | bytes 28
  153.3 33.3 %copy-start.72 = (f32[2]{0:T(128)S(1)}, f32[2]{0:T(128)}, u32[]{:S(2)}) copy-start(f32[2]{0:T(128)} %copy-done.71) | copy-start | bytes 28
  186.3 16.1 %collective-permute-start.2 = (bf16[2048,256]{1,0:T(8,128)(2,1)}, bf16[2048,256]{1,0:T(8,128)(2,1)}, u32[]{:S(2)}, u32[]{:S(2)}) collective-permute-start(bf16[2048,256]{1,0:T(8,128)(2,1)} %collective-permute-done.1), channel_id=1, source_target_pairs={{0,8},{8,0},{16,24},{24,16},{1,9},{9,1},{17,25},{25,17},{2,10},{10... | collective-permute-start | bytes 3145736 | tf_op jit(solution)/shard_map/ppermute | solution.py:928
  195.7 52.9 %copy-start.84 = (bf16[1,4,4,128]{3,1,2,0:T(4,128)(2,1)}, bf16[1,4,4,128]{3,1,2,0:T(4,128)(2,1)S(1)}, u32[]{:S(2)}) copy-start(bf16[1,4,4,128]{3,1,2,0:T(4,128)(2,1)S(1)} %copy.306) | copy-start | bytes 12292
  198.6 49.9 %collective-permute-start.11 = (bf16[512,1024]{1,0:T(8,128)(2,1)}, bf16[512,1024]{1,0:T(8,128)(2,1)}, u32[]{:S(2)}, u32[]{:S(2)}) collective-permute-start(bf16[512,1024]{1,0:T(8,128)(2,1)} %collective-permute-done.10), channel_id=1, source_target_pairs={{0,8},{8,0},{16,24},{24,16},{1,9},{9,1},{17,25},{25,17},{2,10},{10... | collective-permute-start | bytes 3145736 | tf_op jit(solution)/shard_map/ppermute | solution.py:928
  217.5 28.8 %collective-permute-start.3 = (bf16[1,2,128,1024]{3,2,1,0:T(8,128)(2,1)}, bf16[1,2,128,1024]{3,2,1,0:T(8,128)(2,1)S(1)}, u32[]{:S(2)}, u32[]{:S(2)}) collective-permute-start(bf16[1,2,128,1024]{3,2,1,0:T(8,128)(2,1)} %get-tuple-element.138), channel_id=1, source_target_pairs={{0,8},{8,0},{16,24},{24,16},{1,9},{9,1},{17,25},{25,17},{2,10},{10... | collective-permute-start | bytes 1572872 | tf_op jit(solution)/shard_map/ppermute | solution.py:928
  217.9 28.4 %collective-permute-start.4 = (bf16[1,2,128,1024]{3,2,1,0:T(8,128)(2,1)}, bf16[1,2,128,1024]{3,2,1,0:T(8,128)(2,1)}, u32[]{:S(2)}, u32[]{:S(2)}) collective-permute-start(bf16[1,2,128,1024]{3,2,1,0:T(8,128)(2,1)} %get-tuple-element.137), channel_id=1, source_target_pairs={{0,16},{8,24},{16,0},{24,8},{1,17},{9,25},{17,1},{25,9},{2,18},{10... | collective-permute-start | bytes 1572872 | tf_op jit(solution)/shard_map/ppermute | solution.py:928
  219.3 27.1 %collective-permute-start.5 = (bf16[1,2,128,1024]{3,2,1,0:T(8,128)(2,1)S(1)}, bf16[1,2,128,1024]{3,2,1,0:T(8,128)(2,1)}, u32[]{:S(2)}, u32[]{:S(2)}) collective-permute-start(bf16[1,2,128,1024]{3,2,1,0:T(8,128)(2,1)S(1)} %get-tuple-element.136), channel_id=1, source_target_pairs={{0,24},{8,16},{16,8},{24,0},{1,25},{9,17},{17,9},{25,1},{2,26},{10... | collective-permute-start | bytes 1572872 | tf_op jit(solution)/shard_map/ppermute | solution.py:928
  248.5 14.9 %copy-start.24 = (bf16[2,4,128,1024]{3,2,1,0:T(8,128)(2,1)}, bf16[2,4,128,1024]{3,2,1,0:T(8,128)(2,1)S(1)}, u32[]{:S(2)}) copy-start(bf16[2,4,128,1024]{3,2,1,0:T(8,128)(2,1)S(1)} %copy.237) | copy-start | bytes 6291460
  248.5 14.8 %copy-start.87 = (bf16[1024,1024]{1,0:T(8,128)(2,1)S(1)}, bf16[1024,1024]{1,0:T(8,128)(2,1)}, u32[]{:S(2)}) copy-start(bf16[1024,1024]{1,0:T(8,128)(2,1)} %all-gather.3.cloned.1.call-done) | copy-start | bytes 6291460
  267.1 25.2 %collective-permute-start.13 = (bf16[512,1024]{1,0:T(8,128)(2,1)}, bf16[512,1024]{1,0:T(8,128)(2,1)}, u32[]{:S(2)}, u32[]{:S(2)}) collective-permute-start(bf16[512,1024]{1,0:T(8,128)(2,1)} %convolution_convert_fusion.6), channel_id=1, source_target_pairs={{0,8},{8,0},{16,24},{24,16},{1,9},{9,1},{17,25},{25,17},{2,10},{10... | collective-permute-start | bytes 3145736 | tf_op jit(solution)/shard_map/ppermute | solution.py:928
  267.8 12.6 %copy-start.52 = (pred[384,256]{1,0:T(32,128)(4,1)S(1)}, pred[384,256]{1,0:T(32,128)(4,1)}, u32[]{:S(2)}) copy-start(pred[384,256]{1,0:T(32,128)(4,1)} %constant.68) | copy-start | bytes 294916
  267.8 13.2 %copy-start.51 = (pred[384,256]{1,0:T(32,128)(4,1)S(1)}, pred[384,256]{1,0:T(32,128)(4,1)}, u32[]{:S(2)}) copy-start(pred[384,256]{1,0:T(32,128)(4,1)} %constant.67) | copy-start | bytes 294916
  267.8 13.9 %copy-start.50 = (pred[384,256]{1,0:T(32,128)(4,1)S(1)}, pred[384,256]{1,0:T(32,128)(4,1)}, u32[]{:S(2)}) copy-start(pred[384,256]{1,0:T(32,128)(4,1)} %constant.66) | copy-start | bytes 294916
  267.9 14.6 %copy-start.49 = (pred[384,256]{1,0:T(32,128)(4,1)S(1)}, pred[384,256]{1,0:T(32,128)(4,1)}, u32[]{:S(2)}) copy-start(pred[384,256]{1,0:T(32,128)(4,1)} %constant.65) | copy-start | bytes 294916
  267.9 15.2 %copy-start.48 = (pred[384,256]{1,0:T(32,128)(4,1)S(1)}, pred[384,256]{1,0:T(32,128)(4,1)}, u32[]{:S(2)}) copy-start(pred[384,256]{1,0:T(32,128)(4,1)} %constant.64) | copy-start | bytes 294916
  267.9 15.3 %copy-start.47 = (pred[384,256]{1,0:T(32,128)(4,1)S(1)}, pred[384,256]{1,0:T(32,128)(4,1)}, u32[]{:S(2)}) copy-start(pred[384,256]{1,0:T(32,128)(4,1)} %constant.63) | copy-start | bytes 294916
  267.9 15.3 %copy-start.46 = (pred[384,256]{1,0:T(32,128)(4,1)S(1)}, pred[384,256]{1,0:T(32,128)(4,1)}, u32[]{:S(2)}) copy-start(pred[384,256]{1,0:T(32,128)(4,1)} %constant.62) | copy-start | bytes 294916
  267.9 15.4 %copy-start.45 = (pred[384,256]{1,0:T(32,128)(4,1)S(1)}, pred[384,256]{1,0:T(32,128)(4,1)}, u32[]{:S(2)}) copy-start(pred[384,256]{1,0:T(32,128)(4,1)} %constant.61) | copy-start | bytes 294916
  270.9 12.6 %copy-start.41 = (pred[384,256]{1,0:T(32,128)(4,1)S(1)}, pred[384,256]{1,0:T(32,128)(4,1)}, u32[]{:S(2)}) copy-start(pred[384,256]{1,0:T(32,128)(4,1)} %constant.57) | copy-start | bytes 294916
  270.9 12.6 %copy-start.40 = (pred[384,256]{1,0:T(32,128)(4,1)S(1)}, pred[384,256]{1,0:T(32,128)(4,1)}, u32[]{:S(2)}) copy-start(pred[384,256]{1,0:T(32,128)(4,1)} %constant.56) | copy-start | bytes 294916
  270.9 12.7 %copy-start.39 = (pred[384,256]{1,0:T(32,128)(4,1)S(1)}, pred[384,256]{1,0:T(32,128)(4,1)}, u32[]{:S(2)}) copy-start(pred[384,256]{1,0:T(32,128)(4,1)} %constant.55) | copy-start | bytes 294916
  270.9 13.4 %copy-start.38 = (pred[384,256]{1,0:T(32,128)(4,1)S(1)}, pred[384,256]{1,0:T(32,128)(4,1)}, u32[]{:S(2)}) copy-start(pred[384,256]{1,0:T(32,128)(4,1)} %constant.54) | copy-start | bytes 294916
  270.9 14.0 %copy-start.37 = (pred[384,256]{1,0:T(32,128)(4,1)S(1)}, pred[384,256]{1,0:T(32,128)(4,1)}, u32[]{:S(2)}) copy-start(pred[384,256]{1,0:T(32,128)(4,1)} %constant.53) | copy-start | bytes 294916
  271.0 14.7 %copy-start.36 = (pred[384,256]{1,0:T(32,128)(4,1)S(1)}, pred[384,256]{1,0:T(32,128)(4,1)}, u32[]{:S(2)}) copy-start(pred[384,256]{1,0:T(32,128)(4,1)} %constant.52) | copy-start | bytes 294916
  271.0 15.4 %copy-start.35 = (pred[384,256]{1,0:T(32,128)(4,1)S(1)}, pred[384,256]{1,0:T(32,128)(4,1)}, u32[]{:S(2)}) copy-start(pred[384,256]{1,0:T(32,128)(4,1)} %constant.51) | copy-start | bytes 294916
  290.3 7.6 %collective-permute-start.7 = (bf16[512,1024]{1,0:T(8,128)(2,1)S(1)}, bf16[512,1024]{1,0:T(8,128)(2,1)S(1)}, u32[]{:S(2)}, u32[]{:S(2)}) collective-permute-start(bf16[512,1024]{1,0:T(8,128)(2,1)S(1)} %convolution_convert_fusion.8), channel_id=1, source_target_pairs={{0,8},{8,0},{16,24},{24,16},{1,9},{9,1},{17,25},{25,17},{2,10},{10... | collective-permute-start | bytes 3145736 | tf_op jit(solution)/shard_map/ppermute | solution.py:928
  292.1 9.1 %collective-permute-start.12 = (bf16[512,1024]{1,0:T(8,128)(2,1)S(1)}, bf16[512,1024]{1,0:T(8,128)(2,1)S(1)}, u32[]{:S(2)}, u32[]{:S(2)}) collective-permute-start(bf16[512,1024]{1,0:T(8,128)(2,1)S(1)} %convolution_convert_fusion.7), channel_id=1, source_target_pairs={{0,8},{8,0},{16,24},{24,16},{1,9},{9,1},{17,25},{25,17},{2,10},{10... | collective-permute-start | bytes 3145736 | tf_op jit(solution)/shard_map/ppermute | solution.py:928
  294.9 26.0 %collective-permute-start.14 = (bf16[512,1024]{1,0:T(8,128)(2,1)S(1)}, bf16[512,1024]{1,0:T(8,128)(2,1)S(1)}, u32[]{:S(2)}, u32[]{:S(2)}) collective-permute-start(bf16[512,1024]{1,0:T(8,128)(2,1)S(1)} %add_convert_fusion.1), channel_id=1, source_target_pairs={{0,16},{8,24},{16,0},{24,8},{1,17},{9,25},{17,1},{25,9},{2,18},{10... | collective-permute-start | bytes 3145736 | tf_op jit(solution)/shard_map/ppermute | solution.py:928
  296.4 24.6 %slice-start = ((s8[8388608]{0:T(1024)(128)(4,1)}), s8[4194304]{0:T(1024)(128)(4,1)S(1)}, s32[]{:S(2)}) async-start(s8[8388608]{0:T(1024)(128)(4,1)} %bitcast.210), calls=%async_computation.2 | async-start | bytes 8388608
  297.7 23.3 %slice-start.1 = ((s8[8388608]{0:T(1024)(128)(4,1)}), s8[4194304]{0:T(1024)(128)(4,1)S(1)}, s32[]{:S(2)}) async-start(s8[8388608]{0:T(1024)(128)(4,1)} %bitcast.210), calls=%async_computation.3 | async-start | bytes 8388608
  297.7 25.0 %collective-permute-start.6 = (bf16[512,1024]{1,0:T(8,128)(2,1)S(1)}, bf16[512,1024]{1,0:T(8,128)(2,1)S(1)}, u32[]{:S(2)}, u32[]{:S(2)}) collective-permute-start(bf16[512,1024]{1,0:T(8,128)(2,1)S(1)} %convolution_convert_fusion.9), channel_id=1, source_target_pairs={{0,8},{8,0},{16,24},{24,16},{1,9},{9,1},{17,25},{25,17},{2,10},{10... | collective-permute-start | bytes 3145736 | tf_op jit(solution)/shard_map/ppermute | solution.py:928
  299.2 43.8 %collective-permute-start.8 = (bf16[512,1024]{1,0:T(8,128)(2,1)S(1)}, bf16[512,1024]{1,0:T(8,128)(2,1)S(1)}, u32[]{:S(2)}, u32[]{:S(2)}) collective-permute-start(bf16[512,1024]{1,0:T(8,128)(2,1)S(1)} %add_convert_fusion.2), channel_id=1, source_target_pairs={{0,16},{8,24},{16,0},{24,8},{1,17},{9,25},{17,1},{25,9},{2,18},{10... | collective-permute-start | bytes 3145736 | tf_op jit(solution)/shard_map/ppermute | solution.py:928
  346.9 32.1 %copy-start.26 = (bf16[512,1024]{1,0:T(8,128)(2,1)}, bf16[512,1024]{1,0:T(8,128)(2,1)S(1)}, u32[]{:S(2)}) copy-start(bf16[512,1024]{1,0:T(8,128)(2,1)S(1)} %get-tuple-element.122) | copy-start | bytes 3145732
  347.0 24.8 %collective-permute-start.16 = (bf16[512,1024]{1,0:T(8,128)(2,1)S(1)}, bf16[512,1024]{1,0:T(8,128)(2,1)S(1)}, u32[]{:S(2)}, u32[]{:S(2)}) collective-permute-start(bf16[512,1024]{1,0:T(8,128)(2,1)S(1)} %get-tuple-element.122), channel_id=1, source_target_pairs={{0,16},{8,24},{16,0},{24,8},{1,17},{9,25},{17,1},{25,9},{2,18},{10... | collective-permute-start | bytes 3145736 | tf_op jit(solution)/shard_map/ppermute | solution.py:928
  356.7 22.3 %collective-permute-start.15 = (bf16[512,1024]{1,0:T(8,128)(2,1)S(1)}, bf16[512,1024]{1,0:T(8,128)(2,1)S(1)}, u32[]{:S(2)}, u32[]{:S(2)}) collective-permute-start(bf16[512,1024]{1,0:T(8,128)(2,1)S(1)} %get-tuple-element.122), channel_id=1, source_target_pairs={{0,8},{8,0},{16,24},{24,16},{1,9},{9,1},{17,25},{25,17},{2,10},{10... | collective-permute-start | bytes 3145736 | tf_op jit(solution)/shard_map/ppermute | solution.py:928
  371.8 7.3 %collective-permute-start.17 = (bf16[512,1024]{1,0:T(8,128)(2,1)S(1)}, bf16[512,1024]{1,0:T(8,128)(2,1)S(1)}, u32[]{:S(2)}, u32[]{:S(2)}) collective-permute-start(bf16[512,1024]{1,0:T(8,128)(2,1)S(1)} %collective-permute-done.16), channel_id=1, source_target_pairs={{0,8},{8,0},{16,24},{24,16},{1,9},{9,1},{17,25},{25,17},{2,10},{10... | collective-permute-start | bytes 3145736 | tf_op jit(solution)/shard_map/ppermute | solution.py:928
  (57 other events, 356.1 us)
Sparse Core Ops, SparseCore 0:
  10.2 69.2 all-gather.4
  129.9 48.5 all-gather.2

commit v4 on v3

--- a/solution.py
+++ b/solution.py
@@ -38,16 +38,19 @@
     return rows + BLOCK - cols
 
 
-def tile_bias(table):
-    distance = jnp.arange(QTILE, dtype=jnp.int32)[:, None] + BLOCK - jnp.arange(SPAN, dtype=jnp.int32)[None, :]
-    clipped = jnp.clip(distance, 0, BLOCK)
-    edges = jnp.array(BUCKET_EDGES, dtype=jnp.int32)
-    bucket = jnp.minimum(clipped, 16) + jnp.sum((clipped[:, :, None] >= edges).astype(jnp.int32), axis=-1)
-    total = jnp.zeros((table.shape[0],) + bucket.shape, f32)
-    for bucket_id in range(BUCKETS):
-        total = jnp.where((bucket == bucket_id)[None], table[:, bucket_id][:, None, None], total)
-    window = (distance >= 0) & (distance < BLOCK)
-    return jnp.where(window[None], total * LOG2E, -jnp.inf)
+def bias_vector(table):
+    distance = BLOCK - np.arange(2 * BLOCK)
+    inside = (distance >= 0) & (distance < BLOCK)
+    bucket = jnp.asarray(np.where(inside, bucket_of(np.clip(distance, 0, BLOCK)), BUCKETS).astype(np.int32))
+    total = jnp.full((table.shape[0], 2 * BLOCK), -jnp.inf, f32)
+    for i in range(BUCKETS):
+        total = jnp.where((bucket == i)[None], table[:, i : i + 1] * LOG2E, total)
+    return total
+
+
+def tile_bias(vector_ref, head):
+    wide = jnp.broadcast_to(vector_ref[head : head + 1, :], (QTILE, 2 * BLOCK))
+    return pltpu.roll(wide, 0, 1, stride=1, stride_axis=0)[:, :SPAN]
 
 
 def dot(a, b):
@@ -92,7 +95,7 @@
     init_ref,
     query_ref,
     forget_ref,
-    bias_ref,
+    vector_ref,
     att_ref,
     final_ref,
     mem_ref,
@@ -100,6 +103,7 @@
     lse_ref,
     slse_ref,
     memory_ref,
+    bias_ref,
 ):
     block = pl.program_id(0)
     length = length_ref[0]
@@ -109,6 +113,8 @@
     @pl.when(block == 0)
     def _():
         memory_ref[...] = init_ref[...].astype(f32)
+        for head in range(heads):
+            bias_ref[head] = tile_bias(vector_ref, head)
 
     live_block = block * BLOCK < length
     for head in range(heads):
@@ -181,7 +187,7 @@
                 pl.BlockSpec((STATE_VECTORS, width), lambda b, _, at: (0, 0)),
                 pl.BlockSpec((heads, DH, DH), lambda b, _, at: (0, 0, 0)),
                 pl.BlockSpec((1, width), lambda b, _, at: (0, 0)),
-                pl.BlockSpec((heads, QTILE, SPAN), lambda b, _, at: (0, 0, 0)),
+                pl.BlockSpec((heads, 2 * BLOCK), lambda b, _, at: (0, 0)),
             ],
             out_specs=(
                 pl.BlockSpec((BLOCK, width), lambda b, _, at: (at[b], 0)),
@@ -191,7 +197,7 @@
                 pl.BlockSpec((heads, BLOCK), lambda b, _, at: (0, b)),
                 pl.BlockSpec((heads, STATE_VECTORS), lambda b, _, at: (0, b)),
             ),
-            scratch_shapes=[pltpu.VMEM((STATE_VECTORS, width), f32)],
+            scratch_shapes=[pltpu.VMEM((STATE_VECTORS, width), f32), pltpu.VMEM((heads, QTILE, SPAN), f32)],
         ),
         compiler_params=pltpu.CompilerParams(vmem_limit_bytes=40 << 20),
         cost_estimate=pl.CostEstimate(
@@ -217,7 +223,7 @@
     sgrad_ref,
     query_ref,
     forget_ref,
-    bias_ref,
+    vector_ref,
     dqkv_ref,
     dquery_ref,
     dforget_ref,
@@ -226,6 +232,7 @@
     dmem_ref,
     dnext_ref,
     dctx_ref,
+    bias_ref,
 ):
     step = pl.program_id(0)
     block = blocks - 1 - step
@@ -241,6 +248,8 @@
         dforget_ref[...] = jnp.zeros_like(dforget_ref)
         near_ref[...] = jnp.zeros_like(near_ref)
         far_ref[...] = jnp.zeros_like(far_ref)
+        for head in range(heads):
+            bias_ref[head] = tile_bias(vector_ref, head).T
 
     live_block = block * BLOCK < length
     refs = (prev_ref, cur_ref)
@@ -340,7 +349,7 @@
         dqkv_ref[:, value_cols] = dctx_ref[1, BLOCK:].astype(bf16)
 
 
-def attend_back(qkv, dout, out, mem, upd, lse, slse, sgrad, length, state_query, forget, bias_t, heads, order):
+def attend_back(qkv, dout, out, mem, upd, lse, slse, sgrad, length, state_query, forget, bias, heads, order):
     rows, width3 = qkv.shape
     width = heads * DH
     blocks = rows // BLOCK
@@ -369,7 +378,7 @@
                 pl.BlockSpec((STATE_VECTORS, width), lambda b, _, at: (0, 0)),
                 pl.BlockSpec((heads, DH, DH), lambda b, _, at: (0, 0, 0)),
                 pl.BlockSpec((1, width), lambda b, _, at: (0, 0)),
-                pl.BlockSpec((heads, SPAN, QTILE), lambda b, _, at: (0, 0, 0)),
+                pl.BlockSpec((heads, 2 * BLOCK), lambda b, _, at: (0, 0)),
             ],
             out_specs=(
                 pl.BlockSpec((BLOCK, width3), lambda b, _, at: (at[last - b], 0)),
@@ -382,6 +391,7 @@
                 pltpu.VMEM((STATE_VECTORS, width), f32),
                 pltpu.VMEM((2, BLOCK, width), f32),
                 pltpu.VMEM((2, 2 * BLOCK, DH), f32),
+                pltpu.VMEM((heads, SPAN, QTILE), f32),
             ],
         ),
         compiler_params=pltpu.CompilerParams(vmem_limit_bytes=40 << 20),
@@ -389,7 +399,7 @@
             flops=blocks * heads * 512 * 2400 * 128 * 10, bytes_accessed=20 << 20, transcendentals=10 << 20
         ),
         name="attend_back",
-    )(length, order, qkv, qkv, dout, out, mem, upd, lse, slse, sgrad, state_query, forget, bias_t)
+    )(length, order, qkv, qkv, dout, out, mem, upd, lse, slse, sgrad, state_query, forget, bias)
 
 
 def gather_kernel(seq, hi, lo, tok_ref, w_ref, gain_ref, out_ref, toks_ref, ws_ref, gains_ref, outs_ref, here_sem, seq_send, seq_recv, far_send, far_recv, lo_send, lo_recv):
@@ -923,6 +933,273 @@
     )(dn, gq, gu, gd, go, small, mlp_gain, tok, dmid, gain)
 
 
+GELU_P = 0.24
+GELU_C = (
+    0.08951261885080208,
+    0.15562094398234086,
+    -0.15437154502074169,
+    0.6261054138112487,
+    -0.6465313024138201,
+    0.5547927291245551,
+    -0.125128858665134,
+)
+
+
+def gelu_parts(x):
+    size = jnp.abs(x)
+    t = 1.0 / (1.0 + GELU_P * size)
+    poly = GELU_C[-1] * t
+    for c in GELU_C[-2::-1]:
+        poly = (poly + c) * t
+    bell = jnp.exp2(x * x * (-0.5 * LOG2E))
+    tail = poly * bell
+    cdf = jnp.where(x < 0.0, tail, 1.0 - tail)
+    return x * cdf, cdf + x * bell * (1.0 / math.sqrt(2.0 * math.pi))
+
+
+def mlp_kernel(seq, sub, length_ref, *refs):
+    refs = list(refs)
+
+    def take(count):
+        taken = refs[:count]
+        del refs[:count]
+        return taken
+
+    att_refs = take(seq)
+    (tok_ref,) = take(1)
+    grad_refs = take(seq)
+    wo_ref, wu_ref, wd_ref, gain_ref = take(4)
+    mid_ref, dmid_ref, gsum_ref, db_ref, mo_ref, ug_ref, dg_ref = take(7)
+    att_buf, tok_buf, gm, nm, hid, dpre, low, into, acc = take(9)
+    dbv = low.at[0]
+    depth = att_buf.shape[0]
+    load_sem, gm_sem, dn_send, dn_recv, db_send, db_recv, mo_sem, own_sem = take(8)
+
+    me = lax.axis_index("seq")
+    length = length_ref[0]
+    dim = wo_ref.shape[0]
+    width = dim // seq
+    rows = tok_ref.shape[1]
+    share = wu_ref.shape[1]
+    bits = [1 << i for i in range(seq.bit_length() - 1)]
+
+    barrier = pltpu.get_barrier_semaphore()
+    for bit in bits:
+        pl.semaphore_signal(barrier, inc=1, device_id={"seq": me ^ bit}, device_id_type=MESH)
+    pl.semaphore_wait(barrier, len(bits))
+
+    order = list(reversed(range(seq)))
+    gm_loads = {j: pltpu.make_async_copy(grad_refs[j], gm.at[pl.ds(j * rows, rows)], gm_sem.at[j]) for j in order}
+
+    def chunk_loads(n):
+        j, slot = order[n], n % depth
+        copies = [
+            pltpu.make_async_copy(
+                att_refs[k].at[pl.ds((j ^ k) * rows, rows)], att_buf.at[slot, k], load_sem.at[slot, k]
+            )
+            for k in range(seq)
+        ]
+        copies.append(pltpu.make_async_copy(tok_ref.at[j], tok_buf.at[slot], load_sem.at[slot, seq]))
+        return copies
+
+    for c in chunk_loads(0):
+        c.start()
+    for j in order:
+        gm_loads[j].start()
+
+    slots = {}
+    for bit in bits:
+        for j in range(0, seq, 2 * bit):
+            slots[bit, j] = len(slots)
+
+    def dn_copy(bit, j):
+        slot = slots[bit, j]
+        return pltpu.make_async_remote_copy(
+            src_ref=low.at[j ^ bit],
+            dst_ref=into.at[slot],
+            send_sem=dn_send.at[slot],
+            recv_sem=dn_recv.at[slot],
+            device_id={"seq": me ^ bit},
+            device_id_type=MESH,
+        )
+
+    gain = gain_ref[...]
+    for n, j in enumerate(order):
+        slot = n % depth
+        if depth == 1 and n:
+            for c in chunk_loads(n):
+                c.start()
+        for c in chunk_loads(n):
+            c.wait()
+        if depth == 2 and n + 1 < seq:
+            for c in chunk_loads(n + 1):
+                c.start()
+        gm_loads[j].wait()
+        base = (j ^ me) * rows
+
+        @pl.loop(0, rows // sub)
+        def _(s):
+            at = pl.ds(pl.multiple_of(s * sub, sub), sub)
+            here = pl.ds(pl.multiple_of(j * rows + s * sub, sub), sub)
+            position = base + s * sub + lax.broadcasted_iota(jnp.int32, (sub, 1), 0)
+            live = jnp.where(position < length, 1.0, 0.0)
+            masked = (gm[here].astype(f32) * live).astype(bf16)
+            gm[here] = masked
+            mid = tok_buf[slot, at].astype(f32)
+            for k in range(seq):
+                own = pl.ds(pl.multiple_of((me ^ k) * width, width), width)
+                mid = mid + dot(att_buf[slot, k, at], wo_ref[own])
+            rho = lax.rsqrt(jnp.mean(mid * mid, axis=-1, keepdims=True) + EPSILON)
+            normed = (mid * rho * gain).astype(bf16)
+            nm[here] = normed
+            if j == 0:
+                mid_ref[at] = mid
+            for c in range(0, share, 256):
+                cols = slice(c, c + 256)
+                value, slope = gelu_parts(dot(normed, wu_ref[:, cols]))
+                hid[here, cols] = value.astype(bf16)
+                dpre[here, cols] = (dot_t(masked, wd_ref[cols]) * slope).astype(bf16)
+            part = dot_t(dpre[here], wu_ref[...])
+            if j % 2:
+                low[j, at] = part.astype(bf16)
+            else:
+                acc[at] = part
+
+        if j % 2:
+            dn_copy(1, j ^ 1).start()
+        elif j:
+            for bit in bits:
+                if j & bit:
+                    low[j] = acc[...].astype(bf16)
+                    dn_copy(bit, j ^ bit).start()
+                    break
+                dn_copy(bit, j).wait_recv()
+                acc[...] += into[slots[bit, j]].astype(f32)
+
+    for c in range(0, dim, 256):
+        ug_ref[c : c + 256] = t_dot(nm[:, c : c + 256], dpre[...]).astype(bf16)
+
+    for bit in bits:
+        dn_copy(bit, 0).wait_recv()
+    step = 128
+    part = jnp.zeros((8, dim), f32)
+    for r in range(0, rows, step):
+        at = slice(r, r + step)
+        dn = acc[at]
+        for bit in bits:
+            dn = dn + into[slots[bit, 0], at].astype(f32)
+        mid = mid_ref[at]
+        rho = lax.rsqrt(jnp.mean(mid * mid, axis=-1, keepdims=True) + EPSILON)
+        scaled = gain * dn
+        mean = jnp.mean(mid * scaled, axis=-1, keepdims=True)
+        dmid = gm[at].astype(f32) + rho * scaled - mid * (rho * rho * rho * mean)
+        dmid_ref[at] = dmid
+        dbv[at] = dmid.astype(bf16)
+        prod = dn * mid * rho
+        part += functools.reduce(jnp.add, [prod[i : i + 8] for i in range(0, step, 8)])
+    gsum_ref[...] = part
+
+    def db_copy(source, target, bit):
+        return pltpu.make_async_remote_copy(
+            src_ref=db_ref.at[source] if source else dbv,
+            dst_ref=db_ref.at[target],
+            send_sem=db_send.at[target],
+            recv_sem=db_recv.at[target],
+            device_id={"seq": me ^ bit},
+            device_id_type=MESH,
+        )
+
+    own_copy = pltpu.make_async_copy(dbv, db_ref.at[0], own_sem)
+    own_copy.start()
+    sends = []
+    high = [bit for bit in reversed(bits) if bit > 1]
+
+    def send(source, target, bit):
+        sends.append(db_copy(source, target, bit))
+        sends[-1].start()
+
+    if high:
+        send(0, high[0], high[0])
+    if seq > 1:
+        send(0, 1, 1)
+    for c in range(0, share, 256):
+        dg_ref[c : c + 256] = t_dot(hid[:, c : c + 256], gm[...]).astype(bf16)
+    mo_copies = []
+    for j in range(seq):
+        at = slice(j * rows, (j + 1) * rows)
+        nm[at] = dot(hid[at], wd_ref[...]).astype(bf16)
+        mo_copies.append(pltpu.make_async_copy(nm.at[pl.ds(j * rows, rows)], mo_ref.at[j], mo_sem.at[j]))
+        mo_copies[-1].start()
+    have = [0]
+    for n, bit in enumerate(high):
+        if n:
+            for j in have:
+                send(j, j ^ bit, bit)
+        for j in have:
+            db_copy(0, j ^ bit, bit).wait_recv()
+            send(j ^ bit, j ^ bit ^ 1, 1)
+        have += [j ^ bit for j in have]
+    if seq > 1:
+        for j in have:
+            db_copy(0, j ^ 1, 1).wait_recv()
+    for c in sends:
+        c.wait_send()
+    own_copy.wait()
+    for c in mo_copies:
+        c.wait()
+    for bit in bits:
+        for j in range(0, seq, 2 * bit):
+            dn_copy(bit, j).wait_send()
+
+
+def mlp(length, atts, tok, grads, wo, wu, wd, gain):
+    seq, rows, dim = tok.shape
+    share = wu.shape[1]
+    sub = 256
+    depth = 2 if seq <= 4 else 1
+    anywhere = pl.BlockSpec(memory_space=pl.ANY)
+    vmem = pl.BlockSpec(memory_space=pltpu.VMEM)
+    dma = pltpu.SemaphoreType.DMA
+    return pl.pallas_call(
+        functools.partial(mlp_kernel, seq, sub),
+        out_shape=(
+            jax.ShapeDtypeStruct((rows, dim), f32),
+            jax.ShapeDtypeStruct((rows, dim), f32),
+            jax.ShapeDtypeStruct((8, dim), f32),
+            jax.ShapeDtypeStruct((seq, rows, dim), bf16),
+            jax.ShapeDtypeStruct((seq, rows, dim), bf16),
+            jax.ShapeDtypeStruct((dim, share), bf16),
+            jax.ShapeDtypeStruct((share, dim), bf16),
+        ),
+        in_specs=[pl.BlockSpec(memory_space=pltpu.SMEM)] + [anywhere] * (2 * seq + 1) + [vmem] * 4,
+        out_specs=(vmem, vmem, vmem, anywhere, anywhere, vmem, vmem),
+        scratch_shapes=[
+            pltpu.VMEM((depth, seq, rows, dim // seq), bf16),
+            pltpu.VMEM((depth, rows, dim), bf16),
+            pltpu.VMEM((seq * rows, dim), bf16),
+            pltpu.VMEM((seq * rows, dim), bf16),
+            pltpu.VMEM((seq * rows, share), bf16),
+            pltpu.VMEM((seq * rows, share), bf16),
+            pltpu.VMEM((seq, rows, dim), bf16),
+            pltpu.VMEM((max(seq - 1, 1), rows, dim), bf16),
+            pltpu.VMEM((rows, dim), f32),
+            dma((2, seq + 1)),
+            dma((seq,)),
+            dma((seq,)),
+            dma((seq,)),
+            dma((seq,)),
+            dma((seq,)),
+            dma((seq,)),
+            dma,
+        ],
+        compiler_params=pltpu.CompilerParams(collective_id=2, has_side_effects=True, vmem_limit_bytes=60 << 20),
+        cost_estimate=pl.CostEstimate(
+            flops=2 * rows * seq * dim * (dim + 6 * share), bytes_accessed=32 << 20, transcendentals=rows * seq * share
+        ),
+        name="mlp",
+    )(length, *atts, tok, *grads, wo, wu, wd, gain)
+
+
 def swap(value, bit):
     count = lax.axis_size("seq")
     return lax.ppermute(value, "seq", [(i, i ^ bit) for i in range(count)])
@@ -1022,10 +1299,9 @@
     moved = jnp.concatenate(moved, axis=0)
     moved = [lax.dynamic_slice_in_dim(moved, seq_at ^ k, 1, axis=0) for k in range(seq_count)]
     down_w = jnp.swapaxes(jnp.concatenate(moved, axis=0), 0, 1).reshape(fsdp_count * share, dim)
-    all_grad = jnp.concatenate(seq_gather(out_grad[0]), axis=0)
-
-    bias = tile_bias(rel_bias)
-    bias_t = jnp.swapaxes(bias, 1, 2)
+    all_grad = seq_gather(out_grad[0])
+
+    bias = bias_vector(rel_bias)
     forget = jax.nn.sigmoid(gate_bias)
     forget_row = forget.reshape(1, width)
     chunk_ids = jnp.arange(seq_count, dtype=jnp.int32)
@@ -1038,54 +1314,27 @@
         qkv, state_init[0], lengths, state_query, forget_row, bias, heads, order
     )
 
-    from_heads = seq_gather(attended)
-    columns = []
-    for k in range(seq_count):
-        blocks = from_heads[k].reshape(seq_count, tok_rows, width)
-        columns.append(jnp.concatenate([blocks[j ^ k] for j in range(seq_count)], axis=0))
-    all_attended = jnp.concatenate(columns, axis=1)
-    out_w = out_w.reshape(seq_count, width, dim)
-    own_out = lax.dynamic_slice_in_dim(out_w, seq_at, 1, axis=0)[0]
-    out_w = jnp.concatenate(
-        [lax.dynamic_slice_in_dim(out_w, seq_at ^ k, 1, axis=0)[0] for k in range(seq_count)], axis=0
+    out_w = out_w.reshape(dim, dim)
+    own_out = lax.dynamic_slice_in_dim(out_w, seq_at * width, width, axis=0)
+    mid_here, dmid, mlp_gain_grad, dbranch, mlp_parts, up_grad, down_grad = mlp(
+        lengths, seq_gather(attended), all_tokens, all_grad, out_w, up_w, down_w, gain_mlp.reshape(1, dim)
     )
-    mid = inputs + dot(all_attended, out_w)
-    rho_mid = inverse_rms(mid)
-    normed_mid = (mid * rho_mid * gain_mlp).astype(bf16)
-    positions = (order[:, None] * tok_rows + jnp.arange(tok_rows, dtype=jnp.int32)).reshape(rows)
-    live = (positions < lengths[0]).astype(bf16)[:, None]
-    grad_low = all_grad * live
-    pre = dot(normed_mid, up_w)
-    hidden, gelu_pull = jax.vjp(lambda v: jax.nn.gelu(v, approximate=False), pre)
-    hidden = hidden.astype(bf16)
-    dpre = gelu_pull(dot_t(grad_low, down_w))[0].astype(bf16)
-
-    def chunk(value, j):
-        return value[j * tok_rows : (j + 1) * tok_rows]
-
-    dnormed_mid = seq_reduce([dot_t(chunk(dpre, j), up_w) for j in range(seq_count)])
-    down_grad = t_dot(hidden, grad_low)
-    up_grad = t_dot(normed_mid, dpre)
-    mlp_out = seq_reduce([dot(chunk(hidden, j), down_w) for j in range(seq_count)])
-
-    mid_here = chunk(mid, 0)
-    live_here = chunk(live, 0).astype(f32)
-    output = (live_here * (mid_here + mlp_out)).astype(bf16)[None]
-    grad_here = out_grad[0].astype(f32) * live_here
-    through, mlp_gain_grad = norm_back(mid_here, gain_mlp, inverse_rms(mid_here), dnormed_mid)
-    dmid = grad_here + through
-    dbranch = jnp.concatenate(seq_gather(dmid.astype(bf16)), axis=0)
+    dbranch = dbranch.reshape(rows, dim)
     dattended = dot_t(dbranch, own_out).astype(bf16)
     out_w_grad = t_dot(attended, dbranch)
 
     dqkv, dquery, dforget, near, far = attend_back(
-        qkv, dattended, attended, mem, upd, lse, slse, state_grad[0], lengths, state_query, forget_row, bias_t, heads, order
+        qkv, dattended, attended, mem, upd, lse, slse, state_grad[0], lengths, state_query, forget_row, bias, heads, order
     )
+    mlp_parts, dqkv = lax.optimization_barrier((mlp_parts, dqkv))
+    mlp_out = seq_reduce([mlp_parts[j] for j in range(seq_count)])
+    live_here = (seq_at * tok_rows + jnp.arange(tok_rows, dtype=jnp.int32) < lengths[0]).astype(f32)[:, None]
+    output = (live_here * (mid_here + mlp_out)).astype(bf16)[None]
     dnormed = dot_t(dqkv, qkv_w).astype(bf16).reshape(seq_count, tok_rows, dim)
     piece = dim // (seq_count * fsdp_count)
     qkv_grad = t_dot(normed, dqkv).astype(bf16).reshape(seq_count, fsdp_count, piece, 3 * width)
-    up_grad = up_grad.astype(bf16).reshape(seq_count, fsdp_count, piece, hidden_all // seq_count)
-    down_grad = down_grad.astype(bf16).reshape(fsdp_count, share, dim)
+    up_grad = up_grad.reshape(seq_count, fsdp_count, piece, hidden_all // seq_count)
+    down_grad = down_grad.reshape(fsdp_count, share, dim)
     out_w_grad = out_w_grad.astype(bf16).reshape(fsdp_count, piece, dim)
     grad_gate = dforget.reshape(heads, DH) * forget * (1.0 - forget)
     grad_table = jnp.pad(bias_table_grad(near, far), ((0, 0), (0, DH - BUCKETS)))

time: 594 us -> 485 us (0.82)
  matrix products: 106 us -> 23.4 us
  Pallas kernels: 241 us -> 316 us
  local copies, waits for them, and re-layouts: 111 us -> 63.4 us
  waiting for transfers between devices: 55.1 us -> 26.5 us
  other arithmetic: 50.3 us -> 28.9 us
    pallas_call x0 -> x1, Pallas kernels: none -> 76.4 us  [mlp(): pl.pallas_call(functools.partial(mlp_kernel, seq, sub), out_shape=(jax.Sh...]
    eq x32 -> x0, local copies, waits for them, and re-layouts: 50.2 us -> none  [tile_bias(): bucket == bucket_id]
    dot_general x7 -> x1, matrix products: 47.9 us -> 3.62 us  [dot(): return jnp.dot(a, b, preferred_element_type=f32)]
    ppermute x18 -> x12, waiting for transfers between devices: 55.1 us -> 26.5 us  [swap(): return lax.ppermute(value, 'seq', [(i, i ^ bit) for i in range(count)])]
    dot_general x7 -> x2, matrix products: 36.3 us -> 10.4 us  [dot_t(): lax.dot_general(a, b, (((1,), (1,)), ((), ())), preferred_element_type=f32)]
    unnamed x240 -> x214, local copies, waits for them, and re-layouts: 28.4 us -> 44.9 us
    select_n x2 -> x1, other arithmetic: 14 us -> 0.21 us  [bias_vector(): total = jnp.where((bucket == i)[None], table[:, i:i + 1] * LOG2E, total)]
    dot_general x4 -> x2, matrix products: 21.4 us -> 9.33 us  [t_dot(): lax.dot_general(a, b, (((0,), (0,)), ((), ())), preferred_element_type=f32)]
  transfers between devices with their start and end apart: 20 -> 14, of which waited for: 3 -> 3; matrix products, arithmetic and copies ran while one was open for 33% -> 20% of each run, Pallas kernels for 14% -> 41%
where the time goes in v4:
time: 485 us; the launch traced here: 481 us
  Pallas kernels  316 us (65%)
  local copies, waits for them, and re-layouts  63.4 us (13%)
  other arithmetic  28.9 us (6%)
  waiting for transfers between devices  26.5 us (5%)
  matrix products  23.4 us (5%)
  between operations  16.1 us (3%)
  starting transfers between devices  6.48 us (1%)
    pallas_call x1, Pallas kernels, finish(): pl.pallas_call(functools.partial(finish_kernel, seq, hi, lo, chunks), out...  115 us
    pallas_call x1, Pallas kernels, mlp(): pl.pallas_call(functools.partial(mlp_kernel, seq, sub), out_shape=(jax.Sh...  76.4 us
    pallas_call x1, Pallas kernels, gather_start(): pl.pallas_call(functools.partial(gather_kernel, seq, hi, lo), out_shape=(...  62.9 us
    unnamed x214, local copies, waits for them, and re-layouts  44.9 us
    pallas_call x1, Pallas kernels, attend_back(): pl.pallas_call(functools.partial(attend_back_kernel, heads, blocks), out_...  40.5 us
    ppermute x12, waiting for transfers between devices, swap(): return lax.ppermute(value, 'seq', [(i, i ^ bit) for i in range(count)])  26.5 us
    pallas_call x1, Pallas kernels, attend(): pl.pallas_call(functools.partial(attend_kernel, heads), out_shape=(jax.Sh...  20.9 us
    dot_general x2, matrix products, dot_t(): lax.dot_general(a, b, (((1,), (1,)), ((), ())), preferred_element_type=f32)  10.4 us
  transfers between devices with their start and end apart: 14, of which 3 were waited for; matrix products, arithmetic and copies ran while one was open for 20% of the time, Pallas kernels for 41%

profile of v4, /device:TPU:0, one launch (start us, length us, event | category | flops | bytes accessed | tf_op | source)
XLA Modules:
  0.0 480.8 jit_solution(9725404405497073103)
XLA Ops:
  7.3 1.1 copy-done
  8.4 0.7 constant_dynamic-slice_fusion.5
  9.2 1.7 constant_dynamic-slice_fusion.6
  10.9 1.9 multiply_reduce_fusion.1
  12.8 1.6 multiply_reduce_fusion.32
  14.8 0.8 copy.105.w_ref
  16.1 62.9 %gather_start.1 = (bf16[4,512,1024]{2,1,0:T(8,128)(2,1)}, bf16[8,128,768]{2,1,0:T(8,128)(2,1)}, bf16[8,2,128]{2,1,0:T(2,128)(2,1)}, bf16[8,128,1024]{2,1,0:T(8,128)(2,1)}) custom-call(bf16[512,1024]{1,0:T(8,128)(2,1)} %bitcast.122, bf16[128,768]{1,0:T(8,128)(2,1)} %copy.105.w_ref, bf16[2,128]{1,0:T(2,128)(2,1)} %pad_maximum_fusion.2.gain_ref, ...), custom_call_target="tpu_custom_call" | custom-call | tf_op jit(solution)/shard_map/gather_start/pallas_call | solution.py:524
  79.0 3.2 multiply_reduce_fusion
  83.3 1.4 multiply_convert_fusion
  86.0 3.6 convolution_convert_fusion.1.cur_ref.prev_ref
  89.6 20.9 %attend.1 = (bf16[2048,256]{1,0:T(8,128)(2,1)S(1)}, f32[512,256]{1,0:T(8,128)}, f32[4,512,256]{2,1,0:T(8,128)S(1)}, f32[4,512,256]{2,1,0:T(8,128)S(1)}, f32[2,2048]{1,0:T(2,128)S(1)}, /*index=5*/f32[2,2048]{1,0:T(2,128)S(1)}) custom-call(s32[1]{0:T(128)} %copy.185.length_ref, s32[4]{0:T(128)S(1)} %iota_xor_fusion.order_ref, ...), custom_call_target="tpu_custom_call" | custom-call | flops 5033164800 | bytes 16777216 | tf_op jit(solution)/shard_map/attend/pallas_call | solution.py:171
  110.6 1.3 copy-done.11
  111.9 1.3 copy-done.13
  113.2 1.5 collective-permute-start.1
  115.2 2.8 dynamic-slice_bitcast_fusion.3
  118.1 1.5 collective-permute-start.7
  120.0 1.0 copy.170
  120.9 1.6 copy.171
  122.5 1.6 copy.172
  124.1 1.6 copy.173
  126.4 0.7 copy.175
  127.8 1.6 copy.177
  129.3 1.6 copy.178
  130.9 1.6 copy.179
  132.4 1.6 copy.180
  134.0 1.6 copy.181
  135.6 1.5 copy.182
  137.1 1.6 copy.183
  138.7 1.6 copy.184
  140.2 1.6 copy.153
  141.8 1.6 copy.154
  143.3 1.6 copy.155
  144.9 1.5 copy.156
  146.4 0.7 copy.157
  147.1 0.7 copy.158
  151.8 0.7 copy.165
  152.5 0.7 copy.166
  153.5 8.3 %collective-permute-done.4.refs_7_ = bf16[512,1024]{1,0:T(8,128)(2,1)} collective-permute-done((bf16[512,1024]{1,0:T(8,128)(2,1)}, bf16[512,1024]{1,0:T(8,128)(2,1)}, u32[]{:S(2)}, u32[]{:S(2)}) %collective-permute-start.4) | collective-permute-done | bytes 1048608 | tf_op jit(solution)/shard_map/ppermute | solution.py:1205
  162.4 8.0 %collective-permute-done.7 = bf16[1,2,128,1024]{3,2,0,1:T(8,128)(2,1)} collective-permute-done((bf16[1,2,128,1024]{3,2,0,1:T(8,128)(2,1)}, bf16[1,2,128,1024]{3,2,0,1:T(8,128)(2,1)}, u32[]{:S(2)}, u32[]{:S(2)}) %collective-permute-start.7) | collective-permute-done | bytes 524320 | tf_op jit(solution)/shard_map/ppermute | solution.py:1205
  170.4 4.1 fusion.1
  174.5 10.1 %collective-permute-done.8 = bf16[1,2,128,1024]{3,2,0,1:T(8,128)(2,1)S(1)} collective-permute-done((bf16[1,2,128,1024]{3,2,0,1:T(8,128)(2,1)S(1)}, bf16[1,2,128,1024]{3,2,0,1:T(8,128)(2,1)S(1)}, u32[]{:S(2)}, u32[]{:S(2)}) %collective-permute-start.8) | collective-permute-done | bytes 524320 | tf_op jit(solution)/shard_map/ppermute | solution.py:1205
  184.6 1.3 pad_maximum_fusion
  186.1 1.6 pad_maximum_fusion.1
  187.7 76.4 %mlp.1 = (f32[512,1024]{1,0:T(8,128)}, f32[512,1024]{1,0:T(8,128)}, f32[8,1024]{1,0:T(8,128)}, bf16[4,512,1024]{2,1,0:T(8,128)(2,1)}, bf16[4,512,1024]{2,1,0:T(8...) custom-call(s32[1]{0:T(128)} %copy.185.length_ref, bf16[2048,256]{1,0:T(8,128)(2,1)} %copy-done.2, ...), custom_call_target="tpu_custom_call" | custom-call | flops 30064771072 | bytes 33554432 | tf_op jit(solution)/shard_map/mlp/pallas_call | solution.py:1163
  264.2 4.6 convolution_convert_fusion.4
  268.8 2.5 convolution_convert_fusion.2.dout_ref
  272.2 40.5 %attend_back.1 = (bf16[2048,768]{1,0:T(8,128)(2,1)S(1)}, f32[2,128,128]{2,1,0:T(8,128)S(1)}, f32[1,256]{1,0:T(1,128)S(1)}, f32[2,384,256]{2,1,0:T(8,128)S(1)}, f32[2,8,256]{2,1,0:T(8,128)S(1)}) custom-call(s32[1]{0:T(128)} %copy.185.length_ref, s32[4]{0:T(128)S(1)} %iota_xor_fusion.order_ref, bf16[2048,768]{1,0:T(8,128)(2,1)S(1)} %copy-done.10, ...), custom_call_target="tpu_custom_call" | custom-call | flops 12582912000 | bytes 20971520 | tf_op jit(solution)/shard_map/attend_back/pallas_call | solution.py:357
  312.8 1.6 slice_bitcast_fusion.1
  315.6 3.2 select_reduce_fusion.18
  319.0 3.3 select_reduce_fusion
  325.6 8.0 %convolution_convert_fusion = bf16[2048,1024]{1,0:T(8,128)(2,1)} fusion(bf16[2048,768]{1,0:T(8,128)(2,1)} %copy-done.7, bf16[1024,768]{1,0:T(8,128)(2,1)} %bitcast.174), kind=kOutput, calls=%fused_computation.5 | convolution fusion | flops 3223322624 | bytes 8912896 | tf_op jit(solution)/shard_map/dot_general | solution.py:61
  333.5 2.8 fusion.2
  336.4 1.2 collective-permute-start.11
  338.3 4.7 convolution_convert_fusion.3
  343.0 115.2 %finish.1 = (f32[512,1024]{1,0:T(8,128)}, f32[4,32,768]{2,1,0:T(8,128)}, f32[4,32,1024]{2,1,0:T(8,128)}, f32[128,1024]{1,0:T(8,128)}, f32[32,1024]{1,0:T(8,128)}...) custom-call(bf16[4,512,1024]{2,1,0:T(8,128)(2,1)} %bitcast.121, bf16[4,8,32,768]{3,2,1,0:T(8,128)(2,1)} %bitcast.131, ...), custom_call_target="tpu_custom_call" | custom-call | tf_op jit(solution)/shard_map/finish/pallas_call | solution.py:915
  458.2 1.6 slice.180
  459.8 1.2 slice.179
  461.1 1.2 slice.181
  462.3 1.3 reshape.225
  463.9 0.9 reshape.226
  464.9 1.9 copy.148
  467.5 3.5 fusion.7
  471.0 1.3 copy.186
  472.9 0.8 copy.188
  (263 shorter events, 17.2 us)
Async XLA Ops:
  7.2 7.2 %copy-start.20 = (bf16[128,3072]{1,0:T(8,128)(2,1)S(1)}, bf16[128,3072]{1,0:T(8,128)(2,1)}, u32[]{:S(2)}) copy-start(bf16[128,3072]{1,0:T(8,128)(2,1)} %param.19) | copy-start | bytes 2359300
  7.2 8.4 %copy-start.86 = (bf16[128]{0:T(256)(128)(2,1)S(1)}, bf16[128]{0:T(256)(128)(2,1)}, u32[]{:S(2)}) copy-start(bf16[128]{0:T(256)(128)(2,1)} %param.23) | copy-start | bytes 772
  7.2 8.4 %copy-start.85 = (bf16[128]{0:T(256)(128)(2,1)S(1)}, bf16[128]{0:T(256)(128)(2,1)}, u32[]{:S(2)}) copy-start(bf16[128]{0:T(256)(128)(2,1)} %param.24) | copy-start | bytes 772
  7.2 108.0 %all-gather.5.cloned.1.call-start = ((), (), s32[]{:S(2)}) async-start(), calls=%async_computation.1 | async-start | bytes 2359296 | tf_op jit(solution)/shard_map/all_gather | solution.py:1286
  9.2 178.6 %all-gather.3.cloned.1.call-start = ((), (), s32[]{:S(2)}) async-start(), calls=%async_computation | async-start | bytes 2359296 | tf_op jit(solution)/shard_map/all_gather | solution.py:1287
  79.0 3.3 copy-start.50
  79.0 3.9 copy-start.15
  83.3 2.7 copy-start.84
  86.0 3.7 copy-start.4
  86.0 3.7 copy-start.6
  89.6 21.0 %copy-start.9 = (bf16[2048,768]{1,0:T(8,128)(2,1)}, bf16[2048,768]{1,0:T(8,128)(2,1)S(1)}, u32[]{:S(2)}) copy-start(bf16[2048,768]{1,0:T(8,128)(2,1)S(1)} %convolution_convert_fusion.1.cur_ref.prev_ref) | copy-start | bytes 9437188
  113.2 6.4 %copy-start.2 = (bf16[2048,256]{1,0:T(8,128)(2,1)}, bf16[2048,256]{1,0:T(8,128)(2,1)S(1)}, u32[]{:S(2)}) copy-start(bf16[2048,256]{1,0:T(8,128)(2,1)S(1)} %get-tuple-element.46.refs_0_.out_ref) | copy-start | bytes 3145732
  113.2 40.0 %collective-permute-start.1 = (bf16[2048,256]{1,0:T(8,128)(2,1)S(1)}, bf16[2048,256]{1,0:T(8,128)(2,1)}, u32[]{:S(2)}, u32[]{:S(2)}) collective-permute-start(bf16[2048,256]{1,0:T(8,128)(2,1)S(1)} %get-tuple-element.46.refs_0_.out_ref), channel_id=1, source_target_pairs={{0,16},{8,24},{16,0},{24,8},{1,17},{9,25},{17,1},{25,9},{2,18},{10... | collective-permute-start | bytes 3145736 | tf_op jit(solution)/shard_map/ppermute | solution.py:1205
  114.6 47.2 %collective-permute-start.4 = (bf16[512,1024]{1,0:T(8,128)(2,1)}, bf16[512,1024]{1,0:T(8,128)(2,1)}, u32[]{:S(2)}, u32[]{:S(2)}) collective-permute-start(bf16[512,1024]{1,0:T(8,128)(2,1)} %bitcast.12.refs_5_), channel_id=1, source_target_pairs={{0,16},{8,24},{16,0},{24,8},{1,17},{9,25},{17,1},{25,9},{2,18},{10... | collective-permute-start | bytes 3145736 | tf_op jit(solution)/shard_map/ppermute | solution.py:1205
  115.2 4.6 copy-start.48
  115.2 4.6 copy-start.47
  115.2 4.7 copy-start.46
  115.2 10.5 %copy-start.45 = (pred[384,256]{1,0:T(32,128)(4,1)S(1)}, pred[384,256]{1,0:T(32,128)(4,1)}, u32[]{:S(2)}) copy-start(pred[384,256]{1,0:T(32,128)(4,1)} %constant.210) | copy-start | bytes 294916
  115.2 11.2 %copy-start.44 = (pred[384,256]{1,0:T(32,128)(4,1)S(1)}, pred[384,256]{1,0:T(32,128)(4,1)}, u32[]{:S(2)}) copy-start(pred[384,256]{1,0:T(32,128)(4,1)} %constant.209) | copy-start | bytes 294916
  115.2 11.8 %copy-start.43 = (pred[384,256]{1,0:T(32,128)(4,1)S(1)}, pred[384,256]{1,0:T(32,128)(4,1)}, u32[]{:S(2)}) copy-start(pred[384,256]{1,0:T(32,128)(4,1)} %constant.208) | copy-start | bytes 294916
  118.1 43.8 %collective-permute-start.6 = (bf16[1,2,128,1024]{3,2,0,1:T(8,128)(2,1)}, bf16[1,2,128,1024]{3,2,0,1:T(8,128)(2,1)S(1)}, u32[]{:S(2)}, u32[]{:S(2)}) collective-permute-start(bf16[1,2,128,1024]{3,2,0,1:T(8,128)(2,1)} %get-tuple-element.146), channel_id=1, source_target_pairs={{0,8},{8,0},{16,24},{24,16},{1,9},{9,1},{17,25},{25,17},{2,10},{10... | collective-permute-start | bytes 1572872 | tf_op jit(solution)/shard_map/ppermute | solution.py:1205
  118.1 52.3 %collective-permute-start.7 = (bf16[1,2,128,1024]{3,2,0,1:T(8,128)(2,1)}, bf16[1,2,128,1024]{3,2,0,1:T(8,128)(2,1)}, u32[]{:S(2)}, u32[]{:S(2)}) collective-permute-start(bf16[1,2,128,1024]{3,2,0,1:T(8,128)(2,1)} %get-tuple-element.145), channel_id=1, source_target_pairs={{0,16},{8,24},{16,0},{24,8},{1,17},{9,25},{17,1},{25,9},{2,18},{10... | collective-permute-start | bytes 1572872 | tf_op jit(solution)/shard_map/ppermute | solution.py:1205
  119.5 68.1 %collective-permute-start = (bf16[2048,256]{1,0:T(8,128)(2,1)S(1)}, bf16[2048,256]{1,0:T(8,128)(2,1)}, u32[]{:S(2)}, u32[]{:S(2)}) collective-permute-start(bf16[2048,256]{1,0:T(8,128)(2,1)S(1)} %get-tuple-element.46.refs_0_.out_ref), channel_id=1, source_target_pairs={{0,8},{8,0},{16,24},{24,16},{1,9},{9,1},{17,25},{25,17},{2,10},{10... | collective-permute-start | bytes 3145736 | tf_op jit(solution)/shard_map/ppermute | solution.py:1205
  119.8 26.6 %copy-start.42 = (pred[384,256]{1,0:T(32,128)(4,1)S(1)}, pred[384,256]{1,0:T(32,128)(4,1)}, u32[]{:S(2)}) copy-start(pred[384,256]{1,0:T(32,128)(4,1)} %constant.195) | copy-start | bytes 294916
  119.9 27.2 %copy-start.41 = (pred[384,256]{1,0:T(32,128)(4,1)S(1)}, pred[384,256]{1,0:T(32,128)(4,1)}, u32[]{:S(2)}) copy-start(pred[384,256]{1,0:T(32,128)(4,1)} %constant.194) | copy-start | bytes 294916
  119.9 27.9 %copy-start.40 = (pred[384,256]{1,0:T(32,128)(4,1)S(1)}, pred[384,256]{1,0:T(32,128)(4,1)}, u32[]{:S(2)}) copy-start(pred[384,256]{1,0:T(32,128)(4,1)} %constant.193) | copy-start | bytes 294916
  120.9 27.5 %copy-start.39 = (pred[384,256]{1,0:T(32,128)(4,1)S(1)}, pred[384,256]{1,0:T(32,128)(4,1)}, u32[]{:S(2)}) copy-start(pred[384,256]{1,0:T(32,128)(4,1)} %constant.192) | copy-start | bytes 294916
  122.5 26.6 %copy-start.38 = (pred[384,256]{1,0:T(32,128)(4,1)S(1)}, pred[384,256]{1,0:T(32,128)(4,1)}, u32[]{:S(2)}) copy-start(pred[384,256]{1,0:T(32,128)(4,1)} %constant.191) | copy-start | bytes 294916
  124.1 25.7 %copy-start.37 = (pred[384,256]{1,0:T(32,128)(4,1)S(1)}, pred[384,256]{1,0:T(32,128)(4,1)}, u32[]{:S(2)}) copy-start(pred[384,256]{1,0:T(32,128)(4,1)} %constant.190) | copy-start | bytes 294916
  125.7 24.8 %copy-start.36 = (pred[384,256]{1,0:T(32,128)(4,1)S(1)}, pred[384,256]{1,0:T(32,128)(4,1)}, u32[]{:S(2)}) copy-start(pred[384,256]{1,0:T(32,128)(4,1)} %constant.189) | copy-start | bytes 294916
  126.4 24.7 %copy-start.35 = (pred[384,256]{1,0:T(32,128)(4,1)S(1)}, pred[384,256]{1,0:T(32,128)(4,1)}, u32[]{:S(2)}) copy-start(pred[384,256]{1,0:T(32,128)(4,1)} %constant.188) | copy-start | bytes 294916
  127.1 24.7 %copy-start.34 = (pred[384,256]{1,0:T(32,128)(4,1)S(1)}, pred[384,256]{1,0:T(32,128)(4,1)}, u32[]{:S(2)}) copy-start(pred[384,256]{1,0:T(32,128)(4,1)} %constant.187) | copy-start | bytes 294916
  127.8 24.7 %copy-start.33 = (pred[384,256]{1,0:T(32,128)(4,1)S(1)}, pred[384,256]{1,0:T(32,128)(4,1)}, u32[]{:S(2)}) copy-start(pred[384,256]{1,0:T(32,128)(4,1)} %constant.186) | copy-start | bytes 294916
  153.2 34.5 %collective-permute-start.3 = (bf16[512,1024]{1,0:T(8,128)(2,1)}, bf16[512,1024]{1,0:T(8,128)(2,1)}, u32[]{:S(2)}, u32[]{:S(2)}) collective-permute-start(bf16[512,1024]{1,0:T(8,128)(2,1)} %bitcast.12.refs_5_), channel_id=1, source_target_pairs={{0,8},{8,0},{16,24},{24,16},{1,9},{9,1},{17,25},{25,17},{2,10},{10... | collective-permute-start | bytes 3145736 | tf_op jit(solution)/shard_map/ppermute | solution.py:1205
  161.8 25.8 %collective-permute-start.2 = (bf16[2048,256]{1,0:T(8,128)(2,1)}, bf16[2048,256]{1,0:T(8,128)(2,1)}, u32[]{:S(2)}, u32[]{:S(2)}) collective-permute-start(bf16[2048,256]{1,0:T(8,128)(2,1)} %collective-permute-done.1.refs_2_), channel_id=1, source_target_pairs={{0,8},{8,0},{16,24},{24,16},{1,9},{9,1},{17,25},{25,17},{2,10},{10... | collective-permute-start | bytes 3145736 | tf_op jit(solution)/shard_map/ppermute | solution.py:1205
  161.9 25.8 %collective-permute-start.5 = (bf16[512,1024]{1,0:T(8,128)(2,1)}, bf16[512,1024]{1,0:T(8,128)(2,1)}, u32[]{:S(2)}, u32[]{:S(2)}) collective-permute-start(bf16[512,1024]{1,0:T(8,128)(2,1)} %collective-permute-done.4.refs_7_), channel_id=1, source_target_pairs={{0,8},{8,0},{16,24},{24,16},{1,9},{9,1},{17,25},{25,17},{2,10},{10... | collective-permute-start | bytes 3145736 | tf_op jit(solution)/shard_map/ppermute | solution.py:1205
  170.4 14.2 %collective-permute-start.8 = (bf16[1,2,128,1024]{3,2,0,1:T(8,128)(2,1)S(1)}, bf16[1,2,128,1024]{3,2,0,1:T(8,128)(2,1)S(1)}, u32[]{:S(2)}, u32[]{:S(2)}) collective-permute-start(bf16[1,2,128,1024]{3,2,0,1:T(8,128)(2,1)S(1)} %get-tuple-element.147), channel_id=1, source_target_pairs={{0,24},{8,16},{16,8},{24,0},{1,25},{9,17},{17,9},{25,1},{2,26},{10... | collective-permute-start | bytes 1572872 | tf_op jit(solution)/shard_map/ppermute | solution.py:1205
  187.7 76.4 %copy-start.3 = (bf16[2048,256]{1,0:T(8,128)(2,1)S(1)}, bf16[2048,256]{1,0:T(8,128)(2,1)}, u32[]{:S(2)}) copy-start(bf16[2048,256]{1,0:T(8,128)(2,1)} %copy-done.2) | copy-start | bytes 3145732
  264.1 4.7 copy-start.87
  268.8 2.5 copy-start.5
  268.8 2.5 copy-start.10
  268.8 2.8 copy-start.12
  268.8 3.4 copy-start.14
  272.2 40.6 %copy-start.16 = (bf16[4,512,1024]{2,1,0:T(8,128)(2,1)S(1)}, bf16[4,512,1024]{2,1,0:T(8,128)(2,1)}, u32[]{:S(2)}) copy-start(bf16[4,512,1024]{2,1,0:T(8,128)(2,1)} %get-tuple-element.56) | copy-start | bytes 12582916
  312.8 2.3 copy-start.7
  315.0 3.9 copy-start.22
  315.0 3.9 copy-start.23
  315.0 3.9 copy-start.24
  315.0 3.9 copy-start.25
  315.0 3.9 copy-start.26
  315.0 3.9 copy-start.27
  315.1 3.9 copy-start.28
  315.1 3.9 copy-start.29
  315.1 3.9 copy-start.30
  315.1 3.9 copy-start.31
  315.1 18.4 %collective-permute-start.10 = (bf16[512,1024]{1,0:T(8,128)(2,1)}, bf16[512,1024]{1,0:T(8,128)(2,1)S(1)}, u32[]{:S(2)}, u32[]{:S(2)}) collective-permute-start(bf16[512,1024]{1,0:T(8,128)(2,1)} %get-tuple-element.139), channel_id=1, source_target_pairs={{0,8},{8,0},{16,24},{24,16},{1,9},{9,1},{17,25},{25,17},{2,10},{10... | collective-permute-start | bytes 3145736 | tf_op jit(solution)/shard_map/ppermute | solution.py:1205
  325.3 142.2 %collective-permute-start.9 = (bf16[512,1024]{1,0:T(8,128)(2,1)}, bf16[512,1024]{1,0:T(8,128)(2,1)}, u32[]{:S(2)}, u32[]{:S(2)}) collective-permute-start(bf16[512,1024]{1,0:T(8,128)(2,1)} %get-tuple-element.138), channel_id=1, source_target_pairs={{0,8},{8,0},{16,24},{24,16},{1,9},{9,1},{17,25},{25,17},{2,10},{10... | collective-permute-start | bytes 3145736 | tf_op jit(solution)/shard_map/ppermute | solution.py:1205
  325.6 12.7 %copy-start.17 = (bf16[2048,1024]{1,0:T(8,128)(2,1)S(1)}, bf16[2048,1024]{1,0:T(8,128)(2,1)}, u32[]{:S(2)}) copy-start(bf16[2048,1024]{1,0:T(8,128)(2,1)} %fusion.1) | copy-start | bytes 12582916
  333.5 4.7 copy-start.8
  336.4 131.1 %collective-permute-start.11 = (bf16[512,1024]{1,0:T(8,128)(2,1)}, bf16[512,1024]{1,0:T(8,128)(2,1)}, u32[]{:S(2)}, u32[]{:S(2)}) collective-permute-start(bf16[512,1024]{1,0:T(8,128)(2,1)} %fusion.2), channel_id=1, source_target_pairs={{0,16},{8,24},{16,0},{24,8},{1,17},{9,25},{17,1},{25,9},{2,18},{10... | collective-permute-start | bytes 3145736 | tf_op jit(solution)/shard_map/ppermute | solution.py:1205
  458.2 8.6 %copy-start.49 = (f32[16,1024]{1,0:T(8,128)S(1)}, f32[16,1024]{1,0:T(8,128)}, u32[]{:S(2)}) copy-start(f32[16,1024]{1,0:T(8,128)} %get-tuple-element.72) | copy-start | bytes 196612
  462.3 5.1 %copy-start.18 = (f32[512,1024]{1,0:T(8,128)S(1)}, f32[512,1024]{1,0:T(8,128)}, u32[]{:S(2)}) copy-start(f32[512,1024]{1,0:T(8,128)} %get-tuple-element.48) | copy-start | bytes 6291460
  467.4 3.5 copy-start.19
  470.9 2.8 copy-start.1
  (38 other events, 67.0 us)
Sparse Core Ops, SparseCore 0:
  10.8 68.2 all-gather.4
  81.7 48.4 all-gather.2

commit v5 on v4

--- a/solution.py
+++ b/solution.py
@@ -86,17 +86,109 @@
     return raised, total, top + jnp.log2(total)
 
 
+def line_gather(hi, lo, slot, count, z_send, z_recv, y_send, y_recv):
+    f = lax.axis_index("fsdp")
+    z, y = f // lo, f % lo
+
+    def copy(i, origin, target, send, recv):
+        ref = slot(i, origin)
+        return pltpu.make_async_remote_copy(
+            src_ref=ref, dst_ref=ref, send_sem=send, recv_sem=recv, device_id={"fsdp": target}, device_id_type=MESH
+        )
+
+    def right(i, t):
+        return copy(i, (z - t) * lo + y, (z + 1) * lo + y, z_send.at[i, 0, t], z_recv.at[i, 0, t])
+
+    def left(i, t):
+        return copy(i, (z + t) * lo + y, (z - 1) * lo + y, z_send.at[i, 1, t], z_recv.at[i, 1, t])
+
+    def across(i, d):
+        return copy(i, (z + d) * lo + y, z * lo + 1 - y, y_send.at[i, d + hi - 1], y_recv.at[i, d + hi - 1])
+
+    def start(i):
+        pl.when(z + 1 < hi)(lambda: right(i, 0).start())
+        pl.when(z >= 1)(lambda: left(i, 0).start())
+        across(i, 0).start()
+
+    def step(i, t):
+        @pl.when(z - 1 - t >= 0)
+        def _():
+            copy(i, (z - 1 - t) * lo + y, f, z_send.at[i, 0, t], z_recv.at[i, 0, t]).wait_recv()
+            if t + 1 < hi - 1:
+                pl.when(z + 1 < hi)(lambda: right(i, t + 1).start())
+            across(i, -1 - t).start()
+
+        @pl.when(z + 1 + t < hi)
+        def _():
+            copy(i, (z + 1 + t) * lo + y, f, z_send.at[i, 1, t], z_recv.at[i, 1, t]).wait_recv()
+            if t + 1 < hi - 1:
+                pl.when(z >= 1)(lambda: left(i, t + 1).start())
+            across(i, 1 + t).start()
+
+    def arrive(i):
+        for d in range(1 - hi, hi):
+
+            @pl.when((z + d >= 0) & (z + d < hi))
+            def _():
+                copy(
+                    i, (z + d) * lo + 1 - y, f, y_send.at[i, d + hi - 1], y_recv.at[i, d + hi - 1]
+                ).wait_recv()
+
+    def drain(i):
+        for d in range(1 - hi, hi):
+
+            @pl.when((z + d >= 0) & (z + d < hi))
+            def _():
+                across(i, d).wait_send()
+
+        for t in range(hi - 1):
+
+            @pl.when((z + 1 < hi) & (z - t >= 0))
+            def _():
+                right(i, t).wait_send()
+
+            @pl.when((z >= 1) & (z + t < hi))
+            def _():
+                left(i, t).wait_send()
+
+    return start, step, arrive, drain
+
+
+def line_sems(count, hi):
+    dma = pltpu.SemaphoreType.DMA
+    return [dma((count, 2, hi)), dma((count, 2, hi)), dma((count, 2 * hi)), dma((count, 2 * hi))]
+
+
+def greet(seq_targets, hi, lo):
+    me = lax.axis_index("seq")
+    f = lax.axis_index("fsdp")
+    z, y = f // lo, f % lo
+    barrier = pltpu.get_barrier_semaphore()
+    for k in seq_targets:
+        pl.semaphore_signal(barrier, inc=1, device_id={"seq": me ^ k}, device_id_type=MESH)
+    near = (lax.rem(z + 1, hi) * lo + y, lax.rem(z + hi - 1, hi) * lo + y, z * lo + 1 - y)
+    for target in near:
+        pl.semaphore_signal(barrier, inc=1, device_id={"fsdp": target}, device_id_type=MESH)
+    pl.semaphore_wait(barrier, len(seq_targets) + len(near))
+
+
 def attend_kernel(
     heads,
+    seq,
+    hi,
+    lo,
     length_ref,
-    order_ref,
-    cur_ref,
-    prev_ref,
+    qkv_ref,
     init_ref,
     query_ref,
     forget_ref,
     vector_ref,
+    own_out_ref,
+    own_down_ref,
     att_ref,
+    others_ref,
+    outs_ref,
+    downs_ref,
     final_ref,
     mem_ref,
     upd_ref,
@@ -104,107 +196,232 @@
     slse_ref,
     memory_ref,
     bias_ref,
+    own_sem,
+    att_send,
+    att_recv,
+    out_send,
+    out_recv,
+    z_send,
+    z_recv,
+    y_send,
+    y_recv,
 ):
-    block = pl.program_id(0)
+    me = lax.axis_index("seq")
+    f = lax.axis_index("fsdp")
     length = length_ref[0]
     width = heads * DH
     scale2 = SCALE * LOG2E
-
-    @pl.when(block == 0)
-    def _():
-        memory_ref[...] = init_ref[...].astype(f32)
+    blocks = seq
+    bits = [1 << i for i in range(seq.bit_length() - 1)]
+    greet(bits, hi, lo)
+
+    own_copies = [
+        pltpu.make_async_copy(own_down_ref, downs_ref.at[f], own_sem.at[0]),
+        pltpu.make_async_copy(own_out_ref, outs_ref.at[:, me], own_sem.at[1]),
+    ]
+    for c in own_copies:
+        c.start()
+
+    def lowest(k):
+        return k & -k
+
+    def out_copy(k):
+        return pltpu.make_async_remote_copy(
+            src_ref=outs_ref.at[:, me ^ k ^ lowest(k)],
+            dst_ref=outs_ref.at[:, me ^ k ^ lowest(k)],
+            send_sem=out_send.at[k],
+            recv_sem=out_recv.at[k],
+            device_id={"seq": me ^ lowest(k)},
+            device_id_type=MESH,
+        )
+
+    def out_arrival(k):
+        return pltpu.make_async_remote_copy(
+            src_ref=outs_ref.at[:, me ^ k],
+            dst_ref=outs_ref.at[:, me ^ k],
+            send_sem=out_send.at[k],
+            recv_sem=out_recv.at[k],
+            device_id={"seq": me},
+            device_id_type=MESH,
+        )
+
+    def att_copy(k, b):
+        bit = lowest(k)
+        came = k ^ bit
+        here = pl.ds(pl.multiple_of((b ^ me) * BLOCK, BLOCK), BLOCK)
+        there = pl.ds(pl.multiple_of((b ^ me ^ bit) * BLOCK, BLOCK), BLOCK)
+        src = others_ref.at[came, here] if came else att_ref.at[here]
+        return pltpu.make_async_remote_copy(
+            src_ref=src,
+            dst_ref=others_ref.at[k, there],
+            send_sem=att_send.at[k, b],
+            recv_sem=att_recv.at[k, b],
+            device_id={"seq": me ^ bit},
+            device_id_type=MESH,
+        )
+
+    def att_arrival(k, b):
+        here = pl.ds(pl.multiple_of((b ^ me) * BLOCK, BLOCK), BLOCK)
+        return pltpu.make_async_remote_copy(
+            src_ref=others_ref.at[k, here],
+            dst_ref=others_ref.at[k, here],
+            send_sem=att_send.at[k, b],
+            recv_sem=att_recv.at[k, b],
+            device_id={"seq": me},
+            device_id_type=MESH,
+        )
+
+    passing = sorted([k for k in range(2, seq, 2)], key=lambda k: (bin(k).count("1"), -k))
+
+    def onward(k, send):
+        for bit in reversed(bits):
+            if bit < lowest(k):
+                send(k | bit)
+
+    start, step, arrive, drain = line_gather(
+        hi, lo, lambda i, origin: downs_ref.at[origin], 1, z_send, z_recv, y_send, y_recv
+    )
+
+    memory_ref[...] = init_ref[...].astype(f32)
+    for head in range(heads):
+        bias_ref[head] = tile_bias(vector_ref, head)
+    for c in own_copies:
+        c.wait()
+    start(0)
+    for bit in reversed(bits):
+        out_copy(bit).start()
+
+    @pl.loop(0, blocks)
+    def _(block):
+        cur_at = pl.multiple_of((block ^ me) * BLOCK, BLOCK)
+        prev_at = pl.multiple_of((jnp.maximum(block - 1, 0) ^ me) * BLOCK, BLOCK)
+        cur_ref = qkv_ref.at[pl.ds(cur_at, BLOCK)]
+        prev_ref = qkv_ref.at[pl.ds(prev_at, BLOCK)]
+        for t in range(min(hi - 1, blocks - 1)):
+            pl.when(block == t + 1)(lambda t=t: step(0, t))
+
+        live_block = block * BLOCK < length
         for head in range(heads):
-            bias_ref[head] = tile_bias(vector_ref, head)
-
-    live_block = block * BLOCK < length
-    for head in range(heads):
-        own = slice(head * DH, (head + 1) * DH)
-        memory = memory_ref[:, own]
-        low = memory.astype(bf16)
-        mem_ref[0, :, own] = memory
-        refs = (prev_ref, cur_ref)
-        key_cols = slice(width + head * DH, width + (head + 1) * DH)
-        value_cols = slice(2 * width + head * DH, 2 * width + (head + 1) * DH)
-        for tile in range(BLOCK // QTILE):
-            rows = slice(tile * QTILE, (tile + 1) * QTILE)
-            query = cur_ref[rows, own]
-            scores, values = [], []
-            for which, lo, hi, col in context_pieces(tile):
-                s = dot_t(query, refs[which][lo:hi, key_cols])
-                position = (block - 1 + which) * BLOCK + lo + lax.broadcasted_iota(jnp.int32, (1, hi - lo), 1)
-                live = (position >= 0) & (position < length)
-                s = s * scale2 + bias_ref[head, :, col : col + hi - lo]
-                scores.append(jnp.where(live, s, -jnp.inf))
-                values.append(refs[which][lo:hi, value_cols])
-            scores.append(dot_t(query, low) * scale2)
-            values.append(low)
-            raised, total, lse = softmax_parts(scores)
-            out = functools.reduce(jnp.add, [dot(e.astype(bf16), v) for e, v in zip(raised, values)])
-            att_ref[rows, own] = (out / total).astype(bf16)
-            lse_ref[head : head + 1, rows] = to_row(lse)
-        own_key = cur_ref[:, key_cols]
-        own_value = cur_ref[:, value_cols]
-        squeries = dot(low, query_ref[head]).astype(bf16)
-        position = block * BLOCK + lax.broadcasted_iota(jnp.int32, (1, BLOCK), 1)
-        for tile in range(STATE_VECTORS // QTILE):
-            rows = slice(tile * QTILE, (tile + 1) * QTILE)
-            squery = squeries[rows]
-            scores = [
-                dot_t(squery, low) * scale2,
-                jnp.where(position < length, dot_t(squery, own_key) * scale2, -jnp.inf),
-            ]
-            raised, total, lse = softmax_parts(scores)
-            update = dot(raised[0].astype(bf16), low) + dot(raised[1].astype(bf16), own_value)
-            update = update / total
-            upd_ref[0, rows, own] = update
-            slse_ref[head : head + 1, rows] = to_row(lse)
-            forget = forget_ref[:, own]
-            old = memory[rows]
-            memory_ref[rows, own] = jnp.where(live_block, forget * old + (1.0 - forget) * update, old)
+            own = slice(head * DH, (head + 1) * DH)
+            memory = memory_ref[:, own]
+            low = memory.astype(bf16)
+            mem_ref[block, :, own] = memory
+            refs = (prev_ref, cur_ref)
+            key_cols = slice(width + head * DH, width + (head + 1) * DH)
+            value_cols = slice(2 * width + head * DH, 2 * width + (head + 1) * DH)
+            for tile in range(BLOCK // QTILE):
+                rows = slice(tile * QTILE, (tile + 1) * QTILE)
+                query = cur_ref[rows, own]
+                scores, values = [], []
+                for which, at, end, col in context_pieces(tile):
+                    s = dot_t(query, refs[which][at:end, key_cols])
+                    position = (block - 1 + which) * BLOCK + at + lax.broadcasted_iota(jnp.int32, (1, end - at), 1)
+                    live = (position >= 0) & (position < length)
+                    s = s * scale2 + bias_ref[head, :, col : col + end - at]
+                    scores.append(jnp.where(live, s, -jnp.inf))
+                    values.append(refs[which][at:end, value_cols])
+                scores.append(dot_t(query, low) * scale2)
+                values.append(low)
+                raised, total, lse = softmax_parts(scores)
+                out = functools.reduce(jnp.add, [dot(e.astype(bf16), v) for e, v in zip(raised, values)])
+                att_ref[pl.ds(cur_at + tile * QTILE, QTILE), own] = (out / total).astype(bf16)
+                lse_ref[head : head + 1, pl.ds(pl.multiple_of(block * BLOCK, BLOCK) + tile * QTILE, QTILE)] = to_row(lse)
+            own_key = cur_ref[:, key_cols]
+            own_value = cur_ref[:, value_cols]
+            squeries = dot(low, query_ref[head]).astype(bf16)
+            position = block * BLOCK + lax.broadcasted_iota(jnp.int32, (1, BLOCK), 1)
+            for tile in range(STATE_VECTORS // QTILE):
+                rows = slice(tile * QTILE, (tile + 1) * QTILE)
+                squery = squeries[rows]
+                scores = [
+                    dot_t(squery, low) * scale2,
+                    jnp.where(position < length, dot_t(squery, own_key) * scale2, -jnp.inf),
+                ]
+                raised, total, lse = softmax_parts(scores)
+                update = dot(raised[0].astype(bf16), low) + dot(raised[1].astype(bf16), own_value)
+                update = update / total
+                upd_ref[block, rows, own] = update
+                slse_ref[head : head + 1, pl.ds(pl.multiple_of(block * BLOCK, BLOCK) + tile * QTILE, QTILE)] = to_row(
+                    lse
+                )
+                forget = forget_ref[:, own]
+                old = memory[rows]
+                memory_ref[rows, own] = jnp.where(live_block, forget * old + (1.0 - forget) * update, old)
+
+        for bit in reversed(bits):
+            att_copy(bit, block).start()
+
+        @pl.when(block == 0)
+        def _():
+            for k in passing:
+                out_arrival(k).wait_recv()
+                onward(k, lambda target: out_copy(target).start())
+
+        @pl.when(block >= 1)
+        def _():
+            for k in passing:
+                att_arrival(k, block - 1).wait_recv()
+                onward(k, lambda target: att_copy(target, block - 1).start())
+
     final_ref[...] = memory_ref[...]
-
-
-def attend(qkv, init, length, state_query, forget, bias, heads, order):
+    for t in range(min(hi - 1, blocks - 1), hi - 1):
+        step(0, t)
+    for k in passing:
+        att_arrival(k, blocks - 1).wait_recv()
+        onward(k, lambda target: att_copy(target, blocks - 1).start())
+    arrive(0)
+    for k in range(1, seq, 2):
+        out_arrival(k).wait_recv()
+        for b in range(blocks):
+            att_arrival(k, b).wait_recv()
+    drain(0)
+    for k in range(1, seq):
+        out_copy(k).wait_send()
+        for b in range(blocks):
+            att_copy(k, b).wait_send()
+
+
+def attend(qkv, init, length, state_query, forget, bias, own_out, own_down, heads, seq, fsdp):
     rows, width3 = qkv.shape
     width = heads * DH
     blocks = rows // BLOCK
+    lo = 2
+    hi = fsdp // lo
+    dim = own_down.shape[1]
+    anywhere = pl.BlockSpec(memory_space=pl.ANY)
+    vmem = pl.BlockSpec(memory_space=pltpu.VMEM)
+    dma = pltpu.SemaphoreType.DMA
     return pl.pallas_call(
-        functools.partial(attend_kernel, heads),
+        functools.partial(attend_kernel, heads, seq, hi, lo),
         out_shape=(
             jax.ShapeDtypeStruct((rows, width), bf16),
+            jax.ShapeDtypeStruct((seq, rows, width), bf16),
+            jax.ShapeDtypeStruct((fsdp, seq) + own_out.shape[1:], bf16),
+            jax.ShapeDtypeStruct((fsdp,) + own_down.shape, bf16),
             jax.ShapeDtypeStruct((STATE_VECTORS, width), f32),
             jax.ShapeDtypeStruct((blocks, STATE_VECTORS, width), f32),
             jax.ShapeDtypeStruct((blocks, STATE_VECTORS, width), f32),
             jax.ShapeDtypeStruct((heads, rows), f32),
             jax.ShapeDtypeStruct((heads, blocks * STATE_VECTORS), f32),
         ),
-        grid_spec=pltpu.PrefetchScalarGridSpec(
-            num_scalar_prefetch=2,
-            grid=(blocks,),
-            in_specs=[
-                pl.BlockSpec((BLOCK, width3), lambda b, _, at: (at[b], 0)),
-                pl.BlockSpec((BLOCK, width3), lambda b, _, at: (at[jnp.maximum(b - 1, 0)], 0)),
-                pl.BlockSpec((STATE_VECTORS, width), lambda b, _, at: (0, 0)),
-                pl.BlockSpec((heads, DH, DH), lambda b, _, at: (0, 0, 0)),
-                pl.BlockSpec((1, width), lambda b, _, at: (0, 0)),
-                pl.BlockSpec((heads, 2 * BLOCK), lambda b, _, at: (0, 0)),
-            ],
-            out_specs=(
-                pl.BlockSpec((BLOCK, width), lambda b, _, at: (at[b], 0)),
-                pl.BlockSpec((STATE_VECTORS, width), lambda b, _, at: (0, 0)),
-                pl.BlockSpec((1, STATE_VECTORS, width), lambda b, _, at: (b, 0, 0)),
-                pl.BlockSpec((1, STATE_VECTORS, width), lambda b, _, at: (b, 0, 0)),
-                pl.BlockSpec((heads, BLOCK), lambda b, _, at: (0, b)),
-                pl.BlockSpec((heads, STATE_VECTORS), lambda b, _, at: (0, b)),
-            ),
-            scratch_shapes=[pltpu.VMEM((STATE_VECTORS, width), f32), pltpu.VMEM((heads, QTILE, SPAN), f32)],
-        ),
-        compiler_params=pltpu.CompilerParams(vmem_limit_bytes=40 << 20),
+        in_specs=[pl.BlockSpec(memory_space=pltpu.SMEM)] + [vmem] * 5 + [anywhere] * 2,
+        out_specs=(vmem, anywhere, anywhere, anywhere, vmem, vmem, vmem, vmem, vmem),
+        scratch_shapes=[
+            pltpu.VMEM((STATE_VECTORS, width), f32),
+            pltpu.VMEM((heads, QTILE, SPAN), f32),
+            dma((2,)),
+            dma((seq, blocks)),
+            dma((seq, blocks)),
+            dma((seq,)),
+            dma((seq,)),
+        ]
+        + line_sems(1, hi),
+        compiler_params=pltpu.CompilerParams(collective_id=3, has_side_effects=True, vmem_limit_bytes=40 << 20),
         cost_estimate=pl.CostEstimate(
             flops=blocks * heads * 512 * 2400 * 128 * 4, bytes_accessed=16 << 20, transcendentals=10 << 20
         ),
         name="attend",
-    )(length, order, qkv, qkv, init, state_query, forget, bias)
+    )(length, qkv, init, state_query, forget, bias, own_out, own_down)
 
 
 def attend_back_kernel(
@@ -402,143 +619,156 @@
     )(length, order, qkv, qkv, dout, out, mem, upd, lse, slse, sgrad, state_query, forget, bias)
 
 
-def gather_kernel(seq, hi, lo, tok_ref, w_ref, gain_ref, out_ref, toks_ref, ws_ref, gains_ref, outs_ref, here_sem, seq_send, seq_recv, far_send, far_recv, lo_send, lo_recv):
+def gather_kernel(
+    seq,
+    hi,
+    lo,
+    tok_ref,
+    grad_ref,
+    wq_ref,
+    ga_ref,
+    gm_ref,
+    wo_ref,
+    wu_ref,
+    toks_ref,
+    grads_ref,
+    wqs_ref,
+    gas_ref,
+    gms_ref,
+    wos_ref,
+    wus_ref,
+    own_sem,
+    seq_send,
+    seq_recv,
+    z_send,
+    z_recv,
+    y_send,
+    y_recv,
+):
     me = lax.axis_index("seq")
     f = lax.axis_index("fsdp")
-    z, y = f // lo, f % lo
-    pairs = ((w_ref, ws_ref), (gain_ref, gains_ref), (out_ref, outs_ref))
-
-    barrier = pltpu.get_barrier_semaphore()
-    greeted = 0
-    bit = 1
-    while bit < seq:
-        pl.semaphore_signal(barrier, inc=1, device_id={"seq": me ^ bit}, device_id_type=MESH)
-        greeted += 1
-        bit *= 2
-    for target in (lax.rem(z + 1, hi) * lo + y, lax.rem(z + hi - 1, hi) * lo + y):
-        pl.semaphore_signal(barrier, inc=1, device_id={"fsdp": target}, device_id_type=MESH)
-        greeted += 1
-    pl.semaphore_signal(barrier, inc=1, device_id={"fsdp": z * lo + 1 - y}, device_id_type=MESH)
-    greeted += 1
-    pl.semaphore_wait(barrier, greeted)
-
-    own_copies = [pltpu.make_async_copy(tok_ref, toks_ref.at[0], here_sem.at[0])]
-    own_copies += [pltpu.make_async_copy(a, b.at[f], here_sem.at[1 + i]) for i, (a, b) in enumerate(pairs)]
-    for c in own_copies:
-        c.start()
-
-    def seq_copy(source, slot, bit):
-        src = tok_ref if source == 0 else toks_ref.at[source]
-        return pltpu.make_async_remote_copy(
-            src_ref=src, dst_ref=toks_ref.at[slot], send_sem=seq_send.at[slot], recv_sem=seq_recv.at[slot],
-            device_id={"seq": me ^ bit}, device_id_type=MESH,
-        )
-
-    def fsdp_copy(i, origin, own, target, send, recv):
+    fsdp = hi * lo
+    bits = [1 << i for i in range(seq.bit_length() - 1)]
+    greet(bits, hi, lo)
+
+    pairs = ((tok_ref, toks_ref), (grad_ref, grads_ref))
+
+    def seq_copy(i, source, slot, bit):
         src, out = pairs[i]
         return pltpu.make_async_remote_copy(
-            src_ref=src if own else out.at[origin], dst_ref=out.at[origin], send_sem=send, recv_sem=recv,
-            device_id={"fsdp": target}, device_id_type=MESH,
+            src_ref=out.at[source] if source else src,
+            dst_ref=out.at[slot],
+            send_sem=seq_send.at[i, slot],
+            recv_sem=seq_recv.at[i, slot],
+            device_id={"seq": me ^ bit},
+            device_id_type=MESH,
         )
 
-    def right(i, t):
-        return fsdp_copy(i, (z - t) * lo + y, t == 0, (z + 1) * lo + y, far_send.at[i, 0, t], far_recv.at[i, 0, t])
-
-    def left(i, t):
-        return fsdp_copy(i, (z + t) * lo + y, t == 0, (z - 1) * lo + y, far_send.at[i, 1, t], far_recv.at[i, 1, t])
-
-    def across(i, d):
-        return fsdp_copy(i, (z + d) * lo + y, d == 0, z * lo + 1 - y, lo_send.at[i, d + hi - 1], lo_recv.at[i, d + hi - 1])
-
-    both = range(len(pairs))
-    seq_sends = []
-    bits = []
-    bit = seq // 2
-    while bit > 1:
-        bits.append(bit)
-        bit //= 2
-    have = [0]
-    if bits:
-        seq_sends.append(seq_copy(0, bits[0], bits[0]))
-        seq_sends[-1].start()
+    sends = []
+
+    def send(i, source, slot, bit):
+        sends.append(seq_copy(i, source, slot, bit))
+        sends[-1].start()
+
+    high = [bit for bit in reversed(bits) if bit > 1]
+    if high:
+        send(0, 0, high[0], high[0])
     if seq > 1:
-        seq_sends.append(seq_copy(0, 1, 1))
-        seq_sends[-1].start()
-    for i in both:
-        pl.when(z + 1 < hi)(right(i, 0).start)
-        pl.when(z >= 1)(left(i, 0).start)
-        across(i, 0).start()
+        send(0, 0, 1, 1)
+
+    width = wqs_ref.shape[2] // 3
+    share = wus_ref.shape[2] // fsdp
+    every = wq_ref.shape[1] // 3
+    piece = wos_ref.shape[1]
+    copies = [[], [], [], [], []]
+
+    def local(i, src, dst):
+        copies[i].append(pltpu.make_async_copy(src, dst, own_sem.at[i, len(copies[i])]))
+        copies[i][-1].start()
+
+    for c in range(3):
+        cols = pl.ds(pl.multiple_of(c * every + me * width, width), width)
+        local(0, wq_ref.at[:, cols], wqs_ref.at[f, :, pl.ds(c * width, width)])
+    local(1, ga_ref, gas_ref.at[f])
+    local(2, gm_ref, gms_ref.at[f])
+    local(3, wo_ref.at[me], wos_ref.at[f])
+    if wu_ref.shape[1] == wus_ref.shape[2]:
+        local(4, wu_ref, wus_ref.at[f])
+    else:
+        for c in range(fsdp):
+            cols = pl.ds(pl.multiple_of((c * seq + me) * share, share), share)
+            local(4, wu_ref.at[:, cols], wus_ref.at[f, :, pl.ds(c * share, share)])
+    own_rows = [
+        pltpu.make_async_copy(src, out.at[0], own_sem.at[5, i]) for i, (src, out) in enumerate(pairs)
+    ]
+    for c in own_rows:
+        c.start()
+    outs = (wqs_ref, gas_ref, gms_ref, wos_ref, wus_ref)
+    start, step, arrive, drain = line_gather(
+        hi, lo, lambda i, origin: outs[i].at[origin], len(outs), z_send, z_recv, y_send, y_recv
+    )
+    for i in range(len(outs)):
+        for c in copies[i]:
+            c.wait()
+        start(i)
+    if high:
+        send(1, 0, high[0], high[0])
+    if seq > 1:
+        send(1, 0, 1, 1)
     for t in range(hi - 1):
-        for i in both:
-            @pl.when(z - 1 - t >= 0)
-            def _():
-                fsdp_copy(i, (z - 1 - t) * lo + y, False, f, far_send.at[i, 0, t], far_recv.at[i, 0, t]).wait_recv()
-                across(i, -1 - t).start()
-                if t + 1 < hi - 1:
-                    pl.when(z + 1 < hi)(right(i, t + 1).start)
-
-            @pl.when(z + 1 + t < hi)
-            def _():
-                fsdp_copy(i, (z + 1 + t) * lo + y, False, f, far_send.at[i, 1, t], far_recv.at[i, 1, t]).wait_recv()
-                across(i, 1 + t).start()
-                if t + 1 < hi - 1:
-                    pl.when(z >= 1)(left(i, t + 1).start)
-    for n, bit in enumerate(bits):
-        if n:
+        for i in range(len(outs)):
+            step(i, t)
+    for i in range(len(pairs)):
+        have = [0]
+        for n, bit in enumerate(high):
+            if n:
+                for j in have:
+                    send(i, j, j ^ bit, bit)
             for j in have:
-                seq_sends.append(seq_copy(j, j ^ bit, bit))
-                seq_sends[-1].start()
-        for j in list(have):
-            seq_copy(0, j ^ bit, bit).wait_recv()
-            seq_sends.append(seq_copy(j ^ bit, j ^ bit ^ 1, 1))
-            seq_sends[-1].start()
-        have += [j ^ bit for j in have]
-    for j in have if seq > 1 else []:
-        seq_copy(0, j ^ 1, 1).wait_recv()
-    for i in both:
-        for d in range(1 - hi, hi):
-            @pl.when((z + d >= 0) & (z + d < hi))
-            def _():
-                fsdp_copy(i, (z + d) * lo + 1 - y, False, f, lo_send.at[i, d + hi - 1], lo_recv.at[i, d + hi - 1]).wait_recv()
-                across(i, d).wait_send()
-        for t in range(hi - 1):
-            @pl.when((z + 1 < hi) & (z - t >= 0))
-            def _():
-                right(i, t).wait_send()
-
-            @pl.when((z >= 1) & (z + t < hi))
-            def _():
-                left(i, t).wait_send()
-    for c in seq_sends:
+                seq_copy(i, 0, j ^ bit, bit).wait_recv()
+                send(i, j ^ bit, j ^ bit ^ 1, 1)
+            have += [j ^ bit for j in have]
+        if seq > 1:
+            for j in have:
+                seq_copy(i, 0, j ^ 1, 1).wait_recv()
+    for i in range(len(outs)):
+        arrive(i)
+    for i in range(len(outs)):
+        drain(i)
+    for c in sends:
         c.wait_send()
-    for c in own_copies:
+    for c in own_rows:
         c.wait()
 
 
-def gather_start(tokens, weights, seq, fsdp):
+def gather_start(tokens, grads, w_qkv, gain_a, gain_m, w_out, w_up, seq, fsdp):
     lo = 2
     hi = fsdp // lo
-    count = len(weights)
+    dim_rows, hidden = w_up.shape
+    share = hidden // (seq * fsdp)
+    if share % 128:
+        w_up = lax.dynamic_slice_in_dim(w_up.reshape(dim_rows, fsdp, seq, share), lax.axis_index("seq"), 1, axis=2)
+        w_up = w_up.reshape(dim_rows, fsdp * share)
     anywhere = pl.BlockSpec(memory_space=pl.ANY)
     dma = pltpu.SemaphoreType.DMA
+    shapes = (
+        (seq,) + tokens.shape,
+        (seq,) + grads.shape,
+        (fsdp, dim_rows, w_qkv.shape[1] // seq),
+        (fsdp,) + gain_a.shape,
+        (fsdp,) + gain_m.shape,
+        (fsdp,) + w_out.shape[1:],
+        (fsdp, dim_rows, hidden // seq),
+    )
     return pl.pallas_call(
         functools.partial(gather_kernel, seq, hi, lo),
-        out_shape=(jax.ShapeDtypeStruct((seq,) + tokens.shape, tokens.dtype),)
-        + tuple(jax.ShapeDtypeStruct((fsdp,) + w.shape, w.dtype) for w in weights),
-        in_specs=[anywhere] * (1 + count),
-        out_specs=(anywhere,) * (1 + count),
-        scratch_shapes=[
-            dma((1 + count,)),
-            dma((seq,)),
-            dma((seq,)),
-            dma((count, 2, hi)),
-            dma((count, 2, hi)),
-            dma((count, 2 * hi)),
-            dma((count, 2 * hi)),
-        ],
+        out_shape=tuple(jax.ShapeDtypeStruct(shape, bf16) for shape in shapes),
+        in_specs=[anywhere] * 7,
+        out_specs=(anywhere,) * 7,
+        scratch_shapes=[dma((6, max(fsdp, 3))), dma((2, seq)), dma((2, seq))] + line_sems(5, hi),
         compiler_params=pltpu.CompilerParams(collective_id=0, has_side_effects=True),
         name="gather_start",
-    )(tokens, *weights)
+    )(tokens, grads, w_qkv, gain_a, gain_m, w_out, w_up)
 
 
 def finish_kernel(
@@ -965,9 +1195,9 @@
         del refs[:count]
         return taken
 
-    att_refs = take(seq)
-    (tok_ref,) = take(1)
-    grad_refs = take(seq)
+    own_ref, others_ref, tok_ref, grads_ref = take(4)
+    att_refs = [own_ref] + [others_ref.at[k] for k in range(1, seq)]
+    grad_refs = [grads_ref.at[j] for j in range(seq)]
     wo_ref, wu_ref, wd_ref, gain_ref = take(4)
     mid_ref, dmid_ref, gsum_ref, db_ref, mo_ref, ug_ref, dg_ref = take(7)
     att_buf, tok_buf, gm, nm, hid, dpre, low, into, acc = take(9)
@@ -995,7 +1225,7 @@
         j, slot = order[n], n % depth
         copies = [
             pltpu.make_async_copy(
-                att_refs[k].at[pl.ds((j ^ k) * rows, rows)], att_buf.at[slot, k], load_sem.at[slot, k]
+                att_refs[k].at[pl.ds(j * rows, rows)], att_buf.at[slot, k], load_sem.at[slot, k]
             )
             for k in range(seq)
         ]
@@ -1152,7 +1382,7 @@
             dn_copy(bit, j).wait_send()
 
 
-def mlp(length, atts, tok, grads, wo, wu, wd, gain):
+def mlp(length, own, others, tok, grads, wo, wu, wd, gain):
     seq, rows, dim = tok.shape
     share = wu.shape[1]
     sub = 256
@@ -1171,7 +1401,7 @@
             jax.ShapeDtypeStruct((dim, share), bf16),
             jax.ShapeDtypeStruct((share, dim), bf16),
         ),
-        in_specs=[pl.BlockSpec(memory_space=pltpu.SMEM)] + [anywhere] * (2 * seq + 1) + [vmem] * 4,
+        in_specs=[pl.BlockSpec(memory_space=pltpu.SMEM)] + [anywhere] * 4 + [vmem] * 4,
         out_specs=(vmem, vmem, vmem, anywhere, anywhere, vmem, vmem),
         scratch_shapes=[
             pltpu.VMEM((depth, seq, rows, dim // seq), bf16),
@@ -1197,7 +1427,7 @@
             flops=2 * rows * seq * dim * (dim + 6 * share), bytes_accessed=32 << 20, transcendentals=rows * seq * share
         ),
         name="mlp",
-    )(length, *atts, tok, *grads, wo, wu, wd, gain)
+    )(length, own, others, tok, grads, wo, wu, wd, gain)
 
 
 def swap(value, bit):
@@ -1278,28 +1508,23 @@
     hidden_all = w_up.shape[1]
     share = hidden_all // (seq_count * fsdp_count)
 
-    own_qkv = lax.dynamic_slice_in_dim(
-        w_qkv.reshape(w_qkv.shape[0], 3, seq_count, width), seq_at, 1, axis=2
-    ).reshape(w_qkv.shape[0], 3 * width)
-    own_up = lax.dynamic_slice_in_dim(w_up, seq_at * (hidden_all // seq_count), hidden_all // seq_count, axis=1)
-    own_down = lax.dynamic_slice_in_dim(w_down, seq_at * share, share, axis=0)
-    down_w = lax.all_gather(own_down, "fsdp", axis=0, tiled=True)
-    up_w = lax.all_gather(own_up, "fsdp", axis=0, tiled=True)
-    all_tokens, qkv_w, gains, out_w = gather_start(
-        tokens[0], (own_qkv, jnp.stack([norm_attn, norm_mlp]), w_out), seq_count, fsdp_count
+    piece = dim // (seq_count * fsdp_count)
+    all_tokens, all_grad, qkv_w, gain_attn, gain_mlp, own_out, up_w = gather_start(
+        tokens[0],
+        out_grad[0],
+        w_qkv,
+        norm_attn.reshape(1, -1),
+        norm_mlp.reshape(1, -1),
+        w_out.reshape(seq_count, piece, dim),
+        w_up,
+        seq_count,
+        fsdp_count,
     )
     qkv_w = qkv_w.reshape(dim, 3 * width)
-    gains = jnp.swapaxes(gains, 0, 1).reshape(2, dim).astype(f32)
-    gain_attn, gain_mlp = gains[0], gains[1]
-    span = fsdp_count // seq_count
-    down_w = down_w.reshape(seq_count, span, share, dim)
-    moved = [lax.dynamic_slice_in_dim(down_w, seq_at, 1, axis=0)]
-    for k in range(1, seq_count):
-        moved.append(swap(lax.dynamic_slice_in_dim(down_w, seq_at ^ k, 1, axis=0), k))
-    moved = jnp.concatenate(moved, axis=0)
-    moved = [lax.dynamic_slice_in_dim(moved, seq_at ^ k, 1, axis=0) for k in range(seq_count)]
-    down_w = jnp.swapaxes(jnp.concatenate(moved, axis=0), 0, 1).reshape(fsdp_count * share, dim)
-    all_grad = seq_gather(out_grad[0])
+    up_w = up_w.reshape(dim, hidden_all // seq_count)
+    gain_attn = gain_attn.reshape(dim).astype(f32)
+    gain_mlp = gain_mlp.reshape(dim).astype(f32)
+    own_down = lax.dynamic_slice_in_dim(w_down, seq_at * share, share, axis=0)
 
     bias = bias_vector(rel_bias)
     forget = jax.nn.sigmoid(gate_bias)
@@ -1310,14 +1535,24 @@
     inputs = all_tokens.reshape(rows, dim).astype(f32)
     normed = (inputs * inverse_rms(inputs) * gain_attn).astype(bf16)
     qkv = dot(normed, qkv_w).astype(bf16)
-    attended, final_memory, mem, upd, lse, slse = attend(
-        qkv, state_init[0], lengths, state_query, forget_row, bias, heads, order
+    attended, others, out_w, down_w, final_memory, mem, upd, lse, slse = attend(
+        qkv,
+        state_init[0],
+        lengths,
+        state_query,
+        forget_row,
+        bias,
+        own_out,
+        own_down,
+        heads,
+        seq_count,
+        fsdp_count,
     )
-
     out_w = out_w.reshape(dim, dim)
+    down_w = down_w.reshape(fsdp_count * share, dim)
     own_out = lax.dynamic_slice_in_dim(out_w, seq_at * width, width, axis=0)
     mid_here, dmid, mlp_gain_grad, dbranch, mlp_parts, up_grad, down_grad = mlp(
-        lengths, seq_gather(attended), all_tokens, all_grad, out_w, up_w, down_w, gain_mlp.reshape(1, dim)
+        lengths, attended, others, all_tokens, all_grad, out_w, up_w, down_w, gain_mlp.reshape(1, dim)
     )
     dbranch = dbranch.reshape(rows, dim)
     dattended = dot_t(dbranch, own_out).astype(bf16)
@@ -1331,10 +1566,16 @@
     live_here = (seq_at * tok_rows + jnp.arange(tok_rows, dtype=jnp.int32) < lengths[0]).astype(f32)[:, None]
     output = (live_here * (mid_here + mlp_out)).astype(bf16)[None]
     dnormed = dot_t(dqkv, qkv_w).astype(bf16).reshape(seq_count, tok_rows, dim)
-    piece = dim // (seq_count * fsdp_count)
     qkv_grad = t_dot(normed, dqkv).astype(bf16).reshape(seq_count, fsdp_count, piece, 3 * width)
     up_grad = up_grad.reshape(seq_count, fsdp_count, piece, hidden_all // seq_count)
-    down_grad = down_grad.reshape(fsdp_count, share, dim)
+    span = fsdp_count // seq_count
+    down_grad = down_grad.reshape(seq_count, span, share, dim)
+    moved = [lax.dynamic_slice_in_dim(down_grad, seq_at, 1, axis=0)]
+    for k in range(1, seq_count):
+        moved.append(swap(lax.dynamic_slice_in_dim(down_grad, seq_at ^ k, 1, axis=0), k))
+    moved = lax.optimization_barrier(jnp.concatenate(moved, axis=0))
+    moved = [lax.dynamic_slice_in_dim(moved, seq_at ^ k, 1, axis=0) for k in range(seq_count)]
+    down_grad = jnp.swapaxes(jnp.concatenate(moved, axis=0), 0, 1).reshape(fsdp_count, share, dim)
     out_w_grad = out_w_grad.astype(bf16).reshape(fsdp_count, piece, dim)
     grad_gate = dforget.reshape(heads, DH) * forget * (1.0 - forget)
     grad_table = jnp.pad(bias_table_grad(near, far), ((0, 0), (0, DH - BUCKETS)))
@@ -1359,7 +1600,8 @@
     dquery = small[:cut].reshape(heads, DH, DH)
     grad_gate = small[cut : cut + heads]
     grad_table = small[cut + heads : cut + 2 * heads, :BUCKETS]
-    up_part = jnp.swapaxes(up_part, 0, 1).reshape(piece, hidden_all)
+    up_part = up_part.reshape(seq_count, piece, fsdp_count, share)
+    up_part = jnp.transpose(up_part, (1, 2, 0, 3)).reshape(piece, hidden_all)
     qkv_part = qkv_part.reshape(seq_count, piece, 3, width)
     qkv_part = jnp.transpose(qkv_part, (1, 2, 0, 3)).reshape(piece, 3 * H * DH)
     gain_sums = jnp.sum(gain_sums.reshape(2, 8, seq_count * fsdp_count, piece), axis=1)

time: 485 us -> 480 us (0.990)
  Pallas kernels: 316 us -> 360 us
  waiting for transfers between devices: 26.5 us -> 0.02 us
  between operations: 16.1 us -> 2.78 us
  local copies, waits for them, and re-layouts: 63.4 us -> 55 us
    pallas_call x2, Pallas kernels: 83.8 us -> 127 us  [the longest x1 87.7 us: gather_start(): pl.pallas_call(functools.partial(gather_kernel, seq, hi, lo), out_shape=t...]
    ppermute x12 -> x6, waiting for transfers between devices: 26.5 us -> 0.02 us  [swap(): return lax.ppermute(value, 'seq', [(i, i ^ bit) for i in range(count)])]
    unnamed x214 -> x199, local copies, waits for them, and re-layouts: 44.9 us -> 42 us
  transfers between devices with their start and end apart: 14 -> 6, of which waited for: 3 -> 0; matrix products, arithmetic and copies ran while one was open for 20% -> 15% of each run, Pallas kernels for 41% -> 33%
where the time goes in v5:
time: 480 us; the launch traced here: 476 us
  Pallas kernels  360 us (75%)
  local copies, waits for them, and re-layouts  55 us (11%)
  other arithmetic  30.5 us (6%)
  matrix products  24.2 us (5%)
    pallas_call x1, Pallas kernels, finish(): pl.pallas_call(functools.partial(finish_kernel, seq, hi, lo, chunks), out...  116 us
    pallas_call x1, Pallas kernels, gather_start(): pl.pallas_call(functools.partial(gather_kernel, seq, hi, lo), out_shape=t...  87.7 us
    pallas_call x1, Pallas kernels, mlp(): pl.pallas_call(functools.partial(mlp_kernel, seq, sub), out_shape=(jax.Sh...  76.8 us
    unnamed x199, local copies, waits for them, and re-layouts  42 us
    pallas_call x1, Pallas kernels, attend_back(): pl.pallas_call(functools.partial(attend_back_kernel, heads, blocks), out_...  40.4 us
    pallas_call x1, Pallas kernels, attend(): pl.pallas_call(functools.partial(attend_kernel, heads, seq, hi, lo), out_...  39.5 us
    dot_general x2, matrix products, t_dot(): lax.dot_general(a, b, (((0,), (0,)), ((), ())), preferred_element_type=f32)  9.95 us
  transfers between devices with their start and end apart: 6, of which 0 were waited for; matrix products, arithmetic and copies ran while one was open for 15% of the time, Pallas kernels for 33%

profile of v5, /device:TPU:0, one launch (start us, length us, event | category | flops | bytes accessed | tf_op | source)
XLA Modules:
  0.0 475.8 jit_solution(3121062462062065785)
XLA Ops:
  0.7 1.9 multiply_reduce_fusion.1
  2.6 1.6 multiply_reduce_fusion.32
  4.1 87.7 %gather_start.1 = (bf16[4,512,1024]{2,1,0:T(8,128)(2,1)}, bf16[4,512,1024]{2,1,0:T(8,128)(2,1)}, bf16[8,128,768]{2,1,0:T(8,128)(2,1)}, bf16[8,1,128]{2,1,0:T(2,1...) custom-call(bf16[512,1024]{1,0:T(8,128)(2,1)} %bitcast.131, ...), custom_call_target="tpu_custom_call" | custom-call | tf_op jit(solution)/shard_map/gather_start/pallas_call | solution.py:763
  91.8 3.1 multiply_reduce_fusion
  96.8 3.0 multiply_convert_fusion
  100.3 4.8 %convolution_convert_fusion.1.qkv_ref.cur_ref.prev_ref = bf16[2048,768]{1,0:T(8,128)(2,1)} fusion(bf16[2048,1024]{1,0:T(8,128)(2,1)S(1)} %bitcast.133, bf16[1024,768]{1,0:T(8,128)(2,1)S(1)} %bitcast.182), kind=kOutput, calls=%fused_computation.6 | convolution fusion | flops 3222798336 | bytes 8912896 | tf_op jit(solution)/shard_map/dot_general | solution.py:57
  105.8 1.9 copy-done.12
  107.6 39.5 %attend.1 = (bf16[2048,256]{1,0:T(8,128)(2,1)S(1)}, bf16[4,2048,256]{2,1,0:T(8,128)(2,1)}, bf16[8,4,32,1024]{3,2,1,0:T(8,128)(2,1)S(1)}, bf16[8,128,1024]{2,1,0:...) custom-call(s32[1]{0:T(128)} %copy.183.length_ref, ...), custom_call_target="tpu_custom_call" | custom-call | flops 5033164800 | bytes 16777216 | tf_op jit(solution)/shard_map/attend/pallas_call | solution.py:394
  147.2 1.3 copy-done.6
  148.5 1.4 copy-done.7
  149.9 1.0 copy-done.8
  150.8 1.3 copy-done.14
  152.2 1.3 copy-done.16
  153.5 76.8 %mlp.1 = (f32[512,1024]{1,0:T(8,128)}, f32[512,1024]{1,0:T(8,128)}, f32[8,1024]{1,0:T(8,128)}, bf16[4,512,1024]{2,1,0:T(8,128)(2,1)}, bf16[4,512,1024]{2,1,0:T(8...) custom-call(s32[1]{0:T(128)} %copy.183.length_ref, bf16[2048,256]{1,0:T(8,128)(2,1)} %copy-done.8, ...), custom_call_target="tpu_custom_call" | custom-call | flops 30064771072 | bytes 33554432 | tf_op jit(solution)/shard_map/mlp/pallas_call | solution.py:1393
  230.2 2.7 dynamic-slice_bitcast_fusion.3
  234.0 0.8 collective-permute-start.5
  234.8 3.9 convolution_convert_fusion.2.dout_ref
  239.8 40.4 %attend_back.1 = (bf16[2048,768]{1,0:T(8,128)(2,1)S(1)}, f32[2,128,128]{2,1,0:T(8,128)S(1)}, f32[1,256]{1,0:T(1,128)S(1)}, f32[2,384,256]{2,1,0:T(8,128)S(1)}, f32[2,8,256]{2,1,0:T(8,128)S(1)}) custom-call(s32[1]{0:T(128)} %copy.183.length_ref, s32[4]{0:T(128)S(1)} %iota_xor_fusion.order_ref, bf16[2048,768]{1,0:T(8,128)(2,1)S(1)} %copy-done.13, ...), custom_call_target="tpu_custom_call" | custom-call | flops 12582912000 | bytes 20971520 | tf_op jit(solution)/shard_map/attend_back/pallas_call | solution.py:574
  280.2 1.5 slice_bitcast_fusion.1
  282.6 1.6 copy-done.79
  284.2 2.1 convolution_convert_fusion.4
  286.5 0.7 copy.168
  287.2 0.7 copy.169
  287.8 0.7 copy.170
  289.2 0.7 copy.172
  289.9 0.7 copy.173
  291.2 0.7 copy.175
  292.6 0.7 copy.177
  293.3 0.7 copy.178
  294.6 0.7 copy.180
  295.3 0.7 copy.181
  296.7 3.5 select_reduce_fusion
  301.9 0.9 copy.151
  302.9 0.9 copy.152
  303.8 0.9 copy.153
  304.7 0.9 copy.154
  305.6 0.9 copy.155
  306.6 0.9 copy.156
  307.5 0.9 copy.157
  308.4 0.9 copy.158
  309.4 0.9 copy.159
  310.3 0.9 copy.160
  311.2 0.9 copy.161
  312.2 0.9 copy.162
  313.1 0.9 copy.163
  314.0 0.9 copy.164
  314.9 1.9 select_reduce_fusion.18
  318.1 4.3 fusion.1
  322.6 5.5 %convolution_convert_fusion = bf16[2048,1024]{1,0:T(8,128)(2,1)} fusion(bf16[2048,768]{1,0:T(8,128)(2,1)S(1)} %copy-done.11, bf16[1024,768]{1,0:T(8,128)(2,1)S(1)} %bitcast.183), kind=kOutput, calls=%fused_computation.5 | convolution fusion | flops 3223322624 | bytes 8912896 | tf_op jit(solution)/shard_map/dot_general | solution.py:61
  328.2 7.9 %convolution_convert_fusion.3 = bf16[1024,768]{1,0:T(8,128)(2,1)} fusion(bf16[2048,1024]{1,0:T(8,128)(2,1)} %fusion.1, bf16[2048,768]{1,0:T(8,128)(2,1)} %copy-done.10), kind=kOutput, calls=%fused_computation.17 | convolution fusion | flops 3222011904 | bytes 8912896 | tf_op jit(solution)/shard_map/dot_general | solution.py:65
  336.1 2.6 fusion.2
  340.1 1.6 pad_maximum_fusion
  341.9 1.6 pad_maximum_fusion.1
  343.5 115.8 %finish.1 = (f32[512,1024]{1,0:T(8,128)}, f32[4,32,768]{2,1,0:T(8,128)}, f32[4,32,1024]{2,1,0:T(8,128)}, f32[128,1024]{1,0:T(8,128)}, f32[32,1024]{1,0:T(8,128)}...) custom-call(bf16[4,512,1024]{2,1,0:T(8,128)(2,1)} %bitcast.130, bf16[4,8,32,768]{3,2,1,0:T(8,128)(2,1)} %bitcast.139, ...), custom_call_target="tpu_custom_call" | custom-call | tf_op jit(solution)/shard_map/finish/pallas_call | solution.py:1145
  459.3 1.6 slice.164
  461.0 1.2 slice.163
  462.2 1.2 slice.165
  463.4 1.1 copy.146
  465.0 1.0 reshape.265
  466.5 0.9 reshape.263
  468.1 3.8 fusion.7
  472.0 0.8 copy.184
  472.7 1.3 copy.185
  474.7 0.8 copy.187
  (228 shorter events, 15.2 us)
Async XLA Ops:
  0.6 104.5 %copy-start = (bf16[512,1024]{1,0:T(8,128)(2,1)S(1)}, bf16[512,1024]{1,0:T(8,128)(2,1)}, u32[]{:S(2)}) copy-start(bf16[512,1024]{1,0:T(8,128)(2,1)} %param.22) | copy-start | bytes 3145732
  91.8 4.4 copy-start.43
  91.8 4.4 copy-start.44
  99.9 5.3 %copy-start.45 = (pred[1024]{0:T(1024)(128)(4,1)S(1)}, pred[1024]{0:T(1024)(128)(4,1)}, u32[]{:S(2)}) copy-start(pred[1024]{0:T(1024)(128)(4,1)} %constant.172) | copy-start | bytes 3076
  99.9 5.3 %copy-start.46 = (pred[1024]{0:T(1024)(128)(4,1)S(1)}, pred[1024]{0:T(1024)(128)(4,1)}, u32[]{:S(2)}) copy-start(pred[1024]{0:T(1024)(128)(4,1)} %constant.173) | copy-start | bytes 3076
  99.9 5.3 %copy-start.47 = (pred[1024]{0:T(1024)(128)(4,1)S(1)}, pred[1024]{0:T(1024)(128)(4,1)}, u32[]{:S(2)}) copy-start(pred[1024]{0:T(1024)(128)(4,1)} %constant.174) | copy-start | bytes 3076
  99.9 5.3 %copy-start.48 = (pred[1024]{0:T(1024)(128)(4,1)S(1)}, pred[1024]{0:T(1024)(128)(4,1)}, u32[]{:S(2)}) copy-start(pred[1024]{0:T(1024)(128)(4,1)} %constant.175) | copy-start | bytes 3076
  99.9 5.3 %copy-start.49 = (pred[1024]{0:T(1024)(128)(4,1)S(1)}, pred[1024]{0:T(1024)(128)(4,1)}, u32[]{:S(2)}) copy-start(pred[1024]{0:T(1024)(128)(4,1)} %constant.176) | copy-start | bytes 3076
  100.0 5.3 %copy-start.50 = (pred[1024]{0:T(1024)(128)(4,1)S(1)}, pred[1024]{0:T(1024)(128)(4,1)}, u32[]{:S(2)}) copy-start(pred[1024]{0:T(1024)(128)(4,1)} %constant.177) | copy-start | bytes 3076
  100.0 5.3 %copy-start.51 = (pred[1024]{0:T(1024)(128)(4,1)S(1)}, pred[1024]{0:T(1024)(128)(4,1)}, u32[]{:S(2)}) copy-start(pred[1024]{0:T(1024)(128)(4,1)} %constant.178) | copy-start | bytes 3076
  100.0 5.3 %copy-start.52 = (pred[1024]{0:T(1024)(128)(4,1)S(1)}, pred[1024]{0:T(1024)(128)(4,1)}, u32[]{:S(2)}) copy-start(pred[1024]{0:T(1024)(128)(4,1)} %constant.179) | copy-start | bytes 3076
  100.0 5.3 %copy-start.53 = (pred[1024]{0:T(1024)(128)(4,1)S(1)}, pred[1024]{0:T(1024)(128)(4,1)}, u32[]{:S(2)}) copy-start(pred[1024]{0:T(1024)(128)(4,1)} %constant.180) | copy-start | bytes 3076
  100.0 5.3 %copy-start.54 = (pred[1024]{0:T(1024)(128)(4,1)S(1)}, pred[1024]{0:T(1024)(128)(4,1)}, u32[]{:S(2)}) copy-start(pred[1024]{0:T(1024)(128)(4,1)} %constant.181) | copy-start | bytes 3076
  100.0 5.3 %copy-start.55 = (pred[1024]{0:T(1024)(128)(4,1)S(1)}, pred[1024]{0:T(1024)(128)(4,1)}, u32[]{:S(2)}) copy-start(pred[1024]{0:T(1024)(128)(4,1)} %constant.182) | copy-start | bytes 3076
  100.0 5.3 %copy-start.56 = (pred[1024]{0:T(1024)(128)(4,1)S(1)}, pred[1024]{0:T(1024)(128)(4,1)}, u32[]{:S(2)}) copy-start(pred[1024]{0:T(1024)(128)(4,1)} %constant.183) | copy-start | bytes 3076
  100.0 5.3 %copy-start.57 = (pred[1024]{0:T(1024)(128)(4,1)S(1)}, pred[1024]{0:T(1024)(128)(4,1)}, u32[]{:S(2)}) copy-start(pred[1024]{0:T(1024)(128)(4,1)} %constant.27) | copy-start | bytes 3076
  100.1 5.3 %copy-start.58 = (pred[1024]{0:T(1024)(128)(4,1)S(1)}, pred[1024]{0:T(1024)(128)(4,1)}, u32[]{:S(2)}) copy-start(pred[1024]{0:T(1024)(128)(4,1)} %constant.28) | copy-start | bytes 3076
  100.1 5.3 %copy-start.59 = (pred[1024]{0:T(1024)(128)(4,1)S(1)}, pred[1024]{0:T(1024)(128)(4,1)}, u32[]{:S(2)}) copy-start(pred[1024]{0:T(1024)(128)(4,1)} %constant.29) | copy-start | bytes 3076
  100.1 5.3 %copy-start.60 = (pred[1024]{0:T(1024)(128)(4,1)S(1)}, pred[1024]{0:T(1024)(128)(4,1)}, u32[]{:S(2)}) copy-start(pred[1024]{0:T(1024)(128)(4,1)} %constant.30) | copy-start | bytes 3076
  100.1 5.2 %copy-start.61 = (pred[1024]{0:T(1024)(128)(4,1)S(1)}, pred[1024]{0:T(1024)(128)(4,1)}, u32[]{:S(2)}) copy-start(pred[1024]{0:T(1024)(128)(4,1)} %constant.31) | copy-start | bytes 3076
  100.1 5.2 %copy-start.62 = (pred[1024]{0:T(1024)(128)(4,1)S(1)}, pred[1024]{0:T(1024)(128)(4,1)}, u32[]{:S(2)}) copy-start(pred[1024]{0:T(1024)(128)(4,1)} %constant.32) | copy-start | bytes 3076
  100.1 5.2 %copy-start.63 = (pred[1024]{0:T(1024)(128)(4,1)S(1)}, pred[1024]{0:T(1024)(128)(4,1)}, u32[]{:S(2)}) copy-start(pred[1024]{0:T(1024)(128)(4,1)} %constant.33) | copy-start | bytes 3076
  100.1 5.2 %copy-start.64 = (pred[1024]{0:T(1024)(128)(4,1)S(1)}, pred[1024]{0:T(1024)(128)(4,1)}, u32[]{:S(2)}) copy-start(pred[1024]{0:T(1024)(128)(4,1)} %constant.34) | copy-start | bytes 3076
  100.1 5.2 %copy-start.65 = (pred[1024]{0:T(1024)(128)(4,1)S(1)}, pred[1024]{0:T(1024)(128)(4,1)}, u32[]{:S(2)}) copy-start(pred[1024]{0:T(1024)(128)(4,1)} %constant.35) | copy-start | bytes 3076
  100.2 5.2 %copy-start.66 = (pred[1024]{0:T(1024)(128)(4,1)S(1)}, pred[1024]{0:T(1024)(128)(4,1)}, u32[]{:S(2)}) copy-start(pred[1024]{0:T(1024)(128)(4,1)} %constant.36) | copy-start | bytes 3076
  100.2 5.2 %copy-start.67 = (pred[1024]{0:T(1024)(128)(4,1)S(1)}, pred[1024]{0:T(1024)(128)(4,1)}, u32[]{:S(2)}) copy-start(pred[1024]{0:T(1024)(128)(4,1)} %constant.37) | copy-start | bytes 3076
  100.2 5.2 %copy-start.68 = (pred[1024]{0:T(1024)(128)(4,1)S(1)}, pred[1024]{0:T(1024)(128)(4,1)}, u32[]{:S(2)}) copy-start(pred[1024]{0:T(1024)(128)(4,1)} %constant.38) | copy-start | bytes 3076
  100.2 5.2 %copy-start.69 = (pred[1024]{0:T(1024)(128)(4,1)S(1)}, pred[1024]{0:T(1024)(128)(4,1)}, u32[]{:S(2)}) copy-start(pred[1024]{0:T(1024)(128)(4,1)} %constant.39) | copy-start | bytes 3076
  100.2 5.2 %copy-start.70 = (pred[1024]{0:T(1024)(128)(4,1)S(1)}, pred[1024]{0:T(1024)(128)(4,1)}, u32[]{:S(2)}) copy-start(pred[1024]{0:T(1024)(128)(4,1)} %constant.40) | copy-start | bytes 3076
  100.2 5.2 %copy-start.71 = (pred[1024]{0:T(1024)(128)(4,1)S(1)}, pred[1024]{0:T(1024)(128)(4,1)}, u32[]{:S(2)}) copy-start(pred[1024]{0:T(1024)(128)(4,1)} %constant.41) | copy-start | bytes 3076
  100.2 5.2 %copy-start.72 = (pred[1024]{0:T(1024)(128)(4,1)S(1)}, pred[1024]{0:T(1024)(128)(4,1)}, u32[]{:S(2)}) copy-start(pred[1024]{0:T(1024)(128)(4,1)} %constant.42) | copy-start | bytes 3076
  100.2 5.2 %copy-start.73 = (pred[1024]{0:T(1024)(128)(4,1)S(1)}, pred[1024]{0:T(1024)(128)(4,1)}, u32[]{:S(2)}) copy-start(pred[1024]{0:T(1024)(128)(4,1)} %constant.43) | copy-start | bytes 3076
  100.3 5.2 %copy-start.74 = (pred[1024]{0:T(1024)(128)(4,1)S(1)}, pred[1024]{0:T(1024)(128)(4,1)}, u32[]{:S(2)}) copy-start(pred[1024]{0:T(1024)(128)(4,1)} %constant.44) | copy-start | bytes 3076
  100.3 5.2 %copy-start.75 = (pred[1024]{0:T(1024)(128)(4,1)S(1)}, pred[1024]{0:T(1024)(128)(4,1)}, u32[]{:S(2)}) copy-start(pred[1024]{0:T(1024)(128)(4,1)} %constant.45) | copy-start | bytes 3076
  100.3 5.2 %copy-start.76 = (pred[1024]{0:T(1024)(128)(4,1)S(1)}, pred[1024]{0:T(1024)(128)(4,1)}, u32[]{:S(2)}) copy-start(pred[1024]{0:T(1024)(128)(4,1)} %constant.46) | copy-start | bytes 3076
  100.3 5.4 %copy-start.2 = (bf16[8,32,1024]{2,1,0:T(8,128)(2,1)S(1)}, bf16[8,32,1024]{2,1,0:T(8,128)(2,1)}, u32[]{:S(2)}) copy-start(bf16[8,32,1024]{2,1,0:T(8,128)(2,1)} %get-tuple-element.52.own_out_ref) | copy-start | bytes 1572868
  100.3 5.4 %copy-start.3 = (bf16[1,512,256]{2,1,0:T(8,128)(2,1)S(1)}, bf16[1,512,256]{2,1,0:T(8,128)(2,1)}, u32[]{:S(2)}) copy-start(bf16[1,512,256]{2,1,0:T(8,128)(2,1)} %param.18) | copy-start | bytes 786436
  100.3 5.4 %copy-start.5 = (bf16[2,128,128]{2,1,0:T(8,128)(2,1)S(1)}, bf16[2,128,128]{2,1,0:T(8,128)(2,1)}, u32[]{:S(2)}) copy-start(bf16[2,128,128]{2,1,0:T(8,128)(2,1)} %query_ref.3) | copy-start | bytes 196612
  232.9 107.1 %collective-permute-start.3 = (bf16[1,2,128,1024]{3,2,0,1:T(8,128)(2,1)}, bf16[1,2,128,1024]{3,2,0,1:T(8,128)(2,1)}, u32[]{:S(2)}, u32[]{:S(2)}) collective-permute-start(bf16[1,2,128,1024]{3,2,0,1:T(8,128)(2,1)} %get-tuple-element.158), channel_id=1, source_target_pairs={{0,8},{8,0},{16,24},{24,16},{1,9},{9,1},{17,25},{25,17},{2,10},{10... | collective-permute-start | bytes 1572872 | tf_op jit(solution)/shard_map/ppermute | solution.py:1435
  233.3 106.8 %collective-permute-start.4 = (bf16[1,2,128,1024]{3,2,0,1:T(8,128)(2,1)}, bf16[1,2,128,1024]{3,2,0,1:T(8,128)(2,1)}, u32[]{:S(2)}, u32[]{:S(2)}) collective-permute-start(bf16[1,2,128,1024]{3,2,0,1:T(8,128)(2,1)} %get-tuple-element.157), channel_id=1, source_target_pairs={{0,16},{8,24},{16,0},{24,8},{1,17},{9,25},{17,1},{25,9},{2,18},{10... | collective-permute-start | bytes 1572872 | tf_op jit(solution)/shard_map/ppermute | solution.py:1435
  234.0 106.1 %collective-permute-start.5 = (bf16[1,2,128,1024]{3,2,0,1:T(8,128)(2,1)}, bf16[1,2,128,1024]{3,2,0,1:T(8,128)(2,1)}, u32[]{:S(2)}, u32[]{:S(2)}) collective-permute-start(bf16[1,2,128,1024]{3,2,0,1:T(8,128)(2,1)} %get-tuple-element.159), channel_id=1, source_target_pairs={{0,24},{8,16},{16,8},{24,0},{1,25},{9,17},{17,9},{25,1},{2,26},{10... | collective-permute-start | bytes 1572872 | tf_op jit(solution)/shard_map/ppermute | solution.py:1435
  234.8 5.0 %copy-start.17 = (f32[4,512,256]{2,1,0:T(8,128)S(1)}, f32[4,512,256]{2,1,0:T(8,128)}, u32[]{:S(2)}) copy-start(f32[4,512,256]{2,1,0:T(8,128)} %copy-done.16) | copy-start | bytes 6291460
  239.8 40.4 %copy-start.18 = (bf16[4,512,1024]{2,1,0:T(8,128)(2,1)S(1)}, bf16[4,512,1024]{2,1,0:T(8,128)(2,1)}, u32[]{:S(2)}) copy-start(bf16[4,512,1024]{2,1,0:T(8,128)(2,1)} %get-tuple-element.68) | copy-start | bytes 12582916
  280.2 6.1 %copy-start.10 = (bf16[2048,768]{1,0:T(8,128)(2,1)}, bf16[2048,768]{1,0:T(8,128)(2,1)S(1)}, u32[]{:S(2)}) copy-start(bf16[2048,768]{1,0:T(8,128)(2,1)S(1)} %get-tuple-element.70) | copy-start | bytes 9437188
  281.7 54.4 %collective-permute-start.1 = (bf16[512,1024]{1,0:T(8,128)(2,1)}, bf16[512,1024]{1,0:T(8,128)(2,1)S(1)}, u32[]{:S(2)}, u32[]{:S(2)}) collective-permute-start(bf16[512,1024]{1,0:T(8,128)(2,1)} %get-tuple-element.151), channel_id=1, source_target_pairs={{0,8},{8,0},{16,24},{24,16},{1,9},{9,1},{17,25},{25,17},{2,10},{10... | collective-permute-start | bytes 3145736 | tf_op jit(solution)/shard_map/ppermute | solution.py:1435
  282.4 4.8 %copy-start.36 = (pred[384,256]{1,0:T(32,128)(4,1)S(1)}, pred[384,256]{1,0:T(32,128)(4,1)}, u32[]{:S(2)}) copy-start(pred[384,256]{1,0:T(32,128)(4,1)} %constant.211) | copy-start | bytes 294916
  282.4 5.5 %copy-start.35 = (pred[384,256]{1,0:T(32,128)(4,1)S(1)}, pred[384,256]{1,0:T(32,128)(4,1)}, u32[]{:S(2)}) copy-start(pred[384,256]{1,0:T(32,128)(4,1)} %constant.210) | copy-start | bytes 294916
  282.4 6.1 %copy-start.34 = (pred[384,256]{1,0:T(32,128)(4,1)S(1)}, pred[384,256]{1,0:T(32,128)(4,1)}, u32[]{:S(2)}) copy-start(pred[384,256]{1,0:T(32,128)(4,1)} %constant.209) | copy-start | bytes 294916
  282.4 6.8 %copy-start.33 = (pred[384,256]{1,0:T(32,128)(4,1)S(1)}, pred[384,256]{1,0:T(32,128)(4,1)}, u32[]{:S(2)}) copy-start(pred[384,256]{1,0:T(32,128)(4,1)} %constant.208) | copy-start | bytes 294916
  282.4 7.5 %copy-start.32 = (pred[384,256]{1,0:T(32,128)(4,1)S(1)}, pred[384,256]{1,0:T(32,128)(4,1)}, u32[]{:S(2)}) copy-start(pred[384,256]{1,0:T(32,128)(4,1)} %constant.207) | copy-start | bytes 294916
  282.4 8.1 %copy-start.31 = (pred[384,256]{1,0:T(32,128)(4,1)S(1)}, pred[384,256]{1,0:T(32,128)(4,1)}, u32[]{:S(2)}) copy-start(pred[384,256]{1,0:T(32,128)(4,1)} %constant.206) | copy-start | bytes 294916
  282.4 8.8 %copy-start.30 = (pred[384,256]{1,0:T(32,128)(4,1)S(1)}, pred[384,256]{1,0:T(32,128)(4,1)}, u32[]{:S(2)}) copy-start(pred[384,256]{1,0:T(32,128)(4,1)} %constant.205) | copy-start | bytes 294916
  282.5 9.5 %copy-start.29 = (pred[384,256]{1,0:T(32,128)(4,1)S(1)}, pred[384,256]{1,0:T(32,128)(4,1)}, u32[]{:S(2)}) copy-start(pred[384,256]{1,0:T(32,128)(4,1)} %constant.204) | copy-start | bytes 294916
  282.5 10.1 %copy-start.28 = (pred[384,256]{1,0:T(32,128)(4,1)S(1)}, pred[384,256]{1,0:T(32,128)(4,1)}, u32[]{:S(2)}) copy-start(pred[384,256]{1,0:T(32,128)(4,1)} %constant.203) | copy-start | bytes 294916
  282.5 10.8 %copy-start.27 = (pred[384,256]{1,0:T(32,128)(4,1)S(1)}, pred[384,256]{1,0:T(32,128)(4,1)}, u32[]{:S(2)}) copy-start(pred[384,256]{1,0:T(32,128)(4,1)} %constant.202) | copy-start | bytes 294916
  282.5 11.4 %copy-start.26 = (pred[384,256]{1,0:T(32,128)(4,1)S(1)}, pred[384,256]{1,0:T(32,128)(4,1)}, u32[]{:S(2)}) copy-start(pred[384,256]{1,0:T(32,128)(4,1)} %constant.201) | copy-start | bytes 294916
  282.5 12.1 %copy-start.25 = (pred[384,256]{1,0:T(32,128)(4,1)S(1)}, pred[384,256]{1,0:T(32,128)(4,1)}, u32[]{:S(2)}) copy-start(pred[384,256]{1,0:T(32,128)(4,1)} %constant.200) | copy-start | bytes 294916
  282.5 185.6 %collective-permute-start = (bf16[512,1024]{1,0:T(8,128)(2,1)}, bf16[512,1024]{1,0:T(8,128)(2,1)}, u32[]{:S(2)}, u32[]{:S(2)}) collective-permute-start(bf16[512,1024]{1,0:T(8,128)(2,1)} %get-tuple-element.150), channel_id=1, source_target_pairs={{0,8},{8,0},{16,24},{24,16},{1,9},{9,1},{17,25},{25,17},{2,10},{10... | collective-permute-start | bytes 3145736 | tf_op jit(solution)/shard_map/ppermute | solution.py:1435
  286.3 9.0 %copy-start.24 = (pred[384,256]{1,0:T(32,128)(4,1)S(1)}, pred[384,256]{1,0:T(32,128)(4,1)}, u32[]{:S(2)}) copy-start(pred[384,256]{1,0:T(32,128)(4,1)} %constant.199) | copy-start | bytes 294916
  286.3 9.6 %copy-start.23 = (pred[384,256]{1,0:T(32,128)(4,1)S(1)}, pred[384,256]{1,0:T(32,128)(4,1)}, u32[]{:S(2)}) copy-start(pred[384,256]{1,0:T(32,128)(4,1)} %constant.198) | copy-start | bytes 294916
  318.1 4.5 copy-start.78
  338.7 129.4 %collective-permute-start.2 = (bf16[512,1024]{1,0:T(8,128)(2,1)}, bf16[512,1024]{1,0:T(8,128)(2,1)S(1)}, u32[]{:S(2)}, u32[]{:S(2)}) collective-permute-start(bf16[512,1024]{1,0:T(8,128)(2,1)} %fusion.2), channel_id=1, source_target_pairs={{0,16},{8,24},{16,0},{24,8},{1,17},{9,25},{17,1},{25,9},{2,18},{10... | collective-permute-start | bytes 3145736 | tf_op jit(solution)/shard_map/ppermute | solution.py:1435
  459.3 6.7 %copy-start.21 = (f32[4,32,768]{2,1,0:T(8,128)S(1)}, f32[4,32,768]{2,1,0:T(8,128)}, u32[]{:S(2)}) copy-start(f32[4,32,768]{2,1,0:T(8,128)} %get-tuple-element.80) | copy-start | bytes 1179652
  468.1 4.6 copy-start.19
  (22 other events, 66.4 us)

commit v6 on v5

--- a/solution.py
+++ b/solution.py
@@ -86,24 +86,31 @@
     return raised, total, top + jnp.log2(total)
 
 
-def line_gather(hi, lo, slot, count, z_send, z_recv, y_send, y_recv):
+def line_gather(hi, lo, slot, own, z_send, z_recv, y_send, y_recv):
     f = lax.axis_index("fsdp")
     z, y = f // lo, f % lo
 
-    def copy(i, origin, target, send, recv):
+    def copy(i, origin, target, send, recv, first=False):
         ref = slot(i, origin)
         return pltpu.make_async_remote_copy(
-            src_ref=ref, dst_ref=ref, send_sem=send, recv_sem=recv, device_id={"fsdp": target}, device_id_type=MESH
+            src_ref=own(i) if first else ref,
+            dst_ref=ref,
+            send_sem=send,
+            recv_sem=recv,
+            device_id={"fsdp": target},
+            device_id_type=MESH,
         )
 
     def right(i, t):
-        return copy(i, (z - t) * lo + y, (z + 1) * lo + y, z_send.at[i, 0, t], z_recv.at[i, 0, t])
+        return copy(i, (z - t) * lo + y, (z + 1) * lo + y, z_send.at[i, 0, t], z_recv.at[i, 0, t], t == 0)
 
     def left(i, t):
-        return copy(i, (z + t) * lo + y, (z - 1) * lo + y, z_send.at[i, 1, t], z_recv.at[i, 1, t])
+        return copy(i, (z + t) * lo + y, (z - 1) * lo + y, z_send.at[i, 1, t], z_recv.at[i, 1, t], t == 0)
 
     def across(i, d):
-        return copy(i, (z + d) * lo + y, z * lo + 1 - y, y_send.at[i, d + hi - 1], y_recv.at[i, d + hi - 1])
+        return copy(
+            i, (z + d) * lo + y, z * lo + 1 - y, y_send.at[i, d + hi - 1], y_recv.at[i, d + hi - 1], d == 0
+        )
 
     def start(i):
         pl.when(z + 1 < hi)(lambda: right(i, 0).start())
@@ -227,7 +234,7 @@
 
     def out_copy(k):
         return pltpu.make_async_remote_copy(
-            src_ref=outs_ref.at[:, me ^ k ^ lowest(k)],
+            src_ref=outs_ref.at[:, me ^ k ^ lowest(k)] if k ^ lowest(k) else own_out_ref,
             dst_ref=outs_ref.at[:, me ^ k ^ lowest(k)],
             send_sem=out_send.at[k],
             recv_sem=out_recv.at[k],
@@ -279,17 +286,15 @@
                 send(k | bit)
 
     start, step, arrive, drain = line_gather(
-        hi, lo, lambda i, origin: downs_ref.at[origin], 1, z_send, z_recv, y_send, y_recv
+        hi, lo, lambda i, origin: downs_ref.at[origin], lambda i: own_down_ref, z_send, z_recv, y_send, y_recv
     )
 
+    start(0)
+    for bit in reversed(bits):
+        out_copy(bit).start()
     memory_ref[...] = init_ref[...].astype(f32)
     for head in range(heads):
         bias_ref[head] = tile_bias(vector_ref, head)
-    for c in own_copies:
-        c.wait()
-    start(0)
-    for bit in reversed(bits):
-        out_copy(bit).start()
 
     @pl.loop(0, blocks)
     def _(block):
@@ -374,6 +379,8 @@
         out_arrival(k).wait_recv()
         for b in range(blocks):
             att_arrival(k, b).wait_recv()
+    for c in own_copies:
+        c.wait()
     drain(0)
     for k in range(1, seq):
         out_copy(k).wait_send()
@@ -404,7 +411,7 @@
             jax.ShapeDtypeStruct((heads, rows), f32),
             jax.ShapeDtypeStruct((heads, blocks * STATE_VECTORS), f32),
         ),
-        in_specs=[pl.BlockSpec(memory_space=pltpu.SMEM)] + [vmem] * 5 + [anywhere] * 2,
+        in_specs=[pl.BlockSpec(memory_space=pltpu.SMEM)] + [vmem] * 7,
         out_specs=(vmem, anywhere, anywhere, anywhere, vmem, vmem, vmem, vmem, vmem),
         scratch_shapes=[
             pltpu.VMEM((STATE_VECTORS, width), f32),
@@ -637,14 +644,10 @@
     gms_ref,
     wos_ref,
     wus_ref,
-    own_sem,
-    seq_send,
-    seq_recv,
-    z_send,
-    z_recv,
-    y_send,
-    y_recv,
+    *rest,
 ):
+    own_bufs = rest[:7]
+    own_sem, store_sem, seq_send, seq_recv, z_send, z_recv, y_send, y_recv = rest[7:]
     me = lax.axis_index("seq")
     f = lax.axis_index("fsdp")
     fsdp = hi * lo
@@ -679,38 +682,40 @@
     width = wqs_ref.shape[2] // 3
     share = wus_ref.shape[2] // fsdp
     every = wq_ref.shape[1] // 3
-    piece = wos_ref.shape[1]
-    copies = [[], [], [], [], []]
-
-    def local(i, src, dst):
-        copies[i].append(pltpu.make_async_copy(src, dst, own_sem.at[i, len(copies[i])]))
-        copies[i][-1].start()
-
+    loads = [[] for _ in own_bufs]
+
+    def load(i, src, dst):
+        loads[i].append(pltpu.make_async_copy(src, dst, own_sem.at[i, len(loads[i])]))
+        loads[i][-1].start()
+
+    wq_buf, ga_buf, gm_buf, wo_buf, wu_buf, tok_buf, grad_buf = own_bufs
     for c in range(3):
         cols = pl.ds(pl.multiple_of(c * every + me * width, width), width)
-        local(0, wq_ref.at[:, cols], wqs_ref.at[f, :, pl.ds(c * width, width)])
-    local(1, ga_ref, gas_ref.at[f])
-    local(2, gm_ref, gms_ref.at[f])
-    local(3, wo_ref.at[me], wos_ref.at[f])
+        load(0, wq_ref.at[:, cols], wq_buf.at[:, pl.ds(c * width, width)])
+    load(1, ga_ref, ga_buf)
+    load(2, gm_ref, gm_buf)
+    load(3, wo_ref.at[me], wo_buf)
     if wu_ref.shape[1] == wus_ref.shape[2]:
-        local(4, wu_ref, wus_ref.at[f])
+        load(4, wu_ref, wu_buf)
     else:
         for c in range(fsdp):
             cols = pl.ds(pl.multiple_of((c * seq + me) * share, share), share)
-            local(4, wu_ref.at[:, cols], wus_ref.at[f, :, pl.ds(c * share, share)])
-    own_rows = [
-        pltpu.make_async_copy(src, out.at[0], own_sem.at[5, i]) for i, (src, out) in enumerate(pairs)
-    ]
-    for c in own_rows:
-        c.start()
+            load(4, wu_ref.at[:, cols], wu_buf.at[:, pl.ds(c * share, share)])
+    load(5, tok_ref, tok_buf)
+    load(6, grad_ref, grad_buf)
     outs = (wqs_ref, gas_ref, gms_ref, wos_ref, wus_ref)
     start, step, arrive, drain = line_gather(
-        hi, lo, lambda i, origin: outs[i].at[origin], len(outs), z_send, z_recv, y_send, y_recv
+        hi, lo, lambda i, origin: outs[i].at[origin], lambda i: own_bufs[i], z_send, z_recv, y_send, y_recv
     )
-    for i in range(len(outs)):
-        for c in copies[i]:
+    own_stores = []
+    for i in range(len(own_bufs)):
+        for c in loads[i]:
             c.wait()
-        start(i)
+        if i < len(outs):
+            start(i)
+        target = outs[i].at[f] if i < len(outs) else pairs[i - len(outs)][1].at[0]
+        own_stores.append(pltpu.make_async_copy(own_bufs[i], target, store_sem.at[i]))
+        own_stores[-1].start()
     if high:
         send(1, 0, high[0], high[0])
     if seq > 1:
@@ -737,7 +742,7 @@
         drain(i)
     for c in sends:
         c.wait_send()
-    for c in own_rows:
+    for c in own_stores:
         c.wait()
 
 
@@ -765,7 +770,9 @@
         out_shape=tuple(jax.ShapeDtypeStruct(shape, bf16) for shape in shapes),
         in_specs=[anywhere] * 7,
         out_specs=(anywhere,) * 7,
-        scratch_shapes=[dma((6, max(fsdp, 3))), dma((2, seq)), dma((2, seq))] + line_sems(5, hi),
+        scratch_shapes=[pltpu.VMEM(shape[1:], bf16) for shape in shapes[2:] + shapes[:2]]
+        + [dma((7, max(fsdp, 3))), dma((7,)), dma((2, seq)), dma((2, seq))]
+        + line_sems(5, hi),
         compiler_params=pltpu.CompilerParams(collective_id=0, has_side_effects=True),
         name="gather_start",
     )(tokens, grads, w_qkv, gain_a, gain_m, w_out, w_up)

time: 480 us -> 450 us (0.938)
  Pallas kernels: 360 us -> 330 us
    pallas_call x1, Pallas kernels: 87.7 us -> 57 us  [gather_start(): pl.pallas_call(functools.partial(gather_kernel, seq, hi, lo), out_shape=t...]
  transfers between devices with their start and end apart: 6 -> 6, of which waited for: 0 -> 0; matrix products, arithmetic and copies ran while one was open for 15% -> 16% of each run, Pallas kernels for 33% -> 35%
where the time goes in v6:
time: 450 us; the launch traced here: 446 us
  Pallas kernels  330 us (73%)
  local copies, waits for them, and re-layouts  55 us (12%)
  other arithmetic  30.5 us (7%)
  matrix products  24.2 us (5%)
    pallas_call x1, Pallas kernels, finish(): pl.pallas_call(functools.partial(finish_kernel, seq, hi, lo, chunks), out...  116 us
    pallas_call x1, Pallas kernels, mlp(): pl.pallas_call(functools.partial(mlp_kernel, seq, sub), out_shape=(jax.Sh...  76 us
    pallas_call x1, Pallas kernels, gather_start(): pl.pallas_call(functools.partial(gather_kernel, seq, hi, lo), out_shape=t...  57 us
    unnamed x199, local copies, waits for them, and re-layouts  42 us
    pallas_call x1, Pallas kernels, attend(): pl.pallas_call(functools.partial(attend_kernel, heads, seq, hi, lo), out_...  40.5 us
    pallas_call x1, Pallas kernels, attend_back(): pl.pallas_call(functools.partial(attend_back_kernel, heads, blocks), out_...  40.4 us
    dot_general x2, matrix products, t_dot(): lax.dot_general(a, b, (((0,), (0,)), ((), ())), preferred_element_type=f32)  9.95 us
    dot_general x2, matrix products, dot_t(): lax.dot_general(a, b, (((1,), (1,)), ((), ())), preferred_element_type=f32)  9.39 us
  transfers between devices with their start and end apart: 6, of which 0 were waited for; matrix products, arithmetic and copies ran while one was open for 16% of the time, Pallas kernels for 35%

profile of v6, /device:TPU:0, one launch (start us, length us, event | category | flops | bytes accessed | tf_op | source)
XLA Modules:
  0.0 446.2 jit_solution(15501749990607298944)
XLA Ops:
  0.7 1.9 multiply_reduce_fusion.1
  2.6 1.6 multiply_reduce_fusion.32
  4.1 57.0 %gather_start.1 = (bf16[4,512,1024]{2,1,0:T(8,128)(2,1)}, bf16[4,512,1024]{2,1,0:T(8,128)(2,1)}, bf16[8,128,768]{2,1,0:T(8,128)(2,1)}, bf16[8,1,128]{2,1,0:T(2,1...) custom-call(bf16[512,1024]{1,0:T(8,128)(2,1)} %bitcast.131, ...), custom_call_target="tpu_custom_call" | custom-call | tf_op jit(solution)/shard_map/gather_start/pallas_call | solution.py:768
  61.2 3.1 multiply_reduce_fusion
  66.2 3.0 multiply_convert_fusion
  69.7 4.8 %convolution_convert_fusion.1.qkv_ref.cur_ref.prev_ref = bf16[2048,768]{1,0:T(8,128)(2,1)} fusion(bf16[2048,1024]{1,0:T(8,128)(2,1)S(1)} %bitcast.133, bf16[1024,768]{1,0:T(8,128)(2,1)S(1)} %bitcast.182), kind=kOutput, calls=%fused_computation.6 | convolution fusion | flops 3222798336 | bytes 8912896 | tf_op jit(solution)/shard_map/dot_general | solution.py:57
  75.1 1.9 copy-done.12
  77.0 40.5 %attend.1 = (bf16[2048,256]{1,0:T(8,128)(2,1)S(1)}, bf16[4,2048,256]{2,1,0:T(8,128)(2,1)}, bf16[8,4,32,1024]{3,2,1,0:T(8,128)(2,1)S(1)}, bf16[8,128,1024]{2,1,0:...) custom-call(s32[1]{0:T(128)} %copy.183.length_ref, ...), custom_call_target="tpu_custom_call" | custom-call | flops 5033164800 | bytes 16777216 | tf_op jit(solution)/shard_map/attend/pallas_call | solution.py:401
  117.5 1.3 copy-done.6
  118.8 1.4 copy-done.7
  120.2 1.0 copy-done.8
  121.1 1.3 copy-done.14
  122.4 1.3 copy-done.16
  123.8 76.0 %mlp.1 = (f32[512,1024]{1,0:T(8,128)}, f32[512,1024]{1,0:T(8,128)}, f32[8,1024]{1,0:T(8,128)}, bf16[4,512,1024]{2,1,0:T(8,128)(2,1)}, bf16[4,512,1024]{2,1,0:T(8...) custom-call(s32[1]{0:T(128)} %copy.183.length_ref, bf16[2048,256]{1,0:T(8,128)(2,1)} %copy-done.8, ...), custom_call_target="tpu_custom_call" | custom-call | flops 30064771072 | bytes 33554432 | tf_op jit(solution)/shard_map/mlp/pallas_call | solution.py:1400
  199.8 2.7 dynamic-slice_bitcast_fusion.3
  202.9 1.4 collective-permute-start.4
  204.4 3.9 convolution_convert_fusion.2.dout_ref
  209.4 40.4 %attend_back.1 = (bf16[2048,768]{1,0:T(8,128)(2,1)S(1)}, f32[2,128,128]{2,1,0:T(8,128)S(1)}, f32[1,256]{1,0:T(1,128)S(1)}, f32[2,384,256]{2,1,0:T(8,128)S(1)}, f32[2,8,256]{2,1,0:T(8,128)S(1)}) custom-call(s32[1]{0:T(128)} %copy.183.length_ref, s32[4]{0:T(128)S(1)} %iota_xor_fusion.order_ref, bf16[2048,768]{1,0:T(8,128)(2,1)S(1)} %copy-done.13, ...), custom_call_target="tpu_custom_call" | custom-call | flops 12582912000 | bytes 20971520 | tf_op jit(solution)/shard_map/attend_back/pallas_call | solution.py:581
  249.8 1.5 slice_bitcast_fusion.1
  252.2 1.6 copy-done.79
  253.8 2.1 convolution_convert_fusion.4
  256.0 0.7 copy.168
  256.7 0.7 copy.169
  257.4 0.7 copy.170
  258.8 0.7 copy.172
  259.4 0.7 copy.173
  260.8 0.7 copy.175
  262.1 0.7 copy.177
  264.2 0.7 copy.180
  264.8 0.7 copy.181
  266.3 3.5 select_reduce_fusion
  271.5 0.9 copy.151
  272.4 0.9 copy.152
  273.3 0.9 copy.153
  274.3 0.9 copy.154
  275.2 0.9 copy.155
  276.1 0.9 copy.156
  277.1 0.9 copy.157
  278.0 0.9 copy.158
  278.9 0.9 copy.159
  279.9 0.9 copy.160
  280.8 0.9 copy.161
  281.7 0.9 copy.162
  282.6 0.9 copy.163
  283.6 0.9 copy.164
  284.5 1.9 select_reduce_fusion.18
  287.7 4.3 fusion.1
  292.2 5.5 %convolution_convert_fusion = bf16[2048,1024]{1,0:T(8,128)(2,1)} fusion(bf16[2048,768]{1,0:T(8,128)(2,1)S(1)} %copy-done.11, bf16[1024,768]{1,0:T(8,128)(2,1)S(1)} %bitcast.183), kind=kOutput, calls=%fused_computation.5 | convolution fusion | flops 3223322624 | bytes 8912896 | tf_op jit(solution)/shard_map/dot_general | solution.py:61
  297.8 7.9 %convolution_convert_fusion.3 = bf16[1024,768]{1,0:T(8,128)(2,1)} fusion(bf16[2048,1024]{1,0:T(8,128)(2,1)} %fusion.1, bf16[2048,768]{1,0:T(8,128)(2,1)} %copy-done.10), kind=kOutput, calls=%fused_computation.17 | convolution fusion | flops 3222011904 | bytes 8912896 | tf_op jit(solution)/shard_map/dot_general | solution.py:65
  305.7 2.6 fusion.2
  308.3 1.4 collective-permute-start.2
  310.4 1.6 pad_maximum_fusion
  312.2 1.6 pad_maximum_fusion.1
  313.8 115.9 %finish.1 = (f32[512,1024]{1,0:T(8,128)}, f32[4,32,768]{2,1,0:T(8,128)}, f32[4,32,1024]{2,1,0:T(8,128)}, f32[128,1024]{1,0:T(8,128)}, f32[32,1024]{1,0:T(8,128)}...) custom-call(bf16[4,512,1024]{2,1,0:T(8,128)(2,1)} %bitcast.130, bf16[4,8,32,768]{3,2,1,0:T(8,128)(2,1)} %bitcast.139, ...), custom_call_target="tpu_custom_call" | custom-call | tf_op jit(solution)/shard_map/finish/pallas_call | solution.py:1152
  429.7 1.6 slice.164
  431.4 1.2 slice.163
  432.6 1.2 slice.165
  433.8 1.1 copy.146
  435.4 1.0 reshape.265
  436.9 0.9 reshape.263
  438.5 3.8 fusion.7
  442.3 0.8 copy.184
  443.1 1.3 copy.185
  445.1 0.8 copy.187
  (228 shorter events, 14.7 us)
Async XLA Ops:
  0.6 73.9 %copy-start = (bf16[512,1024]{1,0:T(8,128)(2,1)S(1)}, bf16[512,1024]{1,0:T(8,128)(2,1)}, u32[]{:S(2)}) copy-start(bf16[512,1024]{1,0:T(8,128)(2,1)} %param.22) | copy-start | bytes 3145732
  61.2 4.4 copy-start.43
  61.2 4.4 copy-start.44
  69.3 5.3 %copy-start.45 = (pred[1024]{0:T(1024)(128)(4,1)S(1)}, pred[1024]{0:T(1024)(128)(4,1)}, u32[]{:S(2)}) copy-start(pred[1024]{0:T(1024)(128)(4,1)} %constant.172) | copy-start | bytes 3076
  69.3 5.3 %copy-start.46 = (pred[1024]{0:T(1024)(128)(4,1)S(1)}, pred[1024]{0:T(1024)(128)(4,1)}, u32[]{:S(2)}) copy-start(pred[1024]{0:T(1024)(128)(4,1)} %constant.173) | copy-start | bytes 3076
  69.3 5.3 %copy-start.47 = (pred[1024]{0:T(1024)(128)(4,1)S(1)}, pred[1024]{0:T(1024)(128)(4,1)}, u32[]{:S(2)}) copy-start(pred[1024]{0:T(1024)(128)(4,1)} %constant.174) | copy-start | bytes 3076
  69.3 5.3 %copy-start.48 = (pred[1024]{0:T(1024)(128)(4,1)S(1)}, pred[1024]{0:T(1024)(128)(4,1)}, u32[]{:S(2)}) copy-start(pred[1024]{0:T(1024)(128)(4,1)} %constant.175) | copy-start | bytes 3076
  69.3 5.3 %copy-start.49 = (pred[1024]{0:T(1024)(128)(4,1)S(1)}, pred[1024]{0:T(1024)(128)(4,1)}, u32[]{:S(2)}) copy-start(pred[1024]{0:T(1024)(128)(4,1)} %constant.176) | copy-start | bytes 3076
  69.3 5.3 %copy-start.50 = (pred[1024]{0:T(1024)(128)(4,1)S(1)}, pred[1024]{0:T(1024)(128)(4,1)}, u32[]{:S(2)}) copy-start(pred[1024]{0:T(1024)(128)(4,1)} %constant.177) | copy-start | bytes 3076
  69.3 5.3 %copy-start.51 = (pred[1024]{0:T(1024)(128)(4,1)S(1)}, pred[1024]{0:T(1024)(128)(4,1)}, u32[]{:S(2)}) copy-start(pred[1024]{0:T(1024)(128)(4,1)} %constant.178) | copy-start | bytes 3076
  69.4 5.3 %copy-start.52 = (pred[1024]{0:T(1024)(128)(4,1)S(1)}, pred[1024]{0:T(1024)(128)(4,1)}, u32[]{:S(2)}) copy-start(pred[1024]{0:T(1024)(128)(4,1)} %constant.179) | copy-start | bytes 3076
  69.4 5.3 %copy-start.53 = (pred[1024]{0:T(1024)(128)(4,1)S(1)}, pred[1024]{0:T(1024)(128)(4,1)}, u32[]{:S(2)}) copy-start(pred[1024]{0:T(1024)(128)(4,1)} %constant.180) | copy-start | bytes 3076
  69.4 5.3 %copy-start.54 = (pred[1024]{0:T(1024)(128)(4,1)S(1)}, pred[1024]{0:T(1024)(128)(4,1)}, u32[]{:S(2)}) copy-start(pred[1024]{0:T(1024)(128)(4,1)} %constant.181) | copy-start | bytes 3076
  69.4 5.3 %copy-start.55 = (pred[1024]{0:T(1024)(128)(4,1)S(1)}, pred[1024]{0:T(1024)(128)(4,1)}, u32[]{:S(2)}) copy-start(pred[1024]{0:T(1024)(128)(4,1)} %constant.182) | copy-start | bytes 3076
  69.4 5.3 %copy-start.56 = (pred[1024]{0:T(1024)(128)(4,1)S(1)}, pred[1024]{0:T(1024)(128)(4,1)}, u32[]{:S(2)}) copy-start(pred[1024]{0:T(1024)(128)(4,1)} %constant.183) | copy-start | bytes 3076
  69.4 5.3 %copy-start.57 = (pred[1024]{0:T(1024)(128)(4,1)S(1)}, pred[1024]{0:T(1024)(128)(4,1)}, u32[]{:S(2)}) copy-start(pred[1024]{0:T(1024)(128)(4,1)} %constant.27) | copy-start | bytes 3076
  69.4 5.3 %copy-start.58 = (pred[1024]{0:T(1024)(128)(4,1)S(1)}, pred[1024]{0:T(1024)(128)(4,1)}, u32[]{:S(2)}) copy-start(pred[1024]{0:T(1024)(128)(4,1)} %constant.28) | copy-start | bytes 3076
  69.5 5.2 %copy-start.59 = (pred[1024]{0:T(1024)(128)(4,1)S(1)}, pred[1024]{0:T(1024)(128)(4,1)}, u32[]{:S(2)}) copy-start(pred[1024]{0:T(1024)(128)(4,1)} %constant.29) | copy-start | bytes 3076
  69.5 5.2 %copy-start.60 = (pred[1024]{0:T(1024)(128)(4,1)S(1)}, pred[1024]{0:T(1024)(128)(4,1)}, u32[]{:S(2)}) copy-start(pred[1024]{0:T(1024)(128)(4,1)} %constant.30) | copy-start | bytes 3076
  69.5 5.2 %copy-start.61 = (pred[1024]{0:T(1024)(128)(4,1)S(1)}, pred[1024]{0:T(1024)(128)(4,1)}, u32[]{:S(2)}) copy-start(pred[1024]{0:T(1024)(128)(4,1)} %constant.31) | copy-start | bytes 3076
  69.5 5.2 %copy-start.62 = (pred[1024]{0:T(1024)(128)(4,1)S(1)}, pred[1024]{0:T(1024)(128)(4,1)}, u32[]{:S(2)}) copy-start(pred[1024]{0:T(1024)(128)(4,1)} %constant.32) | copy-start | bytes 3076
  69.5 5.2 %copy-start.63 = (pred[1024]{0:T(1024)(128)(4,1)S(1)}, pred[1024]{0:T(1024)(128)(4,1)}, u32[]{:S(2)}) copy-start(pred[1024]{0:T(1024)(128)(4,1)} %constant.33) | copy-start | bytes 3076
  69.5 5.2 %copy-start.64 = (pred[1024]{0:T(1024)(128)(4,1)S(1)}, pred[1024]{0:T(1024)(128)(4,1)}, u32[]{:S(2)}) copy-start(pred[1024]{0:T(1024)(128)(4,1)} %constant.34) | copy-start | bytes 3076
  69.5 5.2 %copy-start.65 = (pred[1024]{0:T(1024)(128)(4,1)S(1)}, pred[1024]{0:T(1024)(128)(4,1)}, u32[]{:S(2)}) copy-start(pred[1024]{0:T(1024)(128)(4,1)} %constant.35) | copy-start | bytes 3076
  69.5 5.2 %copy-start.66 = (pred[1024]{0:T(1024)(128)(4,1)S(1)}, pred[1024]{0:T(1024)(128)(4,1)}, u32[]{:S(2)}) copy-start(pred[1024]{0:T(1024)(128)(4,1)} %constant.36) | copy-start | bytes 3076
  69.6 5.2 %copy-start.67 = (pred[1024]{0:T(1024)(128)(4,1)S(1)}, pred[1024]{0:T(1024)(128)(4,1)}, u32[]{:S(2)}) copy-start(pred[1024]{0:T(1024)(128)(4,1)} %constant.37) | copy-start | bytes 3076
  69.6 5.2 %copy-start.68 = (pred[1024]{0:T(1024)(128)(4,1)S(1)}, pred[1024]{0:T(1024)(128)(4,1)}, u32[]{:S(2)}) copy-start(pred[1024]{0:T(1024)(128)(4,1)} %constant.38) | copy-start | bytes 3076
  69.6 5.2 %copy-start.69 = (pred[1024]{0:T(1024)(128)(4,1)S(1)}, pred[1024]{0:T(1024)(128)(4,1)}, u32[]{:S(2)}) copy-start(pred[1024]{0:T(1024)(128)(4,1)} %constant.39) | copy-start | bytes 3076
  69.6 5.2 %copy-start.70 = (pred[1024]{0:T(1024)(128)(4,1)S(1)}, pred[1024]{0:T(1024)(128)(4,1)}, u32[]{:S(2)}) copy-start(pred[1024]{0:T(1024)(128)(4,1)} %constant.40) | copy-start | bytes 3076
  69.6 5.2 %copy-start.71 = (pred[1024]{0:T(1024)(128)(4,1)S(1)}, pred[1024]{0:T(1024)(128)(4,1)}, u32[]{:S(2)}) copy-start(pred[1024]{0:T(1024)(128)(4,1)} %constant.41) | copy-start | bytes 3076
  69.6 5.2 %copy-start.72 = (pred[1024]{0:T(1024)(128)(4,1)S(1)}, pred[1024]{0:T(1024)(128)(4,1)}, u32[]{:S(2)}) copy-start(pred[1024]{0:T(1024)(128)(4,1)} %constant.42) | copy-start | bytes 3076
  69.6 5.2 %copy-start.73 = (pred[1024]{0:T(1024)(128)(4,1)S(1)}, pred[1024]{0:T(1024)(128)(4,1)}, u32[]{:S(2)}) copy-start(pred[1024]{0:T(1024)(128)(4,1)} %constant.43) | copy-start | bytes 3076
  69.6 5.2 %copy-start.74 = (pred[1024]{0:T(1024)(128)(4,1)S(1)}, pred[1024]{0:T(1024)(128)(4,1)}, u32[]{:S(2)}) copy-start(pred[1024]{0:T(1024)(128)(4,1)} %constant.44) | copy-start | bytes 3076
  69.7 5.2 %copy-start.75 = (pred[1024]{0:T(1024)(128)(4,1)S(1)}, pred[1024]{0:T(1024)(128)(4,1)}, u32[]{:S(2)}) copy-start(pred[1024]{0:T(1024)(128)(4,1)} %constant.45) | copy-start | bytes 3076
  69.7 5.2 %copy-start.76 = (pred[1024]{0:T(1024)(128)(4,1)S(1)}, pred[1024]{0:T(1024)(128)(4,1)}, u32[]{:S(2)}) copy-start(pred[1024]{0:T(1024)(128)(4,1)} %constant.46) | copy-start | bytes 3076
  69.7 5.4 %copy-start.2 = (bf16[8,32,1024]{2,1,0:T(8,128)(2,1)S(1)}, bf16[8,32,1024]{2,1,0:T(8,128)(2,1)}, u32[]{:S(2)}) copy-start(bf16[8,32,1024]{2,1,0:T(8,128)(2,1)} %get-tuple-element.52.own_out_ref) | copy-start | bytes 1572868
  69.7 5.4 %copy-start.3 = (bf16[1,512,256]{2,1,0:T(8,128)(2,1)S(1)}, bf16[1,512,256]{2,1,0:T(8,128)(2,1)}, u32[]{:S(2)}) copy-start(bf16[1,512,256]{2,1,0:T(8,128)(2,1)} %param.18) | copy-start | bytes 786436
  69.7 5.4 %copy-start.5 = (bf16[2,128,128]{2,1,0:T(8,128)(2,1)S(1)}, bf16[2,128,128]{2,1,0:T(8,128)(2,1)}, u32[]{:S(2)}) copy-start(bf16[2,128,128]{2,1,0:T(8,128)(2,1)} %query_ref.3) | copy-start | bytes 196612
  202.5 107.9 %collective-permute-start.3 = (bf16[1,2,128,1024]{3,2,0,1:T(8,128)(2,1)}, bf16[1,2,128,1024]{3,2,0,1:T(8,128)(2,1)}, u32[]{:S(2)}, u32[]{:S(2)}) collective-permute-start(bf16[1,2,128,1024]{3,2,0,1:T(8,128)(2,1)} %get-tuple-element.158), channel_id=1, source_target_pairs={{0,8},{8,0},{16,24},{24,16},{1,9},{9,1},{17,25},{25,17},{2,10},{10... | collective-permute-start | bytes 1572872 | tf_op jit(solution)/shard_map/ppermute | solution.py:1442
  202.9 107.5 %collective-permute-start.4 = (bf16[1,2,128,1024]{3,2,0,1:T(8,128)(2,1)}, bf16[1,2,128,1024]{3,2,0,1:T(8,128)(2,1)}, u32[]{:S(2)}, u32[]{:S(2)}) collective-permute-start(bf16[1,2,128,1024]{3,2,0,1:T(8,128)(2,1)} %get-tuple-element.157), channel_id=1, source_target_pairs={{0,16},{8,24},{16,0},{24,8},{1,17},{9,25},{17,1},{25,9},{2,18},{10... | collective-permute-start | bytes 1572872 | tf_op jit(solution)/shard_map/ppermute | solution.py:1442
  204.3 106.1 %collective-permute-start.5 = (bf16[1,2,128,1024]{3,2,0,1:T(8,128)(2,1)}, bf16[1,2,128,1024]{3,2,0,1:T(8,128)(2,1)}, u32[]{:S(2)}, u32[]{:S(2)}) collective-permute-start(bf16[1,2,128,1024]{3,2,0,1:T(8,128)(2,1)} %get-tuple-element.159), channel_id=1, source_target_pairs={{0,24},{8,16},{16,8},{24,0},{1,25},{9,17},{17,9},{25,1},{2,26},{10... | collective-permute-start | bytes 1572872 | tf_op jit(solution)/shard_map/ppermute | solution.py:1442
  204.4 5.0 %copy-start.17 = (f32[4,512,256]{2,1,0:T(8,128)S(1)}, f32[4,512,256]{2,1,0:T(8,128)}, u32[]{:S(2)}) copy-start(f32[4,512,256]{2,1,0:T(8,128)} %copy-done.16) | copy-start | bytes 6291460
  209.4 40.4 %copy-start.18 = (bf16[4,512,1024]{2,1,0:T(8,128)(2,1)S(1)}, bf16[4,512,1024]{2,1,0:T(8,128)(2,1)}, u32[]{:S(2)}) copy-start(bf16[4,512,1024]{2,1,0:T(8,128)(2,1)} %get-tuple-element.68) | copy-start | bytes 12582916
  249.7 6.1 %copy-start.10 = (bf16[2048,768]{1,0:T(8,128)(2,1)}, bf16[2048,768]{1,0:T(8,128)(2,1)S(1)}, u32[]{:S(2)}) copy-start(bf16[2048,768]{1,0:T(8,128)(2,1)S(1)} %get-tuple-element.70) | copy-start | bytes 9437188
  251.2 54.4 %collective-permute-start.1 = (bf16[512,1024]{1,0:T(8,128)(2,1)}, bf16[512,1024]{1,0:T(8,128)(2,1)S(1)}, u32[]{:S(2)}, u32[]{:S(2)}) collective-permute-start(bf16[512,1024]{1,0:T(8,128)(2,1)} %get-tuple-element.151), channel_id=1, source_target_pairs={{0,8},{8,0},{16,24},{24,16},{1,9},{9,1},{17,25},{25,17},{2,10},{10... | collective-permute-start | bytes 3145736 | tf_op jit(solution)/shard_map/ppermute | solution.py:1442
  251.9 4.8 %copy-start.36 = (pred[384,256]{1,0:T(32,128)(4,1)S(1)}, pred[384,256]{1,0:T(32,128)(4,1)}, u32[]{:S(2)}) copy-start(pred[384,256]{1,0:T(32,128)(4,1)} %constant.211) | copy-start | bytes 294916
  251.9 5.5 %copy-start.35 = (pred[384,256]{1,0:T(32,128)(4,1)S(1)}, pred[384,256]{1,0:T(32,128)(4,1)}, u32[]{:S(2)}) copy-start(pred[384,256]{1,0:T(32,128)(4,1)} %constant.210) | copy-start | bytes 294916
  251.9 6.1 %copy-start.34 = (pred[384,256]{1,0:T(32,128)(4,1)S(1)}, pred[384,256]{1,0:T(32,128)(4,1)}, u32[]{:S(2)}) copy-start(pred[384,256]{1,0:T(32,128)(4,1)} %constant.209) | copy-start | bytes 294916
  252.0 6.8 %copy-start.33 = (pred[384,256]{1,0:T(32,128)(4,1)S(1)}, pred[384,256]{1,0:T(32,128)(4,1)}, u32[]{:S(2)}) copy-start(pred[384,256]{1,0:T(32,128)(4,1)} %constant.208) | copy-start | bytes 294916
  252.0 7.5 %copy-start.32 = (pred[384,256]{1,0:T(32,128)(4,1)S(1)}, pred[384,256]{1,0:T(32,128)(4,1)}, u32[]{:S(2)}) copy-start(pred[384,256]{1,0:T(32,128)(4,1)} %constant.207) | copy-start | bytes 294916
  252.0 8.1 %copy-start.31 = (pred[384,256]{1,0:T(32,128)(4,1)S(1)}, pred[384,256]{1,0:T(32,128)(4,1)}, u32[]{:S(2)}) copy-start(pred[384,256]{1,0:T(32,128)(4,1)} %constant.206) | copy-start | bytes 294916
  252.0 8.8 %copy-start.30 = (pred[384,256]{1,0:T(32,128)(4,1)S(1)}, pred[384,256]{1,0:T(32,128)(4,1)}, u32[]{:S(2)}) copy-start(pred[384,256]{1,0:T(32,128)(4,1)} %constant.205) | copy-start | bytes 294916
  252.0 9.5 %copy-start.29 = (pred[384,256]{1,0:T(32,128)(4,1)S(1)}, pred[384,256]{1,0:T(32,128)(4,1)}, u32[]{:S(2)}) copy-start(pred[384,256]{1,0:T(32,128)(4,1)} %constant.204) | copy-start | bytes 294916
  252.0 10.1 %copy-start.28 = (pred[384,256]{1,0:T(32,128)(4,1)S(1)}, pred[384,256]{1,0:T(32,128)(4,1)}, u32[]{:S(2)}) copy-start(pred[384,256]{1,0:T(32,128)(4,1)} %constant.203) | copy-start | bytes 294916
  252.0 10.8 %copy-start.27 = (pred[384,256]{1,0:T(32,128)(4,1)S(1)}, pred[384,256]{1,0:T(32,128)(4,1)}, u32[]{:S(2)}) copy-start(pred[384,256]{1,0:T(32,128)(4,1)} %constant.202) | copy-start | bytes 294916
  252.0 11.4 %copy-start.26 = (pred[384,256]{1,0:T(32,128)(4,1)S(1)}, pred[384,256]{1,0:T(32,128)(4,1)}, u32[]{:S(2)}) copy-start(pred[384,256]{1,0:T(32,128)(4,1)} %constant.201) | copy-start | bytes 294916
  252.1 12.1 %copy-start.25 = (pred[384,256]{1,0:T(32,128)(4,1)S(1)}, pred[384,256]{1,0:T(32,128)(4,1)}, u32[]{:S(2)}) copy-start(pred[384,256]{1,0:T(32,128)(4,1)} %constant.200) | copy-start | bytes 294916
  252.1 186.4 %collective-permute-start = (bf16[512,1024]{1,0:T(8,128)(2,1)}, bf16[512,1024]{1,0:T(8,128)(2,1)}, u32[]{:S(2)}, u32[]{:S(2)}) collective-permute-start(bf16[512,1024]{1,0:T(8,128)(2,1)} %get-tuple-element.150), channel_id=1, source_target_pairs={{0,8},{8,0},{16,24},{24,16},{1,9},{9,1},{17,25},{25,17},{2,10},{10... | collective-permute-start | bytes 3145736 | tf_op jit(solution)/shard_map/ppermute | solution.py:1442
  255.9 9.0 %copy-start.24 = (pred[384,256]{1,0:T(32,128)(4,1)S(1)}, pred[384,256]{1,0:T(32,128)(4,1)}, u32[]{:S(2)}) copy-start(pred[384,256]{1,0:T(32,128)(4,1)} %constant.199) | copy-start | bytes 294916
  255.9 9.6 %copy-start.23 = (pred[384,256]{1,0:T(32,128)(4,1)S(1)}, pred[384,256]{1,0:T(32,128)(4,1)}, u32[]{:S(2)}) copy-start(pred[384,256]{1,0:T(32,128)(4,1)} %constant.198) | copy-start | bytes 294916
  287.7 4.5 %copy-start.78 = (bf16[8,128,768]{2,1,0:T(8,128)(2,1)S(1)}, bf16[8,128,768]{2,1,0:T(8,128)(2,1)}, u32[]{:S(2)}) copy-start(bf16[8,128,768]{2,1,0:T(8,128)(2,1)} %get-tuple-element.51) | copy-start | bytes 4718596
  308.3 130.2 %collective-permute-start.2 = (bf16[512,1024]{1,0:T(8,128)(2,1)}, bf16[512,1024]{1,0:T(8,128)(2,1)S(1)}, u32[]{:S(2)}, u32[]{:S(2)}) collective-permute-start(bf16[512,1024]{1,0:T(8,128)(2,1)} %fusion.2), channel_id=1, source_target_pairs={{0,16},{8,24},{16,0},{24,8},{1,17},{9,25},{17,1},{25,9},{2,18},{10... | collective-permute-start | bytes 3145736 | tf_op jit(solution)/shard_map/ppermute | solution.py:1442
  429.7 6.7 %copy-start.21 = (f32[4,32,768]{2,1,0:T(8,128)S(1)}, f32[4,32,768]{2,1,0:T(8,128)}, u32[]{:S(2)}) copy-start(f32[4,32,768]{2,1,0:T(8,128)} %get-tuple-element.80) | copy-start | bytes 1179652
  438.5 4.6 %copy-start.19 = (f32[512,1024]{1,0:T(8,128)S(1)}, f32[512,1024]{1,0:T(8,128)}, u32[]{:S(2)}) copy-start(f32[512,1024]{1,0:T(8,128)} %get-tuple-element.79) | copy-start | bytes 6291460
  (22 other events, 66.4 us)

commit v7 on v6

--- a/solution.py
+++ b/solution.py
@@ -431,199 +431,460 @@
     )(length, qkv, init, state_query, forget, bias, own_out, own_down)
 
 
-def attend_back_kernel(
-    heads,
-    blocks,
-    length_ref,
-    order_ref,
-    cur_ref,
-    prev_ref,
-    dout_ref,
-    out_ref,
-    mem_ref,
-    upd_ref,
-    lse_ref,
-    slse_ref,
-    sgrad_ref,
-    query_ref,
-    forget_ref,
-    vector_ref,
-    dqkv_ref,
-    dquery_ref,
-    dforget_ref,
-    near_ref,
-    far_ref,
-    dmem_ref,
-    dnext_ref,
-    dctx_ref,
-    bias_ref,
-):
-    step = pl.program_id(0)
-    block = blocks - 1 - step
+def line_reduce(hi, lo, block, total, from_y, from_z, z_send, z_recv, y_send, y_recv):
+    f = lax.axis_index("fsdp")
+    z, y = f // lo, f % lo
+
+    def remote(src, dst, send, recv, target):
+        return pltpu.make_async_remote_copy(
+            src_ref=src, dst_ref=dst, send_sem=send, recv_sem=recv, device_id={"fsdp": target}, device_id_type=MESH
+        )
+
+    def across(i, d):
+        return remote(
+            block(i, d * lo + 1 - y), from_y[i].at[d], y_send.at[i, d], y_recv.at[i, d], z * lo + 1 - y
+        )
+
+    def start(i):
+        for d in range(hi):
+            across(i, d).start()
+
+    def combine(i):
+        for d in range(hi):
+            across(i, d).wait_recv()
+            own = block(i, d * lo + y)
+            total[i][d] = (own[...].astype(f32) + from_y[i][d].astype(f32)).astype(bf16)
+
+    def hop(i, side, t, at, target):
+        return remote(
+            total[i].at[jnp.clip(at, 0, hi - 1)],
+            from_z[i].at[side, t],
+            z_send.at[i, side, t],
+            z_recv.at[i, side, t],
+            target,
+        )
+
+    def sending(t):
+        d = t - (hi - 1 - z)
+        m = hi - 1 - (t - z)
+        return ((0, d, (d >= 0) & (d < z), z - 1), (1, m, (m > z) & (m < hi), z + 1))
+
+    def zsend(i, t):
+        for side, at, cond, target in sending(t):
+            pl.when(cond)(lambda: hop(i, side, t, at, target * lo + y).start())
+
+    def zrecv(i, t):
+        d = t - (hi - 2 - z)
+        m = hi - 1 - (t - (z - 1))
+        for side, at, cond in ((0, d, (z + 1 < hi) & (d >= 0)), (1, m, (z > 0) & (m < hi))):
+
+            @pl.when(cond)
+            def _():
+                hop(i, side, t, at, f).wait_recv()
+                slot = jnp.clip(at, 0, hi - 1)
+                total[i][slot] = (total[i][slot].astype(f32) + from_z[i][side, t].astype(f32)).astype(bf16)
+
+    def drain_y(i):
+        for d in range(hi):
+            across(i, d).wait_send()
+
+    def drain_z(i):
+        for t in range(hi - 1):
+            for side, at, cond, target in sending(t):
+                pl.when(cond)(lambda: hop(i, side, t, at, f).wait_send())
+
+    return start, combine, zsend, zrecv, drain_y, drain_z
+
+
+def seq_levels(seq):
+    bits = [1 << i for i in range(seq.bit_length() - 1)]
+    slots = {}
+    for bit in bits:
+        for j in range(0, seq, 2 * bit):
+            slots[bit, j] = len(slots)
+    return bits, slots
+
+
+def diagonal_sums(tile):
+    rows, lanes = tile.shape
+    wide = jnp.concatenate([tile, jnp.zeros((rows, lanes), f32)], axis=1)
+    row = lax.broadcasted_iota(jnp.int32, wide.shape, 0)
+    bit = 1
+    while bit < rows:
+        wide = jnp.where((row & bit) != 0, pltpu.roll(wide, 2 * lanes - bit, 1), wide)
+        bit *= 2
+    return jnp.sum(wide, axis=0, keepdims=True)
+
+
+def attend_back_kernel(heads, seq, hi, lo, inside, length_ref, *refs):
+    refs = list(refs)
+
+    def take(count):
+        taken = refs[:count]
+        del refs[:count]
+        return taken
+
+    qkv_ref, db_ref, wout_ref, att_ref, mem_ref, upd_ref, lse_ref, slse_ref = take(8)
+    sgrad_ref, query_ref, forget_ref, vector_ref, up_ref, down_ref, mo_ref, mid_ref = take(8)
+    ow_in = None if inside else take(1)[0]
+    dqkv_ref, small_ref, upart_ref, dtotal_ref, opart_ref, output_ref = take(6)
+    dmem_ref, dnext_ref, dctx_ref, bias_ref, near_ref, far_ref, dout_ref, ow_buf = take(8)
+    moved, to, tu, yo, yu, yd, zo, zu, xu, mo_low, mo_in = take(11)
+    z_send, z_recv, y_send, y_recv, m_send, m_recv, e_send, e_recv, x_send, x_recv = take(10)
+    ow_ref = ow_buf if inside else ow_in
+
+    me = lax.axis_index("seq")
+    f = lax.axis_index("fsdp")
+    z, y = f // lo, f % lo
+    blocks = seq
     length = length_ref[0]
     width = heads * DH
     scale2 = SCALE * LOG2E
-
-    @pl.when(step == 0)
-    def _():
-        dmem_ref[...] = sgrad_ref[...].astype(f32)
-        dnext_ref[...] = jnp.zeros_like(dnext_ref)
-        dquery_ref[...] = jnp.zeros_like(dquery_ref)
-        dforget_ref[...] = jnp.zeros_like(dforget_ref)
-        near_ref[...] = jnp.zeros_like(near_ref)
-        far_ref[...] = jnp.zeros_like(far_ref)
+    tok_rows = mid_ref.shape[0]
+    share = dtotal_ref.shape[1]
+    bits, slots = seq_levels(seq)
+    greet(list(range(1, seq)), hi, lo)
+
+    def mo_copy(bit, j):
+        slot = slots[bit, j]
+        return pltpu.make_async_remote_copy(
+            src_ref=mo_ref.at[j ^ bit] if bit == 1 else mo_low.at[(j ^ bit) // 2],
+            dst_ref=mo_in.at[slot],
+            send_sem=m_send.at[slot],
+            recv_sem=m_recv.at[slot],
+            device_id={"seq": me ^ bit},
+            device_id_type=MESH,
+        )
+
+    def move_copy(k):
+        return pltpu.make_async_remote_copy(
+            src_ref=down_ref.at[me ^ k],
+            dst_ref=moved.at[me],
+            send_sem=e_send.at[k],
+            recv_sem=e_recv.at[k],
+            device_id={"seq": me ^ k},
+            device_id_type=MESH,
+        )
+
+    def move_arrival(k):
+        return pltpu.make_async_remote_copy(
+            src_ref=down_ref.at[me],
+            dst_ref=moved.at[me ^ k],
+            send_sem=e_send.at[k],
+            recv_sem=e_recv.at[k],
+            device_id={"seq": me},
+            device_id_type=MESH,
+        )
+
+    def block_of(i, target):
+        if i == 0:
+            return ow_ref.at[target]
+        if i == 1:
+            return up_ref.at[:, target]
+        return moved.at[target % seq, pl.ds(pl.multiple_of((target // seq) * share, share), share)]
+
+    start, combine, zsend, zrecv, drain_y, drain_z = line_reduce(
+        hi, lo, block_of, (to, tu, dtotal_ref), (yo, yu, yd), (zo, zu), z_send, z_recv, y_send, y_recv
+    )
+
+    def exchange(k, sending):
+        return pltpu.make_async_remote_copy(
+            src_ref=tu.at[z, me ^ k] if sending else tu.at[z, me],
+            dst_ref=xu.at[me] if sending else xu.at[me ^ k],
+            send_sem=x_send.at[k],
+            recv_sem=x_recv.at[k],
+            device_id={"seq": me ^ k if sending else me},
+            device_id_type=MESH,
+        )
+
+    for j in range(seq - 1, 0, -2):
+        mo_copy(1, j ^ 1).start()
+    for k in reversed(range(1, seq)):
+        move_copy(k).start()
+    moved[me] = down_ref[me]
+    if inside:
+        full = t_dot(att_ref[...], db_ref[...]).astype(bf16)
+        ow_buf[...] = full.reshape(ow_buf.shape)
+    start(0)
+    start(1)
+
+    dmem_ref[...] = sgrad_ref[...].astype(f32)
+    dnext_ref[...] = jnp.zeros_like(dnext_ref)
+    small_ref[...] = jnp.zeros_like(small_ref)
+    near_ref[...] = jnp.zeros_like(near_ref)
+    far_ref[...] = jnp.zeros_like(far_ref)
+    for head in range(heads):
+        bias_ref[head] = tile_bias(vector_ref, head).T
+
+    def mo_step(j):
+        for bit in bits:
+            if j & bit:
+                mo_copy(bit, j ^ bit).start()
+                break
+            mo_copy(bit, j).wait_recv()
+            own = mo_ref[j] if bit == 1 else mo_low[j // 2]
+            mo_low[j // 2] = (own.astype(f32) + mo_in[slots[bit, j]].astype(f32)).astype(bf16)
+
+    def down_ready():
+        for k in range(1, seq):
+            move_arrival(k).wait_recv()
+        start(2)
+
+    def up_done():
+        for k in range(1, seq):
+            exchange(k, True).start()
+
+    jobs = [lambda j=j: mo_step(j) for j in range(seq - 2, 0, -2)]
+    jobs.append(lambda: (combine(0), zsend(0, 0)))
+    for t in range(hi - 2):
+        jobs.append(lambda t=t: (zrecv(0, t), zsend(0, t + 1)))
+    jobs.append(lambda: (zrecv(0, hi - 2), down_ready()))
+    jobs.append(lambda: (combine(1), zsend(1, 0)))
+    for t in range(hi - 2):
+        jobs.append(lambda t=t: (zrecv(1, t), zsend(1, t + 1)))
+    jobs.append(lambda: (zrecv(1, hi - 2), up_done()))
+    points = blocks * heads - 1
+
+    dq_row = heads * DH
+
+    @pl.loop(0, blocks)
+    def _(step):
+        block = blocks - 1 - step
+        cur_at = pl.multiple_of((block ^ me) * BLOCK, BLOCK)
+        prev_at = pl.multiple_of((jnp.maximum(block - 1, 0) ^ me) * BLOCK, BLOCK)
+        base = pl.multiple_of(block * BLOCK, BLOCK)
+        cur_ref = qkv_ref.at[pl.ds(cur_at, BLOCK)]
+        prev_ref = qkv_ref.at[pl.ds(prev_at, BLOCK)]
+        live_block = block * BLOCK < length
+        refs = (prev_ref, cur_ref)
+        dout_ref[...] = dot_t(db_ref[pl.ds(cur_at, BLOCK)], wout_ref[...]).astype(bf16)
         for head in range(heads):
-            bias_ref[head] = tile_bias(vector_ref, head).T
-
-    live_block = block * BLOCK < length
-    refs = (prev_ref, cur_ref)
-    for head in range(heads):
-        own = slice(head * DH, (head + 1) * DH)
-        key_cols = slice(width + head * DH, width + (head + 1) * DH)
-        value_cols = slice(2 * width + head * DH, 2 * width + (head + 1) * DH)
-        memory = mem_ref[0, :, own]
-        update = upd_ref[0, :, own]
-        low = memory.astype(bf16)
-        forget = forget_ref[:, own]
-        dmem = dmem_ref[:, own]
-        dupd = jnp.where(live_block, (1.0 - forget) * dmem, 0.0).astype(bf16)
-        moved = jnp.where(live_block, dmem * (memory - update), 0.0)
-        dforget_ref[:, own] += jnp.sum(moved, axis=0, keepdims=True)
-        dmem_new = jnp.where(live_block, forget * dmem, dmem)
-        own_key = cur_ref[:, key_cols]
-        own_value = cur_ref[:, value_cols]
-        squeries = dot(low, query_ref[head]).astype(bf16)
-        sdelta = jnp.sum((dupd.astype(f32) * update).T, axis=0, keepdims=True)
-        slse = slse_ref[head : head + 1, :]
-        dsquery = jnp.zeros((STATE_VECTORS, DH), f32)
-        dkey = []
-        dvalue = []
-        for part in range(2 * STATE_VECTORS // QTILE):
-            own_part = part >= STATE_VECTORS // QTILE
-            lo = (part % (STATE_VECTORS // QTILE)) * QTILE
-            keys = (own_key if own_part else low)[lo : lo + QTILE]
-            values = (own_value if own_part else low)[lo : lo + QTILE]
-            s = dot_t(keys, squeries) * scale2 - slse
-            if own_part:
-                position = block * BLOCK + lo + lax.broadcasted_iota(jnp.int32, (QTILE, 1), 0)
-                s = jnp.where(position < length, s, -jnp.inf)
-            p = jnp.exp2(s)
-            dp = dot_t(values, dupd)
-            ds = (p * (dp - sdelta)).astype(bf16)
-            dvalue.append(dot(p.astype(bf16), dupd))
-            dkey.append(dot(ds, squeries))
-            dsquery += t_dot(ds, keys)
-        half = STATE_VECTORS // QTILE
-        dlow = [dvalue[i] + dkey[i] * SCALE for i in range(half)]
-        dctx_ref[0, 0:BLOCK] = jnp.zeros((BLOCK, DH), f32)
-        dctx_ref[1, 0:BLOCK] = jnp.zeros((BLOCK, DH), f32)
-        for i in range(half):
-            rows = slice(BLOCK + i * QTILE, BLOCK + (i + 1) * QTILE)
-            old = slice(i * QTILE, (i + 1) * QTILE)
-            dctx_ref[0, rows] = dkey[half + i] * SCALE + dnext_ref[0, old, own]
-            dctx_ref[1, rows] = dvalue[half + i] + dnext_ref[1, old, own]
-        dsq = (dsquery * SCALE).astype(bf16)
-        dquery_ref[head] += t_dot(low, dsq)
-        dmem_ref[:, own] = dmem_new + dot_t(dsq, query_ref[head])
-        for tile in range(BLOCK // QTILE):
-            rows = slice(tile * QTILE, (tile + 1) * QTILE)
-            query = cur_ref[rows, own]
-            dout = dout_ref[rows, own]
-            lse = lse_ref[head : head + 1, rows]
-            delta = jnp.sum((dout.astype(f32) * out_ref[rows, own].astype(f32)).T, axis=0, keepdims=True)
-            dq = jnp.zeros((QTILE, DH), f32)
-            for which, lo, hi, col in context_pieces(tile):
-                for at in range(lo, hi, QTILE):
-                    keys = refs[which][at : at + QTILE, key_cols]
-                    values = refs[which][at : at + QTILE, value_cols]
-                    band = col + at - lo
-                    position = (block - 1 + which) * BLOCK + at + lax.broadcasted_iota(jnp.int32, (QTILE, 1), 0)
-                    live = (position >= 0) & (position < length)
-                    s = dot_t(keys, query) * scale2 + bias_ref[head, band : band + QTILE, :] - lse
-                    p = jnp.exp2(jnp.where(live, s, -jnp.inf))
-                    dp = dot_t(values, dout)
-                    ds = (p * (dp - delta)).astype(bf16)
-                    wide = ds.astype(f32)
-                    if band + QTILE <= SPAN - NEAR:
-                        far_ref[head] += functools.reduce(jnp.add, [wide[i : i + 8] for i in range(0, QTILE, 8)])
-                    else:
-                        edge = max(SPAN - NEAR - band, 0)
+            for n, job in enumerate(jobs[:points]):
+                if (n + 1) % heads == head:
+                    pl.when(step == (n + 1) // heads)(lambda job=job: (job(), None)[1])
+            own = slice(head * DH, (head + 1) * DH)
+            key_cols = slice(width + head * DH, width + (head + 1) * DH)
+            value_cols = slice(2 * width + head * DH, 2 * width + (head + 1) * DH)
+            memory = mem_ref[block, :, own]
+            update = upd_ref[block, :, own]
+            low = memory.astype(bf16)
+            forget = forget_ref[:, own]
+            dmem = dmem_ref[:, own]
+            dupd = jnp.where(live_block, (1.0 - forget) * dmem, 0.0).astype(bf16)
+            gone = jnp.where(live_block, dmem * (memory - update), 0.0)
+            small_ref[dq_row + head : dq_row + head + 1, :] += jnp.sum(gone, axis=0, keepdims=True)
+            dmem_new = jnp.where(live_block, forget * dmem, dmem)
+            own_key = cur_ref[:, key_cols]
+            own_value = cur_ref[:, value_cols]
+            squeries = dot(low, query_ref[head]).astype(bf16)
+            sdelta = jnp.sum((dupd.astype(f32) * update).T, axis=0, keepdims=True)
+            slse = slse_ref[head : head + 1, pl.ds(base, BLOCK)]
+            dsquery = jnp.zeros((STATE_VECTORS, DH), f32)
+            dkey = []
+            dvalue = []
+            for part in range(2 * STATE_VECTORS // QTILE):
+                own_part = part >= STATE_VECTORS // QTILE
+                at = (part % (STATE_VECTORS // QTILE)) * QTILE
+                keys = (own_key if own_part else low)[at : at + QTILE]
+                values = (own_value if own_part else low)[at : at + QTILE]
+                s = dot_t(keys, squeries) * scale2 - slse
+                if own_part:
+                    position = block * BLOCK + at + lax.broadcasted_iota(jnp.int32, (QTILE, 1), 0)
+                    s = jnp.where(position < length, s, -jnp.inf)
+                p = jnp.exp2(s)
+                dp = dot_t(values, dupd)
+                ds = (p * (dp - sdelta)).astype(bf16)
+                dvalue.append(dot(p.astype(bf16), dupd))
+                dkey.append(dot(ds, squeries))
+                dsquery += t_dot(ds, keys)
+            half = STATE_VECTORS // QTILE
+            dlow = [dvalue[i] + dkey[i] * SCALE for i in range(half)]
+            dctx_ref[0, 0:BLOCK] = jnp.zeros((BLOCK, DH), f32)
+            dctx_ref[1, 0:BLOCK] = jnp.zeros((BLOCK, DH), f32)
+            for i in range(half):
+                rows = slice(BLOCK + i * QTILE, BLOCK + (i + 1) * QTILE)
+                old = slice(i * QTILE, (i + 1) * QTILE)
+                dctx_ref[0, rows] = dkey[half + i] * SCALE + dnext_ref[0, old, own]
+                dctx_ref[1, rows] = dvalue[half + i] + dnext_ref[1, old, own]
+            dsq = (dsquery * SCALE).astype(bf16)
+            small_ref[head * DH : (head + 1) * DH, :] += t_dot(low, dsq)
+            dmem_ref[:, own] = dmem_new + dot_t(dsq, query_ref[head])
+            for tile in range(BLOCK // QTILE):
+                rows = slice(tile * QTILE, (tile + 1) * QTILE)
+                here = pl.ds(cur_at + tile * QTILE, QTILE)
+                query = cur_ref[rows, own]
+                dout = dout_ref[rows, own]
+                lse = lse_ref[head : head + 1, pl.ds(base + tile * QTILE, QTILE)]
+                delta = jnp.sum((dout.astype(f32) * att_ref[here, own].astype(f32)).T, axis=0, keepdims=True)
+                dq = jnp.zeros((QTILE, DH), f32)
+                for which, first, end, col in context_pieces(tile):
+                    for at in range(first, end, QTILE):
+                        keys = refs[which][at : at + QTILE, key_cols]
+                        values = refs[which][at : at + QTILE, value_cols]
+                        band = col + at - first
+                        position = (block - 1 + which) * BLOCK + at + lax.broadcasted_iota(jnp.int32, (QTILE, 1), 0)
+                        live = (position >= 0) & (position < length)
+                        s = dot_t(keys, query) * scale2 + bias_ref[head, band : band + QTILE, :] - lse
+                        p = jnp.exp2(jnp.where(live, s, -jnp.inf))
+                        dp = dot_t(values, dout)
+                        ds = (p * (dp - delta)).astype(bf16)
+                        wide = ds.astype(f32)
+                        edge = min(max(SPAN - NEAR - band, 0), QTILE)
                         if edge:
                             far_ref[head] += functools.reduce(jnp.add, [wide[i : i + 8] for i in range(0, edge, 8)])
-                        at_near = band + edge - (SPAN - NEAR)
-                        near_ref[head, at_near : at_near + QTILE - edge] += wide[edge:]
-                    into = slice(which * BLOCK + at, which * BLOCK + at + QTILE)
-                    dctx_ref[1, into] += dot(p.astype(bf16), dout)
-                    dctx_ref[0, into] += dot(ds, query) * SCALE
+                        if edge < QTILE:
+                            at_near = band + edge - (SPAN - NEAR)
+                            near_ref[head, at_near : at_near + QTILE - edge] += wide[edge:]
+                        into = slice(which * BLOCK + at, which * BLOCK + at + QTILE)
+                        dctx_ref[1, into] += dot(p.astype(bf16), dout)
+                        dctx_ref[0, into] += dot(ds, query) * SCALE
+                        dq += t_dot(ds, keys)
+                for part in range(half):
+                    keys = low[part * QTILE : (part + 1) * QTILE]
+                    s = dot_t(keys, query) * scale2 - lse
+                    p = jnp.exp2(s)
+                    dp = dot_t(keys, dout)
+                    ds = (p * (dp - delta)).astype(bf16)
+                    dlow[part] += dot(p.astype(bf16), dout) + dot(ds, query) * SCALE
                     dq += t_dot(ds, keys)
+                dqkv_ref[here, own] = (dq * SCALE).astype(bf16)
             for part in range(half):
-                keys = low[part * QTILE : (part + 1) * QTILE]
-                s = dot_t(keys, query) * scale2 - lse
-                p = jnp.exp2(s)
-                dp = dot_t(keys, dout)
-                ds = (p * (dp - delta)).astype(bf16)
-                dlow[part] += dot(p.astype(bf16), dout) + dot(ds, query) * SCALE
-                dq += t_dot(ds, keys)
-            dqkv_ref[rows, own] = (dq * SCALE).astype(bf16)
-        for part in range(half):
-            dmem_ref[part * QTILE : (part + 1) * QTILE, own] += dlow[part]
-        dnext_ref[0, :, own] = dctx_ref[0, 0:BLOCK]
-        dnext_ref[1, :, own] = dctx_ref[1, 0:BLOCK]
-        dqkv_ref[:, key_cols] = dctx_ref[0, BLOCK:].astype(bf16)
-        dqkv_ref[:, value_cols] = dctx_ref[1, BLOCK:].astype(bf16)
-
-
-def attend_back(qkv, dout, out, mem, upd, lse, slse, sgrad, length, state_query, forget, bias, heads, order):
+                dmem_ref[part * QTILE : (part + 1) * QTILE, own] += dlow[part]
+            dnext_ref[0, :, own] = dctx_ref[0, 0:BLOCK]
+            dnext_ref[1, :, own] = dctx_ref[1, 0:BLOCK]
+            dqkv_ref[pl.ds(cur_at, BLOCK), key_cols] = dctx_ref[0, BLOCK:].astype(bf16)
+            dqkv_ref[pl.ds(cur_at, BLOCK), value_cols] = dctx_ref[1, BLOCK:].astype(bf16)
+
+    for job in jobs[points:]:
+        job()
+    near_row = dq_row + heads
+    far_row = near_row + heads * (2 * QTILE // DH)
+    for head in range(heads):
+        sums = diagonal_sums(near_ref[head])
+        for i in range(2 * QTILE // DH):
+            row = near_row + head * (2 * QTILE // DH) + i
+            small_ref[row : row + 1, :] = sums[:, i * DH : (i + 1) * DH]
+        total = jnp.sum(far_ref[head], axis=0, keepdims=True)
+        for i in range(QTILE // DH):
+            row = far_row + head * (QTILE // DH) + i
+            small_ref[row : row + 1, :] = total[:, i * DH : (i + 1) * DH]
+    for bit in bits:
+        mo_copy(bit, 0).wait_recv()
+    step = 128
+    for r in range(0, tok_rows, step):
+        at = slice(r, r + step)
+        value = mid_ref[at] + mo_ref[0, at].astype(f32)
+        for bit in bits:
+            value = value + mo_in[slots[bit, 0], at].astype(f32)
+        position = me * tok_rows + r + lax.broadcasted_iota(jnp.int32, (step, 1), 0)
+        output_ref[at] = (value * jnp.where(position < length, 1.0, 0.0)).astype(bf16)
+    combine(2)
+    opart_ref[...] = to[z].astype(f32)
+    for k in range(1, seq):
+        exchange(k, False).wait_recv()
+    xu[me] = tu[z, me]
+    write_parts(upart_ref, xu, seq, share)
+    for i in range(3):
+        drain_y(i)
+    for i in range(2):
+        drain_z(i)
+    for bit in bits:
+        for j in range(0, seq, 2 * bit):
+            mo_copy(bit, j).wait_send()
+    for k in range(1, seq):
+        move_copy(k).wait_send()
+        exchange(k, True).wait_send()
+
+
+def write_parts(out_ref, pieces, seq, unit):
+    if len(out_ref.shape) == 3:
+        out_ref[...] = pieces[...].astype(f32)
+        return
+    count = pieces.shape[2] // unit
+    for k in range(seq):
+        for c in range(count):
+            at = (c * seq + k) * unit
+            out_ref[:, at : at + unit] = pieces[k, :, c * unit : (c + 1) * unit].astype(f32)
+
+
+def attend_back(
+    qkv, db, wout, att, mem, upd, lse, slse, sgrad, length, state_query, forget, bias, up, down, mo, mid, seq, fsdp
+):
     rows, width3 = qkv.shape
-    width = heads * DH
-    blocks = rows // BLOCK
-    last = blocks - 1
+    width = width3 // 3
+    heads = width // DH
+    dim = db.shape[1]
+    lo = 2
+    hi = fsdp // lo
+    piece = up.shape[2]
+    hidden = up.shape[3]
+    share = hidden // fsdp
+    tok_rows = mid.shape[0]
+    inside = piece % 16 == 0
+    blocks = (piece, dim), (seq, piece, hidden), (share, dim)
+    small_rows = heads * (DH + 1 + 3 * QTILE // DH)
+    small_rows += -small_rows % 8
+    vmem = pl.BlockSpec(memory_space=pltpu.VMEM)
+    dma = pltpu.SemaphoreType.DMA
+
+    def buf(*shape):
+        return pltpu.VMEM(shape, bf16)
+
+    extra = []
+    if not inside:
+        extra.append(t_dot(att, db).astype(bf16).reshape(fsdp, piece, dim))
+    upart = (piece, hidden * seq) if share % 128 == 0 else (seq, piece, hidden)
     return pl.pallas_call(
-        functools.partial(attend_back_kernel, heads, blocks),
+        functools.partial(attend_back_kernel, heads, seq, hi, lo, inside),
         out_shape=(
             jax.ShapeDtypeStruct((rows, width3), bf16),
-            jax.ShapeDtypeStruct((heads, DH, DH), f32),
-            jax.ShapeDtypeStruct((1, width), f32),
-            jax.ShapeDtypeStruct((heads, NEAR, QTILE), f32),
-            jax.ShapeDtypeStruct((heads, 8, QTILE), f32),
+            jax.ShapeDtypeStruct((small_rows, DH), f32),
+            jax.ShapeDtypeStruct(upart, f32),
+            jax.ShapeDtypeStruct((hi, share, dim), bf16),
+            jax.ShapeDtypeStruct((piece, dim), f32),
+            jax.ShapeDtypeStruct((tok_rows, dim), bf16),
         ),
-        grid_spec=pltpu.PrefetchScalarGridSpec(
-            num_scalar_prefetch=2,
-            grid=(blocks,),
-            in_specs=[
-                pl.BlockSpec((BLOCK, width3), lambda b, _, at: (at[last - b], 0)),
-                pl.BlockSpec((BLOCK, width3), lambda b, _, at: (at[jnp.maximum(last - b - 1, 0)], 0)),
-                pl.BlockSpec((BLOCK, width), lambda b, _, at: (at[last - b], 0)),
-                pl.BlockSpec((BLOCK, width), lambda b, _, at: (at[last - b], 0)),
-                pl.BlockSpec((1, STATE_VECTORS, width), lambda b, _, at: (last - b, 0, 0)),
-                pl.BlockSpec((1, STATE_VECTORS, width), lambda b, _, at: (last - b, 0, 0)),
-                pl.BlockSpec((heads, BLOCK), lambda b, _, at: (0, last - b)),
-                pl.BlockSpec((heads, STATE_VECTORS), lambda b, _, at: (0, last - b)),
-                pl.BlockSpec((STATE_VECTORS, width), lambda b, _, at: (0, 0)),
-                pl.BlockSpec((heads, DH, DH), lambda b, _, at: (0, 0, 0)),
-                pl.BlockSpec((1, width), lambda b, _, at: (0, 0)),
-                pl.BlockSpec((heads, 2 * BLOCK), lambda b, _, at: (0, 0)),
-            ],
-            out_specs=(
-                pl.BlockSpec((BLOCK, width3), lambda b, _, at: (at[last - b], 0)),
-                pl.BlockSpec((heads, DH, DH), lambda b, _, at: (0, 0, 0)),
-                pl.BlockSpec((1, width), lambda b, _, at: (0, 0)),
-                pl.BlockSpec((heads, NEAR, QTILE), lambda b, _, at: (0, 0, 0)),
-                pl.BlockSpec((heads, 8, QTILE), lambda b, _, at: (0, 0, 0)),
-            ),
-            scratch_shapes=[
-                pltpu.VMEM((STATE_VECTORS, width), f32),
-                pltpu.VMEM((2, BLOCK, width), f32),
-                pltpu.VMEM((2, 2 * BLOCK, DH), f32),
-                pltpu.VMEM((heads, SPAN, QTILE), f32),
-            ],
-        ),
-        compiler_params=pltpu.CompilerParams(vmem_limit_bytes=40 << 20),
+        in_specs=[pl.BlockSpec(memory_space=pltpu.SMEM)] + [vmem] * (16 + len(extra)),
+        out_specs=(vmem,) * 6,
+        scratch_shapes=[
+            pltpu.VMEM((STATE_VECTORS, width), f32),
+            pltpu.VMEM((2, BLOCK, width), f32),
+            pltpu.VMEM((2, 2 * BLOCK, DH), f32),
+            pltpu.VMEM((heads, SPAN, QTILE), f32),
+            pltpu.VMEM((heads, NEAR, QTILE), f32),
+            pltpu.VMEM((heads, 8, QTILE), f32),
+            buf(BLOCK, width),
+            buf(fsdp, piece, dim),
+            buf(*down.shape),
+            buf(hi, *blocks[0]),
+            buf(hi, *blocks[1]),
+            buf(hi, *blocks[0]),
+            buf(hi, *blocks[1]),
+            buf(hi, *blocks[2]),
+            buf(2, max(hi - 1, 1), *blocks[0]),
+            buf(2, max(hi - 1, 1), *blocks[1]),
+            buf(*blocks[1]),
+            buf(max(seq // 2, 1), tok_rows, dim),
+            buf(max(seq - 1, 1), tok_rows, dim),
+            dma((2, 2, hi)),
+            dma((2, 2, hi)),
+            dma((3, hi)),
+            dma((3, hi)),
+            dma((seq,)),
+            dma((seq,)),
+            dma((seq,)),
+            dma((seq,)),
+            dma((seq,)),
+            dma((seq,)),
+        ],
+        compiler_params=pltpu.CompilerParams(collective_id=4, has_side_effects=True, vmem_limit_bytes=60 << 20),
         cost_estimate=pl.CostEstimate(
-            flops=blocks * heads * 512 * 2400 * 128 * 10, bytes_accessed=20 << 20, transcendentals=10 << 20
+            flops=seq * heads * 512 * 2400 * 128 * 10, bytes_accessed=20 << 20, transcendentals=10 << 20
         ),
         name="attend_back",
-    )(length, order, qkv, qkv, dout, out, mem, upd, lse, slse, sgrad, state_query, forget, bias)
+    )(
+        length, qkv, db, wout, att, mem, upd, lse, slse, sgrad, state_query, forget, bias, up, down, mo, mid, *extra
+    )
 
 
 def gather_kernel(
@@ -778,80 +1039,28 @@
     )(tokens, grads, w_qkv, gain_a, gain_m, w_out, w_up)
 
 
-def finish_kernel(
-    seq,
-    hi,
-    lo,
-    chunks,
-    dn_ref,
-    gq_ref,
-    gu_ref,
-    gd_ref,
-    go_ref,
-    small_ref,
-    mlp_gain_ref,
-    tok_ref,
-    dmid_ref,
-    gain_ref,
-    tg_ref,
-    rq_ref,
-    ru_ref,
-    rd_ref,
-    ro_ref,
-    ssum_ref,
-    gsum_ref,
-    dn_own,
-    dn_in,
-    dn_low,
-    dn_acc,
-    tq,
-    tu,
-    td,
-    to,
-    yq,
-    yu,
-    yd,
-    yo,
-    lq,
-    lu,
-    ld,
-    lq_r,
-    lu_r,
-    ld_r,
-    lo_l,
-    lo_r,
-    xq,
-    xu,
-    sy,
-    sz,
-    gains,
-    gy,
-    gz,
-    gs,
-    load_sem,
-    dn_send,
-    dn_recv,
-    y_send,
-    y_recv,
-    z_send,
-    z_recv,
-    x_send,
-    x_recv,
-    s_send,
-    s_recv,
-    g_send,
-    g_recv,
-):
+def finish_kernel(seq, hi, lo, inside, *refs):
+    refs = list(refs)
+
+    def take(count):
+        taken = refs[:count]
+        del refs[:count]
+        return taken
+
+    dqkv_ref, wqkv_ref, normed_ref, down_ref, small_ref, mlp_gain_ref, tok_ref, dmid_ref, gain_ref = take(9)
+    gq_in = None if inside else take(1)[0]
+    tg_ref, rq_ref, rd_ref, ssum_ref, gsum_ref = take(5)
+    low, into, acc, gq_buf, tq, td, yq, zq, zd, xq, sy, sz, gains, gy, gz, gs = take(16)
+    dn_send, dn_recv, z_send, z_recv, y_send, y_recv, x_send, x_recv, s_send, s_recv, g_send, g_recv = take(12)
+    gq_ref = gq_buf if inside else gq_in
+
     me = lax.axis_index("seq")
     f = lax.axis_index("fsdp")
     z, y = f // lo, f % lo
     peer = z * lo + 1 - y
-    grads = (gq_ref, gu_ref, gd_ref, go_ref)
-    totals = (tq, tu, td, to)
-    from_y = (yq, yu, yd, yo)
-    from_z = ((lq, lq_r), (lu, lu_r), (ld, ld_r), (lo_l, lo_r))
-    tensors = range(4)
-    rows = dn_ref.shape[1] // chunks
+    rows, dim = tok_ref.shape
+    width = xq.shape[2] // 3
+    bits, slots = seq_levels(seq)
 
     barrier = pltpu.get_barrier_semaphore()
     for k in range(1, seq):
@@ -861,186 +1070,126 @@
     pl.semaphore_signal(barrier, inc=1, device_id={"fsdp": peer}, device_id_type=MESH)
     pl.semaphore_wait(barrier, seq + hi - 1)
 
-    def block(i, target):
-        return grads[i].at[:, target] if i < 2 else grads[i].at[target]
-
     def remote(src, dst, send, recv, axis, target):
         return pltpu.make_async_remote_copy(
             src_ref=src, dst_ref=dst, send_sem=send, recv_sem=recv, device_id={axis: target}, device_id_type=MESH
         )
 
-    evens = list(range(0, seq, 2))
-    loads = [pltpu.make_async_copy(dn_ref.at[j], dn_own.at[j // 2], load_sem.at[0, j // 2]) for j in evens]
-    for c in loads:
-        c.start()
-
-    levels = []
-    active = list(range(seq))
-    bit = 1
-    slot = 0
-    while bit < seq:
-        keep = [j for j in active if not j & bit]
-        levels.append((bit, keep, {j: slot + n for n, j in enumerate(keep)}))
-        slot += len(keep)
-        active = keep
-        bit *= 2
-    order = sorted(evens, reverse=True)
-
-    def piece_rows(c):
-        return pl.ds(c * rows, rows)
-
-    def dn_copy(level, j, c):
-        bit, _, slots = levels[level]
-        src = dn_ref.at[j ^ bit, piece_rows(c)] if level == 0 else dn_low.at[(j ^ bit) // 2, piece_rows(c)]
+    def dn_copy(bit, j):
+        slot = slots[bit, j]
+        return remote(low.at[j ^ bit], into.at[slot], dn_send.at[slot], dn_recv.at[slot], "seq", me ^ bit)
+
+    start, combine, zsend, zrecv, drain_y, drain_z = line_reduce(
+        hi,
+        lo,
+        lambda i, target: gq_ref.at[:, target],
+        (tq, td),
+        (yq,),
+        (zq, zd),
+        z_send,
+        z_recv,
+        y_send,
+        y_recv,
+    )
+
+    def exchange(k, sending):
         return remote(
-            src, dn_in.at[slots[j], piece_rows(c)], dn_send.at[slots[j], c], dn_recv.at[slots[j], c], "seq", me ^ bit
-        )
-
-    for c in range(chunks):
-        for j in order[:1]:
-            dn_copy(0, j, c).start()
-    y_copies = {}
-    for i in tensors:
-        for d in range(hi):
-            y_copies[i, d] = remote(
-                block(i, d * lo + 1 - y), from_y[i].at[d], y_send.at[i, d], y_recv.at[i, d], "fsdp", peer
-            )
-    grad_loads = {}
-    for i in tensors:
-        for d in range(hi):
-            grad_loads[i, d] = pltpu.make_async_copy(block(i, d * lo + y), totals[i].at[d], load_sem.at[1 + i, d])
+            tq.at[z, me ^ k] if sending else tq.at[z, me],
+            xq.at[me] if sending else xq.at[me ^ k],
+            x_send.at[k],
+            x_recv.at[k],
+            "seq",
+            me ^ k if sending else me,
+        )
+
     small_y = remote(small_ref, sy, s_send.at[0], s_recv.at[0], "fsdp", peer)
     small_y.start()
-    for d in range(hi):
-        y_copies[0, d].start()
-        grad_loads[0, d].start()
-    for j in order[1:]:
-        for c in range(chunks):
-            dn_copy(0, j, c).start()
-    for i in tensors[1:]:
-        for d in range(hi):
-            y_copies[i, d].start()
-            grad_loads[i, d].start()
-    for c in loads:
-        c.wait()
-    for level, (bit, keep, slots) in enumerate(levels):
-        later = levels[level + 1 :]
-        for j in sorted(keep, reverse=True):
-            for c in range(chunks):
-                if level == len(levels) - 1:
-                    continue
-                dn_copy(level, j, c).wait_recv()
-                at = piece_rows(c)
-                own = dn_own[j // 2, at].astype(f32) if level == 0 else dn_low[j // 2, at].astype(f32)
-                if j == 0:
-                    own = own if level == 0 else dn_acc[at]
-                    dn_acc[at] = own + dn_in[slots[j], at].astype(f32)
-                else:
-                    dn_low[j // 2, at] = (own + dn_in[slots[j], at].astype(f32)).astype(bf16)
-                    nxt = later[0]
-                    if j & nxt[0]:
-                        dn_copy(level + 1, j ^ nxt[0], c).start()
-
+    td[...] = down_ref[...]
+    zsend(1, 0)
+    if not inside:
+        start(0)
+
+    def dn_part(j):
+        part = dot_t(dqkv_ref[j * rows : (j + 1) * rows], wqkv_ref[...])
+        if j % 2:
+            low[j] = part.astype(bf16)
+            dn_copy(1, j ^ 1).start()
+        else:
+            acc[...] = part
+
+    def dn_sum(j):
+        for bit in bits:
+            if j & bit:
+                low[j] = acc[...].astype(bf16)
+                dn_copy(bit, j ^ bit).start()
+                break
+            dn_copy(bit, j).wait_recv()
+            acc[...] += into[slots[bit, j]].astype(f32)
+
+    for j in reversed(range(2, seq)):
+        dn_part(j)
+        if j % 2 == 0:
+            dn_sum(j)
+    if inside:
+        for k in range(seq):
+            cols = slice(k * (dim // seq), (k + 1) * (dim // seq))
+            part = t_dot(normed_ref[:, cols], dqkv_ref[...]).astype(bf16)
+            gq_buf[k] = part.reshape(gq_buf.shape[1:])
+        start(0)
     small_y.wait_recv()
     sz[z] = small_ref[...] + sy[...]
     small_z = []
     for k in range(1, hi):
-        target = lax.rem(z + k, hi)
-        small_z.append(remote(sz.at[z], sz.at[z], s_send.at[k], s_recv.at[k], "fsdp", target * lo + y))
+        small_z.append(
+            remote(sz.at[z], sz.at[z], s_send.at[k], s_recv.at[k], "fsdp", lax.rem(z + k, hi) * lo + y)
+        )
         small_z[-1].start()
-
-    def reduce_tensor(i):
-        total = totals[i]
-        for d in range(hi):
-            grad_loads[i, d].wait()
-            y_copies[i, d].wait_recv()
-            total[d] = (total[d].astype(f32) + from_y[i][d].astype(f32)).astype(bf16)
-        from_right, from_left = from_z[i]
-        for t in range(hi - 1):
-            d = t - (hi - 1 - z)
-            m = hi - 1 - (t - z)
-
-            @pl.when((d >= 0) & (d < z))
-            def _():
-                at = jnp.clip(d, 0, hi - 1)
-                remote(
-                    total.at[at], from_right.at[t], z_send.at[i, 0, t], z_recv.at[i, 0, t], "fsdp", (z - 1) * lo + y
-                ).start()
-
-            @pl.when((m > z) & (m < hi))
-            def _():
-                at = jnp.clip(m, 0, hi - 1)
-                remote(
-                    total.at[at], from_left.at[t], z_send.at[i, 1, t], z_recv.at[i, 1, t], "fsdp", (z + 1) * lo + y
-                ).start()
-
-            dr = t - (hi - 2 - z)
-
-            @pl.when((z + 1 < hi) & (dr >= 0))
-            def _():
-                at = jnp.clip(dr, 0, hi - 1)
-                remote(
-                    total.at[at], from_right.at[t], z_send.at[i, 0, t], z_recv.at[i, 0, t], "fsdp", f
-                ).wait_recv()
-                total[at] = (total[at].astype(f32) + from_right[t].astype(f32)).astype(bf16)
-
-            ml = hi - 1 - (t - (z - 1))
-
-            @pl.when((z > 0) & (ml < hi))
-            def _():
-                at = jnp.clip(ml, 0, hi - 1)
-                remote(
-                    total.at[at], from_left.at[t], z_send.at[i, 1, t], z_recv.at[i, 1, t], "fsdp", f
-                ).wait_recv()
-                total[at] = (total[at].astype(f32) + from_left[t].astype(f32)).astype(bf16)
-
-    exchanged = (xq, xu)
-    results = (rq_ref, ru_ref, rd_ref, ro_ref)
-
-    def exchange(i):
-        for k in range(1, seq):
-            remote(
-                totals[i].at[z, me ^ k], exchanged[i].at[me], x_send.at[i, k], x_recv.at[i, k], "seq", me ^ k
-            ).start()
-
-    reduce_tensor(0)
-    exchange(0)
-
-    if levels:
-        bit, keep, slots = levels[-1]
+    for t in range(hi - 1):
+        zrecv(1, t)
+        if t + 1 < hi - 1:
+            zsend(1, t + 1)
+        if t == 0:
+            for j in reversed(range(min(2, seq))):
+                dn_part(j)
+    rd_ref[...] = td[z].astype(f32)
+
+    for bit in bits:
+        dn_copy(bit, 0).wait_recv()
     gain = gain_ref[...]
-    part = jnp.zeros((8, gain.shape[1]), f32)
-    for c in range(chunks):
-        at = piece_rows(c)
-        if levels:
-            dn_copy(len(levels) - 1, 0, c).wait_recv()
-        if len(levels) > 1:
-            dn = dn_acc[at]
-        else:
-            dn = dn_own[0, at].astype(f32)
-        if levels:
-            dn = dn + dn_in[slots[0], at].astype(f32)
+    part = jnp.zeros((8, dim), f32)
+    step = 128
+    for r in range(0, rows, step):
+        at = slice(r, r + step)
+        dn = acc[at]
+        for bit in bits:
+            dn = dn + into[slots[bit, 0], at].astype(f32)
         x = tok_ref[at].astype(f32)
         rho = lax.rsqrt(jnp.mean(x * x, axis=-1, keepdims=True) + EPSILON)
         scaled = gain * dn
         mean = jnp.mean(x * scaled, axis=-1, keepdims=True)
         tg_ref[at] = dmid_ref[at] + rho * scaled - x * (rho * rho * rho * mean)
         prod = dn * x * rho
-        part += functools.reduce(jnp.add, [prod[n : n + 8] for n in range(0, rows, 8)])
+        part += functools.reduce(jnp.add, [prod[n : n + 8] for n in range(0, step, 8)])
     gains[0:8] = mlp_gain_ref[...]
     gains[8:16] = part
     gain_y = remote(gains, gy, g_send.at[0], g_recv.at[0], "fsdp", peer)
     gain_y.start()
-    reduce_tensor(1)
-    exchange(1)
+    combine(0)
+    zsend(0, 0)
     gain_y.wait_recv()
     gz[z] = gains[...] + gy[...]
     gain_z = []
     for k in range(1, hi):
-        target = lax.rem(z + k, hi)
-        gain_z.append(remote(gz.at[z], gz.at[z], g_send.at[k], g_recv.at[k], "fsdp", target * lo + y))
+        gain_z.append(
+            remote(gz.at[z], gz.at[z], g_send.at[k], g_recv.at[k], "fsdp", lax.rem(z + k, hi) * lo + y)
+        )
         gain_z[-1].start()
-    reduce_tensor(2)
+    for t in range(hi - 1):
+        zrecv(0, t)
+        if t + 1 < hi - 1:
+            zsend(0, t + 1)
+    for k in range(1, seq):
+        exchange(k, True).start()
     for k in range(1, hi):
         source = lax.rem(z + hi - k, hi)
         remote(gz.at[source], gz.at[source], g_send.at[k], g_recv.at[k], "fsdp", f).wait_recv()
@@ -1051,123 +1200,89 @@
         gain_x.append(remote(gs.at[me], gs.at[me], g_send.at[hi + k], g_recv.at[hi + k], "seq", me ^ k))
         gain_x[-1].start()
     ssum_ref[...] = functools.reduce(jnp.add, [sz[d] for d in range(hi)])
-    reduce_tensor(3)
-    rd_ref[...] = td[z].astype(f32)
-    ro_ref[...] = to[z].astype(f32)
-    for i in range(2):
-        for k in range(1, seq):
-            remote(
-                totals[i].at[z, me], exchanged[i].at[me ^ k], x_send.at[i, k], x_recv.at[i, k], "seq", me
-            ).wait_recv()
-        exchanged[i][me] = totals[i][z, me]
-        for k in range(seq):
-            results[i][k] = exchanged[i][k].astype(f32)
+    xq[me] = tq[z, me]
+    for k in range(1, seq):
+        exchange(k, False).wait_recv()
+    write_parts(rq_ref, xq, seq, width)
     for k in range(1, seq):
         remote(gs.at[me ^ k], gs.at[me ^ k], g_send.at[hi + k], g_recv.at[hi + k], "seq", me).wait_recv()
     gsum_ref[...] = functools.reduce(jnp.add, [gs[k] for k in range(seq)])
 
-    for level, (bit, keep, slots) in enumerate(levels):
-        for j in keep:
-            for c in range(chunks):
-                dn_copy(level, j, c).wait_send()
-    for i in tensors:
-        for d in range(hi):
-            y_copies[i, d].wait_send()
-        for t in range(hi - 1):
-            d = t - (hi - 1 - z)
-            m = hi - 1 - (t - z)
-
-            @pl.when((d >= 0) & (d < z))
-            def _():
-                remote(
-                    totals[i].at[0], from_z[i][0].at[t], z_send.at[i, 0, t], z_recv.at[i, 0, t], "fsdp", f
-                ).wait_send()
-
-            @pl.when((m > z) & (m < hi))
-            def _():
-                remote(
-                    totals[i].at[0], from_z[i][1].at[t], z_send.at[i, 1, t], z_recv.at[i, 1, t], "fsdp", f
-                ).wait_send()
+    for bit in bits:
+        for j in range(0, seq, 2 * bit):
+            dn_copy(bit, j).wait_send()
+    drain_y(0)
     for i in range(2):
-        for k in range(1, seq):
-            remote(
-                totals[i].at[z, me], exchanged[i].at[me], x_send.at[i, k], x_recv.at[i, k], "seq", me
-            ).wait_send()
+        drain_z(i)
+    for k in range(1, seq):
+        exchange(k, True).wait_send()
     for c in [small_y, gain_y] + small_z + gain_z + gain_x:
         c.wait_send()
 
 
-def finish(dn, gq, gu, gd, go, small, mlp_gain, tok, dmid, gain, seq, fsdp):
+def finish(dqkv, wqkv, normed, down, small, mlp_gain, tok, dmid, gain, seq, fsdp):
     lo = 2
     hi = fsdp // lo
-    chunks = 4
-    anywhere = pl.BlockSpec(memory_space=pl.ANY)
+    rows, dim = tok.shape
+    width3 = dqkv.shape[1]
+    piece = dim // (seq * fsdp)
+    inside = piece % 16 == 0
     vmem = pl.BlockSpec(memory_space=pltpu.VMEM)
-    block_q = (seq,) + gq.shape[2:]
-    block_u = (seq,) + gu.shape[2:]
-    block_d = gd.shape[1:]
-    block_o = go.shape[1:]
-    blocks = (block_q, block_u, block_d, block_o)
-    tok_rows, dim = tok.shape
-    sides = max(hi - 1, 1)
-
-    def buf(lead, shape, kind=bf16):
-        return pltpu.VMEM((lead,) + tuple(shape), kind)
-
+    dma = pltpu.SemaphoreType.DMA
+
+    def buf(*shape):
+        return pltpu.VMEM(shape, bf16)
+
+    extra = []
+    if not inside:
+        extra.append(t_dot(normed, dqkv).astype(bf16).reshape(seq, fsdp, piece, width3))
     scratch = [
-        buf(max(seq // 2, 1), (tok_rows, dim)),
-        buf(max(seq - 1, 1), (tok_rows, dim)),
-        buf(max(seq // 2, 1), (tok_rows, dim)),
-        pltpu.VMEM((tok_rows, dim), f32),
-    ]
-    scratch += [buf(hi, b) for b in blocks]
-    scratch += [buf(hi, b) for b in blocks]
-    scratch += [buf(sides, b) for b in (block_q, block_u, block_d)] * 2
-    scratch += [buf(sides, block_o), buf(sides, block_o)]
-    scratch += [pltpu.VMEM(block_q, bf16), pltpu.VMEM(block_u, bf16)]
-    scratch += [
+        buf(seq, rows, dim),
+        buf(max(seq - 1, 1), rows, dim),
+        pltpu.VMEM((rows, dim), f32),
+        buf(seq, fsdp, piece, width3) if inside else buf(16, 128),
+        buf(hi, seq, piece, width3),
+        buf(*down.shape),
+        buf(hi, seq, piece, width3),
+        buf(2, max(hi - 1, 1), seq, piece, width3),
+        buf(2, max(hi - 1, 1), *down.shape[1:]),
+        buf(seq, piece, width3),
         pltpu.VMEM(small.shape, f32),
-        buf(hi, small.shape, f32),
+        pltpu.VMEM((hi,) + small.shape, f32),
         pltpu.VMEM((16, dim), f32),
         pltpu.VMEM((16, dim), f32),
-        buf(hi, (16, dim), f32),
-        buf(seq, (16, dim), f32),
-    ]
-    dma = pltpu.SemaphoreType.DMA
-    scratch += [
-        dma((5, max(hi, seq))),
-        dma((seq, chunks)),
-        dma((seq, chunks)),
-        dma((4, hi)),
-        dma((4, hi)),
-        dma((4, 2, hi)),
-        dma((4, 2, hi)),
-        dma((2, seq)),
-        dma((2, seq)),
+        pltpu.VMEM((hi, 16, dim), f32),
+        pltpu.VMEM((seq, 16, dim), f32),
+        dma((seq,)),
+        dma((seq,)),
+        dma((2, 2, hi)),
+        dma((2, 2, hi)),
+        dma((1, hi)),
+        dma((1, hi)),
+        dma((seq,)),
+        dma((seq,)),
         dma((hi,)),
         dma((hi,)),
         dma((hi + seq,)),
         dma((hi + seq,)),
     ]
     return pl.pallas_call(
-        functools.partial(finish_kernel, seq, hi, lo, chunks),
+        functools.partial(finish_kernel, seq, hi, lo, inside),
         out_shape=(
-            jax.ShapeDtypeStruct((tok_rows, dim), f32),
-            jax.ShapeDtypeStruct(block_q, f32),
-            jax.ShapeDtypeStruct(block_u, f32),
-            jax.ShapeDtypeStruct(block_d, f32),
-            jax.ShapeDtypeStruct(block_o, f32),
+            jax.ShapeDtypeStruct((rows, dim), f32),
+            jax.ShapeDtypeStruct((piece, seq * width3), f32),
+            jax.ShapeDtypeStruct(down.shape[1:], f32),
             jax.ShapeDtypeStruct(small.shape, f32),
             jax.ShapeDtypeStruct((16, dim), f32),
         ),
-        in_specs=[anywhere] * 5 + [vmem] * 5,
-        out_specs=(vmem,) * 7,
+        in_specs=[vmem] * (9 + len(extra)),
+        out_specs=(vmem,) * 5,
         scratch_shapes=scratch,
         compiler_params=pltpu.CompilerParams(
-            collective_id=1, has_side_effects=True, vmem_limit_bytes=56 << 20
+            collective_id=1, has_side_effects=True, vmem_limit_bytes=60 << 20
         ),
         name="finish",
-    )(dn, gq, gu, gd, go, small, mlp_gain, tok, dmid, gain)
+    )(dqkv, wqkv, normed, down, small, mlp_gain, tok, dmid, gain, *extra)
 
 
 GELU_P = 0.24
@@ -1437,44 +1552,14 @@
     )(length, own, others, tok, grads, wo, wu, wd, gain)
 
 
-def swap(value, bit):
-    count = lax.axis_size("seq")
-    return lax.ppermute(value, "seq", [(i, i ^ bit) for i in range(count)])
-
-
-def seq_bits():
-    count = lax.axis_size("seq")
-    return [1 << i for i in reversed(range(1, count.bit_length() - 1))]
-
-
-def seq_gather(value):
-    chunks = {0: value}
-    for bit in seq_bits():
-        for j in list(chunks):
-            chunks[j ^ bit] = swap(chunks[j], bit)
-    for j in list(chunks):
-        chunks[j ^ 1] = swap(chunks[j], 1)
-    return [chunks[j] for j in range(len(chunks))]
-
-
-def seq_reduce(parts):
-    count = len(parts)
-    parts = dict(enumerate(parts))
-    for j in range(count - 2, -1, -2):
-        parts[j] = parts[j].astype(f32) + swap(parts.pop(j ^ 1).astype(bf16), 1).astype(f32)
-    for bit in reversed(seq_bits()):
-        keep = [j for j in parts if not j & bit]
-        for j in sorted(keep, reverse=True):
-            parts[j] = parts[j] + swap(parts.pop(j ^ bit).astype(bf16), bit).astype(f32)
-    return parts[0]
-
-
 def bias_table_grad(near, far):
-    distance = tile_distance().T[SPAN - NEAR :]
-    bucket = np.where((distance >= 0) & (distance < BLOCK), bucket_of(np.clip(distance, 0, BLOCK)), BUCKETS)
+    lane = np.arange(2 * QTILE)
+    distance = np.where(lane < QTILE, lane, lane - 2 * QTILE) + NEAR - QTILE
+    inside = (distance >= 0) & (distance < BLOCK)
+    bucket = np.where(inside, bucket_of(np.clip(distance, 0, BLOCK)), BUCKETS)
     bucket = jnp.asarray(bucket.astype(np.int32))
-    columns = [jnp.sum(jnp.where((bucket == i)[None], near, 0.0), axis=(1, 2)) for i in range(BUCKETS)]
-    columns[-1] = columns[-1] + jnp.sum(far, axis=(1, 2))
+    columns = [jnp.sum(jnp.where((bucket == i)[None], near, 0.0), axis=1) for i in range(BUCKETS)]
+    columns[-1] = columns[-1] + jnp.sum(far, axis=1)
     return jnp.stack(columns, axis=1)
 
 
@@ -1536,8 +1621,6 @@
     bias = bias_vector(rel_bias)
     forget = jax.nn.sigmoid(gate_bias)
     forget_row = forget.reshape(1, width)
-    chunk_ids = jnp.arange(seq_count, dtype=jnp.int32)
-    order = chunk_ids ^ seq_at
 
     inputs = all_tokens.reshape(rows, dim).astype(f32)
     normed = (inputs * inverse_rms(inputs) * gain_attn).astype(bf16)
@@ -1561,40 +1644,33 @@
     mid_here, dmid, mlp_gain_grad, dbranch, mlp_parts, up_grad, down_grad = mlp(
         lengths, attended, others, all_tokens, all_grad, out_w, up_w, down_w, gain_mlp.reshape(1, dim)
     )
-    dbranch = dbranch.reshape(rows, dim)
-    dattended = dot_t(dbranch, own_out).astype(bf16)
-    out_w_grad = t_dot(attended, dbranch)
-
-    dqkv, dquery, dforget, near, far = attend_back(
-        qkv, dattended, attended, mem, upd, lse, slse, state_grad[0], lengths, state_query, forget_row, bias, heads, order
+    span = fsdp_count // seq_count
+    dqkv, small, up_part, down_total, out_part, output = attend_back(
+        qkv,
+        dbranch.reshape(rows, dim),
+        own_out,
+        attended,
+        mem,
+        upd,
+        lse,
+        slse,
+        state_grad[0],
+        lengths,
+        state_query,
+        forget_row,
+        bias,
+        up_grad.reshape(seq_count, fsdp_count, piece, hidden_all // seq_count),
+        down_grad.reshape(seq_count, span * share, dim),
+        mlp_parts,
+        mid_here,
+        seq_count,
+        fsdp_count,
     )
-    mlp_parts, dqkv = lax.optimization_barrier((mlp_parts, dqkv))
-    mlp_out = seq_reduce([mlp_parts[j] for j in range(seq_count)])
-    live_here = (seq_at * tok_rows + jnp.arange(tok_rows, dtype=jnp.int32) < lengths[0]).astype(f32)[:, None]
-    output = (live_here * (mid_here + mlp_out)).astype(bf16)[None]
-    dnormed = dot_t(dqkv, qkv_w).astype(bf16).reshape(seq_count, tok_rows, dim)
-    qkv_grad = t_dot(normed, dqkv).astype(bf16).reshape(seq_count, fsdp_count, piece, 3 * width)
-    up_grad = up_grad.reshape(seq_count, fsdp_count, piece, hidden_all // seq_count)
-    span = fsdp_count // seq_count
-    down_grad = down_grad.reshape(seq_count, span, share, dim)
-    moved = [lax.dynamic_slice_in_dim(down_grad, seq_at, 1, axis=0)]
-    for k in range(1, seq_count):
-        moved.append(swap(lax.dynamic_slice_in_dim(down_grad, seq_at ^ k, 1, axis=0), k))
-    moved = lax.optimization_barrier(jnp.concatenate(moved, axis=0))
-    moved = [lax.dynamic_slice_in_dim(moved, seq_at ^ k, 1, axis=0) for k in range(seq_count)]
-    down_grad = jnp.swapaxes(jnp.concatenate(moved, axis=0), 0, 1).reshape(fsdp_count, share, dim)
-    out_w_grad = out_w_grad.astype(bf16).reshape(fsdp_count, piece, dim)
-    grad_gate = dforget.reshape(heads, DH) * forget * (1.0 - forget)
-    grad_table = jnp.pad(bias_table_grad(near, far), ((0, 0), (0, DH - BUCKETS)))
-    cut = heads * DH
-    small = jnp.concatenate([dquery.reshape(cut, DH), grad_gate, grad_table], axis=0)
-    small = jnp.pad(small, ((0, -small.shape[0] % 8), (0, 0)))
-    tokens_grad, qkv_part, up_part, down_part, out_part, small, gain_sums = finish(
-        dnormed,
-        qkv_grad,
-        up_grad,
-        down_grad,
-        out_w_grad,
+    tokens_grad, qkv_part, down_part, small, gain_sums = finish(
+        dqkv,
+        qkv_w,
+        normed,
+        down_total,
         small,
         mlp_gain_grad,
         tokens[0],
@@ -1603,14 +1679,20 @@
         seq_count,
         fsdp_count,
     )
+    output = output[None]
     tokens_grad = tokens_grad[None]
+    cut = heads * DH
+    near_rows, far_rows = 2 * QTILE // DH, QTILE // DH
     dquery = small[:cut].reshape(heads, DH, DH)
-    grad_gate = small[cut : cut + heads]
-    grad_table = small[cut + heads : cut + 2 * heads, :BUCKETS]
-    up_part = up_part.reshape(seq_count, piece, fsdp_count, share)
-    up_part = jnp.transpose(up_part, (1, 2, 0, 3)).reshape(piece, hidden_all)
-    qkv_part = qkv_part.reshape(seq_count, piece, 3, width)
-    qkv_part = jnp.transpose(qkv_part, (1, 2, 0, 3)).reshape(piece, 3 * H * DH)
+    grad_gate = small[cut : cut + heads] * forget * (1.0 - forget)
+    at = cut + heads
+    near = small[at : at + heads * near_rows].reshape(heads, near_rows * DH)
+    at += heads * near_rows
+    far = small[at : at + heads * far_rows].reshape(heads, far_rows * DH)
+    grad_table = bias_table_grad(near, far)
+    if up_part.ndim == 3:
+        up_part = up_part.reshape(seq_count, piece, fsdp_count, share)
+        up_part = jnp.transpose(up_part, (1, 2, 0, 3)).reshape(piece, hidden_all)
     gain_sums = jnp.sum(gain_sums.reshape(2, 8, seq_count * fsdp_count, piece), axis=1)
     mine = seq_at * fsdp_count + lax.axis_index("fsdp")
     gain_sums = lax.dynamic_slice_in_dim(gain_sums, mine, 1, axis=1)[:, 0]

time: 450 us -> 379 us (0.84)
  local copies, waits for them, and re-layouts: 55 us -> 27.5 us
  matrix products: 24.2 us -> 4.8 us
  Pallas kernels: 330 us -> 317 us
  other arithmetic: 30.5 us -> 23.6 us
    unnamed x199 -> x124, local copies, waits for them, and re-layouts: 42 us -> 15.9 us
    dot_general x4 -> x0, matrix products: 19.3 us -> none  [the longest x2 9.95 us: t_dot(): lax.dot_general(a, b, (((0,), (0,)), ((), ())), preferred_element_type=f32)]
    pallas_call x2, Pallas kernels: 156 us -> 143 us  [the longest x1 74.3 us: attend_back(): pl.pallas_call(functools.partial(attend_back_kernel, heads, seq, hi, lo,...]
  transfers between devices with their start and end apart: 6 -> 0, of which waited for: 0 -> 0; matrix products, arithmetic and copies ran while one was open for 16% -> 0% of each run, Pallas kernels for 35% -> 0%
where the time goes in v7:
time: 379 us; the launch traced here: 375 us
  Pallas kernels  317 us (84%)
  local copies, waits for them, and re-layouts  27.5 us (7%)
  other arithmetic  23.6 us (6%)
  matrix products  4.8 us (1%)
    pallas_call x1, Pallas kernels, mlp(): pl.pallas_call(functools.partial(mlp_kernel, seq, sub), out_shape=(jax.Sh...  76.2 us
    pallas_call x1, Pallas kernels, attend_back(): pl.pallas_call(functools.partial(attend_back_kernel, heads, seq, hi, lo,...  74.3 us
    pallas_call x1, Pallas kernels, finish(): pl.pallas_call(functools.partial(finish_kernel, seq, hi, lo, inside), out...  68.8 us
    pallas_call x1, Pallas kernels, gather_start(): pl.pallas_call(functools.partial(gather_kernel, seq, hi, lo), out_shape=t...  57 us
    pallas_call x1, Pallas kernels, attend(): pl.pallas_call(functools.partial(attend_kernel, heads, seq, hi, lo), out_...  40.5 us
    unnamed x124, local copies, waits for them, and re-layouts  15.9 us

profile of v7, /device:TPU:0, one launch (start us, length us, event | category | flops | bytes accessed | tf_op | source)
XLA Modules:
  0.0 375.2 jit_solution(7861523430556607826)
XLA Ops:
  0.7 1.9 multiply_reduce_fusion.1
  2.6 1.6 multiply_reduce_fusion.32
  4.1 1.3 select_select_fusion.vector_ref.refs_11_
  5.4 57.0 %gather_start.1 = (bf16[4,512,1024]{2,1,0:T(8,128)(2,1)}, bf16[4,512,1024]{2,1,0:T(8,128)(2,1)}, bf16[8,128,768]{2,1,0:T(8,128)(2,1)}, bf16[8,1,128]{2,1,0:T(2,1...) custom-call(bf16[512,1024]{1,0:T(8,128)(2,1)} %bitcast.114, ...), custom_call_target="tpu_custom_call" | custom-call | tf_op jit(solution)/shard_map/gather_start/pallas_call | solution.py:1029
  62.5 3.2 multiply_reduce_fusion
  65.7 0.6 convert_bitcast_fusion
  66.3 1.3 multiply_convert_fusion
  67.6 0.1 copy-done.17
  67.8 4.8 %convolution_convert_fusion.qkv_ref.refs_0_ = bf16[2048,768]{1,0:T(8,128)(2,1)} fusion(bf16[2048,1024]{1,0:T(8,128)(2,1)S(1)} %bitcast.113, bf16[1024,768]{1,0:T(8,128)(2,1)S(1)} %bitcast.118), kind=kOutput, calls=%fused_computation.5 | convolution fusion | flops 3222798336 | bytes 8912896 | tf_op jit(solution)/shard_map/dot_general | solution.py:57
  73.3 1.9 copy-done.9
  75.2 40.5 %attend.1 = (bf16[2048,256]{1,0:T(8,128)(2,1)S(1)}, bf16[4,2048,256]{2,1,0:T(8,128)(2,1)}, bf16[8,4,32,1024]{3,2,1,0:T(8,128)(2,1)S(1)}, bf16[8,128,1024]{2,1,0:...) custom-call(s32[1]{0:T(128)S(6)} %copy.69.length_ref, ...), custom_call_target="tpu_custom_call" | custom-call | flops 5033164800 | bytes 16777216 | tf_op jit(solution)/shard_map/attend/pallas_call | solution.py:401
  115.7 1.3 copy-done.2
  117.0 1.3 copy-done.8
  118.3 1.3 copy-done.10
  119.6 1.4 copy-done.11
  121.0 1.0 copy-done.12
  122.0 0.6 copy-done.13
  122.6 0.6 copy-done.14
  123.2 0.6 bitcast_convert_fusion.refs_7_
  123.8 76.2 %mlp.1 = (f32[512,1024]{1,0:T(8,128)}, f32[512,1024]{1,0:T(8,128)}, f32[8,1024]{1,0:T(8,128)}, bf16[4,512,1024]{2,1,0:T(8,128)(2,1)}, bf16[4,512,1024]{2,1,0:T(8...) custom-call(s32[1]{0:T(128)S(6)} %copy.69.length_ref, bf16[2048,256]{1,0:T(8,128)(2,1)} %copy-done.12, ...), custom_call_target="tpu_custom_call" | custom-call | flops 30064771072 | bytes 33554432 | tf_op jit(solution)/shard_map/mlp/pallas_call | solution.py:1515
  200.0 1.9 constant_dynamic-slice_fusion.1.refs_2_
  201.9 74.3 %attend_back.1 = (bf16[2048,768]{1,0:T(8,128)(2,1)}, f32[272,128]{1,0:T(8,128)}, f32[32,4096]{1,0:T(8,128)}, bf16[4,128,1024]{2,1,0:T(8,128)(2,1)}, f32[32,1024]{1,0:T(8,128)}, /*index=5*/bf16[512,1024]{1,0:T(8,128)(2,1)}) custom-call(s32[1]{0:T(128)S(6)} %copy.69.length_ref, bf16[2048,768]{1,0:T(8,128)(2,1)} %convolution_convert_fusion.qkv_ref.refs_0_, ...), custom_call_target="tpu_custom_call" | custom-call | flops 12582912000 | bytes 20971520 | tf_op jit(solution)/shard_map/attend_back/pallas_call | solution.py:837
  276.2 4.1 %fusion.1.refs_2_ = bf16[2048,1024]{1,0:T(8,128)(2,1)} fusion(f32[1024]{0:T(1024)S(1)} %bitcast.124, f32[2048]{0:T(1024)S(1)} %bitcast.125, bf16[4,512,1024]{2,1,0:T(8,128)(2,1)} %get-tuple-element.46.refs_2_), kind=kLoop, calls=%fused_computation.2 | loop fusion | flops 8388608 | bytes 8400896 | tf_op jit(solution)/shard_map/convert_element_type | solution.py:1626
  280.7 68.8 %finish.1 = (f32[512,1024]{1,0:T(8,128)}, f32[32,3072]{1,0:T(8,128)}, f32[128,1024]{1,0:T(8,128)}, f32[272,128]{1,0:T(8,128)}, f32[16,1024]{1,0:T(8,128)}) custom-call(bf16[2048,768]{1,0:T(8,128)(2,1)} %get-tuple-element.68.refs_0_, bf16[1024,768]{1,0:T(8,128)(2,1)} %bitcast.117, bf16[2048,1024]{1,0:T(8,128)(2,1)} %fusion.1.refs_2_, ...), custom_call_target="tpu_custom_call" | custom-call | tf_op jit(solution)/shard_map/finish/pallas_call | solution.py:1269
  349.6 1.0 select_reduce_fusion
  350.7 0.1 reduce_sum.643
  350.8 0.8 slice_reduce_fusion
  351.7 0.1 reduce_sum.646
  352.2 1.0 select_reduce_fusion.2
  353.3 0.1 reduce_sum.410
  353.6 0.1 reduce_sum.494
  353.9 0.1 reduce_sum.500
  354.2 0.1 reduce_sum.503
  354.5 0.1 reduce_sum.610
  354.8 0.1 reduce_sum.613
  355.1 0.1 reduce_sum.616
  355.4 0.1 reduce_sum.619
  356.0 0.1 reduce_sum.625
  356.3 0.1 reduce_sum.628
  356.9 0.1 reduce_sum.634
  357.2 0.1 reduce_sum.637
  357.8 0.1 reduce_sum.419
  358.1 0.1 reduce_sum.425
  358.7 0.1 reduce_sum.434
  359.0 0.1 reduce_sum.440
  360.0 1.0 select_reduce_fusion.1
  361.0 0.1 reduce_sum.455
  361.3 0.1 reduce_sum.458
  361.9 0.1 reduce_sum.470
  362.2 0.1 reduce_sum.473
  363.1 0.1 reduce_sum.488
  363.4 0.1 reduce_sum.640
  363.6 0.7 stack.128
  364.3 1.0 reshape.347
  365.3 0.5 fusion.2
  365.9 1.7 slice.152
  367.5 1.3 subtract_multiply_fusion
  368.8 1.0 copy.70
  369.8 0.8 copy.71
  370.6 1.3 copy.72
  371.9 0.7 copy.73
  372.6 0.7 copy.74
  373.3 0.8 copy.75
  374.1 0.8 copy.76
  (219 shorter events, 7.3 us)
Async XLA Ops:
  0.6 71.9 %copy-start = (bf16[512,1024]{1,0:T(8,128)(2,1)S(1)}, bf16[512,1024]{1,0:T(8,128)(2,1)}, u32[]{:S(2)}) copy-start(bf16[512,1024]{1,0:T(8,128)(2,1)} %param.22) | copy-start | bytes 3145732
  5.4 67.9 %copy-start.3 = (f32[2,1024]{1,0:T(2,128)}, f32[2,1024]{1,0:T(2,128)S(1)}, u32[]{:S(2)}) copy-start(f32[2,1024]{1,0:T(2,128)S(1)} %select_select_fusion.vector_ref.refs_11_) | copy-start | bytes 24580
  62.5 3.3 copy-start.23
  62.5 3.9 %copy-start.15 = (bf16[4,512,1024]{2,1,0:T(8,128)(2,1)S(1)}, bf16[4,512,1024]{2,1,0:T(8,128)(2,1)}, u32[]{:S(2)}) copy-start(bf16[4,512,1024]{2,1,0:T(8,128)(2,1)} %get-tuple-element.46.refs_2_) | copy-start | bytes 12582916
  66.3 1.4 copy-start.17
  67.7 5.5 %copy-start.24 = (f32[2,128]{1,0:T(2,128)S(1)}, f32[2,128]{1,0:T(2,128)}, u32[]{:S(2)}) copy-start(f32[2,128]{1,0:T(2,128)} %param.27) | copy-start | bytes 3076
  67.7 5.5 %copy-start.5 = (bf16[8,32,1024]{2,1,0:T(8,128)(2,1)S(1)}, bf16[8,32,1024]{2,1,0:T(8,128)(2,1)}, u32[]{:S(2)}) copy-start(bf16[8,32,1024]{2,1,0:T(8,128)(2,1)} %get-tuple-element.49.own_out_ref) | copy-start | bytes 1572868
  67.8 5.5 %copy-start.6 = (bf16[1,512,256]{2,1,0:T(8,128)(2,1)S(1)}, bf16[1,512,256]{2,1,0:T(8,128)(2,1)}, u32[]{:S(2)}) copy-start(bf16[1,512,256]{2,1,0:T(8,128)(2,1)} %param.18) | copy-start | bytes 786436
  67.8 5.5 %copy-start.7 = (bf16[2,128,128]{2,1,0:T(8,128)(2,1)S(1)}, bf16[2,128,128]{2,1,0:T(8,128)(2,1)}, u32[]{:S(2)}) copy-start(bf16[2,128,128]{2,1,0:T(8,128)(2,1)} %refs_9_.1) | copy-start | bytes 196612
  73.3 42.4 %copy-start.4 = (f32[2,128]{1,0:T(2,128)}, f32[2,128]{1,0:T(2,128)S(1)}, u32[]{:S(2)}) copy-start(f32[2,128]{1,0:T(2,128)S(1)} %add_divide_fusion) | copy-start | bytes 3076
  73.3 1.9 copy-start.9
  75.2 48.0 %copy-start.25 = (bf16[8,1,128]{2,1,0:T(2,128)(2,1)S(1)}, bf16[8,1,128]{2,1,0:T(2,128)(2,1)}, u32[]{:S(2)}) copy-start(bf16[8,1,128]{2,1,0:T(2,128)(2,1)} %get-tuple-element.56) | copy-start | bytes 6148
  115.7 1.3 copy-start.2
  117.0 1.3 copy-start.8
  118.3 1.3 copy-start.10
  119.6 1.4 copy-start.11
  121.0 1.0 copy-start.12
  122.0 0.6 copy-start.13
  122.6 0.6 copy-start.14
  280.3 69.2 %copy-start.57 = (pred[4,128]{1,0:T(4,128)(4,1)S(1)}, pred[4,128]{1,0:T(4,128)(4,1)}, u32[]{:S(2)}) copy-start(pred[4,128]{1,0:T(4,128)(4,1)} %constant.178) | copy-start | bytes 1540
  280.3 69.2 %copy-start.56 = (pred[4,128]{1,0:T(4,128)(4,1)S(1)}, pred[4,128]{1,0:T(4,128)(4,1)}, u32[]{:S(2)}) copy-start(pred[4,128]{1,0:T(4,128)(4,1)} %constant.180) | copy-start | bytes 1540
  280.3 69.2 %copy-start.55 = (pred[4,128]{1,0:T(4,128)(4,1)S(1)}, pred[4,128]{1,0:T(4,128)(4,1)}, u32[]{:S(2)}) copy-start(pred[4,128]{1,0:T(4,128)(4,1)} %constant.182) | copy-start | bytes 1540
  280.3 69.2 %copy-start.54 = (pred[4,128]{1,0:T(4,128)(4,1)S(1)}, pred[4,128]{1,0:T(4,128)(4,1)}, u32[]{:S(2)}) copy-start(pred[4,128]{1,0:T(4,128)(4,1)} %constant.184) | copy-start | bytes 1540
  280.3 69.2 %copy-start.53 = (pred[4,128]{1,0:T(4,128)(4,1)S(1)}, pred[4,128]{1,0:T(4,128)(4,1)}, u32[]{:S(2)}) copy-start(pred[4,128]{1,0:T(4,128)(4,1)} %constant.186) | copy-start | bytes 1540
  280.3 69.2 %copy-start.52 = (pred[4,128]{1,0:T(4,128)(4,1)S(1)}, pred[4,128]{1,0:T(4,128)(4,1)}, u32[]{:S(2)}) copy-start(pred[4,128]{1,0:T(4,128)(4,1)} %constant.188) | copy-start | bytes 1540
  280.3 69.3 %copy-start.51 = (pred[4,128]{1,0:T(4,128)(4,1)S(1)}, pred[4,128]{1,0:T(4,128)(4,1)}, u32[]{:S(2)}) copy-start(pred[4,128]{1,0:T(4,128)(4,1)} %constant.190) | copy-start | bytes 1540
  280.3 69.3 %copy-start.50 = (pred[4,128]{1,0:T(4,128)(4,1)S(1)}, pred[4,128]{1,0:T(4,128)(4,1)}, u32[]{:S(2)}) copy-start(pred[4,128]{1,0:T(4,128)(4,1)} %constant.192) | copy-start | bytes 1540
  280.3 69.3 %copy-start.49 = (pred[4,128]{1,0:T(4,128)(4,1)S(1)}, pred[4,128]{1,0:T(4,128)(4,1)}, u32[]{:S(2)}) copy-start(pred[4,128]{1,0:T(4,128)(4,1)} %constant.238) | copy-start | bytes 1540
  280.4 71.6 %copy-start.48 = (pred[4,128]{1,0:T(4,128)(4,1)S(1)}, pred[4,128]{1,0:T(4,128)(4,1)}, u32[]{:S(2)}) copy-start(pred[4,128]{1,0:T(4,128)(4,1)} %constant.176) | copy-start | bytes 1540
  280.4 71.5 %copy-start.47 = (pred[4,128]{1,0:T(4,128)(4,1)S(1)}, pred[4,128]{1,0:T(4,128)(4,1)}, u32[]{:S(2)}) copy-start(pred[4,128]{1,0:T(4,128)(4,1)} %constant.210) | copy-start | bytes 1540
  280.4 71.5 %copy-start.46 = (pred[4,128]{1,0:T(4,128)(4,1)S(1)}, pred[4,128]{1,0:T(4,128)(4,1)}, u32[]{:S(2)}) copy-start(pred[4,128]{1,0:T(4,128)(4,1)} %constant.212) | copy-start | bytes 1540
  280.4 71.6 %copy-start.45 = (pred[4,128]{1,0:T(4,128)(4,1)S(1)}, pred[4,128]{1,0:T(4,128)(4,1)}, u32[]{:S(2)}) copy-start(pred[4,128]{1,0:T(4,128)(4,1)} %constant.214) | copy-start | bytes 1540
  280.4 71.6 %copy-start.44 = (pred[4,128]{1,0:T(4,128)(4,1)S(1)}, pred[4,128]{1,0:T(4,128)(4,1)}, u32[]{:S(2)}) copy-start(pred[4,128]{1,0:T(4,128)(4,1)} %constant.216) | copy-start | bytes 1540
  280.4 71.6 %copy-start.43 = (pred[4,128]{1,0:T(4,128)(4,1)S(1)}, pred[4,128]{1,0:T(4,128)(4,1)}, u32[]{:S(2)}) copy-start(pred[4,128]{1,0:T(4,128)(4,1)} %constant.218) | copy-start | bytes 1540
  280.4 71.6 %copy-start.42 = (pred[4,128]{1,0:T(4,128)(4,1)S(1)}, pred[4,128]{1,0:T(4,128)(4,1)}, u32[]{:S(2)}) copy-start(pred[4,128]{1,0:T(4,128)(4,1)} %constant.220) | copy-start | bytes 1540
  280.4 71.6 %copy-start.41 = (pred[4,128]{1,0:T(4,128)(4,1)S(1)}, pred[4,128]{1,0:T(4,128)(4,1)}, u32[]{:S(2)}) copy-start(pred[4,128]{1,0:T(4,128)(4,1)} %constant.222) | copy-start | bytes 1540
  280.5 71.6 %copy-start.40 = (pred[4,128]{1,0:T(4,128)(4,1)S(1)}, pred[4,128]{1,0:T(4,128)(4,1)}, u32[]{:S(2)}) copy-start(pred[4,128]{1,0:T(4,128)(4,1)} %constant.224) | copy-start | bytes 1540
  280.5 71.6 %copy-start.39 = (pred[4,128]{1,0:T(4,128)(4,1)S(1)}, pred[4,128]{1,0:T(4,128)(4,1)}, u32[]{:S(2)}) copy-start(pred[4,128]{1,0:T(4,128)(4,1)} %constant.226) | copy-start | bytes 1540
  280.5 71.6 %copy-start.38 = (pred[4,128]{1,0:T(4,128)(4,1)S(1)}, pred[4,128]{1,0:T(4,128)(4,1)}, u32[]{:S(2)}) copy-start(pred[4,128]{1,0:T(4,128)(4,1)} %constant.228) | copy-start | bytes 1540
  280.5 71.6 %copy-start.37 = (pred[4,128]{1,0:T(4,128)(4,1)S(1)}, pred[4,128]{1,0:T(4,128)(4,1)}, u32[]{:S(2)}) copy-start(pred[4,128]{1,0:T(4,128)(4,1)} %constant.230) | copy-start | bytes 1540
  280.5 71.6 %copy-start.36 = (pred[4,128]{1,0:T(4,128)(4,1)S(1)}, pred[4,128]{1,0:T(4,128)(4,1)}, u32[]{:S(2)}) copy-start(pred[4,128]{1,0:T(4,128)(4,1)} %constant.232) | copy-start | bytes 1540
  280.5 71.6 %copy-start.35 = (pred[4,128]{1,0:T(4,128)(4,1)S(1)}, pred[4,128]{1,0:T(4,128)(4,1)}, u32[]{:S(2)}) copy-start(pred[4,128]{1,0:T(4,128)(4,1)} %constant.234) | copy-start | bytes 1540
  280.5 79.3 %copy-start.34 = (pred[4,128]{1,0:T(4,128)(4,1)S(1)}, pred[4,128]{1,0:T(4,128)(4,1)}, u32[]{:S(2)}) copy-start(pred[4,128]{1,0:T(4,128)(4,1)} %constant.194) | copy-start | bytes 1540
  280.5 79.3 %copy-start.33 = (pred[4,128]{1,0:T(4,128)(4,1)S(1)}, pred[4,128]{1,0:T(4,128)(4,1)}, u32[]{:S(2)}) copy-start(pred[4,128]{1,0:T(4,128)(4,1)} %constant.196) | copy-start | bytes 1540
  280.6 79.3 %copy-start.32 = (pred[4,128]{1,0:T(4,128)(4,1)S(1)}, pred[4,128]{1,0:T(4,128)(4,1)}, u32[]{:S(2)}) copy-start(pred[4,128]{1,0:T(4,128)(4,1)} %constant.198) | copy-start | bytes 1540
  280.6 79.3 %copy-start.31 = (pred[4,128]{1,0:T(4,128)(4,1)S(1)}, pred[4,128]{1,0:T(4,128)(4,1)}, u32[]{:S(2)}) copy-start(pred[4,128]{1,0:T(4,128)(4,1)} %constant.200) | copy-start | bytes 1540
  280.6 79.3 %copy-start.30 = (pred[4,128]{1,0:T(4,128)(4,1)S(1)}, pred[4,128]{1,0:T(4,128)(4,1)}, u32[]{:S(2)}) copy-start(pred[4,128]{1,0:T(4,128)(4,1)} %constant.202) | copy-start | bytes 1540
  280.6 79.3 %copy-start.29 = (pred[4,128]{1,0:T(4,128)(4,1)S(1)}, pred[4,128]{1,0:T(4,128)(4,1)}, u32[]{:S(2)}) copy-start(pred[4,128]{1,0:T(4,128)(4,1)} %constant.204) | copy-start | bytes 1540
  280.6 79.3 %copy-start.28 = (pred[4,128]{1,0:T(4,128)(4,1)S(1)}, pred[4,128]{1,0:T(4,128)(4,1)}, u32[]{:S(2)}) copy-start(pred[4,128]{1,0:T(4,128)(4,1)} %constant.206) | copy-start | bytes 1540
  280.6 79.3 %copy-start.27 = (pred[4,128]{1,0:T(4,128)(4,1)S(1)}, pred[4,128]{1,0:T(4,128)(4,1)}, u32[]{:S(2)}) copy-start(pred[4,128]{1,0:T(4,128)(4,1)} %constant.208) | copy-start | bytes 1540
  280.6 79.3 %copy-start.26 = (pred[4,128]{1,0:T(4,128)(4,1)S(1)}, pred[4,128]{1,0:T(4,128)(4,1)}, u32[]{:S(2)}) copy-start(pred[4,128]{1,0:T(4,128)(4,1)} %constant.236) | copy-start | bytes 1540
  280.6 88.1 %copy-start.18 = (bf16[512,1024]{1,0:T(8,128)(2,1)S(1)}, bf16[512,1024]{1,0:T(8,128)(2,1)}, u32[]{:S(2)}) copy-start(bf16[512,1024]{1,0:T(8,128)(2,1)} %get-tuple-element.66) | copy-start | bytes 3145732
  361.2 10.7 %copy-start.21 = (f32[32,3072]{1,0:T(8,128)S(1)}, f32[32,3072]{1,0:T(8,128)}, u32[]{:S(2)}) copy-start(f32[32,3072]{1,0:T(8,128)} %get-tuple-element.182) | copy-start | bytes 1179652
  365.3 5.2 %copy-start.16 = (f32[512,1024]{1,0:T(8,128)S(1)}, f32[512,1024]{1,0:T(8,128)}, u32[]{:S(2)}) copy-start(f32[512,1024]{1,0:T(8,128)} %get-tuple-element.73) | copy-start | bytes 6291460
  365.9 6.8 %copy-start.22 = (f32[32,1024]{1,0:T(8,128)S(1)}, f32[32,1024]{1,0:T(8,128)}, u32[]{:S(2)}) copy-start(f32[32,1024]{1,0:T(8,128)} %get-tuple-element.183) | copy-start | bytes 393220
  368.8 4.5 %copy-start.19 = (f32[32,4096]{1,0:T(8,128)S(1)}, f32[32,4096]{1,0:T(8,128)}, u32[]{:S(2)}) copy-start(f32[32,4096]{1,0:T(8,128)} %get-tuple-element.184) | copy-start | bytes 1572868
  368.8 5.3 %copy-start.20 = (f32[128,1024]{1,0:T(8,128)S(1)}, f32[128,1024]{1,0:T(8,128)}, u32[]{:S(2)}) copy-start(f32[128,1024]{1,0:T(8,128)} %get-tuple-element.185) | copy-start | bytes 1572868
  368.8 6.1 %copy-start.1 = (bf16[512,1024]{1,0:T(8,128)(2,1)S(1)}, bf16[512,1024]{1,0:T(8,128)(2,1)}, u32[]{:S(2)}) copy-start(bf16[512,1024]{1,0:T(8,128)(2,1)} %param.22) | copy-start | bytes 3145732
